TPU v7x, 32 devices: a whole 2x2x4 slice. The times are simulated.
32 devices in a mesh: shard: 4 (over z), ctx: 4 (over y, x), tp: 2 (over core).
Axes of the slice: x: 2, y: 2, z: 4, core: 2. Of those that a mesh axis runs over, the one named last changes fastest.
Arguments:
- inputs: float32 [16, 2048, 768], P(('shard', 'tp'), 'ctx'), may hold values from -6 to 6
- cotangent: float32 [16, 2048, 768], P(('shard', 'tp'), 'ctx'), may hold values from -6 to 6
- rand_blocks: int32 [12, 30, 3], replicated, may hold values from 1 to 30, as said below
- slot_of: int32 [12], replicated, may hold values from 0 to 11, as said below
- master: float32 [12, 768, 768], P('shard', ('ctx', 'tp'))
- moment_one: float32 [12, 768, 768], P('shard', ('ctx', 'tp'))
- moment_two: float32 [12, 768, 768], P('shard', ('ctx', 'tp')), as said below
- small_params: float32 [9216], P(('shard', 'ctx', 'tp'))
- small_one: float32 [9216], P(('shard', 'ctx', 'tp'))
- small_two: float32 [9216], P(('shard', 'ctx', 'tp')), as said below
Outputs:
- layer_out: float32 [16, 2048, 768], P(('shard', 'tp'), 'ctx')
- input_grad: float32 [16, 2048, 768], P(('shard', 'tp'), 'ctx')
- master_new: float32 [12, 768, 768], P('shard', ('ctx', 'tp'))
- moment_one_new: float32 [12, 768, 768], P('shard', ('ctx', 'tp'))
- moment_two_new: float32 [12, 768, 768], P('shard', ('ctx', 'tp'))
- small_new: float32 [9216], P(('shard', 'ctx', 'tp'))
- small_one_new: float32 [9216], P(('shard', 'ctx', 'tp'))
- small_two_new: float32 [9216], P(('shard', 'ctx', 'tp'))
Inputs may be any that keep to these rules, and one draw needn't show every extreme that they name: For head h and middle query block i (1 to 30), rand_blocks[h, i - 1] names three different key blocks, none of them 0, 31, i - 1, i or i + 1. `slot_of`: the 12 entries name different slots; slot s belongs to index s // 3 of the shard axis; some index holds exactly 3 matrices, the others as many as the draw gives. `moment_two`: every entry is positive. `small_two`: every entry is positive.
All inputs are finite; a program needn't handle non-finite values.
Results may differ from a plain program's by a relative error of at most 0.023.
Values may be sent and summed in bfloat16 or wider, within the bound.
A program may use at most 256 MiB of HBM per device.

v0:
```python
import jax
import jax.numpy as jnp
from jax import lax
from jax.sharding import PartitionSpec as P

FF = 3072
BLOCK = 64
STEP = 5


highest = lax.Precision.HIGHEST
norm_eps = 1e-12
beta_one = 0.9
beta_two = 0.999
adam_eps = 1e-08
rate_value = 0.04
small_rate = 0.25
score_scale = 0.125
masked_score = -1e30


def layer_norm(field, gain, shift):
    centred = field - jnp.mean(field, axis=-1, keepdims=True)
    spread = jnp.mean(centred * centred, axis=-1, keepdims=True)
    return centred * lax.rsqrt(spread + norm_eps) * gain + shift


def gelu_tanh(field):
    return jax.nn.gelu(field, approximate=True)


def split_small(params, model_width):
    ffn_width = params.shape[0] - 8 * model_width
    pieces = [params[index * model_width : (index + 1) * model_width] for index in range(5)]
    up_start = 5 * model_width
    pieces.append(params[up_start : up_start + ffn_width])
    tail_start = up_start + ffn_width
    for index in range(3):
        pieces.append(
            params[tail_start + index * model_width : tail_start + (index + 1) * model_width]
        )
    return tuple(pieces)


def adam_update(weight, first, second, grad, decay, rate):
    count = float(STEP)
    first_new = beta_one * first + (1.0 - beta_one) * grad
    second_new = beta_two * second + (1.0 - beta_two) * grad * grad
    first_hat = first_new / (1.0 - beta_one**count)
    second_hat = second_new / (1.0 - beta_two**count)
    weight_new = weight - rate * (first_hat / (jnp.sqrt(second_hat) + adam_eps) + decay * weight)
    return (weight_new, first_new, second_new)


def take_blocks(blocks, key_picks):

    def pick_one(source, chosen):
        return jnp.take(source, chosen, axis=1)

    return jax.vmap(pick_one)(blocks, key_picks)


def attend_forward(query_seq, key_seq, value_seq, key_picks, valid_keys, head_dim):
    groups = key_picks.shape[0]
    middle = key_picks.shape[1]
    nblocks = middle + 2
    shaped = (groups, head_dim, nblocks, -1)
    query_blocks = query_seq.reshape(shaped)
    key_blocks = key_seq.reshape(shaped)
    value_blocks = value_seq.reshape(shaped)
    query_mid = query_blocks[:, :, 1 : nblocks - 1]
    key_mid = take_blocks(key_blocks, key_picks).reshape(groups, head_dim, middle, -1)
    value_mid = take_blocks(value_blocks, key_picks).reshape(groups, head_dim, middle, -1)
    score_mid = (
        jnp.einsum("gdmq,gdmk->gmqk", query_mid, key_mid, preferred_element_type=jnp.float32)
        * score_scale
    )
    score_mid = jnp.where(valid_keys[None, :, None, :], score_mid, masked_score)
    total_mid = jax.nn.logsumexp(score_mid, axis=-1)
    prob_mid = jnp.exp(score_mid - total_mid[..., None]).astype(jnp.bfloat16)
    out_mid = jnp.einsum("gmqk,gdmk->gdmq", prob_mid, value_mid, preferred_element_type=jnp.float32)
    query_edge = jnp.stack([query_blocks[:, :, 0], query_blocks[:, :, nblocks - 1]], axis=2)
    key_full = key_seq.reshape(groups, head_dim, -1)
    value_full = value_seq.reshape(groups, head_dim, -1)
    score_edge = (
        jnp.einsum("gdtq,gdk->gtqk", query_edge, key_full, preferred_element_type=jnp.float32)
        * score_scale
    )
    total_edge = jax.nn.logsumexp(score_edge, axis=-1)
    prob_edge = jnp.exp(score_edge - total_edge[..., None]).astype(jnp.bfloat16)
    out_edge = jnp.einsum(
        "gtqk,gdk->gdtq", prob_edge, value_full, preferred_element_type=jnp.float32
    )
    outputs = jnp.concatenate([out_edge[:, :, :1], out_mid, out_edge[:, :, 1:]], axis=2)
    totals = jnp.concatenate([total_edge[:, :1], total_mid, total_edge[:, 1:]], axis=1)
    return (outputs.astype(jnp.bfloat16).reshape(groups * head_dim, -1), totals.reshape(groups, -1))


def attend_backward(
    query_seq, key_seq, value_seq, total_seq, grad_seq, key_picks, valid_keys, placer, head_dim
):
    groups = key_picks.shape[0]
    middle = key_picks.shape[1]
    nblocks = middle + 2
    shaped = (groups, head_dim, nblocks, -1)
    query_blocks = query_seq.reshape(shaped)
    key_blocks = key_seq.reshape(shaped)
    value_blocks = value_seq.reshape(shaped)
    grad_blocks = grad_seq.reshape(shaped)
    total_blocks = total_seq.reshape(groups, nblocks, -1)
    query_mid = query_blocks[:, :, 1 : nblocks - 1]
    grad_mid = grad_blocks[:, :, 1 : nblocks - 1]
    key_mid = take_blocks(key_blocks, key_picks).reshape(groups, head_dim, middle, -1)
    value_mid = take_blocks(value_blocks, key_picks).reshape(groups, head_dim, middle, -1)
    score_mid = (
        jnp.einsum("gdmq,gdmk->gmqk", query_mid, key_mid, preferred_element_type=jnp.float32)
        * score_scale
    )
    score_mid = jnp.where(valid_keys[None, :, None, :], score_mid, masked_score)
    prob_mid = jnp.exp(score_mid - total_blocks[:, 1 : nblocks - 1, :, None])
    gp_mid = jnp.einsum("gdmq,gdmk->gmqk", grad_mid, value_mid, preferred_element_type=jnp.float32)
    delta_mid = jnp.sum(prob_mid * gp_mid, axis=-1, keepdims=True)
    ds_mid = (prob_mid * (gp_mid - delta_mid)).astype(jnp.bfloat16)
    dq_mid = (
        jnp.einsum("gmqk,gdmk->gdmq", ds_mid, key_mid, preferred_element_type=jnp.float32)
        * score_scale
    )
    dk_picked = (
        jnp.einsum("gmqk,gdmq->gdmk", ds_mid, query_mid, preferred_element_type=jnp.float32)
        * score_scale
    )
    dv_picked = jnp.einsum(
        "gmqk,gdmq->gdmk",
        prob_mid.astype(jnp.bfloat16),
        grad_mid,
        preferred_element_type=jnp.float32,
    )
    picked_shape = (groups, head_dim, middle, key_picks.shape[2], -1)
    dk_mid = jnp.einsum(
        "gdmkb,gmkn->gdnb", dk_picked.reshape(picked_shape), placer, precision=highest
    )
    dv_mid = jnp.einsum(
        "gdmkb,gmkn->gdnb", dv_picked.reshape(picked_shape), placer, precision=highest
    )
    query_edge = jnp.stack([query_blocks[:, :, 0], query_blocks[:, :, nblocks - 1]], axis=2)
    grad_edge = jnp.stack([grad_blocks[:, :, 0], grad_blocks[:, :, nblocks - 1]], axis=2)
    total_edge = jnp.stack([total_blocks[:, 0], total_blocks[:, nblocks - 1]], axis=1)
    key_full = key_seq.reshape(groups, head_dim, -1)
    value_full = value_seq.reshape(groups, head_dim, -1)
    score_edge = (
        jnp.einsum("gdtq,gdk->gtqk", query_edge, key_full, preferred_element_type=jnp.float32)
        * score_scale
    )
    prob_edge = jnp.exp(score_edge - total_edge[..., None])
    gp_edge = jnp.einsum(
        "gdtq,gdk->gtqk", grad_edge, value_full, preferred_element_type=jnp.float32
    )
    delta_edge = jnp.sum(prob_edge * gp_edge, axis=-1, keepdims=True)
    ds_edge = (prob_edge * (gp_edge - delta_edge)).astype(jnp.bfloat16)
    dq_edge = (
        jnp.einsum("gtqk,gdk->gdtq", ds_edge, key_full, preferred_element_type=jnp.float32)
        * score_scale
    )
    dk_edge = (
        jnp.einsum("gtqk,gdtq->gdk", ds_edge, query_edge, preferred_element_type=jnp.float32)
        * score_scale
    )
    dv_edge = jnp.einsum(
        "gtqk,gdtq->gdk",
        prob_edge.astype(jnp.bfloat16),
        grad_edge,
        preferred_element_type=jnp.float32,
    )
    grad_query = jnp.concatenate([dq_edge[:, :, :1], dq_mid, dq_edge[:, :, 1:]], axis=2).reshape(
        groups * head_dim, -1
    )
    grad_key = (dk_mid.reshape(groups, head_dim, -1) + dk_edge).reshape(groups * head_dim, -1)
    grad_value = (dv_mid.reshape(groups, head_dim, -1) + dv_edge).reshape(groups * head_dim, -1)
    return (
        grad_query.astype(jnp.bfloat16),
        grad_key.astype(jnp.bfloat16),
        grad_value.astype(jnp.bfloat16),
    )


def shards(
    inputs,
    cotangent,
    rand_blocks,
    slot_of,
    master,
    moment_one,
    moment_two,
    small_params,
    small_one,
    small_two,
):
    n_shard = lax.axis_size("shard")
    n_ctx = lax.axis_size("ctx")
    n_tp = lax.axis_size("tp")
    seq_count, piece_len, model_width = inputs.shape
    head_count = rand_blocks.shape[0]
    head_dim = model_width // head_count
    groups = head_count // n_ctx
    seq_len = piece_len * n_ctx
    nblocks = seq_len // BLOCK
    middle = nblocks - 2
    ffn_blocks = FF // model_width
    slots_all = master.shape[0] * n_shard
    small_span = small_params.shape[0]
    tok_count = seq_count * piece_len
    picker = (slot_of[:, None] == jnp.arange(slots_all, dtype=jnp.int32)[None, :]).astype(
        jnp.float32
    )
    slot_rows, small_rows = (
        lax.all_gather(master.astype(jnp.bfloat16), "shard", axis=0, tiled=True),
        lax.all_gather(
            small_params.astype(jnp.bfloat16).reshape(1, 1, small_span), "shard", axis=0, tiled=True
        ),
    )
    chosen = jnp.einsum(
        "ms,srd->mrd", picker.astype(jnp.bfloat16), slot_rows, preferred_element_type=jnp.float32
    ).astype(jnp.bfloat16)
    matrices, small_whole = (
        lax.all_gather(chosen, ("ctx", "tp"), axis=1, tiled=True),
        lax.all_gather(small_rows, ("ctx", "tp"), axis=1, tiled=True),
    )
    params = small_whole.reshape(-1).astype(jnp.float32)
    q_bias, v_bias, o_bias, gain_one, shift_one, up_bias, down_bias, gain_two, shift_two = (
        split_small(params, model_width)
    )
    up_weights = matrices[4 : 4 + ffn_blocks]
    down_weights = matrices[4 + ffn_blocks : 4 + 2 * ffn_blocks]
    head_table = lax.dynamic_slice_in_dim(rand_blocks, lax.axis_index("ctx") * groups, groups, 0)
    middle_ids = jnp.arange(1, nblocks - 1, dtype=jnp.int32)
    fixed_ids = jnp.stack(
        [
            jnp.zeros_like(middle_ids),
            jnp.full_like(middle_ids, nblocks - 1),
            middle_ids - 1,
            middle_ids,
            middle_ids + 1,
        ],
        axis=1,
    )
    key_picks = jnp.concatenate(
        [jnp.broadcast_to(fixed_ids[None], (groups, middle, 5)), head_table], axis=2
    )
    always_on = jnp.ones((middle,), dtype=bool)
    fixed_valid = jnp.stack(
        [always_on, always_on, middle_ids - 1 != 0, always_on, middle_ids + 1 != nblocks - 1],
        axis=1,
    )
    valid_blocks = jnp.concatenate(
        [fixed_valid, jnp.ones((middle, head_table.shape[2]), dtype=bool)], axis=1
    )
    valid_keys = jnp.repeat(valid_blocks, BLOCK, axis=1)
    placer = (key_picks[..., None] == jnp.arange(nblocks, dtype=jnp.int32)).astype(jnp.float32)
    x_low = inputs.astype(jnp.bfloat16)

    def project(weight):
        return jnp.einsum("spd,de->sep", x_low, weight, preferred_element_type=jnp.float32)

    query_piece = (project(matrices[0]) + q_bias[None, :, None]).astype(jnp.bfloat16)
    key_piece = project(matrices[1]).astype(jnp.bfloat16)
    value_piece = (project(matrices[2]) + v_bias[None, :, None]).astype(jnp.bfloat16)
    query_heads, key_heads, value_heads = (
        lax.all_to_all(query_piece, "ctx", split_axis=1, concat_axis=2, tiled=True),
        lax.all_to_all(key_piece, "ctx", split_axis=1, concat_axis=2, tiled=True),
        lax.all_to_all(value_piece, "ctx", split_axis=1, concat_axis=2, tiled=True),
    )

    def forward_seq(parts):
        return attend_forward(parts[0], parts[1], parts[2], key_picks, valid_keys, head_dim)

    context_heads, totals = lax.map(forward_seq, (query_heads, key_heads, value_heads))
    context = lax.all_to_all(context_heads, "ctx", split_axis=2, concat_axis=1, tiled=True)
    attn_out = (
        jnp.einsum("sep,ef->spf", context, matrices[3], preferred_element_type=jnp.float32) + o_bias
    )
    after_attn, norm_one_pull = jax.vjp(layer_norm, inputs + attn_out, gain_one, shift_one)
    ffn_in = after_attn.astype(jnp.bfloat16).reshape(tok_count, model_width)
    up_proj = jnp.einsum(
        "td,bdh->tbh", ffn_in, up_weights, preferred_element_type=jnp.float32
    ) + up_bias.reshape(ffn_blocks, model_width)
    up_act, gelu_pull = jax.vjp(gelu_tanh, up_proj)
    hidden = up_act.astype(jnp.bfloat16)
    ffn_out = (
        jnp.einsum("tbh,beh->te", hidden, down_weights, preferred_element_type=jnp.float32)
        + down_bias
    )
    layer_out, norm_two_pull = jax.vjp(
        layer_norm,
        after_attn + ffn_out.reshape(seq_count, piece_len, model_width),
        gain_two,
        shift_two,
    )
    grad_h2, grad_gain_two, grad_shift_two = norm_two_pull(cotangent)
    grad_mixed = grad_h2.astype(jnp.bfloat16).reshape(tok_count, model_width)
    grad_down_bias = jnp.sum(grad_mixed, axis=0, dtype=jnp.float32)
    ffn_stack = None
    grad_hidden = jnp.einsum(
        "te,beh->tbh", grad_mixed, down_weights, preferred_element_type=jnp.float32
    )
    grad_down = jnp.einsum("te,tbh->beh", grad_mixed, hidden, preferred_element_type=jnp.float32)
    grad_up_proj = gelu_pull(grad_hidden)[0].astype(jnp.bfloat16)
    grad_up_bias = jnp.sum(grad_up_proj, axis=0, dtype=jnp.float32)
    grad_up = jnp.einsum("td,tbh->bdh", ffn_in, grad_up_proj, preferred_element_type=jnp.float32)
    grad_ffn_in = jnp.einsum(
        "tbh,bdh->td", grad_up_proj, up_weights, preferred_element_type=jnp.float32
    )
    ffn_stack = jnp.concatenate([grad_up, grad_down], axis=0)
    grad_y = grad_h2 + grad_ffn_in.reshape(seq_count, piece_len, model_width)
    grad_h1, grad_gain_one, grad_shift_one = norm_one_pull(grad_y)
    grad_attn = grad_h1.astype(jnp.bfloat16)
    grad_o_bias = jnp.sum(grad_attn, axis=(0, 1), dtype=jnp.float32)
    grad_wo = jnp.einsum("sep,spf->ef", context, grad_attn, preferred_element_type=jnp.float32)
    grad_context = jnp.einsum(
        "spf,ef->sep", grad_attn, matrices[3], preferred_element_type=jnp.float32
    ).astype(jnp.bfloat16)
    grad_context_heads = lax.all_to_all(
        grad_context, "ctx", split_axis=1, concat_axis=2, tiled=True
    )

    def backward_seq(parts):
        return attend_backward(
            parts[0],
            parts[1],
            parts[2],
            parts[3],
            parts[4],
            key_picks,
            valid_keys,
            placer,
            head_dim,
        )

    grad_q_heads, grad_k_heads, grad_v_heads = lax.map(
        backward_seq, (query_heads, key_heads, value_heads, totals, grad_context_heads)
    )
    grad_query, grad_key, grad_value = (
        lax.all_to_all(grad_q_heads, "ctx", split_axis=2, concat_axis=1, tiled=True),
        lax.all_to_all(grad_k_heads, "ctx", split_axis=2, concat_axis=1, tiled=True),
        lax.all_to_all(grad_v_heads, "ctx", split_axis=2, concat_axis=1, tiled=True),
    )
    grad_q_bias = jnp.sum(grad_query, axis=(0, 2), dtype=jnp.float32)
    grad_v_bias = jnp.sum(grad_value, axis=(0, 2), dtype=jnp.float32)

    def weight_grad(grad_proj):
        return jnp.einsum("spd,sep->de", x_low, grad_proj, preferred_element_type=jnp.float32)

    def input_part(grad_proj, weight):
        return jnp.einsum("sep,de->spd", grad_proj, weight, preferred_element_type=jnp.float32)

    input_grad = (
        grad_h1
        + input_part(grad_query, matrices[0])
        + input_part(grad_key, matrices[1])
        + input_part(grad_value, matrices[2])
    )
    attn_grads = jnp.stack(
        [weight_grad(grad_query), weight_grad(grad_key), weight_grad(grad_value), grad_wo], axis=0
    )
    small_grad = jnp.concatenate(
        [
            grad_q_bias,
            grad_v_bias,
            grad_o_bias,
            grad_gain_one,
            grad_shift_one,
            grad_up_bias.reshape(-1),
            grad_down_bias,
            grad_gain_two,
            grad_shift_two,
        ]
    )
    small_grid = small_grad.reshape(n_shard, n_ctx * n_tp, small_span)
    grad_stack = jnp.concatenate([attn_grads, ffn_stack], axis=0)
    summed_rows, small_summed = (
        lax.psum_scatter(
            grad_stack.astype(jnp.bfloat16), ("ctx", "tp"), scatter_dimension=1, tiled=True
        ).astype(jnp.float32),
        lax.psum_scatter(
            small_grid.astype(jnp.bfloat16), ("ctx", "tp"), scatter_dimension=1, tiled=True
        ).astype(jnp.float32),
    )
    packed = jnp.einsum("ms,mrd->srd", picker, summed_rows, precision=highest)
    slot_grads, small_owned = (
        lax.psum_scatter(
            packed.astype(jnp.bfloat16), "shard", scatter_dimension=0, tiled=True
        ).astype(jnp.float32),
        lax.psum_scatter(
            small_summed.astype(jnp.bfloat16), "shard", scatter_dimension=0, tiled=True
        ).astype(jnp.float32),
    )
    master_new, first_new, second_new = adam_update(
        master, moment_one, moment_two, slot_grads, 0.01, rate_value
    )
    small_new, small_first, small_second = adam_update(
        small_params, small_one, small_two, small_owned.reshape(-1), 0.0, small_rate
    )
    return (
        layer_out,
        input_grad,
        master_new,
        first_new,
        second_new,
        small_new,
        small_first,
        small_second,
    )


def solution(mesh):
    placed = (
        P(("shard", "tp"), "ctx", None),
        P(("shard", "tp"), "ctx", None),
        P(),
        P(),
        P("shard", ("ctx", "tp"), None),
        P("shard", ("ctx", "tp"), None),
        P("shard", ("ctx", "tp"), None),
        P(("shard", "ctx", "tp")),
        P(("shard", "ctx", "tp")),
        P(("shard", "ctx", "tp")),
    )
    return jax.shard_map(
        shards,
        mesh=mesh,
        in_specs=placed,
        out_specs=(
            P(("shard", "tp"), "ctx", None),
            P(("shard", "tp"), "ctx", None),
            P("shard", ("ctx", "tp"), None),
            P("shard", ("ctx", "tp"), None),
            P("shard", ("ctx", "tp"), None),
            P(("shard", "ctx", "tp")),
            P(("shard", "ctx", "tp")),
            P(("shard", "ctx", "tp")),
        ),
        check_vma=False,
    )
```

profile of v0, /device:TPU:0, one launch (start us, length us, event | category | flops | bytes accessed | tf_op | source)
XLA Modules:
  0.0 1625.7 jit_solution(16393668700588255389)
XLA Ops:
  9.3 43.9 %all-gather.4.cloned.1.call-done = bf16[12,96,768]{2,1,0:T(8,128)(2,1)} async-done(((bf16[3,96,768]{2,1,0:T(8,128)(2,1)}), bf16[12,96,768]{2,1,0:T(8,128)(2,1)}) %all-gather.4.cloned.1.call-update) | async-done | bytes 1769488 | tf_op jit(solution)/shard_map/all_gather | solution.py:216
  59.4 9.8 all-reduce
  69.2 8.9 all_gather.15
  80.7 54.9 %all-gather.6.cloned.1.call-done = bf16[12,768,768]{2,1,0:T(8,128)(2,1)} async-done(((bf16[12,96,768]{2,1,0:T(8,128)(2,1)}), bf16[12,768,768]{2,1,0:T(8,128)(2,1)}) %all-gather.6.cloned.1.call-update) | async-done | bytes 14155792 | tf_op jit(solution)/shard_map/all_gather | solution.py:225
  150.8 14.4 all-to-all-done
  175.0 13.1 all-to-all-done.1
  217.6 286.6 %while.29 = (s32[]{:T(128)}, bf16[2,192,2048]{2,1,0:T(8,128)(2,1)}, f32[2,3,2048]{2,1,0:T(4,128)S(1)}, bf16[2,192,2048]{2,1,0:T(8,128)(2,1)}, bf16[2,192,2048]{2...) while((s32[]{:T(128)}, bf16[2,192,2048]{2,1,0:T(8,128)(2,1)}, ...), condition=%wide.region_5.7_spmd.clone, body=%wide.region_0.6_spmd.clone.sunk | while | flops 1000609664 | bytes 243318960 | solution.py:276
  246.8 10.6 gather_fusion
  262.9 10.8 gather_fusion.1
  273.6 13.2 select_bitcast_fusion.6
  286.8 12.5 copy.466
  299.3 16.3 %reshape.491 = bf16[3,64,30,512]{3,1,2,0:T(8,128)(2,1)} reshape(bf16[3,64,30,8,64]{4,3,1,2,0:T(8,128)(2,1)} %copy.466) | data formatting | bytes 11796480 | tf_op jit(solution)/shard_map/while/body/eval_jaxpr/reshape | solution.py:73
  315.9 15.1 copy.467
  331.0 16.3 %reshape.492 = bf16[3,64,30,512]{3,1,2,0:T(8,128)(2,1)} reshape(bf16[3,64,30,8,64]{4,3,1,2,0:T(8,128)(2,1)} %copy.467) | data formatting | bytes 11796480 | tf_op jit(solution)/shard_map/while/body/eval_jaxpr/reshape | solution.py:72
  382.2 10.6 gather_fusion
  398.3 10.8 gather_fusion.1
  409.0 13.2 select_bitcast_fusion.6
  422.2 12.5 copy.466
  434.7 16.3 %reshape.491 = bf16[3,64,30,512]{3,1,2,0:T(8,128)(2,1)} reshape(bf16[3,64,30,8,64]{4,3,1,2,0:T(8,128)(2,1)} %copy.466) | data formatting | bytes 11796480 | tf_op jit(solution)/shard_map/while/body/eval_jaxpr/reshape | solution.py:73
  451.3 15.1 copy.467
  466.3 16.3 %reshape.492 = bf16[3,64,30,512]{3,1,2,0:T(8,128)(2,1)} reshape(bf16[3,64,30,8,64]{4,3,1,2,0:T(8,128)(2,1)} %copy.467) | data formatting | bytes 11796480 | tf_op jit(solution)/shard_map/while/body/eval_jaxpr/reshape | solution.py:72
  514.0 24.1 %all-to-all-done.3 = bf16[2,192,2048]{1,0,2:T(2,128)(2,1)S(1)} async-done(((bf16[2,192,2048]{1,0,2:T(2,128)(2,1)}), bf16[2,192,2048]{1,0,2:T(2,128)(2,1)S(1)}, u32[]{:S(2)}, u32[]{:S(2)}) %all-to-all-start.3) | async-done | bytes 1572896 | tf_op jit(solution)/shard_map/all_to_all | solution.py:277
  549.3 11.1 fusion.78
  560.5 10.8 bitcast_add_fusion
  579.8 17.2 %fusion.140 = (bf16[4,768]{1,0:T(4,128)(2,1)}, bf16[1024,4,768]{2,0,1:T(8,128)(2,1)}) fusion(f32[1024,4,768]{2,0,1:T(8,128)} %fusion.78, f32[4,768]{1,0:T(4,128)S(1)} %slice_convert_fusion, bf16[1024,768,1]{1,0,2:T(8,128)(2,1)S(1)} %bitcast.410, bf16[12,768,768]{2,1,0:T(8,128)(2,1)S(1)} %bitcast.421), kind=kOutput, calls=%fused_computation.235 | convolution fusion | flops 4901041152 | bytes 25184256 | tf_op jit(solution)/shard_map/te,beh->tbh/dot_general | solution.py:302
  614.5 21.7 %all_to_all.144 = bf16[2,768,512]{2,0,1:T(2,128)(2,1)S(1)} all-to-all(bf16[2,768,512]{2,0,1:T(2,128)(2,1)S(1)} %copy.353), channel_id=1, replica_groups=mesh['shard'=4,'ctx'=4,'tp'=2] {'ctx'}, dimensions={1} | all-to-all | bytes 3145728 | tf_op jit(solution)/shard_map/all_to_all | solution.py:321
  642.6 645.2 %while.30 = (s32[]{:T(128)}, bf16[2,192,2048]{2,1,0:T(8,128)(2,1)}, bf16[2,192,2048]{2,1,0:T(8,128)(2,1)}, bf16[2,192,2048]{2,1,0:T(8,128)(2,1)}, bf16[2,192,204...) while((s32[]{:T(128)}, bf16[2,192,2048]{2,1,0:T(8,128)(2,1)}, ...), condition=%wide.region_17.19_spmd.clone.clone, body=%wide.region_14.18_spmd.clone.clone.sunk | while | flops 4718786560 | bytes 516228704 | solution.py:338
  668.9 10.6 gather_fusion.2
  684.2 10.8 gather_fusion.3
  695.0 13.2 select_bitcast_fusion.7
  708.1 13.0 copy.477
  721.1 16.5 %reshape.503 = bf16[3,64,30,512]{3,1,2,0:T(8,128)(2,1)} reshape(bf16[3,64,30,8,64]{4,3,1,2,0:T(8,128)(2,1)} %copy.477) | data formatting | bytes 11796480 | tf_op jit(solution)/shard_map/while/body/eval_jaxpr/reshape | solution.py:113
  740.2 9.1 fusion.263
  755.0 15.1 copy.480
  770.1 16.4 %reshape.504 = bf16[3,64,30,512]{3,1,2,0:T(8,128)(2,1)} reshape(bf16[3,64,30,8,64]{4,3,1,2,0:T(8,128)(2,1)} %copy.480) | data formatting | bytes 11796480 | tf_op jit(solution)/shard_map/while/body/eval_jaxpr/reshape | solution.py:114
  786.5 11.1 multiply_reduce_fusion.11
  797.7 9.2 multiply_convert_fusion.9
  823.7 17.9 %reshape.505 = f32[3,64,30,8,64]{4,3,1,2,0:T(8,128)} reshape(f32[3,64,30,512]{3,1,2,0:T(8,128)} %fusion.265) | data formatting | bytes 23592960 | tf_op jit(solution)/shard_map/while/body/eval_jaxpr/reshape | solution.py:143
  841.7 39.1 %fusion.266 = f32[3,64,32,64]{3,2,1,0:T(8,128)} fusion(f32[3,64,30,8,64]{4,3,1,2,0:T(8,128)} %reshape.505, s32[3,30,8]{1,2,0:T(8,128)S(1)} %copy.482), kind=kOutput, calls=%fused_computation.77.clone.1 | convolution fusion | flops 1132508160 | bytes 13372224 | tf_op jit(solution)/shard_map/while/body/eval_jaxpr/gdmkb,gmkn->gdnb/dot_general | solution.py:142
  896.1 17.8 %reshape.507 = f32[3,64,30,8,64]{4,3,1,2,0:T(8,128)} reshape(f32[3,64,30,512]{3,1,2,0:T(8,128)} %multiply_bitcast_fusion.2) | data formatting | bytes 23592960 | tf_op jit(solution)/shard_map/while/body/eval_jaxpr/reshape | solution.py:140
  914.0 39.3 %fusion.268 = f32[3,64,32,64]{3,2,1,0:T(8,128)} fusion(f32[3,64,30,8,64]{4,3,1,2,0:T(8,128)} %reshape.507, s32[3,30,8]{1,2,0:T(8,128)S(1)} %copy.482), kind=kOutput, calls=%fused_computation.76.clone.1 | convolution fusion | flops 1132508160 | bytes 13372224 | tf_op jit(solution)/shard_map/while/body/eval_jaxpr/gdmkb,gmkn->gdnb/dot_general | solution.py:139
  986.6 10.6 gather_fusion.2
  1001.9 10.8 gather_fusion.3
  1012.7 13.2 select_bitcast_fusion.7
  1025.8 12.8 copy.477
  1038.6 16.5 %reshape.503 = bf16[3,64,30,512]{3,1,2,0:T(8,128)(2,1)} reshape(bf16[3,64,30,8,64]{4,3,1,2,0:T(8,128)(2,1)} %copy.477) | data formatting | bytes 11796480 | tf_op jit(solution)/shard_map/while/body/eval_jaxpr/reshape | solution.py:113
  1057.7 9.1 fusion.263
  1072.5 15.1 copy.480
  1087.6 16.4 %reshape.504 = bf16[3,64,30,512]{3,1,2,0:T(8,128)(2,1)} reshape(bf16[3,64,30,8,64]{4,3,1,2,0:T(8,128)(2,1)} %copy.480) | data formatting | bytes 11796480 | tf_op jit(solution)/shard_map/while/body/eval_jaxpr/reshape | solution.py:114
  1104.0 11.4 multiply_reduce_fusion.11
  1115.5 9.2 multiply_convert_fusion.9
  1132.8 8.8 fusion.265
  1141.5 17.9 %reshape.505 = f32[3,64,30,8,64]{4,3,1,2,0:T(8,128)} reshape(f32[3,64,30,512]{3,1,2,0:T(8,128)} %fusion.265) | data formatting | bytes 23592960 | tf_op jit(solution)/shard_map/while/body/eval_jaxpr/reshape | solution.py:143
  1159.5 39.0 %fusion.266 = f32[3,64,32,64]{3,2,1,0:T(8,128)} fusion(f32[3,64,30,8,64]{4,3,1,2,0:T(8,128)} %reshape.505, s32[3,30,8]{1,2,0:T(8,128)S(1)} %copy.482), kind=kOutput, calls=%fused_computation.77.clone.1 | convolution fusion | flops 1132508160 | bytes 13372224 | tf_op jit(solution)/shard_map/while/body/eval_jaxpr/gdmkb,gmkn->gdnb/dot_general | solution.py:142
  1213.9 17.8 %reshape.507 = f32[3,64,30,8,64]{4,3,1,2,0:T(8,128)} reshape(f32[3,64,30,512]{3,1,2,0:T(8,128)} %multiply_bitcast_fusion.2) | data formatting | bytes 23592960 | tf_op jit(solution)/shard_map/while/body/eval_jaxpr/reshape | solution.py:140
  1231.7 39.1 %fusion.268 = f32[3,64,32,64]{3,2,1,0:T(8,128)} fusion(f32[3,64,30,8,64]{4,3,1,2,0:T(8,128)} %reshape.507, s32[3,30,8]{1,2,0:T(8,128)S(1)} %copy.482), kind=kOutput, calls=%fused_computation.76.clone.1 | convolution fusion | flops 1132508160 | bytes 13372224 | tf_op jit(solution)/shard_map/while/body/eval_jaxpr/gdmkb,gmkn->gdnb/dot_general | solution.py:139
  1303.5 16.8 %all-to-all-done.6 = bf16[2,192,2048]{1,0,2:T(2,128)(2,1)S(1)} async-done(((bf16[2,192,2048]{1,0,2:T(2,128)(2,1)}), bf16[2,192,2048]{1,0,2:T(2,128)(2,1)S(1)}, u32[]{:S(2)}, u32[]{:S(2)}) %all-to-all-start.6) | async-done | bytes 1572896 | tf_op jit(solution)/shard_map/all_to_all | solution.py:343
  1330.9 18.3 %all-to-all-done.5 = bf16[2,192,2048]{1,0,2:T(2,128)(2,1)} async-done(((bf16[2,192,2048]{1,0,2:T(2,128)(2,1)}), bf16[2,192,2048]{1,0,2:T(2,128)(2,1)}, u32[]{:S(2)}, u32[]{:S(2)}) %all-to-all-start.5) | async-done | bytes 1572896 | tf_op jit(solution)/shard_map/all_to_all | solution.py:342
  1401.6 9.5 bitcast_dynamic-update-slice_fusion.2
  1411.1 24.0 %copy.409 = bf16[12,768,768]{2,0,1:T(8,128)(2,1)} copy(bf16[12,768,768]{1,2,0:T(8,128)(2,1)} %bitcast_dynamic-update-slice_fusion.2) | data formatting | bytes 28311552
  1435.0 16.9 %copy.420 = bf16[96,8,12,768]{3,1,2,0:T(8,128)(2,1)} copy(bf16[96,8,12,768]{3,2,1,0:T(8,128)(2,1)} %bitcast.395) | data formatting | bytes 28311552
  1452.0 100.8 %reduce-scatter.7.cloned.1.call-done = bf16[96,9216]{1,0:T(8,128)(2,1)} async-done(((bf16[768,9216]{1,0:T(8,128)(2,1)}), bf16[96,9216]{1,0:T(8,128)(2,1)}) %reduce-scatter.7.cloned.1.call-update) | async-done | bytes 1769488
  1565.9 23.7 %all-reduce.1 = bf16[4,8,288]{2,0,1:T(4,128)(2,1)S(1)} all-reduce(bf16[4,8,288]{2,0,1:T(4,128)(2,1)S(1)} %copy.376), channel_id=5, replica_groups=mesh['shard'=4,'ctx'=4,'tp'=2] {'ctx','tp'}, use_global_device_ids=true, to_apply=%region_29.31.clone | all-reduce | flops 9216 | bytes 36864
  1590.3 12.7 all-reduce.2
  (562 shorter events, 453.8 us)
Async XLA Ops:
  7.2 185.3 %copy-start = (s32[12,30,3]{1,2,0:T(4,128)S(1)}, s32[12,30,3]{1,2,0:T(4,128)}, u32[]{:S(2)}) copy-start(s32[12,30,3]{1,2,0:T(4,128)} %param.18) | copy-start | bytes 12964
  7.2 46.0 %all-gather.4.cloned.1.call-start = ((), (), s32[]{:S(2)}) async-start(), calls=%async_computation.10 | async-start | bytes 2211840 | tf_op jit(solution)/shard_map/all_gather | solution.py:216
  9.2 126.4 %all-gather.6.cloned.1.call-start = ((), (), s32[]{:S(2)}) async-start(), calls=%async_computation.11 | async-start | bytes 15925248 | tf_op jit(solution)/shard_map/all_gather | solution.py:225
  55.9 22.8 %copy-start.35 = (f32[2,512,768]{2,1,0:T(8,128)S(1)}, f32[2,512,768]{2,1,0:T(8,128)}, u32[]{:S(2)}) copy-start(f32[2,512,768]{2,1,0:T(8,128)} %param.16) | copy-start | bytes 9437188
  141.6 23.5 %all-to-all-start = ((bf16[2,768,512]{2,0,1:T(2,128)(2,1)}), bf16[2,768,512]{2,0,1:T(2,128)(2,1)S(1)}, u32[]{:S(2)}, u32[]{:S(2)}) async-start(bf16[2,768,512]{2,0,1:T(2,128)(2,1)} %copy.338), calls=%async_computation | async-start | bytes 3145728 | tf_op jit(solution)/shard_map/all_to_all | solution.py:270
  165.1 22.9 %all-to-all-start.1 = ((bf16[2,768,512]{2,0,1:T(2,128)(2,1)}), bf16[2,768,512]{2,0,1:T(2,128)(2,1)S(1)}, u32[]{:S(2)}, u32[]{:S(2)}) async-start(bf16[2,768,512]{2,0,1:T(2,128)(2,1)} %copy.341), calls=%async_computation.1 | async-start | bytes 3145728 | tf_op jit(solution)/shard_map/all_to_all | solution.py:268
  188.1 23.1 %all-to-all-start.2 = ((bf16[2,768,512]{2,0,1:T(2,128)(2,1)}), bf16[2,768,512]{2,0,1:T(2,128)(2,1)}, u32[]{:S(2)}, u32[]{:S(2)}) async-start(bf16[2,768,512]{2,0,1:T(2,128)(2,1)} %copy.344), calls=%async_computation.2 | async-start | bytes 3145728 | tf_op jit(solution)/shard_map/all_to_all | solution.py:269
  234.1 7.0 copy-start.16
  347.3 11.1 slice-start.2
  348.1 10.3 slice-start.3
  369.5 7.0 copy-start.16
  482.7 11.1 slice-start.2
  483.5 10.3 slice-start.3
  504.1 9.7 copy-start.55
  510.2 27.9 %all-to-all-start.3 = ((bf16[2,192,2048]{1,0,2:T(2,128)(2,1)}), bf16[2,192,2048]{1,0,2:T(2,128)(2,1)S(1)}, u32[]{:S(2)}, u32[]{:S(2)}) async-start(bf16[2,192,2048]{1,0,2:T(2,128)(2,1)} %copy.348), calls=%async_computation.3 | async-start | bytes 4194304 | tf_op jit(solution)/shard_map/all_to_all | solution.py:277
  514.0 65.8 %copy-start.61 = (f32[4,768]{1,0:T(4,128)}, f32[4,768]{1,0:T(4,128)S(1)}, u32[]{:S(2)}) copy-start(f32[4,768]{1,0:T(4,128)S(1)} %slice_convert_fusion) | copy-start | bytes 36868
  538.1 6.5 copy-start.73
  548.7 11.8 slice-start.4
  549.3 11.2 copy-start.46
  549.3 11.2 slice-start.5
  549.3 11.2 slice-start.6
  549.3 11.2 slice-start.7
  549.3 11.2 copy-start.72
  579.8 17.2 %copy-start.37 = (bf16[2,512,768]{2,1,0:T(8,128)(2,1)}, bf16[2,512,768]{2,1,0:T(8,128)(2,1)S(1)}, u32[]{:S(2)}) copy-start(bf16[2,512,768]{2,1,0:T(8,128)(2,1)S(1)} %get-tuple-element.333) | copy-start | bytes 4718596
  642.8 6.5 copy-start.50
  642.8 9.5 copy-start.52
  642.8 36.7 %copy-start.18 = (s32[3,30,8]{2,1,0:T(8,128)}, s32[3,30,8]{2,1,0:T(8,128)S(1)}, u32[]{:S(2)}) copy-start(s32[3,30,8]{2,1,0:T(8,128)S(1)} %get-tuple-element.633) | copy-start | bytes 8644 | tf_op jit(solution)/shard_map/while
  652.4 7.4 copy-start.31
  668.9 10.7 copy-start.7
  721.1 16.5 %copy-start.15 = (bf16[3,64,32,64]{3,2,1,0:T(8,128)(2,1)S(1)}, bf16[3,64,32,64]{3,2,1,0:T(8,128)(2,1)}, u32[]{:S(2)}) copy-start(bf16[3,64,32,64]{3,2,1,0:T(8,128)(2,1)} %reshape.499) | copy-start | bytes 2359300 | tf_op jit(solution)/shard_map/while
  740.1 9.2 copy-start.10
  740.2 9.2 copy-start.32
  740.2 10.1 copy-start.14
  770.1 36.8 %slice-start = ((s8[5898240]{0:T(1024)(128)(4,1)}), s8[1703936]{0:T(1024)(128)(4,1)S(1)}, s32[]{:S(2)}) async-start(s8[5898240]{0:T(1024)(128)(4,1)} %bitcast.380), calls=%async_computation.14 | async-start | bytes 3407872 | tf_op jit(solution)/shard_map/while
  786.5 20.3 %slice-start.1 = ((s8[5898240]{0:T(1024)(128)(4,1)}), s8[4194304]{0:T(1024)(128)(4,1)S(1)}, s32[]{:S(2)}) async-start(s8[5898240]{0:T(1024)(128)(4,1)} %bitcast.380), calls=%async_computation.15 | async-start | bytes 8388608 | tf_op jit(solution)/shard_map/while
  823.7 17.9 %copy-start.19 = (s32[3,30,8]{2,1,0:T(8,128)S(1)}, s32[3,30,8]{2,1,0:T(8,128)}, u32[]{:S(2)}) copy-start(s32[3,30,8]{2,1,0:T(8,128)} %copy-done.18) | copy-start | bytes 8644 | tf_op jit(solution)/shard_map/while
  960.5 6.5 copy-start.50
  960.5 9.5 copy-start.52
  960.5 36.8 %copy-start.18 = (s32[3,30,8]{2,1,0:T(8,128)}, s32[3,30,8]{2,1,0:T(8,128)S(1)}, u32[]{:S(2)}) copy-start(s32[3,30,8]{2,1,0:T(8,128)S(1)} %get-tuple-element.633) | copy-start | bytes 8644 | tf_op jit(solution)/shard_map/while
  970.1 7.4 copy-start.31
  986.6 10.7 copy-start.7
  1038.6 16.5 %copy-start.15 = (bf16[3,64,32,64]{3,2,1,0:T(8,128)(2,1)S(1)}, bf16[3,64,32,64]{3,2,1,0:T(8,128)(2,1)}, u32[]{:S(2)}) copy-start(bf16[3,64,32,64]{3,2,1,0:T(8,128)(2,1)} %reshape.499) | copy-start | bytes 2359300 | tf_op jit(solution)/shard_map/while
  1057.6 9.2 copy-start.10
  1057.7 9.2 copy-start.32
  1057.7 10.1 copy-start.14
  1087.6 37.0 %slice-start = ((s8[5898240]{0:T(1024)(128)(4,1)}), s8[1703936]{0:T(1024)(128)(4,1)S(1)}, s32[]{:S(2)}) async-start(s8[5898240]{0:T(1024)(128)(4,1)} %bitcast.380), calls=%async_computation.14 | async-start | bytes 3407872 | tf_op jit(solution)/shard_map/while
  1104.0 20.6 %slice-start.1 = ((s8[5898240]{0:T(1024)(128)(4,1)}), s8[4194304]{0:T(1024)(128)(4,1)S(1)}, s32[]{:S(2)}) async-start(s8[5898240]{0:T(1024)(128)(4,1)} %bitcast.380), calls=%async_computation.15 | async-start | bytes 8388608 | tf_op jit(solution)/shard_map/while
  1141.5 17.9 %copy-start.19 = (s32[3,30,8]{2,1,0:T(8,128)S(1)}, s32[3,30,8]{2,1,0:T(8,128)}, u32[]{:S(2)}) copy-start(s32[3,30,8]{2,1,0:T(8,128)} %copy-done.18) | copy-start | bytes 8644 | tf_op jit(solution)/shard_map/while
  1293.8 26.5 %all-to-all-start.6 = ((bf16[2,192,2048]{1,0,2:T(2,128)(2,1)}), bf16[2,192,2048]{1,0,2:T(2,128)(2,1)S(1)}, u32[]{:S(2)}, u32[]{:S(2)}) async-start(bf16[2,192,2048]{1,0,2:T(2,128)(2,1)} %copy.361), calls=%async_computation.6 | async-start | bytes 4194304 | tf_op jit(solution)/shard_map/all_to_all | solution.py:343
  1320.4 28.8 %all-to-all-start.5 = ((bf16[2,192,2048]{1,0,2:T(2,128)(2,1)}), bf16[2,192,2048]{1,0,2:T(2,128)(2,1)}, u32[]{:S(2)}, u32[]{:S(2)}) async-start(bf16[2,192,2048]{1,0,2:T(2,128)(2,1)} %copy.357), calls=%async_computation.5 | async-start | bytes 4194304 | tf_op jit(solution)/shard_map/all_to_all | solution.py:342
  1349.2 28.8 %all-to-all-start.7 = ((bf16[2,192,2048]{1,0,2:T(2,128)(2,1)}), bf16[2,192,2048]{1,0,2:T(2,128)(2,1)}, u32[]{:S(2)}, u32[]{:S(2)}) async-start(bf16[2,192,2048]{1,0,2:T(2,128)(2,1)} %copy.365), calls=%async_computation.7 | async-start | bytes 4194304 | tf_op jit(solution)/shard_map/all_to_all | solution.py:344
  1353.6 199.2 %reduce-scatter.7.cloned.1.call-start = ((), (), s32[]{:S(2)}) async-start(), calls=%async_computation.13 | async-start | bytes 15925248
  1384.0 6.9 copy-start.25
  1393.4 8.1 slice-start.8
  1394.5 7.0 copy-start.38
  1394.5 7.0 copy-start.62
  1394.6 7.0 slice-start.9
  1394.6 7.0 slice-start.10
  1452.0 105.1 %copy-start.74 = (s32[12]{0:T(128)S(1)}, s32[12]{0:T(128)}, u32[]{:S(2)}) copy-start(s32[12]{0:T(128)} %param.19) | copy-start | bytes 148
  1452.0 163.7 %reduce-scatter.5.cloned.1.call-start = ((), (), s32[]{:S(2)}) async-start(), calls=%async_computation.12 | async-start | bytes 2211840 | tf_op jit(solution)/shard_map/reduce_scatter | solution.py:389
  1561.3 42.3 %copy-start.68 = (f32[288]{0:T(512)S(1)}, f32[288]{0:T(512)}, u32[]{:S(2)}) copy-start(f32[288]{0:T(512)} %param.23) | copy-start | bytes 3460
  1561.3 42.3 %copy-start.75 = (f32[288]{0:T(512)S(1)}, f32[288]{0:T(512)}, u32[]{:S(2)}) copy-start(f32[288]{0:T(512)} %param.24) | copy-start | bytes 3460
  1561.3 42.3 %copy-start.76 = (f32[288]{0:T(512)S(1)}, f32[288]{0:T(512)}, u32[]{:S(2)}) copy-start(f32[288]{0:T(512)} %param.25) | copy-start | bytes 3460
  1610.5 8.2 copy-start.1
  (73 other events, 206.1 us)
Sparse Core Ops, SparseCore 0:
  10.2 43.0 all-gather.3
  57.8 77.7 all-gather.5
  1452.1 100.7 reduce-scatter.6
  1561.5 38.7 reduce-scatter.4
where the time goes:
time: 1640 us; the launch traced here: 1630 us
  local copies, waits for them, and re-layouts  691 us (42%)
  matrix products  383 us (23%)
  waiting for transfers between devices  300 us (18%)
  other arithmetic  104 us (6%)
  blocking collectives  76.7 us (5%)
  starting transfers between devices  28 us (2%)
  loops' own time  27.3 us (2%)
    select_n x8, local copies, waits for them, and re-layouts, pick_one(): return jnp.take(source, chosen, axis=1)  111 us
    unnamed x5, waiting for transfers between devices  101 us
    gather x12, local copies, waits for them, and re-layouts, pick_one(): return jnp.take(source, chosen, axis=1)  85.9 us
    dot_general x2, matrix products, attend_backward(): jnp.einsum('gdmkb,gmkn->gdnb', dk_picked.reshape(picked_shape), placer, p...  78.3 us
    dot_general x2, matrix products, attend_backward(): jnp.einsum('gdmkb,gmkn->gdnb', dv_picked.reshape(picked_shape), placer, p...  78.1 us
    unnamed x135, local copies, waits for them, and re-layouts  55.8 us
    all_gather x1, waiting for transfers between devices, shards(): lax.all_gather(chosen, ('ctx', 'tp'), axis=1, tiled=True)  54.9 us
    select_n x4, other arithmetic, pick_one(): return jnp.take(source, chosen, axis=1)  52.6 us
  transfers between devices with their start and end apart: 11, of which 10 were waited for; matrix products, arithmetic and copies ran while one was open for 4% of the time, Pallas kernels for 0%

commit v1 on v0

v1 whole, which is shorter than its diff:
```python
import functools

import jax
import jax.numpy as jnp
from jax import lax
from jax.experimental import pallas as pl
from jax.experimental.pallas import tpu as pltpu
from jax.sharding import PartitionSpec as P

STEP = 5
norm_eps = 1e-12
beta_one = 0.9
beta_two = 0.999
adam_eps = 1e-08
rate_value = 0.04
small_rate = 0.25
score_scale = 0.125
gelu_root = 0.7978845608
gelu_cube = 0.044715

BLOCK = 64
HEAD = 64
PACK = 4
masked_score = -1e30


def wide_dot(a, b, dims):
    return lax.dot_general(a, b, (dims, ((), ())), preferred_element_type=jnp.float32)


def head_masks(rows):
    lane = lax.broadcasted_iota(jnp.int32, (rows, PACK * HEAD), 1) // HEAD
    return [lane == h for h in range(PACK)]


def spread_heads(block, masks):
    zero = jnp.zeros_like(block)
    return jnp.concatenate([jnp.where(m, block, zero) for m in masks], axis=0)


def own_heads(full, masks):
    total = None
    for h, m in enumerate(masks):
        piece = jnp.where(m, full[h * BLOCK : (h + 1) * BLOCK], 0.0)
        total = piece if total is None else total + piece
    return total


def rows_of(ref, index, count=1):
    return ref[pl.ds(pl.multiple_of(index * BLOCK, BLOCK), count * BLOCK), :]


def picked_rows(ref, picks, low_half):
    halves = []
    for pair in range(PACK // 2):
        cols = pl.ds(pair * 2 * HEAD, 2 * HEAD)
        first = ref[pl.ds(pl.multiple_of(picks[2 * pair] * BLOCK, BLOCK), BLOCK), cols]
        second = ref[pl.ds(pl.multiple_of(picks[2 * pair + 1] * BLOCK, BLOCK), BLOCK), cols]
        halves.append(jnp.where(low_half, first, second))
    return jnp.concatenate(halves, axis=1)


def gathered(ref, block, last, picks, low_half):
    pieces = [rows_of(ref, 0), rows_of(ref, last), rows_of(ref, block - 1, 3)]
    pieces += [picked_rows(ref, p, low_half) for p in picks]
    return jnp.concatenate(pieces, axis=0)


def middle_scores(keys, spread, block, last):
    scores = wide_dot(keys, spread, ((1,), (1,)))
    first_off = jnp.where(block == 1, masked_score, 0.0)
    last_off = jnp.where(block == last - 1, masked_score, 0.0)
    b = BLOCK
    return jnp.concatenate(
        [
            scores[: 2 * b],
            scores[2 * b : 3 * b] + first_off,
            scores[3 * b : 4 * b],
            scores[4 * b : 5 * b] + last_off,
            scores[5 * b :],
        ],
        axis=0,
    )


def attend_kernel(unroll, half_ref, table_ref, q_ref, k_ref, v_ref, out_ref, lse_ref, kept):
    half = half_ref[0]
    group = pl.program_id(0)
    nblocks = k_ref.shape[0] // BLOCK
    local = q_ref.shape[0] // BLOCK
    last = nblocks - 1
    picks_each = table_ref.shape[2]
    masks = head_masks(BLOCK)
    low_half = lax.broadcasted_iota(jnp.int32, (BLOCK, 2 * HEAD), 1) < HEAD

    def middle(step, carry):
        mine = step + 1 - half
        block = mine + local * half
        picks = [
            [table_ref[group * PACK + h, block - 1, r] for h in range(PACK)]
            for r in range(picks_each)
        ]
        spread = spread_heads(rows_of(q_ref, mine), masks)
        keys = gathered(k_ref, block, last, picks, low_half)
        values = gathered(v_ref, block, last, picks, low_half)
        scores = middle_scores(keys, spread, block, last)
        top = jnp.max(scores, axis=0, keepdims=True)
        probs = jnp.exp(scores - top)
        total = jnp.sum(probs, axis=0, keepdims=True)
        low = (probs * (1.0 / total)).astype(jnp.bfloat16)
        full = wide_dot(low, values, ((0,), (0,)))
        out_ref[pl.ds(pl.multiple_of(mine * BLOCK, BLOCK), BLOCK), :] = own_heads(
            full, masks
        ).astype(jnp.bfloat16)
        lse_ref[0, pl.ds(mine, 1), :] = top + jnp.log(total)
        return carry

    lax.fori_loop(0, local - 1, middle, 0, unroll=unroll)

    edge = (local - 1) * half
    spread = spread_heads(rows_of(q_ref, edge), masks)
    span = 8 * BLOCK
    chunks = nblocks // 8
    top = None
    for c in range(chunks):
        scores = wide_dot(k_ref[c * span : (c + 1) * span, :], spread, ((1,), (1,)))
        kept[c * span : (c + 1) * span, :] = scores
        high = jnp.max(scores, axis=0, keepdims=True)
        top = high if top is None else jnp.maximum(top, high)
    total = None
    for c in range(chunks):
        probs = jnp.exp(kept[c * span : (c + 1) * span, :] - top)
        kept[c * span : (c + 1) * span, :] = probs
        part = jnp.sum(probs, axis=0, keepdims=True)
        total = part if total is None else total + part
    scale = 1.0 / total
    full = None
    for c in range(chunks):
        low = (kept[c * span : (c + 1) * span, :] * scale).astype(jnp.bfloat16)
        part = wide_dot(low, v_ref[c * span : (c + 1) * span, :], ((0,), (0,)))
        full = part if full is None else full + part
    out_ref[pl.ds(pl.multiple_of(edge * BLOCK, BLOCK), BLOCK), :] = own_heads(
        full, masks
    ).astype(jnp.bfloat16)
    lse_ref[0, pl.ds(edge, 1), :] = top + jnp.log(total)


def attend(half, table, q, k, v, unroll=3):
    tokens, width = q.shape
    seq = k.shape[0]
    lanes = PACK * HEAD
    groups = width // lanes
    blocks = tokens // BLOCK
    spec = pltpu.PrefetchScalarGridSpec(
        num_scalar_prefetch=2,
        grid=(groups,),
        in_specs=[
            pl.BlockSpec((tokens, lanes), lambda g, *_: (0, g)),
            pl.BlockSpec((seq, lanes), lambda g, *_: (0, g)),
            pl.BlockSpec((seq, lanes), lambda g, *_: (0, g)),
        ],
        out_specs=[
            pl.BlockSpec((tokens, lanes), lambda g, *_: (0, g)),
            pl.BlockSpec((1, blocks, lanes), lambda g, *_: (g, 0, 0)),
        ],
        scratch_shapes=[pltpu.VMEM((seq, lanes), jnp.float32)],
    )
    return pl.pallas_call(
        functools.partial(attend_kernel, unroll),
        grid_spec=spec,
        out_shape=[
            jax.ShapeDtypeStruct((tokens, width), jnp.bfloat16),
            jax.ShapeDtypeStruct((groups, blocks, lanes), jnp.float32),
        ],
        name="attend",
        compiler_params=pltpu.CompilerParams(vmem_limit_bytes=56 << 20),
        cost_estimate=pl.CostEstimate(
            flops=60_000_000_000, bytes_accessed=12 << 20, transcendentals=16_000_000
        ),
    )(half, table, q, k, v)


def attend_back_kernel(
    unroll,
    half_ref,
    table_ref,
    q_ref,
    k_ref,
    v_ref,
    lse_ref,
    do_ref,
    dq_ref,
    dk_ref,
    dv_ref,
    dk_acc,
    dv_acc,
    kept_p,
    kept_g,
):
    half = half_ref[0]
    group = pl.program_id(0)
    nblocks = k_ref.shape[0] // BLOCK
    local = q_ref.shape[0] // BLOCK
    last = nblocks - 1
    picks_each = table_ref.shape[2]
    masks = head_masks(BLOCK)
    low_half = lax.broadcasted_iota(jnp.int32, (BLOCK, 2 * HEAD), 1) < HEAD
    span = 8 * BLOCK
    chunks = nblocks // 8

    edge = (local - 1) * half
    spread = spread_heads(rows_of(q_ref, edge), masks)
    spread_do = spread_heads(rows_of(do_ref, edge), masks)
    lse = lse_ref[0, pl.ds(edge, 1), :]
    delta = None
    for c in range(chunks):
        rows = slice(c * span, (c + 1) * span)
        probs = jnp.exp(wide_dot(k_ref[rows, :], spread, ((1,), (1,))) - lse)
        gp = wide_dot(v_ref[rows, :], spread_do, ((1,), (1,)))
        kept_p[rows, :] = probs
        kept_g[rows, :] = gp
        part = jnp.sum(probs * gp, axis=0, keepdims=True)
        delta = part if delta is None else delta + part
    full = None
    for c in range(chunks):
        rows = slice(c * span, (c + 1) * span)
        probs = kept_p[rows, :]
        ds = (probs * (kept_g[rows, :] - delta)).astype(jnp.bfloat16)
        dv_acc[rows, :] = wide_dot(probs.astype(jnp.bfloat16), spread_do, ((1,), (0,)))
        dk_acc[rows, :] = wide_dot(ds, spread, ((1,), (0,)))
        part = wide_dot(ds, k_ref[rows, :], ((0,), (0,)))
        full = part if full is None else full + part
    dq_ref[pl.ds(pl.multiple_of(edge * BLOCK, BLOCK), BLOCK), :] = (
        own_heads(full, masks) * 0.125
    ).astype(jnp.bfloat16)

    def scatter(acc, piece, block, picks):
        b = BLOCK
        acc[0:b, :] += piece[:b]
        acc[last * b : (last + 1) * b, :] += piece[b : 2 * b]
        window = pl.ds(pl.multiple_of((block - 1) * b, b), 3 * b)
        acc[window, :] += piece[2 * b : 5 * b]
        for r, p in enumerate(picks):
            part = piece[(5 + r) * b : (6 + r) * b]
            for pair in range(PACK // 2):
                lanes = slice(pair * 2 * HEAD, (pair + 1) * 2 * HEAD)
                cols = pl.ds(pair * 2 * HEAD, 2 * HEAD)
                sub = part[:, lanes]
                acc[pl.ds(pl.multiple_of(p[2 * pair] * b, b), b), cols] += jnp.where(
                    low_half, sub, 0.0
                )
                acc[pl.ds(pl.multiple_of(p[2 * pair + 1] * b, b), b), cols] += jnp.where(
                    low_half, 0.0, sub
                )

    def middle(step, carry):
        mine = step + 1 - half
        block = mine + local * half
        picks = [
            [table_ref[group * PACK + h, block - 1, r] for h in range(PACK)]
            for r in range(picks_each)
        ]
        spread = spread_heads(rows_of(q_ref, mine), masks)
        spread_do = spread_heads(rows_of(do_ref, mine), masks)
        keys = gathered(k_ref, block, last, picks, low_half)
        values = gathered(v_ref, block, last, picks, low_half)
        scores = middle_scores(keys, spread, block, last)
        probs = jnp.exp(scores - lse_ref[0, pl.ds(mine, 1), :])
        gp = wide_dot(values, spread_do, ((1,), (1,)))
        delta = jnp.sum(probs * gp, axis=0, keepdims=True)
        ds = (probs * (gp - delta)).astype(jnp.bfloat16)
        low = probs.astype(jnp.bfloat16)
        scatter(dv_acc, wide_dot(low, spread_do, ((1,), (0,))), block, picks)
        scatter(dk_acc, wide_dot(ds, spread, ((1,), (0,))), block, picks)
        full = wide_dot(ds, keys, ((0,), (0,)))
        dq_ref[pl.ds(pl.multiple_of(mine * BLOCK, BLOCK), BLOCK), :] = (
            own_heads(full, masks) * 0.125
        ).astype(jnp.bfloat16)
        return carry

    lax.fori_loop(0, local - 1, middle, 0, unroll=unroll)
    dk_ref[...] = dk_acc[...].astype(jnp.bfloat16)
    dv_ref[...] = dv_acc[...].astype(jnp.bfloat16)


def attend_back(half, table, q, k, v, lse, do, unroll=3):
    tokens, width = q.shape
    seq = k.shape[0]
    lanes = PACK * HEAD
    groups = width // lanes
    blocks = tokens // BLOCK
    mine = pl.BlockSpec((tokens, lanes), lambda g, *_: (0, g))
    whole = pl.BlockSpec((seq, lanes), lambda g, *_: (0, g))
    spec = pltpu.PrefetchScalarGridSpec(
        num_scalar_prefetch=2,
        grid=(groups,),
        in_specs=[
            mine,
            whole,
            whole,
            pl.BlockSpec((1, blocks, lanes), lambda g, *_: (g, 0, 0)),
            mine,
        ],
        out_specs=[mine, whole, whole],
        scratch_shapes=[pltpu.VMEM((seq, lanes), jnp.float32)] * 4,
    )
    return pl.pallas_call(
        functools.partial(attend_back_kernel, unroll),
        grid_spec=spec,
        out_shape=[
            jax.ShapeDtypeStruct((tokens, width), jnp.bfloat16),
            jax.ShapeDtypeStruct((seq, width), jnp.bfloat16),
            jax.ShapeDtypeStruct((seq, width), jnp.bfloat16),
        ],
        name="attend_back",
        compiler_params=pltpu.CompilerParams(vmem_limit_bytes=56 << 20),
        cost_estimate=pl.CostEstimate(
            flops=120_000_000_000, bytes_accessed=24 << 20, transcendentals=16_000_000
        ),
    )(half, table, q, k, v, lse, do)


TILE = 256
MID = 512


def cols_mean(value):
    return jnp.mean(value, axis=-1, keepdims=True)


def normed(field):
    centred = field - cols_mean(field)
    rate = lax.rsqrt(cols_mean(centred * centred) + norm_eps)
    return centred * rate, rate


def norm_back(cot, normal, rate, gain):
    dn = cot * gain
    return rate * (dn - cols_mean(dn) - normal * cols_mean(dn * normal))


def matrix(ref):
    value = ref[...]
    return value.reshape(value.shape[1] * value.shape[3], value.shape[4])


def add_row(ref, row, value):
    ref[row : row + 1, :] += jnp.sum(value, axis=0, keepdims=True)


SLOT_AT = 5


def weight_spec(weights, which, single=True):
    shards, groups, held, rows, width = weights.shape

    def place(step, info):
        slot = info[SLOT_AT + which(step)]
        return (slot // held, 0, slot % held, 0, 0)

    mode = pl.Buffered(1) if single else None
    return pl.BlockSpec((1, groups, 1, rows, width), place, pipeline_mode=mode)


def fixed(shape):
    return pl.BlockSpec(shape, lambda step, info: (0,) * len(shape), pipeline_mode=pl.Buffered(1))


def resident(shape):
    return pl.BlockSpec(shape, lambda step, info: (0,) * len(shape))


def call(kernel, name, info, grid, in_specs, out_specs, out_shape, scratch, args, flops, moved):
    return pl.pallas_call(
        kernel,
        name=name,
        grid_spec=pltpu.PrefetchScalarGridSpec(
            num_scalar_prefetch=1,
            grid=(grid,),
            in_specs=in_specs,
            out_specs=out_specs,
            scratch_shapes=scratch,
        ),
        out_shape=out_shape,
        compiler_params=pltpu.CompilerParams(vmem_limit_bytes=60 << 20),
        cost_estimate=pl.CostEstimate(
            flops=flops, bytes_accessed=moved, transcendentals=0
        ),
    )(info, *args)


def bf16_of(*shape):
    return jax.ShapeDtypeStruct(shape, jnp.bfloat16)


def f32_of(*shape):
    return jax.ShapeDtypeStruct(shape, jnp.float32)


NN = ((1,), (0,))
NT = ((1,), (1,))
TN = ((0,), (0,))


def project_kernel(info, x_ref, small, wq, wk, wv, q_ref, k_ref, v_ref):
    x = x_ref[0]

    @pl.when(pl.program_id(0) < 2)
    def own():
        q = wide_dot(x, matrix(wq), NN) + small[0:1, :]
        q_ref[...] = q.astype(jnp.bfloat16) * jnp.bfloat16(score_scale)

    k_ref[...] = wide_dot(x, matrix(wk), NN).astype(jnp.bfloat16)
    v_ref[...] = (wide_dot(x, matrix(wv), NN) + small[1:2, :]).astype(jnp.bfloat16)


def project(info, x_all, small, weights):
    _, mid, width = x_all.shape

    def chunk(step, info):
        return lax.rem(step + 2 * info[0], 4)

    return call(
        project_kernel,
        "project",
        info,
        4,
        [
            pl.BlockSpec((1, mid, width), lambda g, info: (info[1 + chunk(g, info)], 0, 0)),
            fixed(small.shape),
            weight_spec(weights, lambda g: 0),
            weight_spec(weights, lambda g: 1),
            weight_spec(weights, lambda g: 2),
        ],
        [
            pl.BlockSpec((mid, width), lambda g, info: (jnp.minimum(g, 1), 0)),
            pl.BlockSpec((mid, width), lambda g, info: (chunk(g, info), 0)),
            pl.BlockSpec((mid, width), lambda g, info: (chunk(g, info), 0)),
        ],
        [bf16_of(2 * mid, width), bf16_of(4 * mid, width), bf16_of(4 * mid, width)],
        [],
        (x_all, small, weights, weights, weights),
        6_000_000_000,
        16 << 20,
    )


def front_kernel(
    info,
    ctx_ref,
    x_ref,
    cot_ref,
    small,
    wo,
    u0,
    u1,
    u2,
    u3,
    v0,
    v1,
    v2,
    v3,
    out_ref,
    n1_ref,
    r1_ref,
    fi_ref,
    fit_ref,
    hid_ref,
    gel_ref,
    gh2_ref,
    gmt_ref,
    sums_ref,
):
    attn_out = wide_dot(ctx_ref[...], matrix(wo), NN) + small[2:3, :]
    n1, r1 = normed(x_ref[0].astype(jnp.float32) + attn_out)
    n1_ref[...] = n1
    r1_ref[...] = jnp.broadcast_to(r1, r1_ref.shape)
    after = n1 * small[3:4, :] + small[4:5, :]
    ffn_in = after.astype(jnp.bfloat16)
    fi_ref[...] = ffn_in
    fit_ref[...] = ffn_in.T
    total = after + small[9:10, :]
    for b, (up_w, down_w) in enumerate(((u0, v0), (u1, v1), (u2, v2), (u3, v3))):
        up = wide_dot(ffn_in, matrix(up_w), NN) + small[5 + b : 6 + b, :]
        square = up * up
        bent = jnp.tanh(gelu_root * up * (1.0 + gelu_cube * square))
        rise = 0.5 * (1.0 + bent)
        hidden = (up * rise).astype(jnp.bfloat16)
        hid_ref[b] = hidden
        slope = rise + (0.5 * gelu_root) * up * (1.0 - bent * bent) * (
            1.0 + (3.0 * gelu_cube) * square
        )
        gel_ref[b] = slope.astype(jnp.bfloat16)
        total = total + wide_dot(hidden, matrix(down_w), NT)
    n2, r2 = normed(total)
    out_ref[0] = (n2 * small[10:11, :] + small[11:12, :]).astype(jnp.bfloat16)
    cot = cot_ref[0].astype(jnp.float32)
    gh2 = norm_back(cot, n2, r2, small[10:11, :])
    gh2_ref[...] = gh2
    mixed = gh2.astype(jnp.bfloat16)
    gmt_ref[...] = mixed.T

    @pl.when(pl.program_id(0) == 0)
    def clear():
        sums_ref[...] = jnp.zeros_like(sums_ref)

    add_row(sums_ref, 0, mixed.astype(jnp.float32))
    add_row(sums_ref, 1, cot * n2)
    add_row(sums_ref, 2, cot)


def front(info, ctx, x_all, cot, small, weights):
    tokens, width = ctx.shape
    mid = x_all.shape[1]
    per = mid // TILE
    steps = tokens // TILE

    def arrived(t, info):
        return (info[1 + 2 * info[0] + t // per], t % per, 0)

    def rows(dtype_shape):
        return pl.BlockSpec(dtype_shape, lambda t, info: (t, 0))

    specs = [weight_spec(weights, lambda t, m=m: m) for m in range(3, 12)]
    wide4 = pl.BlockSpec((4, TILE, width), lambda t, info: (0, t, 0))
    flipped = pl.BlockSpec((width, TILE), lambda t, info: (0, t))
    return call(
        front_kernel,
        "front",
        info,
        steps,
        [
            rows((TILE, width)),
            pl.BlockSpec((1, TILE, width), arrived),
            pl.BlockSpec((1, TILE, width), arrived),
            fixed(small.shape),
            *specs,
        ],
        [
            pl.BlockSpec((1, TILE, width), arrived),
            rows((TILE, width)),
            rows((TILE, 128)),
            rows((TILE, width)),
            flipped,
            wide4,
            wide4,
            rows((TILE, width)),
            flipped,
            resident((8, width)),
        ],
        [
            bf16_of(2, mid, width),
            f32_of(tokens, width),
            f32_of(tokens, 128),
            bf16_of(tokens, width),
            bf16_of(width, tokens),
            bf16_of(4, tokens, width),
            bf16_of(4, tokens, width),
            f32_of(tokens, width),
            bf16_of(width, tokens),
            f32_of(8, width),
        ],
        [],
        (ctx, x_all, cot, small, *([weights] * 9)),
        11_000_000_000,
        40 << 20,
    )


def back_kernel(
    info,
    gh2_ref,
    hid_ref,
    gel_ref,
    fit_ref,
    gmt_ref,
    n1_ref,
    r1_ref,
    ctx_ref,
    small,
    up_w,
    down_w,
    wo,
    pair_ref,
    dwo_ref,
    gh1_ref,
    dctx_ref,
    sums_ref,
    gy,
    gu,
):
    step = pl.program_id(0)
    tokens, width = gh2_ref.shape
    tiles = tokens // TILE
    groups, _, rows, _ = pair_ref.shape

    @pl.when(step == 0)
    def clear():
        sums_ref[...] = jnp.zeros_like(sums_ref)
        gy[...] = gh2_ref[...]

    @pl.when(step < 4)
    def ffn():
        up_block = matrix(up_w)
        down_block = matrix(down_w)

        def one(t, carry):
            at = pl.ds(pl.multiple_of(t * TILE, TILE), TILE)
            mixed = gh2_ref[at, :].astype(jnp.bfloat16)
            grad = wide_dot(mixed, down_block, NN) * gel_ref[0, at, :].astype(jnp.float32)
            low = grad.astype(jnp.bfloat16)
            gu[at, :] = low
            gy[at, :] += wide_dot(low, up_block, NT)
            sums_ref[pl.ds(step, 1), :] += jnp.sum(
                low.astype(jnp.float32), axis=0, keepdims=True
            )
            return carry

        lax.fori_loop(0, tiles, one, 0)
        grad_up = wide_dot(fit_ref[...], gu[...], NN).astype(jnp.bfloat16)
        pair_ref[:, 0:1] = grad_up.reshape(groups, 1, rows, width)
        grad_down = wide_dot(gmt_ref[...], hid_ref[0], NN).astype(jnp.bfloat16)
        pair_ref[:, 1:2] = grad_down.reshape(groups, 1, rows, width)

    @pl.when(step == 4)
    def first_norm():
        out_w = matrix(wo)

        def one(t, carry):
            at = pl.ds(pl.multiple_of(t * TILE, TILE), TILE)
            grad = gy[at, :]
            n1 = n1_ref[at, :]
            gh1 = norm_back(grad, n1, r1_ref[at, 0:1], small[3:4, :])
            gh1_ref[at, :] = gh1
            low = gh1.astype(jnp.bfloat16)
            gu[at, :] = low
            dctx_ref[at, :] = wide_dot(low, out_w, NT).astype(jnp.bfloat16)
            add_row(sums_ref, 4, low.astype(jnp.float32))
            add_row(sums_ref, 5, grad * n1)
            add_row(sums_ref, 6, grad)
            return carry

        lax.fori_loop(0, tiles, one, 0)
        grad_out = wide_dot(ctx_ref[...].T, gu[...], NN).astype(jnp.bfloat16)
        dwo_ref[...] = grad_out.reshape(dwo_ref.shape)


def back(info, gh2, hid, gel, fit, gmt, n1, r1, ctx, small, weights):
    tokens, width = gh2.shape
    _, groups, _, rows, _ = weights.shape

    def block(b, info):
        return (jnp.minimum(b, 3), 0, 0)

    return call(
        back_kernel,
        "back",
        info,
        5,
        [
            fixed((tokens, width)),
            pl.BlockSpec((1, tokens, width), block),
            pl.BlockSpec((1, tokens, width), block),
            fixed((width, tokens)),
            fixed((width, tokens)),
            fixed((tokens, width)),
            fixed((tokens, 128)),
            fixed((tokens, width)),
            fixed(small.shape),
            weight_spec(weights, lambda b: 4 + jnp.minimum(b, 3), False),
            weight_spec(weights, lambda b: 8 + jnp.minimum(b, 3), False),
            weight_spec(weights, lambda b: 3),
        ],
        [
            pl.BlockSpec((groups, 2, rows, width), lambda b, info: (0, jnp.minimum(b, 3), 0, 0)),
            resident((groups, rows, width)),
            resident((tokens, width)),
            resident((tokens, width)),
            resident((8, width)),
        ],
        [
            bf16_of(groups, 8, rows, width),
            bf16_of(groups, rows, width),
            f32_of(tokens, width),
            bf16_of(tokens, width),
            f32_of(8, width),
        ],
        [pltpu.VMEM((tokens, width), jnp.float32), pltpu.VMEM((tokens, width), jnp.bfloat16)],
        (gh2, hid, gel, fit, gmt, n1, r1, ctx, small, weights, weights, weights),
        22_000_000_000,
        40 << 20,
    )


def spill_kernel(info, dk_ref, dv_ref, wk, wv, out_ref):
    total = wide_dot(dk_ref[...], matrix(wk), NT) + wide_dot(dv_ref[...], matrix(wv), NT)
    out_ref[...] = total.astype(jnp.bfloat16)


def spill(info, dk, dv, weights):
    seq, width = dk.shape
    mid = seq // 4

    def other(b, info):
        return (2 * (1 - info[0]) + b, 0)

    return call(
        spill_kernel,
        "spill",
        info,
        2,
        [
            pl.BlockSpec((mid, width), other),
            pl.BlockSpec((mid, width), other),
            weight_spec(weights, lambda b: 1),
            weight_spec(weights, lambda b: 2),
        ],
        [pl.BlockSpec((mid, width), lambda b, info: (b, 0))],
        [bf16_of(2 * mid, width)],
        [],
        (dk, dv, weights, weights),
        2_400_000_000,
        8 << 20,
    )[0]


def weight_grads_kernel(
    info, x_ref, dq_ref, dk_ref, dv_ref, out_ref, sums_ref, q_acc, k_acc, v_acc
):
    step = pl.program_id(0)

    @pl.when(step == 0)
    def clear():
        sums_ref[...] = jnp.zeros_like(sums_ref)
        k_acc[...] = jnp.zeros_like(k_acc)
        v_acc[...] = jnp.zeros_like(v_acc)
        q_acc[...] = jnp.zeros_like(q_acc)

    flipped = x_ref[0].T
    k_acc[...] += wide_dot(flipped, dk_ref[...], NN)
    v_acc[...] += wide_dot(flipped, dv_ref[...], NN)
    add_row(sums_ref, 1, dv_ref[...].astype(jnp.float32))

    @pl.when(step < 2)
    def own():
        q_acc[...] += wide_dot(flipped, dq_ref[...], NN)
        add_row(sums_ref, 0, dq_ref[...].astype(jnp.float32))

    @pl.when(step == 3)
    def finish():
        groups, _, rows, width = out_ref.shape
        for m, acc in enumerate((q_acc, k_acc, v_acc)):
            out_ref[:, m : m + 1] = (
                acc[...].astype(jnp.bfloat16).reshape(groups, 1, rows, width)
            )


def weight_grads(info, x_all, dq, dk, dv, groups):
    _, mid, width = x_all.shape
    rows = width // groups

    def chunk(step, info):
        return lax.rem(step + 2 * info[0], 4)

    return call(
        weight_grads_kernel,
        "weight_grads",
        info,
        4,
        [
            pl.BlockSpec((1, mid, width), lambda g, info: (info[1 + chunk(g, info)], 0, 0)),
            pl.BlockSpec((mid, width), lambda g, info: (jnp.minimum(g, 1), 0)),
            pl.BlockSpec((mid, width), lambda g, info: (chunk(g, info), 0)),
            pl.BlockSpec((mid, width), lambda g, info: (chunk(g, info), 0)),
        ],
        [resident((groups, 3, rows, width)), resident((8, width))],
        [bf16_of(groups, 3, rows, width), f32_of(8, width)],
        [pltpu.VMEM((width, width), jnp.float32)] * 3,
        (x_all, dq, dk, dv),
        6_000_000_000,
        14 << 20,
    )


def input_grads_kernel(info, gh1_ref, dq_ref, dk_ref, dv_ref, more_ref, wq, wk, wv, out_ref):
    total = gh1_ref[...] + more_ref[...].astype(jnp.float32)
    total = total + wide_dot(dq_ref[...], matrix(wq), NT)
    total = total + wide_dot(dk_ref[...], matrix(wk), NT)
    total = total + wide_dot(dv_ref[...], matrix(wv), NT)
    out_ref[0] = total.astype(jnp.bfloat16)


def input_grads(info, gh1, dq, dk, dv, more, weights):
    tokens, width = gh1.shape
    steps = tokens // TILE
    mid = tokens // 2
    per = mid // TILE
    mine = pl.BlockSpec((TILE, width), lambda t, info: (t, 0))
    place = pl.BlockSpec((TILE, width), lambda t, info: (info[0] * steps + t, 0))

    return call(
        input_grads_kernel,
        "input_grads",
        info,
        steps,
        [
            mine,
            mine,
            place,
            place,
            mine,
            weight_spec(weights, lambda t: 0),
            weight_spec(weights, lambda t: 1),
            weight_spec(weights, lambda t: 2),
        ],
        [
            pl.BlockSpec(
                (1, TILE, width),
                lambda t, info: (info[1 + 2 * info[0] + t // per], t % per, 0),
            )
        ],
        [bf16_of(2, mid, width)],
        [],
        (gh1, dq, dk, dv, more, weights, weights, weights),
        3_700_000_000,
        14 << 20,
    )[0]


def adam_update(weight, first, second, grad, decay, rate):
    count = float(STEP)
    first_new = beta_one * first + (1.0 - beta_one) * grad
    second_new = beta_two * second + (1.0 - beta_two) * grad * grad
    first_hat = first_new / (1.0 - beta_one**count)
    second_hat = second_new / (1.0 - beta_two**count)
    weight_new = weight - rate * (first_hat / (jnp.sqrt(second_hat) + adam_eps) + decay * weight)
    return (weight_new, first_new, second_new)


def moves(n_ctx, n_tp, pick):
    pairs = []
    for c in range(n_ctx):
        for t in range(n_tp):
            side, core = t // 2, t % 2
            to_ctx = 2 * core + (pick ^ (c & 1))
            to_tp = 2 * side + c // 2
            pairs.append((c * n_tp + t, to_ctx * n_tp + to_tp))
    return pairs


def shards(
    inputs,
    cotangent,
    rand_blocks,
    slot_of,
    master,
    moment_one,
    moment_two,
    small_params,
    small_one,
    small_two,
):
    n_shard = lax.axis_size("shard")
    n_ctx = lax.axis_size("ctx")
    n_tp = lax.axis_size("tp")
    groups = n_ctx * n_tp
    held, rows, width = master.shape
    span = small_params.shape[0]
    my_ctx = lax.axis_index("ctx")
    my_tp = lax.axis_index("tp")
    parity = lax.rem(my_ctx, 2)
    half = lax.rem(my_tp, 2)
    plane = ("ctx", "tp")
    forth = [moves(n_ctx, n_tp, pick) for pick in range(2)]
    home = [[(b, a) for a, b in pairs] for pairs in forth]
    swap = [(t, t ^ 1) for t in range(n_tp)]

    arrival = [(b ^ parity) + 2 * (half ^ (j // 2)) for j, b in enumerate((0, 1, 0, 1))]
    info = jnp.concatenate([jnp.stack([half, *arrival]).astype(jnp.int32), slot_of])
    half_one = info[:1]

    def sent(field, pick):
        low = field.astype(jnp.bfloat16)
        return jnp.where(parity == 0, low[pick], low[1 - pick])

    def brought(field):
        pieces = [lax.ppermute(sent(field, pick), plane, forth[pick]) for pick in range(2)]
        return jnp.stack(pieces)

    def returned(field):
        first, second = [lax.ppermute(field[pick], plane, home[pick]) for pick in range(2)]
        swapped = parity == 1
        out = jnp.stack(
            [jnp.where(swapped, second, first), jnp.where(swapped, first, second)]
        )
        return out.astype(jnp.float32)

    x_own = brought(inputs)
    x_other = lax.ppermute(x_own, "tp", swap)
    x_all = jnp.concatenate([x_own, x_other])
    low = master.astype(jnp.bfloat16)
    weights = lax.all_gather(low, ("shard", "ctx", "tp"), axis=0)
    weights = weights.reshape(n_shard, groups, held, rows, width)
    small_low = small_params.astype(jnp.bfloat16)
    small = lax.all_gather(small_low, ("shard", "ctx", "tp"), axis=0, tiled=True)
    small = small.reshape(-1, width).astype(jnp.float32)

    q, k, v = project(info, x_all, small, weights)
    context, lse = attend(half_one, rand_blocks, q, k, v, 5)
    cot = brought(cotangent)
    out_low, n1, r1, fi, fit, hid, gel, gh2, gmt, sums_two = front(
        info, context, x_all, cot, small, weights
    )
    layer_out = returned(out_low)
    ffn_grads, out_grad, gh1, dctx, sums_one = back(
        info, gh2, hid, gel, fit, gmt, n1, r1, context, small, weights
    )
    ffn_rows = lax.psum_scatter(ffn_grads, plane, scatter_dimension=0, tiled=False)
    dq, dk, dv = attend_back(half_one, rand_blocks, q, k, v, lse, dctx, 5)
    more = lax.ppermute(spill(info, dk, dv, weights), "tp", swap)
    qkv_grads, sums_qkv = weight_grads(info, x_all, dq, dk, dv, groups)
    small_grad = jnp.concatenate(
        [
            sums_qkv[0],
            sums_qkv[1],
            sums_one[4],
            sums_one[5],
            sums_one[6],
            sums_one[0:4].reshape(-1),
            sums_two[0],
            sums_two[1],
            sums_two[2],
        ]
    )
    extra = -(-n_shard * span // width)
    small_rows = small_grad.reshape(n_shard, groups, span).transpose(1, 0, 2)
    small_rows = jnp.pad(
        small_rows.reshape(groups, n_shard * span), ((0, 0), (0, extra * width - n_shard * span))
    ).reshape(groups, extra, width)
    late = jnp.concatenate(
        [
            qkv_grads.reshape(groups, 3 * rows, width),
            out_grad,
            small_rows.astype(jnp.bfloat16),
        ],
        axis=1,
    )
    late_rows = lax.psum_scatter(late, plane, scatter_dimension=0, tiled=False)
    input_low = input_grads(info, gh1, dq, dk, dv, more, weights)
    input_grad = returned(input_low)

    own_rows = jnp.concatenate(
        [
            late_rows[: 4 * rows].reshape(4, rows, width),
            ffn_rows[0::2],
            ffn_rows[1::2],
        ]
    )
    picker = slot_of[None, :] == jnp.arange(n_shard * held, dtype=jnp.int32)[:, None]
    packed = jnp.einsum(
        "sm,mrd->srd", picker.astype(jnp.bfloat16), own_rows, preferred_element_type=jnp.float32
    ).astype(jnp.bfloat16)
    small_sum = late_rows[4 * rows :].reshape(-1)[: n_shard * span].reshape(n_shard, span)
    small_sum = jnp.pad(small_sum, ((0, 0), (0, width - span)))[:, None, :]
    final = jnp.concatenate([packed.reshape(n_shard, held * rows, width), small_sum], axis=1)
    final = lax.psum_scatter(final, "shard", scatter_dimension=0, tiled=False).astype(jnp.float32)
    slot_grads = final[: held * rows].reshape(held, rows, width)
    small_owned = final[held * rows, :span]
    master_new, first_new, second_new = adam_update(
        master, moment_one, moment_two, slot_grads, 0.01, rate_value
    )
    small_new, small_first, small_second = adam_update(
        small_params, small_one, small_two, small_owned, 0.0, small_rate
    )
    return (
        layer_out,
        input_grad,
        master_new,
        first_new,
        second_new,
        small_new,
        small_first,
        small_second,
    )


def solution(mesh):
    tokens = P(("shard", "tp"), "ctx", None)
    stored = P("shard", ("ctx", "tp"), None)
    spread = P(("shard", "ctx", "tp"))
    return jax.shard_map(
        shards,
        mesh=mesh,
        in_specs=(tokens, tokens, P(), P(), stored, stored, stored, spread, spread, spread),
        out_specs=(tokens, tokens, stored, stored, stored, spread, spread, spread),
        check_vma=False,
    )
```

time: 1640 us -> 502 us (0.31)
  local copies, waits for them, and re-layouts: 691 us -> 14.4 us
  matrix products: 383 us -> 1.19 us
  Pallas kernels: 0 us -> 180 us
  waiting for transfers between devices: 300 us -> 171 us
  other arithmetic: 104 us -> 27.7 us
  loops' own time: 27.3 us -> 0 us
    dot_general x52 -> x1, matrix products: 383 us -> 1.19 us  [shards(): jnp.einsum('sm,mrd->srd', picker.astype(jnp.bfloat16), own_rows, preferre...]
    reshape x41 -> x5, local copies, waits for them, and re-layouts: 266 us -> 0.31 us  [the longest x2 0.11 us: shards(): late_rows[4 * rows:].reshape(-1)[:n_shard * span].reshape(n_shard, span)]
    pallas_call x0 -> x8, Pallas kernels: none -> 180 us  [the longest x6 112 us: call(): pl.pallas_call(kernel, name=name, grid_spec=pltpu.PrefetchScalarGridSpec(...]
    reduce_scatter x1 -> x3, waiting for transfers between devices: 0.01 us -> 126 us  [the longest x1 79.1 us: shards(): lax.psum_scatter(ffn_grads, plane, scatter_dimension=0, tiled=False)]
    select_n x8 -> x0, local copies, waits for them, and re-layouts: 111 us -> none  [pick_one(): return jnp.take(source, chosen, axis=1)]
    unnamed x5 -> x4, waiting for transfers between devices: 101 us -> 0.73 us
    all_to_all x7 -> x0, waiting for transfers between devices: 100 us -> none  [the longest x1 24.1 us: shards(): lax.all_to_all(context_heads, 'ctx', split_axis=2, concat_axis=1, tiled=T...]
    all_gather x2 -> x1, waiting for transfers between devices: 98.8 us -> 11.6 us  [shards(): weights = lax.all_gather(low, ('shard', 'ctx', 'tp'), axis=0)]
  transfers between devices with their start and end apart: 11 -> 14, of which waited for: 10 -> 5; matrix products, arithmetic and copies ran while one was open for 4% -> 6% of each run, Pallas kernels for 0% -> 3%
where the time goes in v1:
time: 502 us; the launch traced here: 500 us
  Pallas kernels  180 us (36%)
  waiting for transfers between devices  171 us (34%)
  blocking collectives  63.5 us (13%)
  starting transfers between devices  28 us (6%)
  other arithmetic  27.7 us (6%)
  local copies, waits for them, and re-layouts  14.4 us (3%)
  between operations  14.1 us (3%)
    pallas_call x6, Pallas kernels, call(): pl.pallas_call(kernel, name=name, grid_spec=pltpu.PrefetchScalarGridSpec(...  112 us
    reduce_scatter x1, waiting for transfers between devices, shards(): lax.psum_scatter(ffn_grads, plane, scatter_dimension=0, tiled=False)  79.1 us
    unnamed x1, blocking collectives  63.5 us
    reduce_scatter x1, waiting for transfers between devices, shards(): late_rows = lax.psum_scatter(late, plane, scatter_dimension=0, tiled=False)  47.1 us
    pallas_call x1, Pallas kernels, attend_back(): pl.pallas_call(functools.partial(attend_back_kernel, unroll), grid_spec=s...  39.3 us
    pallas_call x1, Pallas kernels, attend(): pl.pallas_call(functools.partial(attend_kernel, unroll), grid_spec=spec,...  28.6 us
    ppermute x4, waiting for transfers between devices, brought(): lax.ppermute(sent(field, pick), plane, forth[pick])  19.3 us
    ppermute x4, waiting for transfers between devices, returned(): lax.ppermute(field[pick], plane, home[pick])  13.4 us
  transfers between devices with their start and end apart: 14, of which 5 were waited for; matrix products, arithmetic and copies ran while one was open for 6% of the time, Pallas kernels for 3%

profile of v1, /device:TPU:0, one launch (start us, length us, event | category | flops | bytes accessed | tf_op | source)
XLA Modules:
  0.0 500.0 jit_solution(8440427641253339983)
XLA Ops:
  7.2 2.0 convert_element_type.47
  9.3 2.0 convert_element_type.43
  11.4 0.8 collective-permute-start
  12.3 3.0 collective-permute-start.1
  15.3 19.3 %collective-permute-done.1 = bf16[512,768]{1,0:T(8,128)(2,1)S(1)} collective-permute-done((bf16[512,768]{1,0:T(8,128)(2,1)S(1)}, bf16[512,768]{1,0:T(8,128)(2,1)S(1)}, u32[]{:S(2)}, u32[]{:S(2)}) %collective-permute-start.1) | collective-permute-done | bytes 786464 | tf_op jit(solution)/shard_map/ppermute | solution.py:887
  34.6 0.1 pad_maximum_fusion.4
  34.8 3.8 collective-permute-start.2
  38.6 0.2 convert_element_type.48
  38.8 1.2 select_bitcast_fusion.5
  40.0 7.4 %collective-permute-start.3 = (bf16[512,768]{1,0:T(8,128)(2,1)}, bf16[512,768]{1,0:T(8,128)(2,1)}, u32[]{:S(2)}, u32[]{:S(2)}) collective-permute-start(bf16[512,768]{1,0:T(8,128)(2,1)} %get-tuple-element.78), channel_id=1, source_target_pairs={{0,0},{1,4},{2,2},{3,6},{4,1},{5,5},{6,3},{7,7},{8,8},{9,12},{10,1... | collective-permute-start | bytes 2359304 | tf_op jit(solution)/shard_map/ppermute | solution.py:887
  47.5 1.3 collective-permute-start.4
  48.7 0.3 dynamic-update-slice
  49.0 63.5 %all-reduce.2 = bf16[9216]{0:T(1024)(128)(2,1)S(1)} all-reduce(bf16[9216]{0:T(1024)(128)(2,1)S(1)} %dynamic-update-slice), channel_id=1, replica_groups=mesh['shard'=4,'ctx'=4,'tp'=2] {'shard','ctx','tp'}, use_global_device_ids=true, to_apply=%add.2 | all-reduce | flops 9216 | bytes 36864
  112.5 0.7 reshape.80.small
  113.1 0.9 copy.33.table_ref
  114.0 0.6 concatenate.20.info
  114.6 2.8 pad_maximum_fusion.5.cot_ref
  117.4 3.4 pad_maximum_fusion.1.x_ref
  120.8 11.6 %all-gather.3.cloned.1.call-done = bf16[96,96,768]{2,1,0:T(8,128)(2,1)} async-done(((bf16[3,96,768]{2,1,0:T(8,128)(2,1)}), bf16[96,96,768]{2,1,0:T(8,128)(2,1)}) %all-gather.3.cloned.1.call-update) | async-done | bytes 14155792 | tf_op jit(solution)/shard_map/all_gather | solution.py:902
  132.3 11.7 %project.1 = (bf16[1024,768]{1,0:T(8,128)(2,1)}, bf16[2048,768]{1,0:T(8,128)(2,1)}, bf16[2048,768]{1,0:T(8,128)(2,1)}) custom-call(s32[17]{0:T(128)} %concatenate.20.info, bf16[4,512,768]{2,1,0:T(8,128)(2,1)} %pad_maximum_fusion.1.x_ref, f32[12,768]{1,0:T(8,128)} %reshape.80.small, bf16[4,8,3,96,768]{4,3,2,1,0:T(8,128)(2,1)} %bitcast.49, ...), custom_call_target="tpu_custom_call" | custom-call | flops 6000000000 | bytes 16777216 | tf_op jit(solution)/shard_map/project/pallas_call | solution.py:374
  144.0 28.6 %attend.1 = (bf16[1024,768]{1,0:T(8,128)(2,1)}, f32[3,16,256]{2,1,0:T(8,128)}) custom-call(s32[1]{0:T(128)} %bitcast.half_ref, s32[12,30,3]{2,1,0:T(8,128)} %copy.33.table_ref, bf16[1024,768]{1,0:T(8,128)(2,1)} %get-tuple-element.32.q_ref, bf16[2048,768]{1,0:T(8,128)(2,1)} %get-tuple-element.33.k_ref, bf16[2048,768]{1,0:T(8,128)(2,1)} %get-tuple-element.34.v_ref), custom_call_target="tpu_custom_call" | custom-call | flops 60000002048 | bytes 12582912 | tf_op jit(solution)/shard_map/attend/pallas_call | solution.py:168
  172.7 28.9 %front.1 = (bf16[2,512,768]{2,1,0:T(8,128)(2,1)}, f32[1024,768]{1,0:T(8,128)}, f32[1024,128]{1,0:T(8,128)}, bf16[1024,768]{1,0:T(8,128)(2,1)}, bf16[768,1024]{1,...) custom-call(s32[17]{0:T(128)} %concatenate.20.info, ...), custom_call_target="tpu_custom_call" | custom-call | flops 11000000512 | bytes 41943040 | tf_op jit(solution)/shard_map/front/pallas_call | solution.py:374
  201.6 41.9 %back.1 = (bf16[8,8,96,768]{3,2,1,0:T(8,128)(2,1)}, bf16[8,96,768]{2,1,0:T(8,128)(2,1)}, f32[1024,768]{1,0:T(8,128)}, bf16[1024,768]{1,0:T(8,128)(2,1)}, f32[8,768]{1,0:T(8,128)}) custom-call(s32[17]{0:T(128)} %concatenate.20.info, f32[1024,768]{1,0:T(8,128)} %get-tuple-element.37.gh2_ref, bf16[4,1024,768]{2,1,0:T(8,128)(2,1)} %get-tuple-element.38.hid_ref, ...), custom_call_target="tpu_custom_call" | custom-call | flops 22000001024 | bytes 41943040 | tf_op jit(solution)/shard_map/back/pallas_call | solution.py:374
  243.5 0.7 convert.40
  244.4 39.3 %attend_back.1 = (bf16[1024,768]{1,0:T(8,128)(2,1)}, bf16[2048,768]{1,0:T(8,128)(2,1)}, bf16[2048,768]{1,0:T(8,128)(2,1)}) custom-call(s32[1]{0:T(128)} %bitcast.half_ref, s32[12,30,3]{2,1,0:T(8,128)} %copy.33.table_ref, bf16[1024,768]{1,0:T(8,128)(2,1)} %get-tuple-element.32.q_ref, bf16[2048,768]{1,0:T(8,128)(2,1)} %get-tuple-element.33.k_ref, ...), custom_call_target="tpu_custom_call" | custom-call | flops 120000004096 | bytes 25165824 | tf_op jit(solution)/shard_map/attend_back/pallas_call | solution.py:307
  283.7 13.3 %weight_grads.1 = (bf16[8,3,96,768]{3,2,1,0:T(8,128)(2,1)}, f32[8,768]{1,0:T(8,128)}) custom-call(s32[17]{0:T(128)} %concatenate.20.info, bf16[4,512,768]{2,1,0:T(8,128)(2,1)} %pad_maximum_fusion.1.x_ref, bf16[1024,768]{1,0:T(8,128)(2,1)} %get-tuple-element.47.dq_ref, bf16[2048,768]{1,0:T(8,128)(2,1)} %get-tuple-element.48.dk_ref, ...), custom_call_target="tpu_custom_call" | custom-call | flops 6000000000 | bytes 14680064 | tf_op jit(solution)/shard_map/weight_grads/pallas_call | solution.py:374
  297.0 0.7 convert.39
  297.8 0.2 dynamic-update-slice.1
  298.1 0.2 dynamic-update-slice.2
  298.3 0.2 dynamic-update-slice.3
  298.5 0.2 dynamic-update-slice.4
  298.7 0.2 dynamic-update-slice.5
  298.9 0.3 dynamic-update-slice.6
  299.1 0.2 dynamic-update-slice.7
  299.3 0.2 dynamic-update-slice.8
  299.5 0.2 dynamic-update-slice.9
  300.0 3.9 pad_maximum_fusion
  304.0 0.7 reduce-scatter.6.cloned.1.call-update
  304.7 6.6 %spill.1 = bf16[1024,768]{1,0:T(8,128)(2,1)} custom-call(s32[17]{0:T(128)} %concatenate.20.info, bf16[2048,768]{1,0:T(8,128)(2,1)} %get-tuple-element.48.dk_ref, bf16[2048,768]{1,0:T(8,128)(2,1)} %get-tuple-element.49.dv_ref, bf16[4,8,3,96,768]{4,3,2,1,0:T(8,128)(2,1)} %bitcast.64, bf16[4,8,3,96,768]{4,3,2,1,0:T(8,128)(2,1)} %bitcast.65), custom_call_target="tpu_custom_call" | custom-call | flops 2400000000 | bytes 8388608 | tf_op jit(solution)/shard_map/spill/pallas_call | solution.py:374
  311.3 0.3 collective-permute-start.7
  311.6 47.1 %reduce-scatter.4.cloned.1.call-done = bf16[1,386,768]{2,1,0:T(8,128)(2,1)} async-done(((bf16[8,386,768]{2,1,0:T(8,128)(2,1)}), bf16[1,386,768]{2,1,0:T(8,128)(2,1)}) %reduce-scatter.4.cloned.1.call-update) | async-done | bytes 592912 | tf_op jit(solution)/shard_map/reduce_scatter | solution.py:948
  358.8 0.8 slice.128
  359.7 79.1 %reduce-scatter.6.cloned.1.call-done = bf16[1,8,96,768]{3,2,1,0:T(8,128)(2,1)} async-done(((bf16[8,8,96,768]{3,2,1,0:T(8,128)(2,1)}), bf16[1,8,96,768]{3,2,1,0:T(8,128)(2,1)}) %reduce-scatter.6.cloned.1.call-update) | async-done | bytes 1179664 | tf_op jit(solution)/shard_map/reduce_scatter | solution.py:918
  438.7 1.3 fusion.12
  440.1 0.2 pad_maximum_fusion.3
  440.3 0.4 copy-done.13
  440.7 1.2 fusion.2
  441.9 0.5 copy.38
  442.5 1.4 pad_maximum_fusion.2
  443.8 2.6 slice_bitcast_fusion.3
  446.5 1.4 collective-permute-start.5
  447.8 7.4 %collective-permute-start.6 = (bf16[512,768]{1,0:T(8,128)(2,1)}, bf16[512,768]{1,0:T(8,128)(2,1)}, u32[]{:S(2)}, u32[]{:S(2)}) collective-permute-start(bf16[512,768]{1,0:T(8,128)(2,1)} %get-tuple-element.77), channel_id=1, source_target_pairs={{0,0},{4,1},{2,2},{6,3},{1,4},{5,5},{3,6},{7,7},{8,8},{12,9},{10,1... | collective-permute-start | bytes 2359304 | tf_op jit(solution)/shard_map/ppermute | solution.py:891
  455.3 1.1 copy-done.3
  456.4 9.6 %input_grads.1 = bf16[2,512,768]{2,1,0:T(8,128)(2,1)} custom-call(s32[17]{0:T(128)} %concatenate.20.info, f32[1024,768]{1,0:T(8,128)} %get-tuple-element.44.gh1_ref, bf16[1024,768]{1,0:T(8,128)(2,1)} %get-tuple-element.47.dq_ref, bf16[2048,768]{1,0:T(8,128)(2,1)} %get-tuple-element.48.dk_ref, bf16[2048,768]{1,0:T(8,128)(2,1)} %get-tuple-element.49.dv_ref, ...), custom_call_target="tpu_custom_call" | custom-call | flops 3700000000 | bytes 14680064 | tf_op jit(solution)/shard_map/input_grads/pallas_call | solution.py:374
  466.0 2.6 slice_bitcast_fusion.1
  468.6 0.6 collective-permute-start.8
  469.2 1.8 collective-permute-start.9
  471.0 13.4 %collective-permute-done.8 = bf16[512,768]{1,0:T(8,128)(2,1)S(1)} collective-permute-done((bf16[512,768]{1,0:T(8,128)(2,1)}, bf16[512,768]{1,0:T(8,128)(2,1)S(1)}, u32[]{:S(2)}, u32[]{:S(2)}) %collective-permute-start.8) | collective-permute-done | bytes 786464 | tf_op jit(solution)/shard_map/ppermute | solution.py:891
  484.4 1.3 select_bitcast_fusion.1
  485.7 1.9 maximum_convert_fusion.1
  487.6 1.9 maximum_convert_fusion
  489.5 1.2 convert_bitcast_fusion
  490.8 0.6 multiply_subtract_fusion.1
  491.5 2.0 multiply_subtract_fusion
  (69 shorter events, 1.0 us)
Async XLA Ops:
  7.2 125.2 %all-gather.3.cloned.1.call-start = ((), (), s32[]{:S(2)}) async-start(), calls=%async_computation.6 | async-start | bytes 14598144 | tf_op jit(solution)/shard_map/all_gather | solution.py:902
  9.2 349.5 %reduce-scatter.4.cloned.1.call-start = ((), (), s32[]{:S(2)}) async-start(), calls=%async_computation.3 | async-start | bytes 5419008 | tf_op jit(solution)/shard_map/reduce_scatter | solution.py:948
  11.4 27.1 %copy-start.2 = (f32[2,512,768]{2,1,0:T(8,128)S(1)}, f32[2,512,768]{2,1,0:T(8,128)}, u32[]{:S(2)}) copy-start(f32[2,512,768]{2,1,0:T(8,128)} %param.11) | copy-start | bytes 9437188
  11.4 3.9 collective-permute-start
  12.3 22.3 %collective-permute-start.1 = (bf16[512,768]{1,0:T(8,128)(2,1)S(1)}, bf16[512,768]{1,0:T(8,128)(2,1)S(1)}, u32[]{:S(2)}, u32[]{:S(2)}) collective-permute-start(bf16[512,768]{1,0:T(8,128)(2,1)S(1)} %get-tuple-element.81), channel_id=1, source_target_pairs={{0,2},{1,6},{2,0},{3,4},{4,3},{5,7},{6,1},{7,5},{8,10},{9,14},{10,... | collective-permute-start | bytes 2359304 | tf_op jit(solution)/shard_map/ppermute | solution.py:887
  34.8 82.6 %collective-permute-start.2 = (bf16[2,512,768]{2,1,0:T(8,128)(2,1)S(1)}, bf16[2,512,768]{2,1,0:T(8,128)(2,1)}, u32[]{:S(2)}, u32[]{:S(2)}) collective-permute-start(bf16[2,512,768]{2,1,0:T(8,128)(2,1)S(1)} %pad_maximum_fusion.4), channel_id=1, source_target_pairs={{0,1},{1,0},{2,3},{3,2},{4,5},{5,4},{6,7},{7,6},{8,9},{9,8},{10,11... | collective-permute-start | bytes 4718600 | tf_op jit(solution)/shard_map/ppermute | solution.py:899
  38.7 10.0 %copy-start.10 = (f32[288]{0:T(512)S(1)}, f32[288]{0:T(512)}, u32[]{:S(2)}) copy-start(f32[288]{0:T(512)} %param.17) | copy-start | bytes 3460
  38.7 74.4 %copy-start.7 = (s32[12,30,3]{1,2,0:T(4,128)S(1)}, s32[12,30,3]{1,2,0:T(4,128)}, u32[]{:S(2)}) copy-start(s32[12,30,3]{1,2,0:T(4,128)} %param.12) | copy-start | bytes 12964
  38.8 75.2 %copy-start.12 = (s32[12]{0:T(128)S(1)}, s32[12]{0:T(128)}, u32[]{:S(2)}) copy-start(s32[12]{0:T(128)} %param.13) | copy-start | bytes 148
  40.0 74.5 %collective-permute-start.3 = (bf16[512,768]{1,0:T(8,128)(2,1)}, bf16[512,768]{1,0:T(8,128)(2,1)}, u32[]{:S(2)}, u32[]{:S(2)}) collective-permute-start(bf16[512,768]{1,0:T(8,128)(2,1)} %get-tuple-element.78), channel_id=1, source_target_pairs={{0,0},{1,4},{2,2},{3,6},{4,1},{5,5},{6,3},{7,7},{8,8},{9,12},{10,1... | collective-permute-start | bytes 2359304 | tf_op jit(solution)/shard_map/ppermute | solution.py:887
  47.5 67.1 %collective-permute-start.4 = (bf16[512,768]{1,0:T(8,128)(2,1)}, bf16[512,768]{1,0:T(8,128)(2,1)}, u32[]{:S(2)}, u32[]{:S(2)}) collective-permute-start(bf16[512,768]{1,0:T(8,128)(2,1)} %get-tuple-element.79), channel_id=1, source_target_pairs={{0,2},{1,6},{2,0},{3,4},{4,3},{5,7},{6,1},{7,5},{8,10},{9,14},{10,... | collective-permute-start | bytes 2359304 | tf_op jit(solution)/shard_map/ppermute | solution.py:887
  201.6 42.7 %copy-start.8 = (f32[8,768]{1,0:T(8,128)S(1)}, f32[8,768]{1,0:T(8,128)}, u32[]{:S(2)}) copy-start(f32[8,768]{1,0:T(8,128)} %get-tuple-element.54) | copy-start | bytes 73732
  283.7 14.1 %copy-start.9 = (bf16[9216]{0:T(1024)(128)(2,1)S(1)}, bf16[9216]{0:T(1024)(128)(2,1)}, u32[]{:S(2)}) copy-start(bf16[9216]{0:T(1024)(128)(2,1)} %custom-call) | copy-start | bytes 55300
  283.7 16.3 %copy-start.4 = (bf16[8,96,768]{2,1,0:T(8,128)(2,1)S(1)}, bf16[8,96,768]{2,1,0:T(8,128)(2,1)}, u32[]{:S(2)}) copy-start(bf16[8,96,768]{2,1,0:T(8,128)(2,1)} %get-tuple-element.51) | copy-start | bytes 3538948
  303.9 134.8 %reduce-scatter.6.cloned.1.call-start = ((), (), s32[]{:S(2)}) async-start(), calls=%async_computation.4 | async-start | bytes 10616832 | tf_op jit(solution)/shard_map/reduce_scatter | solution.py:918
  304.7 184.8 %reduce-scatter.8.cloned.1.call-start = ((), (), s32[]{:S(2)}) async-start(), calls=%async_computation.5 | async-start | bytes 2273280 | tf_op jit(solution)/shard_map/reduce_scatter | solution.py:966
  311.3 143.9 %collective-permute-start.7 = (bf16[1024,768]{1,0:T(8,128)(2,1)}, bf16[1024,768]{1,0:T(8,128)(2,1)S(1)}, u32[]{:S(2)}, u32[]{:S(2)}) collective-permute-start(bf16[1024,768]{1,0:T(8,128)(2,1)} %spill.1), channel_id=1, source_target_pairs={{0,1},{1,0},{2,3},{3,2},{4,5},{5,4},{6,7},{7,6},{8,9},{9,8},{10,11... | collective-permute-start | bytes 4718600 | tf_op jit(solution)/shard_map/ppermute | solution.py:920
  358.8 81.3 %slice-start = ((bf16[1,386,768]{2,1,0:T(8,128)(2,1)}), bf16[1,384,768]{2,1,0:T(8,128)(2,1)S(1)}, s32[]{:S(2)}) async-start(bf16[1,386,768]{2,1,0:T(8,128)(2,1)} %reduce-scatter.4.cloned.1.call-done), calls=%async_computation.7 | async-start | bytes 1179648 | tf_op jit(solution)/shard_map/slice | solution.py:954
  440.1 0.7 copy-start.13
  446.5 24.5 %collective-permute-start.5 = (bf16[512,768]{1,0:T(8,128)(2,1)}, bf16[512,768]{1,0:T(8,128)(2,1)S(1)}, u32[]{:S(2)}, u32[]{:S(2)}) collective-permute-start(bf16[512,768]{1,0:T(8,128)(2,1)} %get-tuple-element.76), channel_id=1, source_target_pairs={{2,0},{6,1},{0,2},{4,3},{3,4},{7,5},{1,6},{5,7},{10,8},{14,9},{8,1... | collective-permute-start | bytes 2359304 | tf_op jit(solution)/shard_map/ppermute | solution.py:891
  447.8 23.2 %collective-permute-start.6 = (bf16[512,768]{1,0:T(8,128)(2,1)}, bf16[512,768]{1,0:T(8,128)(2,1)}, u32[]{:S(2)}, u32[]{:S(2)}) collective-permute-start(bf16[512,768]{1,0:T(8,128)(2,1)} %get-tuple-element.77), channel_id=1, source_target_pairs={{0,0},{4,1},{2,2},{6,3},{1,4},{5,5},{3,6},{7,7},{8,8},{12,9},{10,1... | collective-permute-start | bytes 2359304 | tf_op jit(solution)/shard_map/ppermute | solution.py:891
  455.3 1.1 copy-start.3
  468.6 15.8 %collective-permute-start.8 = (bf16[512,768]{1,0:T(8,128)(2,1)}, bf16[512,768]{1,0:T(8,128)(2,1)S(1)}, u32[]{:S(2)}, u32[]{:S(2)}) collective-permute-start(bf16[512,768]{1,0:T(8,128)(2,1)} %get-tuple-element.72), channel_id=1, source_target_pairs={{2,0},{6,1},{0,2},{4,3},{3,4},{7,5},{1,6},{5,7},{10,8},{14,9},{8,1... | collective-permute-start | bytes 2359304 | tf_op jit(solution)/shard_map/ppermute | solution.py:891
  469.2 15.2 %collective-permute-start.9 = (bf16[512,768]{1,0:T(8,128)(2,1)}, bf16[512,768]{1,0:T(8,128)(2,1)S(1)}, u32[]{:S(2)}, u32[]{:S(2)}) collective-permute-start(bf16[512,768]{1,0:T(8,128)(2,1)} %get-tuple-element.73), channel_id=1, source_target_pairs={{0,0},{4,1},{2,2},{6,3},{1,4},{5,5},{3,6},{7,7},{8,8},{12,9},{10,1... | collective-permute-start | bytes 2359304 | tf_op jit(solution)/shard_map/ppermute | solution.py:891
  487.6 3.2 copy-start.11
  487.6 3.2 copy-start.14
  487.6 3.2 copy-start.15
  489.5 2.0 copy-start.1
  489.5 1.9 copy-start
  489.5 2.0 copy-start.5
  489.5 2.0 copy-start.6
Sparse Core Ops, SparseCore 0:
  11.5 120.8 all-gather.2
  304.0 54.6 reduce-scatter.3
  362.3 76.4 reduce-scatter.5
  444.0 39.3 reduce-scatter.7

commit v2 on v1

--- a/solution.py
+++ b/solution.py
@@ -945,6 +945,7 @@
         ],
         axis=1,
     )
+    late, ffn_rows = lax.optimization_barrier((late, ffn_rows))
     late_rows = lax.psum_scatter(late, plane, scatter_dimension=0, tiled=False)
     input_low = input_grads(info, gh1, dq, dk, dv, more, weights)
     input_grad = returned(input_low)

time: 502 us -> 440 us (0.88)
  waiting for transfers between devices: 171 us -> 113 us
  starting transfers between devices: 28 us -> 22.2 us
    reduce_scatter x1, waiting for transfers between devices: 79.1 us -> 14.3 us  [shards(): lax.psum_scatter(ffn_grads, plane, scatter_dimension=0, tiled=False)]
    ppermute x4, starting transfers between devices: 11.2 us -> 5.69 us  [returned(): lax.ppermute(field[pick], plane, home[pick])]
  transfers between devices with their start and end apart: 14 -> 14, of which waited for: 5 -> 6; matrix products, arithmetic and copies ran while one was open for 6% -> 8% of each run, Pallas kernels for 3% -> 16%
where the time goes in v2:
time: 440 us; the launch traced here: 436 us
  Pallas kernels  180 us (41%)
  waiting for transfers between devices  113 us (26%)
  blocking collectives  63.5 us (14%)
  other arithmetic  25.8 us (6%)
  starting transfers between devices  22.2 us (5%)
  local copies, waits for them, and re-layouts  15.4 us (4%)
  between operations  14.1 us (3%)
    pallas_call x6, Pallas kernels, call(): pl.pallas_call(kernel, name=name, grid_spec=pltpu.PrefetchScalarGridSpec(...  112 us
    unnamed x1, blocking collectives  63.5 us
    reduce_scatter x1, waiting for transfers between devices, shards(): late_rows = lax.psum_scatter(late, plane, scatter_dimension=0, tiled=False)  50.1 us
    pallas_call x1, Pallas kernels, attend_back(): pl.pallas_call(functools.partial(attend_back_kernel, unroll), grid_spec=s...  39.7 us
    pallas_call x1, Pallas kernels, attend(): pl.pallas_call(functools.partial(attend_kernel, unroll), grid_spec=spec,...  28.7 us
    ppermute x4, waiting for transfers between devices, brought(): lax.ppermute(sent(field, pick), plane, forth[pick])  19.3 us
    ppermute x4, waiting for transfers between devices, returned(): lax.ppermute(field[pick], plane, home[pick])  18 us
    reduce_scatter x1, waiting for transfers between devices, shards(): lax.psum_scatter(ffn_grads, plane, scatter_dimension=0, tiled=False)  14.3 us
  transfers between devices with their start and end apart: 14, of which 6 were waited for; matrix products, arithmetic and copies ran while one was open for 8% of the time, Pallas kernels for 16%

profile of v2, /device:TPU:0, one launch (start us, length us, event | category | flops | bytes accessed | tf_op | source)
XLA Modules:
  0.0 435.8 jit_solution(13785083378783118294)
XLA Ops:
  7.2 2.0 convert_element_type.47
  9.3 2.0 convert_element_type.43
  11.4 0.8 collective-permute-start
  12.3 3.0 collective-permute-start.1
  15.3 19.3 %collective-permute-done.1 = bf16[512,768]{1,0:T(8,128)(2,1)S(1)} collective-permute-done((bf16[512,768]{1,0:T(8,128)(2,1)S(1)}, bf16[512,768]{1,0:T(8,128)(2,1)S(1)}, u32[]{:S(2)}, u32[]{:S(2)}) %collective-permute-start.1) | collective-permute-done | bytes 786464 | tf_op jit(solution)/shard_map/ppermute | solution.py:887
  34.8 3.8 collective-permute-start.2
  38.6 0.2 convert_element_type.48
  38.8 1.2 select_bitcast_fusion.5
  40.0 7.4 %collective-permute-start.3 = (bf16[512,768]{1,0:T(8,128)(2,1)}, bf16[512,768]{1,0:T(8,128)(2,1)}, u32[]{:S(2)}, u32[]{:S(2)}) collective-permute-start(bf16[512,768]{1,0:T(8,128)(2,1)} %get-tuple-element.82), channel_id=1, source_target_pairs={{0,0},{1,4},{2,2},{3,6},{4,1},{5,5},{6,3},{7,7},{8,8},{9,12},{10,1... | collective-permute-start | bytes 2359304 | tf_op jit(solution)/shard_map/ppermute | solution.py:887
  47.5 1.3 collective-permute-start.4
  48.7 0.3 dynamic-update-slice
  49.0 63.5 %all-reduce.2 = bf16[9216]{0:T(1024)(128)(2,1)S(1)} all-reduce(bf16[9216]{0:T(1024)(128)(2,1)S(1)} %dynamic-update-slice), channel_id=1, replica_groups=mesh['shard'=4,'ctx'=4,'tp'=2] {'shard','ctx','tp'}, use_global_device_ids=true, to_apply=%add.2 | all-reduce | flops 9216 | bytes 36864
  112.5 0.7 reshape.80.small
  113.1 0.8 copy.33.table_ref
  114.0 0.6 concatenate.20.info
  114.6 2.8 pad_maximum_fusion.5.cot_ref
  117.4 3.4 pad_maximum_fusion.1.x_ref
  120.8 11.6 %all-gather.3.cloned.1.call-done = bf16[96,96,768]{2,1,0:T(8,128)(2,1)} async-done(((bf16[3,96,768]{2,1,0:T(8,128)(2,1)}), bf16[96,96,768]{2,1,0:T(8,128)(2,1)}) %all-gather.3.cloned.1.call-update) | async-done | bytes 14155792 | tf_op jit(solution)/shard_map/all_gather | solution.py:902
  132.3 11.7 %project.1 = (bf16[1024,768]{1,0:T(8,128)(2,1)}, bf16[2048,768]{1,0:T(8,128)(2,1)}, bf16[2048,768]{1,0:T(8,128)(2,1)}) custom-call(s32[17]{0:T(128)} %concatenate.20.info, bf16[4,512,768]{2,1,0:T(8,128)(2,1)} %pad_maximum_fusion.1.x_ref, f32[12,768]{1,0:T(8,128)} %reshape.80.small, bf16[4,8,3,96,768]{4,3,2,1,0:T(8,128)(2,1)} %bitcast.49, ...), custom_call_target="tpu_custom_call" | custom-call | flops 6000000000 | bytes 16777216 | tf_op jit(solution)/shard_map/project/pallas_call | solution.py:374
  144.0 28.7 %attend.1 = (bf16[1024,768]{1,0:T(8,128)(2,1)}, f32[3,16,256]{2,1,0:T(8,128)}) custom-call(s32[1]{0:T(128)} %bitcast.half_ref, s32[12,30,3]{2,1,0:T(8,128)} %copy.33.table_ref, bf16[1024,768]{1,0:T(8,128)(2,1)} %get-tuple-element.34.q_ref, bf16[2048,768]{1,0:T(8,128)(2,1)} %get-tuple-element.35.k_ref, bf16[2048,768]{1,0:T(8,128)(2,1)} %get-tuple-element.36.v_ref), custom_call_target="tpu_custom_call" | custom-call | flops 60000002048 | bytes 12582912 | tf_op jit(solution)/shard_map/attend/pallas_call | solution.py:168
  172.7 28.9 %front.1 = (bf16[2,512,768]{2,1,0:T(8,128)(2,1)}, f32[1024,768]{1,0:T(8,128)}, f32[1024,128]{1,0:T(8,128)}, bf16[1024,768]{1,0:T(8,128)(2,1)}, bf16[768,1024]{1,...) custom-call(s32[17]{0:T(128)} %concatenate.20.info, ...), custom_call_target="tpu_custom_call" | custom-call | flops 11000000512 | bytes 41943040 | tf_op jit(solution)/shard_map/front/pallas_call | solution.py:374
  201.6 41.8 %back.1 = (bf16[8,8,96,768]{3,2,1,0:T(8,128)(2,1)}, bf16[8,96,768]{2,1,0:T(8,128)(2,1)}, f32[1024,768]{1,0:T(8,128)}, bf16[1024,768]{1,0:T(8,128)(2,1)}, f32[8,768]{1,0:T(8,128)}) custom-call(s32[17]{0:T(128)} %concatenate.20.info, f32[1024,768]{1,0:T(8,128)} %get-tuple-element.39.gh2_ref, bf16[4,1024,768]{2,1,0:T(8,128)(2,1)} %get-tuple-element.40.hid_ref, ...), custom_call_target="tpu_custom_call" | custom-call | flops 22000001024 | bytes 41943040 | tf_op jit(solution)/shard_map/back/pallas_call | solution.py:374
  243.6 0.6 copy-done.9
  244.3 39.7 %attend_back.1 = (bf16[1024,768]{1,0:T(8,128)(2,1)}, bf16[2048,768]{1,0:T(8,128)(2,1)}, bf16[2048,768]{1,0:T(8,128)(2,1)}) custom-call(s32[1]{0:T(128)} %bitcast.half_ref, s32[12,30,3]{2,1,0:T(8,128)} %copy.33.table_ref, bf16[1024,768]{1,0:T(8,128)(2,1)} %get-tuple-element.34.q_ref, bf16[2048,768]{1,0:T(8,128)(2,1)} %get-tuple-element.35.k_ref, ...), custom_call_target="tpu_custom_call" | custom-call | flops 120000004096 | bytes 25165824 | tf_op jit(solution)/shard_map/attend_back/pallas_call | solution.py:307
  283.9 13.1 %weight_grads.1 = (bf16[8,3,96,768]{3,2,1,0:T(8,128)(2,1)}, f32[8,768]{1,0:T(8,128)}) custom-call(s32[17]{0:T(128)} %concatenate.20.info, bf16[4,512,768]{2,1,0:T(8,128)(2,1)} %pad_maximum_fusion.1.x_ref, bf16[1024,768]{1,0:T(8,128)(2,1)} %get-tuple-element.49.dq_ref, bf16[2048,768]{1,0:T(8,128)(2,1)} %get-tuple-element.50.dk_ref, ...), custom_call_target="tpu_custom_call" | custom-call | flops 6000000000 | bytes 14680064 | tf_op jit(solution)/shard_map/weight_grads/pallas_call | solution.py:374
  297.0 0.7 convert.39
  297.8 0.2 dynamic-update-slice.1
  298.0 0.2 dynamic-update-slice.2
  298.3 0.2 dynamic-update-slice.3
  298.5 0.2 dynamic-update-slice.4
  298.7 0.2 dynamic-update-slice.5
  298.9 0.3 dynamic-update-slice.6
  299.2 0.2 dynamic-update-slice.7
  299.5 0.2 dynamic-update-slice.8
  299.7 0.2 dynamic-update-slice.9
  300.1 3.9 pad_maximum_fusion
  304.0 14.3 %reduce-scatter.4.cloned.1.call-done = bf16[1,8,96,768]{3,2,1,0:T(8,128)(2,1)} async-done(((bf16[8,8,96,768]{3,2,1,0:T(8,128)(2,1)}), bf16[1,8,96,768]{3,2,1,0:T(8,128)(2,1)}) %reduce-scatter.4.cloned.1.call-update) | async-done | bytes 1179664 | tf_op jit(solution)/shard_map/reduce_scatter | solution.py:918
  318.4 6.8 %spill.1 = bf16[1024,768]{1,0:T(8,128)(2,1)} custom-call(s32[17]{0:T(128)} %concatenate.20.info, bf16[2048,768]{1,0:T(8,128)(2,1)} %get-tuple-element.50.dk_ref, bf16[2048,768]{1,0:T(8,128)(2,1)} %get-tuple-element.51.dv_ref, bf16[4,8,3,96,768]{4,3,2,1,0:T(8,128)(2,1)} %bitcast.64, bf16[4,8,3,96,768]{4,3,2,1,0:T(8,128)(2,1)} %bitcast.65), custom_call_target="tpu_custom_call" | custom-call | flops 2400000000 | bytes 8388608 | tf_op jit(solution)/shard_map/spill/pallas_call | solution.py:374
  325.2 1.3 fusion.12
  326.6 50.1 %reduce-scatter.6.cloned.1.call-done = bf16[1,386,768]{2,1,0:T(8,128)(2,1)} async-done(((bf16[8,386,768]{2,1,0:T(8,128)(2,1)}), bf16[1,386,768]{2,1,0:T(8,128)(2,1)}) %reduce-scatter.6.cloned.1.call-update) | async-done | bytes 592912 | tf_op jit(solution)/shard_map/reduce_scatter | solution.py:949
  376.6 0.7 slice.128
  377.5 1.1 slice.127
  378.6 0.2 pad_maximum_fusion.3
  378.8 0.4 copy-done.14
  379.2 1.2 fusion.2
  380.5 0.5 copy.38
  381.0 1.3 pad_maximum_fusion.2
  382.4 0.7 copy-done.4
  383.1 1.3 slice_bitcast_fusion.3
  384.3 1.4 collective-permute-start.5
  385.7 1.8 collective-permute-start.6
  387.5 1.1 copy-done.3
  388.7 9.5 %input_grads.1 = bf16[2,512,768]{2,1,0:T(8,128)(2,1)} custom-call(s32[17]{0:T(128)} %concatenate.20.info, f32[1024,768]{1,0:T(8,128)} %get-tuple-element.46.gh1_ref, bf16[1024,768]{1,0:T(8,128)(2,1)} %get-tuple-element.49.dq_ref, bf16[2048,768]{1,0:T(8,128)(2,1)} %get-tuple-element.50.dk_ref, bf16[2048,768]{1,0:T(8,128)(2,1)} %get-tuple-element.51.dv_ref, ...), custom_call_target="tpu_custom_call" | custom-call | flops 3700000000 | bytes 14680064 | tf_op jit(solution)/shard_map/input_grads/pallas_call | solution.py:374
  398.2 2.6 slice_bitcast_fusion.1
  400.8 0.7 collective-permute-start.8
  401.5 1.8 collective-permute-start.9
  403.3 1.4 collective-permute-done.5
  404.7 16.6 %collective-permute-done.8 = bf16[512,768]{1,0:T(8,128)(2,1)S(1)} collective-permute-done((bf16[512,768]{1,0:T(8,128)(2,1)}, bf16[512,768]{1,0:T(8,128)(2,1)S(1)}, u32[]{:S(2)}, u32[]{:S(2)}) %collective-permute-start.8) | collective-permute-done | bytes 786464 | tf_op jit(solution)/shard_map/ppermute | solution.py:891
  421.3 0.2 select_bitcast_fusion.1
  421.5 1.9 maximum_convert_fusion.1
  423.4 1.9 maximum_convert_fusion
  425.3 1.2 convert_bitcast_fusion
  426.6 0.6 multiply_subtract_fusion.1
  427.3 2.0 multiply_subtract_fusion
  (70 shorter events, 1.2 us)
Async XLA Ops:
  7.2 125.2 %all-gather.3.cloned.1.call-start = ((), (), s32[]{:S(2)}) async-start(), calls=%async_computation.6 | async-start | bytes 14598144 | tf_op jit(solution)/shard_map/all_gather | solution.py:902
  9.2 309.1 %reduce-scatter.4.cloned.1.call-start = ((), (), s32[]{:S(2)}) async-start(), calls=%async_computation.3 | async-start | bytes 10616832 | tf_op jit(solution)/shard_map/reduce_scatter | solution.py:918
  11.4 27.1 %copy-start.2 = (f32[2,512,768]{2,1,0:T(8,128)S(1)}, f32[2,512,768]{2,1,0:T(8,128)}, u32[]{:S(2)}) copy-start(f32[2,512,768]{2,1,0:T(8,128)} %param.11) | copy-start | bytes 9437188
  11.4 3.9 collective-permute-start
  12.3 22.3 %collective-permute-start.1 = (bf16[512,768]{1,0:T(8,128)(2,1)S(1)}, bf16[512,768]{1,0:T(8,128)(2,1)S(1)}, u32[]{:S(2)}, u32[]{:S(2)}) collective-permute-start(bf16[512,768]{1,0:T(8,128)(2,1)S(1)} %get-tuple-element.85), channel_id=1, source_target_pairs={{0,2},{1,6},{2,0},{3,4},{4,3},{5,7},{6,1},{7,5},{8,10},{9,14},{10,... | collective-permute-start | bytes 2359304 | tf_op jit(solution)/shard_map/ppermute | solution.py:887
  34.8 82.6 %collective-permute-start.2 = (bf16[2,512,768]{2,1,0:T(8,128)(2,1)S(1)}, bf16[2,512,768]{2,1,0:T(8,128)(2,1)}, u32[]{:S(2)}, u32[]{:S(2)}) collective-permute-start(bf16[2,512,768]{2,1,0:T(8,128)(2,1)S(1)} %pad_maximum_fusion.4), channel_id=1, source_target_pairs={{0,1},{1,0},{2,3},{3,2},{4,5},{5,4},{6,7},{7,6},{8,9},{9,8},{10,11... | collective-permute-start | bytes 4718600 | tf_op jit(solution)/shard_map/ppermute | solution.py:899
  38.7 10.0 %copy-start.11 = (f32[288]{0:T(512)S(1)}, f32[288]{0:T(512)}, u32[]{:S(2)}) copy-start(f32[288]{0:T(512)} %param.17) | copy-start | bytes 3460
  38.7 74.4 %copy-start.8 = (s32[12,30,3]{1,2,0:T(4,128)S(1)}, s32[12,30,3]{1,2,0:T(4,128)}, u32[]{:S(2)}) copy-start(s32[12,30,3]{1,2,0:T(4,128)} %param.12) | copy-start | bytes 12964
  38.8 75.2 %copy-start.13 = (s32[12]{0:T(128)S(1)}, s32[12]{0:T(128)}, u32[]{:S(2)}) copy-start(s32[12]{0:T(128)} %param.13) | copy-start | bytes 148
  40.0 74.6 %collective-permute-start.3 = (bf16[512,768]{1,0:T(8,128)(2,1)}, bf16[512,768]{1,0:T(8,128)(2,1)}, u32[]{:S(2)}, u32[]{:S(2)}) collective-permute-start(bf16[512,768]{1,0:T(8,128)(2,1)} %get-tuple-element.82), channel_id=1, source_target_pairs={{0,0},{1,4},{2,2},{3,6},{4,1},{5,5},{6,3},{7,7},{8,8},{9,12},{10,1... | collective-permute-start | bytes 2359304 | tf_op jit(solution)/shard_map/ppermute | solution.py:887
  47.5 67.1 %collective-permute-start.4 = (bf16[512,768]{1,0:T(8,128)(2,1)}, bf16[512,768]{1,0:T(8,128)(2,1)}, u32[]{:S(2)}, u32[]{:S(2)}) collective-permute-start(bf16[512,768]{1,0:T(8,128)(2,1)} %get-tuple-element.83), channel_id=1, source_target_pairs={{0,2},{1,6},{2,0},{3,4},{4,3},{5,7},{6,1},{7,5},{8,10},{9,14},{10,... | collective-permute-start | bytes 2359304 | tf_op jit(solution)/shard_map/ppermute | solution.py:887
  243.5 0.7 copy-start.9
  243.5 0.7 copy-start.10
  243.5 133.1 %reduce-scatter.6.cloned.1.call-start = ((), (), s32[]{:S(2)}) async-start(), calls=%async_computation.4 | async-start | bytes 5419008 | tf_op jit(solution)/shard_map/reduce_scatter | solution.py:949
  283.9 16.2 %copy-start.5 = (bf16[8,96,768]{2,1,0:T(8,128)(2,1)S(1)}, bf16[8,96,768]{2,1,0:T(8,128)(2,1)}, u32[]{:S(2)}) copy-start(bf16[8,96,768]{2,1,0:T(8,128)(2,1)} %get-tuple-element.53) | copy-start | bytes 3538948
  318.3 106.9 %reduce-scatter.8.cloned.1.call-start = ((), (), s32[]{:S(2)}) async-start(), calls=%async_computation.5 | async-start | bytes 2273280 | tf_op jit(solution)/shard_map/reduce_scatter | solution.py:967
  325.2 62.3 %collective-permute-start.7 = (bf16[1024,768]{1,0:T(8,128)(2,1)}, bf16[1024,768]{1,0:T(8,128)(2,1)S(1)}, u32[]{:S(2)}, u32[]{:S(2)}) collective-permute-start(bf16[1024,768]{1,0:T(8,128)(2,1)} %spill.1), channel_id=1, source_target_pairs={{0,1},{1,0},{2,3},{3,2},{4,5},{5,4},{6,7},{7,6},{8,9},{9,8},{10,11... | collective-permute-start | bytes 4718600 | tf_op jit(solution)/shard_map/ppermute | solution.py:920
  378.6 0.7 copy-start.14
  381.0 2.1 copy-start.4
  384.3 20.4 %collective-permute-start.5 = (bf16[512,768]{1,0:T(8,128)(2,1)}, bf16[512,768]{1,0:T(8,128)(2,1)S(1)}, u32[]{:S(2)}, u32[]{:S(2)}) collective-permute-start(bf16[512,768]{1,0:T(8,128)(2,1)} %get-tuple-element.80), channel_id=1, source_target_pairs={{2,0},{6,1},{0,2},{4,3},{3,4},{7,5},{1,6},{5,7},{10,8},{14,9},{8,1... | collective-permute-start | bytes 2359304 | tf_op jit(solution)/shard_map/ppermute | solution.py:891
  385.7 19.0 %collective-permute-start.6 = (bf16[512,768]{1,0:T(8,128)(2,1)}, bf16[512,768]{1,0:T(8,128)(2,1)S(1)}, u32[]{:S(2)}, u32[]{:S(2)}) collective-permute-start(bf16[512,768]{1,0:T(8,128)(2,1)} %get-tuple-element.81), channel_id=1, source_target_pairs={{0,0},{4,1},{2,2},{6,3},{1,4},{5,5},{3,6},{7,7},{8,8},{12,9},{10,1... | collective-permute-start | bytes 2359304 | tf_op jit(solution)/shard_map/ppermute | solution.py:891
  387.5 1.1 copy-start.3
  400.8 20.5 %collective-permute-start.8 = (bf16[512,768]{1,0:T(8,128)(2,1)}, bf16[512,768]{1,0:T(8,128)(2,1)S(1)}, u32[]{:S(2)}, u32[]{:S(2)}) collective-permute-start(bf16[512,768]{1,0:T(8,128)(2,1)} %get-tuple-element.76), channel_id=1, source_target_pairs={{2,0},{6,1},{0,2},{4,3},{3,4},{7,5},{1,6},{5,7},{10,8},{14,9},{8,1... | collective-permute-start | bytes 2359304 | tf_op jit(solution)/shard_map/ppermute | solution.py:891
  401.5 19.8 %collective-permute-start.9 = (bf16[512,768]{1,0:T(8,128)(2,1)}, bf16[512,768]{1,0:T(8,128)(2,1)S(1)}, u32[]{:S(2)}, u32[]{:S(2)}) collective-permute-start(bf16[512,768]{1,0:T(8,128)(2,1)} %get-tuple-element.77), channel_id=1, source_target_pairs={{0,0},{4,1},{2,2},{6,3},{1,4},{5,5},{3,6},{7,7},{8,8},{12,9},{10,1... | collective-permute-start | bytes 2359304 | tf_op jit(solution)/shard_map/ppermute | solution.py:891
  423.4 3.2 copy-start.12
  423.4 3.2 copy-start.15
  423.4 3.2 copy-start.16
  425.3 2.0 copy-start.1
  425.3 1.9 copy-start
  425.3 2.0 copy-start.6
  425.3 2.0 copy-start.7
Sparse Core Ops, SparseCore 0:
  11.5 120.8 all-gather.2
  243.7 74.6 reduce-scatter.3
  321.8 54.8 reduce-scatter.5
  382.5 39.2 reduce-scatter.7

commit v3 on v2

--- a/solution.py
+++ b/solution.py
@@ -341,25 +341,26 @@
 
 def matrix(ref):
     value = ref[...]
-    return value.reshape(value.shape[1] * value.shape[3], value.shape[4])
+    return value.reshape(-1, value.shape[-1])
 
 
 def add_row(ref, row, value):
     ref[row : row + 1, :] += jnp.sum(value, axis=0, keepdims=True)
 
 
-SLOT_AT = 5
-
-
-def weight_spec(weights, which, single=True):
-    shards, groups, held, rows, width = weights.shape
-
-    def place(step, info):
-        slot = info[SLOT_AT + which(step)]
-        return (slot // held, 0, slot % held, 0, 0)
-
+def first_spec(first, rows, which):
+    groups, _, width = first.shape
+    return pl.BlockSpec(
+        (groups, rows, width), lambda step, info: (0, which, 0), pipeline_mode=pl.Buffered(1)
+    )
+
+
+def rest_spec(rest, which, single=True):
+    groups, _, rows, width = rest.shape
     mode = pl.Buffered(1) if single else None
-    return pl.BlockSpec((1, groups, 1, rows, width), place, pipeline_mode=mode)
+    return pl.BlockSpec(
+        (groups, 1, rows, width), lambda step, info: (0, which(step) - 3, 0, 0), pipeline_mode=mode
+    )
 
 
 def fixed(shape):
@@ -414,7 +415,7 @@
     v_ref[...] = (wide_dot(x, matrix(wv), NN) + small[1:2, :]).astype(jnp.bfloat16)
 
 
-def project(info, x_all, small, weights):
+def project(info, x_all, small, first, rows):
     _, mid, width = x_all.shape
 
     def chunk(step, info):
@@ -428,9 +429,7 @@
         [
             pl.BlockSpec((1, mid, width), lambda g, info: (info[1 + chunk(g, info)], 0, 0)),
             fixed(small.shape),
-            weight_spec(weights, lambda g: 0),
-            weight_spec(weights, lambda g: 1),
-            weight_spec(weights, lambda g: 2),
+            *[first_spec(first, rows, m) for m in range(3)],
         ],
         [
             pl.BlockSpec((mid, width), lambda g, info: (jnp.minimum(g, 1), 0)),
@@ -439,7 +438,7 @@
         ],
         [bf16_of(2 * mid, width), bf16_of(4 * mid, width), bf16_of(4 * mid, width)],
         [],
-        (x_all, small, weights, weights, weights),
+        (x_all, small, first, first, first),
         6_000_000_000,
         16 << 20,
     )
@@ -509,7 +508,7 @@
     add_row(sums_ref, 2, cot)
 
 
-def front(info, ctx, x_all, cot, small, weights):
+def front(info, ctx, x_all, cot, small, rest):
     tokens, width = ctx.shape
     mid = x_all.shape[1]
     per = mid // TILE
@@ -521,7 +520,7 @@
     def rows(dtype_shape):
         return pl.BlockSpec(dtype_shape, lambda t, info: (t, 0))
 
-    specs = [weight_spec(weights, lambda t, m=m: m) for m in range(3, 12)]
+    specs = [rest_spec(rest, lambda t, m=m: m) for m in range(3, 12)]
     wide4 = pl.BlockSpec((4, TILE, width), lambda t, info: (0, t, 0))
     flipped = pl.BlockSpec((width, TILE), lambda t, info: (0, t))
     return call(
@@ -561,7 +560,7 @@
             f32_of(8, width),
         ],
         [],
-        (ctx, x_all, cot, small, *([weights] * 9)),
+        (ctx, x_all, cot, small, *([rest] * 9)),
         11_000_000_000,
         40 << 20,
     )
@@ -645,9 +644,9 @@
         dwo_ref[...] = grad_out.reshape(dwo_ref.shape)
 
 
-def back(info, gh2, hid, gel, fit, gmt, n1, r1, ctx, small, weights):
+def back(info, gh2, hid, gel, fit, gmt, n1, r1, ctx, small, rest):
     tokens, width = gh2.shape
-    _, groups, _, rows, _ = weights.shape
+    groups, _, rows, _ = rest.shape
 
     def block(b, info):
         return (jnp.minimum(b, 3), 0, 0)
@@ -667,9 +666,9 @@
             fixed((tokens, 128)),
             fixed((tokens, width)),
             fixed(small.shape),
-            weight_spec(weights, lambda b: 4 + jnp.minimum(b, 3), False),
-            weight_spec(weights, lambda b: 8 + jnp.minimum(b, 3), False),
-            weight_spec(weights, lambda b: 3),
+            rest_spec(rest, lambda b: 4 + jnp.minimum(b, 3), False),
+            rest_spec(rest, lambda b: 8 + jnp.minimum(b, 3), False),
+            rest_spec(rest, lambda b: 3),
         ],
         [
             pl.BlockSpec((groups, 2, rows, width), lambda b, info: (0, jnp.minimum(b, 3), 0, 0)),
@@ -686,7 +685,7 @@
             f32_of(8, width),
         ],
         [pltpu.VMEM((tokens, width), jnp.float32), pltpu.VMEM((tokens, width), jnp.bfloat16)],
-        (gh2, hid, gel, fit, gmt, n1, r1, ctx, small, weights, weights, weights),
+        (gh2, hid, gel, fit, gmt, n1, r1, ctx, small, rest, rest, rest),
         22_000_000_000,
         40 << 20,
     )
@@ -697,7 +696,7 @@
     out_ref[...] = total.astype(jnp.bfloat16)
 
 
-def spill(info, dk, dv, weights):
+def spill(info, dk, dv, first, rows):
     seq, width = dk.shape
     mid = seq // 4
 
@@ -712,13 +711,13 @@
         [
             pl.BlockSpec((mid, width), other),
             pl.BlockSpec((mid, width), other),
-            weight_spec(weights, lambda b: 1),
-            weight_spec(weights, lambda b: 2),
+            first_spec(first, rows, 1),
+            first_spec(first, rows, 2),
         ],
         [pl.BlockSpec((mid, width), lambda b, info: (b, 0))],
         [bf16_of(2 * mid, width)],
         [],
-        (dk, dv, weights, weights),
+        (dk, dv, first, first),
         2_400_000_000,
         8 << 20,
     )[0]
@@ -790,7 +789,7 @@
     out_ref[0] = total.astype(jnp.bfloat16)
 
 
-def input_grads(info, gh1, dq, dk, dv, more, weights):
+def input_grads(info, gh1, dq, dk, dv, more, first, rows):
     tokens, width = gh1.shape
     steps = tokens // TILE
     mid = tokens // 2
@@ -809,9 +808,7 @@
             place,
             place,
             mine,
-            weight_spec(weights, lambda t: 0),
-            weight_spec(weights, lambda t: 1),
-            weight_spec(weights, lambda t: 2),
+            *[first_spec(first, rows, m) for m in range(3)],
         ],
         [
             pl.BlockSpec(
@@ -821,10 +818,314 @@
         ],
         [bf16_of(2, mid, width)],
         [],
-        (gh1, dq, dk, dv, more, weights, weights, weights),
+        (gh1, dq, dk, dv, more, first, first, first),
         3_700_000_000,
         14 << 20,
     )[0]
+
+
+MESH = pl.DeviceIdType.MESH
+KINDS = 3
+
+
+def place_of():
+    c, t = lax.axis_index("ctx"), lax.axis_index("tp")
+    return lax.axis_index("shard"), c, t
+
+
+def send(src, dst, sems, index, target):
+    send_sems, recv_sems = sems
+    return pltpu.make_async_remote_copy(
+        src_ref=src,
+        dst_ref=dst,
+        send_sem=send_sems.at[index],
+        recv_sem=recv_sems.at[index],
+        device_id=target,
+        device_id_type=MESH,
+    )
+
+
+def bring_kernel(
+    n_shard,
+    n_ctx,
+    n_tp,
+    slots,
+    part_ref,
+    low_ref,
+    xs_ref,
+    x_ref,
+    first_ref,
+    rest_ref,
+    got,
+    mine,
+    total,
+    pool,
+    sel,
+    x_s,
+    x_r,
+    xt_s,
+    xt_r,
+    za_s,
+    za_r,
+    zb_s,
+    zb_r,
+    zc_s,
+    zc_r,
+    q_s,
+    q_r,
+    qt_s,
+    qt_r,
+    r_s,
+    r_r,
+    rt_s,
+    rt_r,
+    own_sem,
+):
+    z, c, t = place_of()
+    side, core, bit = t // 2, lax.rem(t, 2), lax.rem(c, 2)
+    held = low_ref.shape[0]
+    piece = mine.shape[0]
+    chunks, per = 3, 3
+    me = c * n_tp + t
+
+    def far(dz):
+        return (lax.rem(z + dz, n_shard), c, t)
+
+    def across(mask):
+        return (z, c ^ mask, t)
+
+    def beside(dt):
+        return (z, c, lax.rem(t + dt, n_tp))
+
+    barrier = pltpu.get_barrier_semaphore()
+    friends = [far(dz) for dz in range(1, n_shard)]
+    friends += [(z, c ^ m, t) for m in range(1, n_ctx)]
+    friends += [beside(dt) for dt in range(1, n_tp)]
+    friends += [(z, c ^ m, t ^ 1) for m in range(1, n_ctx)]
+    for friend in friends:
+        pl.semaphore_signal(barrier, inc=1, device_id=friend, device_id_type=MESH)
+    pl.semaphore_wait(barrier, len(friends))
+
+    stays = c // 2 == core
+    goes = [(z, 2 * core + (p ^ bit), 2 * side + c // 2) for p in range(2)]
+    x_moves = [send(xs_ref.at[p], x_ref.at[p], (x_s, x_r), p, goes[p]) for p in range(2)]
+    x_keep = pltpu.make_async_copy(xs_ref.at[0], x_ref.at[0], x_r.at[0])
+
+    za = [
+        send(
+            part_ref.at[pl.ds(pl.multiple_of(far(dz)[0] * piece, piece), piece)],
+            got.at[dz - 1],
+            (za_s, za_r),
+            dz - 1,
+            far(dz),
+        )
+        for dz in range(1, n_shard)
+    ]
+    for copy in za:
+        copy.start()
+
+    @pl.when(stays)
+    def keep():
+        x_keep.start()
+
+    @pl.when(jnp.logical_not(stays))
+    def leave():
+        x_moves[0].start()
+
+    x_moves[1].start()
+    summed = part_ref[pl.ds(pl.multiple_of(z * piece, piece), piece), :]
+    for dz, copy in enumerate(za):
+        copy.wait_recv()
+        summed = summed + got[dz]
+    mine[...] = summed
+    here = pl.ds(pl.multiple_of(z * piece, piece), piece)
+    zb = [
+        send(mine, total.at[here], (zb_s, zb_r), dz - 1, far(dz)) for dz in range(1, n_shard)
+    ]
+    for copy in zb:
+        copy.start()
+    total[here, :] = summed
+    pool_here = pl.ds(z * held, held)
+    zc = [
+        send(low_ref, pool.at[pool_here], (zc_s, zc_r), dz - 1, far(dz))
+        for dz in range(1, n_shard)
+    ]
+    for copy in zc:
+        copy.start()
+    pool_own = pltpu.make_async_copy(low_ref, pool.at[pool_here], own_sem.at[0])
+    pool_own.start()
+    for copy in zb:
+        copy.wait_recv()
+
+    q_moves = [
+        send(total, first_ref.at[me], (q_s, q_r), k, across(m)) for k, m in enumerate((1, 2, 3))
+    ]
+    for copy in q_moves:
+        copy.start()
+    first_own = pltpu.make_async_copy(total, first_ref.at[me], own_sem.at[1])
+    first_own.start()
+    qt_own = [
+        send(total, first_ref.at[me], (qt_s, qt_r), dt - 1, beside(dt)) for dt in range(1, n_tp)
+    ]
+    for copy in qt_own:
+        copy.start()
+
+    x_over = [
+        send(x_ref.at[p], x_ref.at[2 + p], (xt_s, xt_r), p, (z, c, t ^ 1)) for p in range(2)
+    ]
+
+    @pl.when(stays)
+    def kept():
+        x_keep.wait()
+
+    @pl.when(jnp.logical_not(stays))
+    def came():
+        x_moves[0].wait_recv()
+
+    x_over[0].start()
+    x_moves[1].wait_recv()
+    x_over[1].start()
+
+    qt_on = []
+    for k, m in enumerate((1, 2, 3)):
+        q_moves[k].wait_recv()
+        place = (c ^ m) * n_tp + t
+        for dt in range(1, n_tp):
+            copy = send(
+                first_ref.at[place],
+                first_ref.at[place],
+                (qt_s, qt_r),
+                (k + 1) * (n_tp - 1) + dt - 1,
+                beside(dt),
+            )
+            copy.start()
+            qt_on.append(copy)
+
+    for copy in zc:
+        copy.wait_recv()
+    pool_own.wait()
+    for m in range(chunks * per):
+        sel[m] = pool[slots[KINDS + m]]
+    rest_own = pltpu.make_async_copy(sel, rest_ref.at[me], own_sem.at[2])
+    rest_own.start()
+    r_moves = []
+    rt_moves = []
+    for k in range(chunks):
+        span = pl.ds(k * per, per)
+        pair = [
+            send(
+                sel.at[span],
+                rest_ref.at[me, span],
+                (r_s, r_r),
+                k * 3 + j,
+                across(m),
+            )
+            for j, m in enumerate((1, 2))
+        ]
+        for copy in pair:
+            copy.start()
+        r_moves.append(pair)
+        for dt in range(1, n_tp):
+            copy = send(
+                sel.at[span],
+                rest_ref.at[me, span],
+                (rt_s, rt_r),
+                (k * 4) * (n_tp - 1) + dt - 1,
+                beside(dt),
+            )
+            copy.start()
+            rt_moves.append(copy)
+
+    def pass_on(k, which, place):
+        span = pl.ds(k * per, per)
+        for dt in range(1, n_tp):
+            copy = send(
+                rest_ref.at[place, span],
+                rest_ref.at[place, span],
+                (rt_s, rt_r),
+                (k * 4 + which) * (n_tp - 1) + dt - 1,
+                beside(dt),
+            )
+            copy.start()
+            rt_moves.append(copy)
+
+    onward = []
+    for k in range(chunks):
+        span = pl.ds(k * per, per)
+        for j in range(2):
+            r_moves[k][j].wait_recv()
+        odd = lax.rem(core + k, 2)
+        source = jnp.where(odd == 0, c ^ 1, c ^ 2) * n_tp + t
+        target = (z, jnp.where(odd == 0, c ^ 2, c ^ 1), t)
+        copy = send(
+            rest_ref.at[source, span], rest_ref.at[source, span], (r_s, r_r), k * 3 + 2, target
+        )
+        copy.start()
+        onward.append(copy)
+        pass_on(k, 1, (c ^ 1) * n_tp + t)
+        pass_on(k, 2, (c ^ 2) * n_tp + t)
+    for k in range(chunks):
+        onward[k].wait_recv()
+        pass_on(k, 3, (c ^ 3) * n_tp + t)
+
+    for copy in x_over:
+        copy.wait()
+
+    @pl.when(jnp.logical_not(stays))
+    def left():
+        x_moves[0].wait_send()
+
+    x_moves[1].wait_send()
+    for copy in (*za, *zb, *zc, *q_moves, *onward):
+        copy.wait_send()
+    for pair in r_moves:
+        for copy in pair:
+            copy.wait_send()
+    for copy in (*qt_own, *qt_on, *rt_moves):
+        copy.wait()
+    first_own.wait()
+    rest_own.wait()
+
+
+def bring(slots, part, low, xs, n_shard, n_ctx, n_tp):
+    held, rows, width = low.shape
+    total_rows = part.shape[0]
+    groups = n_ctx * n_tp
+    mid = xs.shape[1]
+    anywhere = pl.BlockSpec(memory_space=pl.ANY)
+    dma = pltpu.SemaphoreType.DMA
+    pairs = [2, 2, n_shard - 1, n_shard - 1, n_shard - 1, 3]
+    pairs += [4 * (n_tp - 1), 9, 12 * (n_tp - 1)]
+    sems = [dma((n,)) for n in pairs for _ in range(2)]
+    return pl.pallas_call(
+        functools.partial(bring_kernel, n_shard, n_ctx, n_tp),
+        name="bring",
+        in_specs=[
+            pl.BlockSpec(memory_space=pltpu.SMEM),
+            pl.BlockSpec(memory_space=pltpu.VMEM),
+            anywhere,
+            anywhere,
+        ],
+        out_specs=[anywhere, anywhere, anywhere],
+        out_shape=[
+            jax.ShapeDtypeStruct((4, mid, width), jnp.bfloat16),
+            jax.ShapeDtypeStruct((groups, total_rows, width), jnp.bfloat16),
+            jax.ShapeDtypeStruct((groups, 9, rows, width), jnp.bfloat16),
+        ],
+        scratch_shapes=[
+            pltpu.VMEM((n_shard - 1, total_rows // n_shard, width), jnp.bfloat16),
+            pltpu.VMEM((total_rows // n_shard, width), jnp.bfloat16),
+            pltpu.VMEM((total_rows, width), jnp.bfloat16),
+            pltpu.VMEM((n_shard * held, rows, width), jnp.bfloat16),
+            pltpu.VMEM((9, rows, width), jnp.bfloat16),
+            *sems,
+            dma((3,)),
+        ],
+        compiler_params=pltpu.CompilerParams(
+            collective_id=0, has_side_effects=True, vmem_limit_bytes=40 << 20
+        ),
+        cost_estimate=pl.CostEstimate(flops=0, bytes_accessed=40 << 20, transcendentals=0),
+    )(slots, part, low, xs)
 
 
 def adam_update(weight, first, second, grad, decay, rate):
@@ -876,16 +1177,12 @@
     swap = [(t, t ^ 1) for t in range(n_tp)]
 
     arrival = [(b ^ parity) + 2 * (half ^ (j // 2)) for j, b in enumerate((0, 1, 0, 1))]
-    info = jnp.concatenate([jnp.stack([half, *arrival]).astype(jnp.int32), slot_of])
+    info = jnp.stack([half, *arrival]).astype(jnp.int32)
     half_one = info[:1]
 
     def sent(field, pick):
         low = field.astype(jnp.bfloat16)
         return jnp.where(parity == 0, low[pick], low[1 - pick])
-
-    def brought(field):
-        pieces = [lax.ppermute(sent(field, pick), plane, forth[pick]) for pick in range(2)]
-        return jnp.stack(pieces)
 
     def returned(field):
         first, second = [lax.ppermute(field[pick], plane, home[pick]) for pick in range(2)]
@@ -895,29 +1192,43 @@
         )
         return out.astype(jnp.float32)
 
-    x_own = brought(inputs)
-    x_other = lax.ppermute(x_own, "tp", swap)
-    x_all = jnp.concatenate([x_own, x_other])
     low = master.astype(jnp.bfloat16)
-    weights = lax.all_gather(low, ("shard", "ctx", "tp"), axis=0)
-    weights = weights.reshape(n_shard, groups, held, rows, width)
-    small_low = small_params.astype(jnp.bfloat16)
-    small = lax.all_gather(small_low, ("shard", "ctx", "tp"), axis=0, tiled=True)
+    my_shard = lax.axis_index("shard")
+    mine = my_shard * held + jnp.arange(held, dtype=jnp.int32)
+    zero = jnp.zeros_like(low)
+    parts = [
+        jnp.sum(jnp.where((slot_of[m] == mine)[:, None, None], low, zero), axis=0, dtype=jnp.float32)
+        for m in range(3)
+    ]
+    spread = (jnp.arange(n_shard) == my_shard)[:, None]
+    small_part = jnp.where(spread, small_params[None, :], 0.0).reshape(-1)
+    used = 3 * rows * width + n_shard * span
+    total_rows = -(-used // (width * 16 * n_shard)) * 16 * n_shard
+    small_part = jnp.pad(small_part, (0, total_rows * width - used)).reshape(-1, width)
+    part = jnp.concatenate([*parts, small_part]).astype(jnp.bfloat16)
+    xs = jnp.stack([sent(inputs, pick) for pick in range(2)])
+    x_all, first, rest = bring(slot_of, part, low, xs, n_shard, n_ctx, n_tp)
+    small = first[:, 3 * rows :, :].reshape(groups, -1)[:, : n_shard * span]
+    small = small.reshape(groups, n_shard, span).transpose(1, 0, 2)
     small = small.reshape(-1, width).astype(jnp.float32)
 
-    q, k, v = project(info, x_all, small, weights)
+    cots, x_all = lax.optimization_barrier(
+        ([sent(cotangent, pick) for pick in range(2)], x_all)
+    )
+    cot = jnp.stack([lax.ppermute(cots[pick], plane, forth[pick]) for pick in range(2)])
+
+    q, k, v = project(info, x_all, small, first, rows)
     context, lse = attend(half_one, rand_blocks, q, k, v, 5)
-    cot = brought(cotangent)
     out_low, n1, r1, fi, fit, hid, gel, gh2, gmt, sums_two = front(
-        info, context, x_all, cot, small, weights
+        info, context, x_all, cot, small, rest
     )
     layer_out = returned(out_low)
     ffn_grads, out_grad, gh1, dctx, sums_one = back(
-        info, gh2, hid, gel, fit, gmt, n1, r1, context, small, weights
+        info, gh2, hid, gel, fit, gmt, n1, r1, context, small, rest
     )
     ffn_rows = lax.psum_scatter(ffn_grads, plane, scatter_dimension=0, tiled=False)
     dq, dk, dv = attend_back(half_one, rand_blocks, q, k, v, lse, dctx, 5)
-    more = lax.ppermute(spill(info, dk, dv, weights), "tp", swap)
+    more = lax.ppermute(spill(info, dk, dv, first, rows), "tp", swap)
     qkv_grads, sums_qkv = weight_grads(info, x_all, dq, dk, dv, groups)
     small_grad = jnp.concatenate(
         [
@@ -947,7 +1258,7 @@
     )
     late, ffn_rows = lax.optimization_barrier((late, ffn_rows))
     late_rows = lax.psum_scatter(late, plane, scatter_dimension=0, tiled=False)
-    input_low = input_grads(info, gh1, dq, dk, dv, more, weights)
+    input_low = input_grads(info, gh1, dq, dk, dv, more, first, rows)
     input_grad = returned(input_low)
 
     own_rows = jnp.concatenate(

time: 440 us -> 455 us (1.034)
  Pallas kernels: 180 us -> 283 us
  blocking collectives: 63.5 us -> 0 us
  starting transfers between devices: 22.2 us -> 8.66 us
  waiting for transfers between devices: 113 us -> 102 us
  local copies, waits for them, and re-layouts: 15.4 us -> 20.1 us
    pallas_call x0 -> x1, Pallas kernels: none -> 103 us  [bring(): pl.pallas_call(functools.partial(bring_kernel, n_shard, n_ctx, n_tp), nam...]
    unnamed x1 -> x0, blocking collectives: 63.5 us -> none
    ppermute x6 -> x3, waiting for transfers between devices: 19.3 us -> 0.01 us  [the longest x2 0.01 us: shards(): lax.ppermute(cots[pick], plane, forth[pick])]
    reduce_scatter x1, waiting for transfers between devices: 14.3 us -> 28.7 us  [shards(): lax.psum_scatter(ffn_grads, plane, scatter_dimension=0, tiled=False)]
    ppermute x6 -> x3, starting transfers between devices: 16.4 us -> 2.62 us  [the longest x2 2.62 us: shards(): lax.ppermute(cots[pick], plane, forth[pick])]
    all_gather x1 -> x0, waiting for transfers between devices: 11.6 us -> none  [shards(): weights = lax.all_gather(low, ('shard', 'ctx', 'tp'), axis=0)]
    reduce_scatter x1, waiting for transfers between devices: 50.1 us -> 56.9 us  [shards(): late_rows = lax.psum_scatter(late, plane, scatter_dimension=0, tiled=False)]
    unnamed x45 -> x51, local copies, waits for them, and re-layouts: 5.88 us -> 11.4 us
  transfers between devices with their start and end apart: 14 -> 10, of which waited for: 6 -> 4; matrix products, arithmetic and copies ran while one was open for 8% -> 4% of each run, Pallas kernels for 16% -> 24%
where the time goes in v3:
time: 455 us; the launch traced here: 452 us
  Pallas kernels  283 us (62%)
  waiting for transfers between devices  102 us (22%)
  other arithmetic  23.6 us (5%)
  local copies, waits for them, and re-layouts  20.1 us (4%)
  between operations  14.2 us (3%)
  starting transfers between devices  8.66 us (2%)
    pallas_call x6, Pallas kernels, call(): pl.pallas_call(kernel, name=name, grid_spec=pltpu.PrefetchScalarGridSpec(...  111 us
    pallas_call x1, Pallas kernels, bring(): pl.pallas_call(functools.partial(bring_kernel, n_shard, n_ctx, n_tp), nam...  103 us
    reduce_scatter x1, waiting for transfers between devices, shards(): late_rows = lax.psum_scatter(late, plane, scatter_dimension=0, tiled=False)  56.9 us
    pallas_call x1, Pallas kernels, attend_back(): pl.pallas_call(functools.partial(attend_back_kernel, unroll), grid_spec=s...  39.3 us
    reduce_scatter x1, waiting for transfers between devices, shards(): lax.psum_scatter(ffn_grads, plane, scatter_dimension=0, tiled=False)  28.7 us
    pallas_call x1, Pallas kernels, attend(): pl.pallas_call(functools.partial(attend_kernel, unroll), grid_spec=spec,...  28.6 us
    ppermute x4, waiting for transfers between devices, returned(): lax.ppermute(field[pick], plane, home[pick])  16.4 us
    unnamed x51, local copies, waits for them, and re-layouts  11.4 us
  transfers between devices with their start and end apart: 10, of which 4 were waited for; matrix products, arithmetic and copies ran while one was open for 4% of the time, Pallas kernels for 24%

profile of v3, /device:TPU:0, one launch (start us, length us, event | category | flops | bytes accessed | tf_op | source)
XLA Modules:
  0.0 452.4 jit_solution(12768086282148162568)
XLA Ops:
  7.2 1.4 fusion.16
  8.6 0.8 select_convert_fusion
  9.5 2.2 convert_element_type.61
  11.7 0.6 copy-done.7
  12.8 0.7 fusion.12
  13.5 1.3 fusion.10
  15.0 0.4 select_reduce_fusion.2
  15.6 103.5 %bring.1 = (bf16[4,512,768]{2,1,0:T(8,128)(2,1)S(1)}, bf16[8,320,768]{2,1,0:T(8,128)(2,1)S(1)}, bf16[8,9,96,768]{3,2,1,0:T(8,128)(2,1)}) custom-call(s32[12]{0:T(128)S(1)} %copy-done.2, bf16[320,768]{1,0:T(8,128)(2,1)S(1)} %pad_maximum_fusion.5.part_ref, bf16[3,96,768]{2,1,0:T(8,128)(2,1)S(1)} %get-tuple-element.89.low_ref, ...), custom_call_target="tpu_custom_call" | custom-call | bytes 41943040 | tf_op jit(solution)/shard_map/bring/pallas_call | solution.py:1100
  119.1 1.9 copy-done
  121.0 1.7 copy-done.1
  122.7 0.9 collective-permute-start
  123.5 1.7 collective-permute-start.1
  125.3 1.0 slice_bitcast_fusion.4
  126.3 0.2 copy.35
  126.7 0.7 reshape.106.small
  127.4 0.8 copy.28.table_ref
  128.2 0.7 stack.55.info
  128.9 11.6 %project.1 = (bf16[1024,768]{1,0:T(8,128)(2,1)}, bf16[2048,768]{1,0:T(8,128)(2,1)}, bf16[2048,768]{1,0:T(8,128)(2,1)}) custom-call(s32[5]{0:T(128)} %stack.55.info, bf16[4,512,768]{2,1,0:T(8,128)(2,1)} %copy-done.1, f32[12,768]{1,0:T(8,128)} %reshape.106.small, bf16[8,320,768]{2,1,0:T(8,128)(2,1)} %copy-done, bf16[8,320,768]{2,1,0:T(8,128)(2,1)} %copy-done, ...), custom_call_target="tpu_custom_call" | custom-call | flops 6000000000 | bytes 16777216 | tf_op jit(solution)/shard_map/project/pallas_call | solution.py:375
  140.5 28.6 %attend.1 = (bf16[1024,768]{1,0:T(8,128)(2,1)}, f32[3,16,256]{2,1,0:T(8,128)}) custom-call(s32[1]{0:T(128)} %bitcast.half_ref, s32[12,30,3]{2,1,0:T(8,128)} %copy.28.table_ref, bf16[1024,768]{1,0:T(8,128)(2,1)} %get-tuple-element.43.q_ref, bf16[2048,768]{1,0:T(8,128)(2,1)} %get-tuple-element.44.k_ref, bf16[2048,768]{1,0:T(8,128)(2,1)} %get-tuple-element.45.v_ref), custom_call_target="tpu_custom_call" | custom-call | flops 60000002048 | bytes 12582912 | tf_op jit(solution)/shard_map/attend/pallas_call | solution.py:168
  169.1 1.3 pad_maximum_fusion.4.cot_ref
  170.4 28.4 %front.1 = (bf16[2,512,768]{2,1,0:T(8,128)(2,1)}, f32[1024,768]{1,0:T(8,128)}, f32[1024,128]{1,0:T(8,128)}, bf16[1024,768]{1,0:T(8,128)(2,1)}, bf16[768,1024]{1,...) custom-call(s32[5]{0:T(128)} %stack.55.info, ...), custom_call_target="tpu_custom_call" | custom-call | flops 11000000512 | bytes 41943040 | tf_op jit(solution)/shard_map/front/pallas_call | solution.py:375
  198.8 41.8 %back.1 = (bf16[8,8,96,768]{3,2,1,0:T(8,128)(2,1)}, bf16[8,96,768]{2,1,0:T(8,128)(2,1)}, f32[1024,768]{1,0:T(8,128)}, bf16[1024,768]{1,0:T(8,128)(2,1)}, f32[8,768]{1,0:T(8,128)}) custom-call(s32[5]{0:T(128)} %stack.55.info, f32[1024,768]{1,0:T(8,128)} %get-tuple-element.51.gh2_ref, bf16[4,1024,768]{2,1,0:T(8,128)(2,1)} %get-tuple-element.52.hid_ref, ...), custom_call_target="tpu_custom_call" | custom-call | flops 22000001024 | bytes 41943040 | tf_op jit(solution)/shard_map/back/pallas_call | solution.py:375
  240.7 39.3 %attend_back.1 = (bf16[1024,768]{1,0:T(8,128)(2,1)}, bf16[2048,768]{1,0:T(8,128)(2,1)}, bf16[2048,768]{1,0:T(8,128)(2,1)}) custom-call(s32[1]{0:T(128)} %bitcast.half_ref, s32[12,30,3]{2,1,0:T(8,128)} %copy.28.table_ref, bf16[1024,768]{1,0:T(8,128)(2,1)} %get-tuple-element.43.q_ref, bf16[2048,768]{1,0:T(8,128)(2,1)} %get-tuple-element.44.k_ref, ...), custom_call_target="tpu_custom_call" | custom-call | flops 120000004096 | bytes 25165824 | tf_op jit(solution)/shard_map/attend_back/pallas_call | solution.py:307
  280.0 13.3 %weight_grads.1 = (bf16[8,3,96,768]{3,2,1,0:T(8,128)(2,1)}, f32[8,768]{1,0:T(8,128)}) custom-call(s32[5]{0:T(128)} %stack.55.info, bf16[4,512,768]{2,1,0:T(8,128)(2,1)} %copy-done.1, bf16[1024,768]{1,0:T(8,128)(2,1)} %get-tuple-element.61.dq_ref, bf16[2048,768]{1,0:T(8,128)(2,1)} %get-tuple-element.62.dk_ref, bf16[2048,768]{1,0:T(8,128)(2,1)} %get-tuple-element.63.dv_ref), custom_call_target="tpu_custom_call" | custom-call | flops 6000000000 | bytes 14680064 | tf_op jit(solution)/shard_map/weight_grads/pallas_call | solution.py:375
  293.3 0.7 convert.61
  294.1 0.2 dynamic-update-slice
  294.3 0.2 dynamic-update-slice.1
  294.6 0.2 dynamic-update-slice.2
  294.8 0.2 dynamic-update-slice.3
  295.0 0.2 dynamic-update-slice.4
  295.2 0.3 dynamic-update-slice.5
  295.5 0.2 dynamic-update-slice.6
  295.8 0.2 dynamic-update-slice.7
  296.4 3.8 pad_maximum_fusion
  300.2 28.7 %reduce-scatter.4.cloned.1.call-done = bf16[1,8,96,768]{3,2,1,0:T(8,128)(2,1)} async-done(((bf16[8,8,96,768]{3,2,1,0:T(8,128)(2,1)}), bf16[1,8,96,768]{3,2,1,0:T(8,128)(2,1)}) %reduce-scatter.4.cloned.1.call-update) | async-done | bytes 1179664 | tf_op jit(solution)/shard_map/reduce_scatter | solution.py:1229
  328.9 0.3 reduce-scatter.8.cloned.1.call-start
  329.2 0.9 copy-done.10
  330.2 56.9 %reduce-scatter.6.cloned.1.call-done = bf16[1,386,768]{2,1,0:T(8,128)(2,1)} async-done(((bf16[8,386,768]{2,1,0:T(8,128)(2,1)}), bf16[1,386,768]{2,1,0:T(8,128)(2,1)}) %reduce-scatter.6.cloned.1.call-update) | async-done | bytes 592912 | tf_op jit(solution)/shard_map/reduce_scatter | solution.py:1260
  387.1 1.1 slice.148
  388.5 0.4 copy-done.3
  388.9 1.2 fusion.2
  390.1 0.5 copy.33
  390.6 0.7 slice.149
  391.5 1.3 pad_maximum_fusion.1
  392.9 6.7 %spill.1 = bf16[1024,768]{1,0:T(8,128)(2,1)} custom-call(s32[5]{0:T(128)} %stack.55.info, bf16[2048,768]{1,0:T(8,128)(2,1)} %get-tuple-element.62.dk_ref, bf16[2048,768]{1,0:T(8,128)(2,1)} %get-tuple-element.63.dv_ref, bf16[8,320,768]{2,1,0:T(8,128)(2,1)} %copy-done, bf16[8,320,768]{2,1,0:T(8,128)(2,1)} %copy-done), custom_call_target="tpu_custom_call" | custom-call | flops 2400000000 | bytes 8388608 | tf_op jit(solution)/shard_map/spill/pallas_call | solution.py:375
  399.6 1.0 slice_bitcast_fusion.3
  400.6 1.4 collective-permute-start.2
  402.0 1.5 collective-permute-start.3
  403.5 1.1 copy-done.8
  404.6 9.5 %input_grads.1 = bf16[2,512,768]{2,1,0:T(8,128)(2,1)} custom-call(s32[5]{0:T(128)} %stack.55.info, f32[1024,768]{1,0:T(8,128)} %get-tuple-element.58.gh1_ref, bf16[1024,768]{1,0:T(8,128)(2,1)} %get-tuple-element.61.dq_ref, bf16[2048,768]{1,0:T(8,128)(2,1)} %get-tuple-element.62.dk_ref, bf16[2048,768]{1,0:T(8,128)(2,1)} %get-tuple-element.63.dv_ref, ...), custom_call_target="tpu_custom_call" | custom-call | flops 3700000000 | bytes 14680064 | tf_op jit(solution)/shard_map/input_grads/pallas_call | solution.py:375
  414.1 1.5 slice_bitcast_fusion.1
  415.6 1.2 collective-permute-start.5
  416.8 1.6 collective-permute-start.6
  418.4 2.6 collective-permute-done.2
  421.0 1.2 select_bitcast_fusion.3
  422.2 1.9 maximum_convert_fusion
  424.1 13.8 %collective-permute-done.5 = bf16[512,768]{1,0:T(8,128)(2,1)} collective-permute-done((bf16[512,768]{1,0:T(8,128)(2,1)S(1)}, bf16[512,768]{1,0:T(8,128)(2,1)}, u32[]{:S(2)}, u32[]{:S(2)}) %collective-permute-start.5) | collective-permute-done | bytes 786464 | tf_op jit(solution)/shard_map/ppermute | solution.py:1188
  437.9 1.5 select_bitcast_fusion.1
  439.4 1.9 maximum_convert_fusion.1
  441.3 1.2 convert_bitcast_fusion
  442.7 0.3 copy-done.12
  443.0 0.3 copy-done.13
  443.3 2.0 multiply_subtract_fusion
  445.2 0.6 multiply_subtract_fusion.1
  (78 shorter events, 2.4 us)
Async XLA Ops:
  7.2 321.7 %reduce-scatter.4.cloned.1.call-start = ((), (), s32[]{:S(2)}) async-start(), calls=%async_computation.3 | async-start | bytes 10616832 | tf_op jit(solution)/shard_map/reduce_scatter | solution.py:1229
  9.5 2.8 copy-start.7
  12.8 2.2 copy-start.5
  15.0 0.7 copy-start.2
  15.6 111.8 %copy-start.14 = (s32[12,30,3]{1,2,0:T(4,128)S(1)}, s32[12,30,3]{1,2,0:T(4,128)}, u32[]{:S(2)}) copy-start(s32[12,30,3]{1,2,0:T(4,128)} %param.12) | copy-start | bytes 12964
  119.1 1.9 copy-start
  121.0 1.7 copy-start.1
  122.7 46.5 %collective-permute-start = (bf16[512,768]{1,0:T(8,128)(2,1)S(1)}, bf16[512,768]{1,0:T(8,128)(2,1)S(1)}, u32[]{:S(2)}, u32[]{:S(2)}) collective-permute-start(bf16[512,768]{1,0:T(8,128)(2,1)S(1)} %get-tuple-element.47), channel_id=1, source_target_pairs={{0,0},{1,4},{2,2},{3,6},{4,1},{5,5},{6,3},{7,7},{8,8},{9,12},{10,1... | collective-permute-start | bytes 2359304 | tf_op jit(solution)/shard_map/ppermute | solution.py:1218
  123.5 45.6 %collective-permute-start.1 = (bf16[512,768]{1,0:T(8,128)(2,1)S(1)}, bf16[512,768]{1,0:T(8,128)(2,1)S(1)}, u32[]{:S(2)}, u32[]{:S(2)}) collective-permute-start(bf16[512,768]{1,0:T(8,128)(2,1)S(1)} %get-tuple-element.48), channel_id=1, source_target_pairs={{0,2},{1,6},{2,0},{3,4},{4,3},{5,7},{6,1},{7,5},{8,10},{9,14},{10,... | collective-permute-start | bytes 2359304 | tf_op jit(solution)/shard_map/ppermute | solution.py:1218
  240.6 146.5 %reduce-scatter.6.cloned.1.call-start = ((), (), s32[]{:S(2)}) async-start(), calls=%async_computation.4 | async-start | bytes 5419008 | tf_op jit(solution)/shard_map/reduce_scatter | solution.py:1260
  280.0 14.0 %copy-start.16 = (f32[8,768]{1,0:T(8,128)S(1)}, f32[8,768]{1,0:T(8,128)}, u32[]{:S(2)}) copy-start(f32[8,768]{1,0:T(8,128)} %get-tuple-element.67) | copy-start | bytes 73732
  280.0 14.1 %copy-start.15 = (f32[8,768]{1,0:T(8,128)S(1)}, f32[8,768]{1,0:T(8,128)}, u32[]{:S(2)}) copy-start(f32[8,768]{1,0:T(8,128)} %get-tuple-element.68) | copy-start | bytes 73732
  280.0 16.4 %copy-start.11 = (bf16[8,96,768]{2,1,0:T(8,128)(2,1)S(1)}, bf16[8,96,768]{2,1,0:T(8,128)(2,1)}, u32[]{:S(2)}) copy-start(bf16[8,96,768]{2,1,0:T(8,128)(2,1)} %get-tuple-element.65) | copy-start | bytes 3538948
  328.9 1.3 copy-start.10
  328.9 112.4 %reduce-scatter.8.cloned.1.call-start = ((), (), s32[]{:S(2)}) async-start(), calls=%async_computation.5 | async-start | bytes 2273280 | tf_op jit(solution)/shard_map/reduce_scatter | solution.py:1278
  388.2 0.7 copy-start.3
  392.9 6.7 %copy-start.9 = (bf16[2,512,768]{2,1,0:T(8,128)(2,1)S(1)}, bf16[2,512,768]{2,1,0:T(8,128)(2,1)}, u32[]{:S(2)}) copy-start(bf16[2,512,768]{2,1,0:T(8,128)(2,1)} %get-tuple-element.50) | copy-start | bytes 4718596
  399.6 3.9 collective-permute-start.4
  400.6 20.4 %collective-permute-start.2 = (bf16[512,768]{1,0:T(8,128)(2,1)}, bf16[512,768]{1,0:T(8,128)(2,1)S(1)}, u32[]{:S(2)}, u32[]{:S(2)}) collective-permute-start(bf16[512,768]{1,0:T(8,128)(2,1)} %get-tuple-element.96), channel_id=1, source_target_pairs={{2,0},{6,1},{0,2},{4,3},{3,4},{7,5},{1,6},{5,7},{10,8},{14,9},{8,1... | collective-permute-start | bytes 2359304 | tf_op jit(solution)/shard_map/ppermute | solution.py:1188
  402.0 19.0 %collective-permute-start.3 = (bf16[512,768]{1,0:T(8,128)(2,1)S(1)}, bf16[512,768]{1,0:T(8,128)(2,1)}, u32[]{:S(2)}, u32[]{:S(2)}) collective-permute-start(bf16[512,768]{1,0:T(8,128)(2,1)S(1)} %get-tuple-element.97), channel_id=1, source_target_pairs={{0,0},{4,1},{2,2},{6,3},{1,4},{5,5},{3,6},{7,7},{8,8},{12,9},{10,1... | collective-permute-start | bytes 2359304 | tf_op jit(solution)/shard_map/ppermute | solution.py:1188
  403.5 1.1 copy-start.8
  415.6 22.3 %collective-permute-start.5 = (bf16[512,768]{1,0:T(8,128)(2,1)S(1)}, bf16[512,768]{1,0:T(8,128)(2,1)}, u32[]{:S(2)}, u32[]{:S(2)}) collective-permute-start(bf16[512,768]{1,0:T(8,128)(2,1)S(1)} %get-tuple-element.92), channel_id=1, source_target_pairs={{2,0},{6,1},{0,2},{4,3},{3,4},{7,5},{1,6},{5,7},{10,8},{14,9},{8,1... | collective-permute-start | bytes 2359304 | tf_op jit(solution)/shard_map/ppermute | solution.py:1188
  416.8 21.1 %collective-permute-start.6 = (bf16[512,768]{1,0:T(8,128)(2,1)S(1)}, bf16[512,768]{1,0:T(8,128)(2,1)}, u32[]{:S(2)}, u32[]{:S(2)}) collective-permute-start(bf16[512,768]{1,0:T(8,128)(2,1)S(1)} %get-tuple-element.93), channel_id=1, source_target_pairs={{0,0},{4,1},{2,2},{6,3},{1,4},{5,5},{3,6},{7,7},{8,8},{12,9},{10,1... | collective-permute-start | bytes 2359304 | tf_op jit(solution)/shard_map/ppermute | solution.py:1188
  441.3 1.4 copy-start.6
  441.3 1.3 copy-start.4
  441.3 1.7 copy-start.12
  441.3 2.0 copy-start.13
  443.2 2.0 copy-start.17
  443.3 2.0 copy-start.18
  443.3 2.0 copy-start.19
Sparse Core Ops, SparseCore 0:
  240.7 88.1 reduce-scatter.3
  332.3 54.7 reduce-scatter.5
  393.0 39.2 reduce-scatter.7

commit v4 on v3

--- a/solution.py
+++ b/solution.py
@@ -691,139 +691,6 @@
     )
 
 
-def spill_kernel(info, dk_ref, dv_ref, wk, wv, out_ref):
-    total = wide_dot(dk_ref[...], matrix(wk), NT) + wide_dot(dv_ref[...], matrix(wv), NT)
-    out_ref[...] = total.astype(jnp.bfloat16)
-
-
-def spill(info, dk, dv, first, rows):
-    seq, width = dk.shape
-    mid = seq // 4
-
-    def other(b, info):
-        return (2 * (1 - info[0]) + b, 0)
-
-    return call(
-        spill_kernel,
-        "spill",
-        info,
-        2,
-        [
-            pl.BlockSpec((mid, width), other),
-            pl.BlockSpec((mid, width), other),
-            first_spec(first, rows, 1),
-            first_spec(first, rows, 2),
-        ],
-        [pl.BlockSpec((mid, width), lambda b, info: (b, 0))],
-        [bf16_of(2 * mid, width)],
-        [],
-        (dk, dv, first, first),
-        2_400_000_000,
-        8 << 20,
-    )[0]
-
-
-def weight_grads_kernel(
-    info, x_ref, dq_ref, dk_ref, dv_ref, out_ref, sums_ref, q_acc, k_acc, v_acc
-):
-    step = pl.program_id(0)
-
-    @pl.when(step == 0)
-    def clear():
-        sums_ref[...] = jnp.zeros_like(sums_ref)
-        k_acc[...] = jnp.zeros_like(k_acc)
-        v_acc[...] = jnp.zeros_like(v_acc)
-        q_acc[...] = jnp.zeros_like(q_acc)
-
-    flipped = x_ref[0].T
-    k_acc[...] += wide_dot(flipped, dk_ref[...], NN)
-    v_acc[...] += wide_dot(flipped, dv_ref[...], NN)
-    add_row(sums_ref, 1, dv_ref[...].astype(jnp.float32))
-
-    @pl.when(step < 2)
-    def own():
-        q_acc[...] += wide_dot(flipped, dq_ref[...], NN)
-        add_row(sums_ref, 0, dq_ref[...].astype(jnp.float32))
-
-    @pl.when(step == 3)
-    def finish():
-        groups, _, rows, width = out_ref.shape
-        for m, acc in enumerate((q_acc, k_acc, v_acc)):
-            out_ref[:, m : m + 1] = (
-                acc[...].astype(jnp.bfloat16).reshape(groups, 1, rows, width)
-            )
-
-
-def weight_grads(info, x_all, dq, dk, dv, groups):
-    _, mid, width = x_all.shape
-    rows = width // groups
-
-    def chunk(step, info):
-        return lax.rem(step + 2 * info[0], 4)
-
-    return call(
-        weight_grads_kernel,
-        "weight_grads",
-        info,
-        4,
-        [
-            pl.BlockSpec((1, mid, width), lambda g, info: (info[1 + chunk(g, info)], 0, 0)),
-            pl.BlockSpec((mid, width), lambda g, info: (jnp.minimum(g, 1), 0)),
-            pl.BlockSpec((mid, width), lambda g, info: (chunk(g, info), 0)),
-            pl.BlockSpec((mid, width), lambda g, info: (chunk(g, info), 0)),
-        ],
-        [resident((groups, 3, rows, width)), resident((8, width))],
-        [bf16_of(groups, 3, rows, width), f32_of(8, width)],
-        [pltpu.VMEM((width, width), jnp.float32)] * 3,
-        (x_all, dq, dk, dv),
-        6_000_000_000,
-        14 << 20,
-    )
-
-
-def input_grads_kernel(info, gh1_ref, dq_ref, dk_ref, dv_ref, more_ref, wq, wk, wv, out_ref):
-    total = gh1_ref[...] + more_ref[...].astype(jnp.float32)
-    total = total + wide_dot(dq_ref[...], matrix(wq), NT)
-    total = total + wide_dot(dk_ref[...], matrix(wk), NT)
-    total = total + wide_dot(dv_ref[...], matrix(wv), NT)
-    out_ref[0] = total.astype(jnp.bfloat16)
-
-
-def input_grads(info, gh1, dq, dk, dv, more, first, rows):
-    tokens, width = gh1.shape
-    steps = tokens // TILE
-    mid = tokens // 2
-    per = mid // TILE
-    mine = pl.BlockSpec((TILE, width), lambda t, info: (t, 0))
-    place = pl.BlockSpec((TILE, width), lambda t, info: (info[0] * steps + t, 0))
-
-    return call(
-        input_grads_kernel,
-        "input_grads",
-        info,
-        steps,
-        [
-            mine,
-            mine,
-            place,
-            place,
-            mine,
-            *[first_spec(first, rows, m) for m in range(3)],
-        ],
-        [
-            pl.BlockSpec(
-                (1, TILE, width),
-                lambda t, info: (info[1 + 2 * info[0] + t // per], t % per, 0),
-            )
-        ],
-        [bf16_of(2, mid, width)],
-        [],
-        (gh1, dq, dk, dv, more, first, first, first),
-        3_700_000_000,
-        14 << 20,
-    )[0]
-
-
 MESH = pl.DeviceIdType.MESH
 KINDS = 3
 
@@ -1128,6 +995,305 @@
     )(slots, part, low, xs)
 
 
+def late_kernel(
+    n_ctx,
+    n_tp,
+    x_hbm,
+    dq_hbm,
+    dk_hbm,
+    dv_hbm,
+    gh1_hbm,
+    first_hbm,
+    wo_hbm,
+    small_ref,
+    home_ref,
+    rows_ref,
+    total_ref,
+    x_s,
+    dq_s,
+    dk_s,
+    dv_s,
+    gh1_s,
+    first_s,
+    flipped,
+    grads,
+    arrived,
+    partial,
+    met,
+    over,
+    more,
+    back_s,
+    small_s,
+    small_t,
+    small_p,
+    in_sem,
+    c_s,
+    c_r,
+    p_s,
+    p_r,
+    o_s,
+    o_r,
+    h_s,
+    h_r,
+    sc_s,
+    sc_r,
+    sp_s,
+    sp_r,
+    keep_sem,
+):
+    z, c, t = place_of()
+    side, core, bit = t // 2, lax.rem(t, 2), lax.rem(c, 2)
+    _, mid, width = x_s.shape
+    tokens = 2 * mid
+    rows = rows_ref.shape[1]
+    groups = n_ctx * n_tp
+    per = groups // 2
+    band = width // 2
+    tile = mid // 2
+
+    loads = [
+        pltpu.make_async_copy(src, dst, in_sem.at[i])
+        for i, (src, dst) in enumerate(
+            (
+                (x_hbm, x_s),
+                (dk_hbm, dk_s),
+                (dv_hbm, dv_s),
+                (dq_hbm, dq_s),
+                (first_hbm, first_s),
+                (gh1_hbm, gh1_s),
+                (wo_hbm, grads.at[:, 3]),
+            )
+        )
+    ]
+    for load in loads:
+        load.start()
+
+    def across(mask):
+        return (z, c ^ mask, t)
+
+    def beside(dt):
+        return (z, c, lax.rem(t + dt, n_tp))
+
+    barrier = pltpu.get_barrier_semaphore()
+    friends = [(z, c ^ m, t) for m in range(1, n_ctx)]
+    friends += [beside(dt) for dt in range(1, n_tp)]
+    friends += [(z, c ^ m, t ^ 1) for m in range(1, n_ctx)]
+    for friend in friends:
+        pl.semaphore_signal(barrier, inc=1, device_id=friend, device_id_type=MESH)
+    pl.semaphore_wait(barrier, len(friends))
+
+    core_moves = []
+
+    def exchange(m):
+        for dt in range(1, n_tp):
+            other = lax.rem(t + dt, n_tp)
+            for k in range(n_ctx):
+                copy = send(
+                    grads.at[k * n_tp + other, m],
+                    arrived.at[dt - 1, k, m],
+                    (c_s, c_r),
+                    ((dt - 1) * n_ctx + k) * 4 + m,
+                    beside(dt),
+                )
+                copy.start()
+                core_moves.append((m, copy))
+
+    plane_moves = []
+
+    def meet(m):
+        for which, copy in core_moves:
+            if which == m:
+                copy.wait_recv()
+        for k in range(n_ctx):
+            value = grads[k * n_tp + t, m]
+            for dt in range(1, n_tp):
+                value = value + arrived[dt - 1, k, m]
+            partial[k, m] = value
+        for j in range(1, n_ctx):
+            copy = send(
+                partial.at[c ^ j, m], met.at[j - 1, m], (p_s, p_r), (j - 1) * 4 + m, across(j)
+            )
+            copy.start()
+            plane_moves.append(copy)
+
+    loads[6].wait()
+    exchange(3)
+    loads[0].wait()
+    for a in range(4):
+        own = 1 if a < 2 else 0
+        chunk = 2 * (core if own else 1 - core) + ((a % 2) ^ bit)
+        flipped[:, pl.ds(pl.multiple_of(chunk * mid, mid), mid)] = x_s[a].T
+
+    mine = pl.ds(pl.multiple_of(core * tokens, tokens), tokens)
+    def weight_grad(m, left_at, right):
+        def one(i, carry):
+            left = flipped[pl.ds(pl.multiple_of(i * band, band), band), left_at]
+            value = wide_dot(left, right[...], NN).astype(jnp.bfloat16)
+            grads[pl.ds(i * per, per), m] = value.reshape(per, rows, width)
+            return carry
+
+        lax.fori_loop(0, 2, one, 0)
+
+    loads[1].wait()
+    weight_grad(1, slice(None), dk_s)
+    exchange(1)
+    meet(3)
+    loads[2].wait()
+    weight_grad(2, slice(None), dv_s)
+    exchange(2)
+    meet(1)
+    loads[3].wait()
+    weight_grad(0, mine, dq_s)
+    exchange(0)
+    meet(2)
+
+    row = lax.broadcasted_iota(jnp.int32, small_ref.shape, 0)
+    q_sum = jnp.sum(dq_s[...].astype(jnp.float32), axis=0, keepdims=True)
+    v_sum = jnp.sum(dv_s[...].astype(jnp.float32), axis=0, keepdims=True)
+    sums = jnp.where(row == 0, q_sum, jnp.where(row == 1, v_sum, small_ref[...]))
+    small_s[...] = sums.astype(jnp.bfloat16)
+    small_core = [
+        send(small_s, small_t.at[dt - 1], (sc_s, sc_r), dt - 1, beside(dt)) for dt in range(1, n_tp)
+    ]
+    for copy in small_core:
+        copy.start()
+
+    loads[4].wait()
+
+    def weight(m):
+        return first_s[:, m * rows : (m + 1) * rows, :].reshape(width, width)
+
+    wq, wk, wv = weight(0), weight(1), weight(2)
+    over_moves = []
+    for b in range(2):
+        at = pl.ds(pl.multiple_of((1 - core) * tokens + b * mid, mid), mid)
+        value = wide_dot(dk_s[at, :], wk, NT) + wide_dot(dv_s[at, :], wv, NT)
+        over[b] = value.astype(jnp.bfloat16)
+        copy = send(over.at[b], more.at[b], (o_s, o_r), b, (z, c, t ^ 1))
+        copy.start()
+        over_moves.append(copy)
+
+    meet(0)
+    value = small_s[...]
+    for dt, copy in enumerate(small_core):
+        copy.wait_recv()
+        value = value + small_t[dt]
+    total_ref[...] = value
+    small_plane = [
+        send(total_ref, small_p.at[j - 1], (sp_s, sp_r), j - 1, across(j)) for j in range(1, n_ctx)
+    ]
+    for copy in small_plane:
+        copy.start()
+
+    loads[5].wait()
+    stays = c // 2 == core
+    home_moves = []
+    for copy in over_moves:
+        copy.wait_recv()
+    for move in range(2):
+        chunk = move ^ bit
+        for i in range(2):
+            at = pl.ds(pl.multiple_of(core * tokens + chunk * mid + i * tile, tile), tile)
+            here = pl.ds(pl.multiple_of(chunk * mid + i * tile, tile), tile)
+            value = gh1_s[here, :]
+            value = value + more[chunk, i * tile : (i + 1) * tile, :].astype(jnp.float32)
+            value = value + wide_dot(dq_s[here, :], wq, NT)
+            value = value + wide_dot(dk_s[at, :], wk, NT)
+            value = value + wide_dot(dv_s[at, :], wv, NT)
+            back_s[move, i * tile : (i + 1) * tile, :] = value.astype(jnp.bfloat16)
+        target = (z, 2 * core + chunk, 2 * side + c // 2)
+        home_moves.append(send(back_s.at[move], home_ref.at[move], (h_s, h_r), move, target))
+        if move == 0:
+            keep = pltpu.make_async_copy(back_s.at[0], home_ref.at[0], keep_sem.at[0])
+
+            @pl.when(stays)
+            def kept():
+                keep.start()
+
+            @pl.when(jnp.logical_not(stays))
+            def left():
+                home_moves[0].start()
+
+        else:
+            home_moves[1].start()
+
+    for copy in plane_moves:
+        copy.wait_recv()
+    for m in range(4):
+        value = partial[c, m]
+        for j in range(n_ctx - 1):
+            value = value + met[j, m]
+        rows_ref[m] = value
+    value = total_ref[...]
+    for j, copy in enumerate(small_plane):
+        copy.wait()
+        value = value + small_p[j]
+    total_ref[...] = value
+
+    @pl.when(stays)
+    def done():
+        keep.wait()
+
+    @pl.when(jnp.logical_not(stays))
+    def gone():
+        home_moves[0].wait()
+
+    home_moves[1].wait()
+    for _, copy in core_moves:
+        copy.wait_send()
+    for copy in (*plane_moves, *over_moves, *small_core):
+        copy.wait_send()
+
+
+def late(x_all, dq, dk, dv, gh1, first, out_grad, small, rows, n_ctx, n_tp):
+    _, mid, width = x_all.shape
+    groups = n_ctx * n_tp
+    anywhere = pl.BlockSpec(memory_space=pl.ANY)
+    vmem = pl.BlockSpec(memory_space=pltpu.VMEM)
+    dma = pltpu.SemaphoreType.DMA
+    low = jnp.bfloat16
+    pairs = [4 * n_ctx * (n_tp - 1), 4 * (n_ctx - 1), 2, 2, n_tp - 1, n_ctx - 1]
+    return pl.pallas_call(
+        functools.partial(late_kernel, n_ctx, n_tp),
+        name="late",
+        in_specs=[anywhere] * 7 + [vmem],
+        out_specs=[anywhere, vmem, vmem],
+        out_shape=[
+            bf16_of(2, mid, width),
+            bf16_of(4, rows, width),
+            bf16_of(*small.shape),
+        ],
+        scratch_shapes=[
+            pltpu.VMEM(x_all.shape, low),
+            pltpu.VMEM(dq.shape, low),
+            pltpu.VMEM(dk.shape, low),
+            pltpu.VMEM(dv.shape, low),
+            pltpu.VMEM(gh1.shape, jnp.float32),
+            pltpu.VMEM(first.shape, low),
+            pltpu.VMEM((width, 4 * mid), low),
+            pltpu.VMEM((groups, 4, rows, width), low),
+            pltpu.VMEM((n_tp - 1, n_ctx, 4, rows, width), low),
+            pltpu.VMEM((n_ctx, 4, rows, width), low),
+            pltpu.VMEM((n_ctx - 1, 4, rows, width), low),
+            pltpu.VMEM((2, mid, width), low),
+            pltpu.VMEM((2, mid, width), low),
+            pltpu.VMEM((2, mid, width), low),
+            pltpu.VMEM(small.shape, low),
+            pltpu.VMEM((n_tp - 1, *small.shape), low),
+            pltpu.VMEM((n_ctx - 1, *small.shape), low),
+            dma((7,)),
+            *[dma((n,)) for n in pairs for _ in range(2)],
+            dma((1,)),
+        ],
+        compiler_params=pltpu.CompilerParams(
+            collective_id=1, has_side_effects=True, vmem_limit_bytes=60 << 20
+        ),
+        cost_estimate=pl.CostEstimate(
+            flops=12_000_000_000, bytes_accessed=30 << 20, transcendentals=0
+        ),
+    )(x_all, dq, dk, dv, gh1, first, out_grad, small)
+
+
 def adam_update(weight, first, second, grad, decay, rate):
     count = float(STEP)
     first_new = beta_one * first + (1.0 - beta_one) * grad
@@ -1136,6 +1302,93 @@
     second_hat = second_new / (1.0 - beta_two**count)
     weight_new = weight - rate * (first_hat / (jnp.sqrt(second_hat) + adam_eps) + decay * weight)
     return (weight_new, first_new, second_new)
+
+
+def owner_kernel(
+    n_shard,
+    holder,
+    early_ref,
+    late_ref,
+    small_ref,
+    w_ref,
+    one_ref,
+    two_ref,
+    w_out,
+    one_out,
+    two_out,
+    small_out,
+    every,
+    packed,
+    met,
+    small_met,
+    z_s,
+    z_r,
+    s_s,
+    s_r,
+):
+    z, c, t = place_of()
+    held = w_ref.shape[0]
+
+    def far(dz):
+        return (lax.rem(z + dz, n_shard), c, t)
+
+    barrier = pltpu.get_barrier_semaphore()
+    for dz in range(1, n_shard):
+        pl.semaphore_signal(barrier, inc=1, device_id=far(dz), device_id_type=MESH)
+    every[0:4] = late_ref[...]
+    every[4:12] = early_ref[...]
+    every[12] = jnp.zeros_like(every[12])
+    for s in range(n_shard * held):
+        packed[s // held, s % held] = every[holder[s]]
+    pl.semaphore_wait(barrier, n_shard - 1)
+    moves = [
+        send(packed.at[far(dz)[0]], met.at[dz - 1], (z_s, z_r), dz - 1, far(dz))
+        for dz in range(1, n_shard)
+    ]
+    moves += [
+        send(small_ref, small_met.at[dz - 1], (s_s, s_r), dz - 1, far(dz))
+        for dz in range(1, n_shard)
+    ]
+    for copy in moves:
+        copy.start()
+    for copy in moves:
+        copy.wait()
+    for j in range(held):
+        grad = packed[z, j].astype(jnp.float32)
+        for dz in range(n_shard - 1):
+            grad = grad + met[dz, j].astype(jnp.float32)
+        w, one, two = adam_update(w_ref[j], one_ref[j], two_ref[j], grad, 0.01, rate_value)
+        w_out[j] = w
+        one_out[j] = one
+        two_out[j] = two
+    total = small_ref[...].astype(jnp.float32)
+    for dz in range(n_shard - 1):
+        total = total + small_met[dz].astype(jnp.float32)
+    small_out[...] = total
+
+
+def owner(holder, early, late_rows, small, master, one, two, n_shard):
+    held, rows, width = master.shape
+    vmem = pl.BlockSpec(memory_space=pltpu.VMEM)
+    dma = pltpu.SemaphoreType.DMA
+    return pl.pallas_call(
+        functools.partial(owner_kernel, n_shard),
+        name="owner",
+        in_specs=[pl.BlockSpec(memory_space=pltpu.SMEM)] + [vmem] * 6,
+        out_specs=[vmem] * 4,
+        out_shape=[f32_of(held, rows, width)] * 3 + [f32_of(*small.shape)],
+        scratch_shapes=[
+            pltpu.VMEM((13, rows, width), jnp.bfloat16),
+            pltpu.VMEM((n_shard, held, rows, width), jnp.bfloat16),
+            pltpu.VMEM((n_shard - 1, held, rows, width), jnp.bfloat16),
+            pltpu.VMEM((n_shard - 1, *small.shape), jnp.bfloat16),
+            *[dma((n_shard - 1,)) for _ in range(4)],
+        ],
+        compiler_params=pltpu.CompilerParams(
+            collective_id=2, has_side_effects=True, vmem_limit_bytes=40 << 20
+        ),
+        cost_estimate=pl.CostEstimate(flops=0, bytes_accessed=12 << 20, transcendentals=0),
+    )(holder, early, late_rows, small, master, one, two)
 
 
 def moves(n_ctx, n_tp, pick):
@@ -1184,8 +1437,7 @@
         low = field.astype(jnp.bfloat16)
         return jnp.where(parity == 0, low[pick], low[1 - pick])
 
-    def returned(field):
-        first, second = [lax.ppermute(field[pick], plane, home[pick]) for pick in range(2)]
+    def returned(first, second):
         swapped = parity == 1
         out = jnp.stack(
             [jnp.where(swapped, second, first), jnp.where(swapped, first, second)]
@@ -1222,65 +1474,30 @@
     out_low, n1, r1, fi, fit, hid, gel, gh2, gmt, sums_two = front(
         info, context, x_all, cot, small, rest
     )
-    layer_out = returned(out_low)
+    layer_out = returned(*[lax.ppermute(out_low[p], plane, home[p]) for p in range(2)])
     ffn_grads, out_grad, gh1, dctx, sums_one = back(
         info, gh2, hid, gel, fit, gmt, n1, r1, context, small, rest
     )
     ffn_rows = lax.psum_scatter(ffn_grads, plane, scatter_dimension=0, tiled=False)
     dq, dk, dv = attend_back(half_one, rand_blocks, q, k, v, lse, dctx, 5)
-    more = lax.ppermute(spill(info, dk, dv, first, rows), "tp", swap)
-    qkv_grads, sums_qkv = weight_grads(info, x_all, dq, dk, dv, groups)
-    small_grad = jnp.concatenate(
-        [
-            sums_qkv[0],
-            sums_qkv[1],
-            sums_one[4],
-            sums_one[5],
-            sums_one[6],
-            sums_one[0:4].reshape(-1),
-            sums_two[0],
-            sums_two[1],
-            sums_two[2],
-        ]
-    )
-    extra = -(-n_shard * span // width)
-    small_rows = small_grad.reshape(n_shard, groups, span).transpose(1, 0, 2)
     small_rows = jnp.pad(
-        small_rows.reshape(groups, n_shard * span), ((0, 0), (0, extra * width - n_shard * span))
-    ).reshape(groups, extra, width)
-    late = jnp.concatenate(
-        [
-            qkv_grads.reshape(groups, 3 * rows, width),
-            out_grad,
-            small_rows.astype(jnp.bfloat16),
-        ],
-        axis=1,
-    )
-    late, ffn_rows = lax.optimization_barrier((late, ffn_rows))
-    late_rows = lax.psum_scatter(late, plane, scatter_dimension=0, tiled=False)
-    input_low = input_grads(info, gh1, dq, dk, dv, more, first, rows)
-    input_grad = returned(input_low)
-
-    own_rows = jnp.concatenate(
-        [
-            late_rows[: 4 * rows].reshape(4, rows, width),
-            ffn_rows[0::2],
-            ffn_rows[1::2],
-        ]
-    )
-    picker = slot_of[None, :] == jnp.arange(n_shard * held, dtype=jnp.int32)[:, None]
-    packed = jnp.einsum(
-        "sm,mrd->srd", picker.astype(jnp.bfloat16), own_rows, preferred_element_type=jnp.float32
-    ).astype(jnp.bfloat16)
-    small_sum = late_rows[4 * rows :].reshape(-1)[: n_shard * span].reshape(n_shard, span)
-    small_sum = jnp.pad(small_sum, ((0, 0), (0, width - span)))[:, None, :]
-    final = jnp.concatenate([packed.reshape(n_shard, held * rows, width), small_sum], axis=1)
-    final = lax.psum_scatter(final, "shard", scatter_dimension=0, tiled=False).astype(jnp.float32)
-    slot_grads = final[: held * rows].reshape(held, rows, width)
-    small_owned = final[held * rows, :span]
-    master_new, first_new, second_new = adam_update(
-        master, moment_one, moment_two, slot_grads, 0.01, rate_value
-    )
+        jnp.concatenate([sums_one[4:7], sums_one[0:4], sums_two[0:3]]), ((2, 4), (0, 0))
+    )
+    came, late_rows, small_late = late(
+        x_all, dq, dk, dv, gh1, first, out_grad, small_rows, rows, n_ctx, n_tp
+    )
+    input_grad = returned(came[0], came[1])
+
+    stands = jnp.array([0, 1, 2, 3, 4, 6, 8, 10, 5, 7, 9, 11], jnp.int32)
+    slots_all = jnp.arange(n_shard * held, dtype=jnp.int32)
+    holder = 12 + jnp.sum(
+        jnp.where(slot_of[None, :] == slots_all[:, None], stands[None, :] - 12, 0), axis=1
+    )
+    master_new, first_new, second_new, small_sum = owner(
+        holder.astype(jnp.int32), ffn_rows, late_rows, small_late, master, moment_one, moment_two, n_shard
+    )
+    start = ((my_shard * n_ctx + my_ctx) * n_tp + my_tp) * span
+    small_owned = lax.dynamic_slice_in_dim(small_sum.reshape(-1), start, span)
     small_new, small_first, small_second = adam_update(
         small_params, small_one, small_two, small_owned, 0.0, small_rate
     )

time: 455 us -> 438 us (0.963)
  waiting for transfers between devices: 102 us -> 0.03 us
  Pallas kernels: 283 us -> 382 us
  other arithmetic: 23.6 us -> 13.9 us
  starting transfers between devices: 8.66 us -> 3.89 us
    pallas_call x0 -> x2, Pallas kernels: none -> 129 us  [the longest x1 79.5 us: late(): pl.pallas_call(functools.partial(late_kernel, n_ctx, n_tp), name='late',...]
    reduce_scatter x2 -> x0, waiting for transfers between devices: 56.9 us -> none  [the longest x1 56.9 us: shards(): late_rows = lax.psum_scatter(late, plane, scatter_dimension=0, tiled=False)]
    pallas_call x6 -> x3, Pallas kernels: 111 us -> 81.6 us  [call(): pl.pallas_call(kernel, name=name, grid_spec=pltpu.PrefetchScalarGridSpec(...]
    reduce_scatter x1, waiting for transfers between devices: 28.7 us -> 0.01 us  [shards(): lax.psum_scatter(ffn_grads, plane, scatter_dimension=0, tiled=False)]
    ppermute x5 -> x2, waiting for transfers between devices: 16.4 us -> 0.01 us  [shards(): lax.ppermute(out_low[p], plane, home[p])]
    unnamed x51 -> x52, local copies, waits for them, and re-layouts: 11.4 us -> 18.9 us
    concatenate x3 -> x1, other arithmetic: 5.35 us -> 0.64 us  [shards(): jnp.concatenate([sums_one[4:7], sums_one[0:4], sums_two[0:3]])]
    ppermute x5 -> x2, starting transfers between devices: 5.66 us -> 1.1 us  [shards(): lax.ppermute(out_low[p], plane, home[p])]
  transfers between devices with their start and end apart: 10 -> 5, of which waited for: 4 -> 0; matrix products, arithmetic and copies ran while one was open for 4% -> 2% of each run, Pallas kernels for 24% -> 36%
where the time goes in v4:
time: 438 us; the launch traced here: 437 us
  Pallas kernels  382 us (87%)
  local copies, waits for them, and re-layouts  22.8 us (5%)
  between operations  14.4 us (3%)
  other arithmetic  13.9 us (3%)
    pallas_call x1, Pallas kernels, bring(): pl.pallas_call(functools.partial(bring_kernel, n_shard, n_ctx, n_tp), nam...  103 us
    pallas_call x3, Pallas kernels, call(): pl.pallas_call(kernel, name=name, grid_spec=pltpu.PrefetchScalarGridSpec(...  81.6 us
    pallas_call x1, Pallas kernels, late(): pl.pallas_call(functools.partial(late_kernel, n_ctx, n_tp), name='late',...  79.5 us
    pallas_call x1, Pallas kernels, owner(): pl.pallas_call(functools.partial(owner_kernel, n_shard), name='owner', in...  49.1 us
    pallas_call x1, Pallas kernels, attend_back(): pl.pallas_call(functools.partial(attend_back_kernel, unroll), grid_spec=s...  39.3 us
    pallas_call x1, Pallas kernels, attend(): pl.pallas_call(functools.partial(attend_kernel, unroll), grid_spec=spec,...  28.7 us
    unnamed x52, local copies, waits for them, and re-layouts  18.9 us
  transfers between devices with their start and end apart: 5, of which 0 were waited for; matrix products, arithmetic and copies ran while one was open for 2% of the time, Pallas kernels for 36%

profile of v4, /device:TPU:0, one launch (start us, length us, event | category | flops | bytes accessed | tf_op | source)
XLA Modules:
  0.0 436.8 jit_solution(13415764804827560579)
XLA Ops:
  7.2 0.0 reduce-scatter.2.cloned.1.call-start
  7.2 1.4 fusion.6
  8.6 0.8 select_convert_fusion
  9.3 0.1 select_n.85
  9.4 0.1 reshape.61
  9.5 2.2 convert_element_type.45
  11.7 0.6 copy-done.14
  12.4 0.2 convert_element_type.40
  12.5 0.1 broadcast_select_fusion.3
  12.6 0.1 select_bitcast_fusion.2
  12.8 0.7 fusion.4
  13.4 1.3 fusion.2
  14.7 0.1 pad_maximum_fusion.xs_ref
  14.9 0.0 copy-start.13
  14.9 1.0 copy-done
  15.9 0.4 select_reduce_fusion.2
  16.4 103.5 %bring.1 = (bf16[4,512,768]{2,1,0:T(8,128)(2,1)S(1)}, bf16[8,320,768]{2,1,0:T(8,128)(2,1)S(1)}, bf16[8,9,96,768]{3,2,1,0:T(8,128)(2,1)}) custom-call(s32[12]{0:T(128)S(1)} %copy-done.13, bf16[320,768]{1,0:T(8,128)(2,1)S(1)} %pad_maximum_fusion.2.part_ref, bf16[3,96,768]{2,1,0:T(8,128)(2,1)S(1)} %get-tuple-element.84.low_ref, ...), custom_call_target="tpu_custom_call" | custom-call | bytes 41943040 | tf_op jit(solution)/shard_map/bring/pallas_call | solution.py:967
  119.9 1.7 copy-done.2
  121.5 1.9 copy-done.11
  123.4 1.0 collective-permute-start
  124.4 1.7 collective-permute-start.1
  126.2 1.0 slice_bitcast_fusion.2
  127.2 0.2 copy.27
  127.4 0.1 reshape.65
  127.5 0.7 reshape.64.small
  128.3 0.8 copy.25.table_ref
  129.1 0.6 stack.51.info
  129.7 11.6 %project.1 = (bf16[1024,768]{1,0:T(8,128)(2,1)}, bf16[2048,768]{1,0:T(8,128)(2,1)}, bf16[2048,768]{1,0:T(8,128)(2,1)}) custom-call(s32[5]{0:T(128)} %stack.51.info, bf16[4,512,768]{2,1,0:T(8,128)(2,1)} %copy-done.2, f32[12,768]{1,0:T(8,128)} %reshape.64.small, bf16[8,320,768]{2,1,0:T(8,128)(2,1)} %copy-done.11, bf16[8,320,768]{2,1,0:T(8,128)(2,1)} %copy-done.11, ...), custom_call_target="tpu_custom_call" | custom-call | flops 6000000000 | bytes 16777216 | tf_op jit(solution)/shard_map/project/pallas_call | solution.py:375
  141.3 28.7 %attend.1 = (bf16[1024,768]{1,0:T(8,128)(2,1)}, f32[3,16,256]{2,1,0:T(8,128)}) custom-call(s32[1]{0:T(128)} %bitcast.half_ref, s32[12,30,3]{2,1,0:T(8,128)} %copy.25.table_ref, bf16[1024,768]{1,0:T(8,128)(2,1)} %get-tuple-element.46.q_ref, bf16[2048,768]{1,0:T(8,128)(2,1)} %get-tuple-element.47.k_ref, bf16[2048,768]{1,0:T(8,128)(2,1)} %get-tuple-element.48.v_ref), custom_call_target="tpu_custom_call" | custom-call | flops 60000002048 | bytes 12582912 | tf_op jit(solution)/shard_map/attend/pallas_call | solution.py:168
  170.0 1.3 pad_maximum_fusion.1.cot_ref
  171.3 28.4 %front.1 = (bf16[2,512,768]{2,1,0:T(8,128)(2,1)}, f32[1024,768]{1,0:T(8,128)}, f32[1024,128]{1,0:T(8,128)}, bf16[1024,768]{1,0:T(8,128)(2,1)}, bf16[768,1024]{1,...) custom-call(s32[5]{0:T(128)} %stack.51.info, ...), custom_call_target="tpu_custom_call" | custom-call | flops 11000000512 | bytes 41943040 | tf_op jit(solution)/shard_map/front/pallas_call | solution.py:375
  199.7 41.6 %back.1 = (bf16[8,8,96,768]{3,2,1,0:T(8,128)(2,1)}, bf16[8,96,768]{2,1,0:T(8,128)(2,1)}, f32[1024,768]{1,0:T(8,128)}, bf16[1024,768]{1,0:T(8,128)(2,1)}, f32[8,768]{1,0:T(8,128)}) custom-call(s32[5]{0:T(128)} %stack.51.info, f32[1024,768]{1,0:T(8,128)} %get-tuple-element.55.gh2_ref, bf16[4,1024,768]{2,1,0:T(8,128)(2,1)} %get-tuple-element.56.hid_ref, ...), custom_call_target="tpu_custom_call" | custom-call | flops 22000001024 | bytes 41943040 | tf_op jit(solution)/shard_map/back/pallas_call | solution.py:375
  241.3 0.0 copy-start.22
  241.4 0.0 reduce-scatter.2.cloned.1.call-update
  241.4 0.6 copy-done.22
  242.0 0.1 select_reduce_fusion.3
  242.2 0.6 copy-done.15
  242.8 0.1 slice_bitcast_fusion.1
  242.9 0.4 collective-permute-start.2
  243.3 0.7 collective-permute-start.3
  244.0 0.6 select_maximum_fusion.small_ref
  244.6 39.3 %attend_back.1 = (bf16[1024,768]{1,0:T(8,128)(2,1)}, bf16[2048,768]{1,0:T(8,128)(2,1)}, bf16[2048,768]{1,0:T(8,128)(2,1)}) custom-call(s32[1]{0:T(128)} %bitcast.half_ref, s32[12,30,3]{2,1,0:T(8,128)} %copy.25.table_ref, bf16[1024,768]{1,0:T(8,128)(2,1)} %get-tuple-element.46.q_ref, bf16[2048,768]{1,0:T(8,128)(2,1)} %get-tuple-element.47.k_ref, ...), custom_call_target="tpu_custom_call" | custom-call | flops 120000004096 | bytes 25165824 | tf_op jit(solution)/shard_map/attend_back/pallas_call | solution.py:307
  284.0 79.5 %late.1 = (bf16[2,512,768]{2,1,0:T(8,128)(2,1)}, bf16[4,96,768]{2,1,0:T(8,128)(2,1)}, bf16[16,768]{1,0:T(8,128)(2,1)}) custom-call(bf16[4,512,768]{2,1,0:T(8,128)(2,1)} %copy-done.2, bf16[1024,768]{1,0:T(8,128)(2,1)} %get-tuple-element.63.dq_hbm, bf16[2048,768]{1,0:T(8,128)(2,1)} %get-tuple-element.64.dk_hbm, bf16[2048,768]{1,0:T(8,128)(2,1)} %get-tuple-element.65.dv_hbm, ...), custom_call_target="tpu_custom_call" | custom-call | flops 12000000000 | bytes 31457280 | tf_op jit(solution)/shard_map/late/pallas_call | solution.py:1256
  363.5 1.5 broadcast_select_fusion.1
  365.0 1.9 maximum_convert_fusion.1
  366.8 0.1 select_bitcast_fusion.1
  367.0 0.0 copy-start.4
  367.0 0.0 copy-start.5
  367.0 1.9 maximum_convert_fusion
  368.9 0.2 copy-done.4
  369.1 0.7 copy-done.5
  369.8 1.3 copy-done.3
  371.1 1.1 copy-done.9
  372.1 0.7 copy-done.12
  372.9 49.1 %owner.1 = (f32[3,96,768]{2,1,0:T(8,128)S(1)}, f32[3,96,768]{2,1,0:T(8,128)S(1)}, f32[3,96,768]{2,1,0:T(8,128)S(1)}, f32[16,768]{1,0:T(8,128)S(1)}) custom-call(s32[12]{0:T(128)S(1)} %broadcast_add_fusion.holder, bf16[8,96,768]{2,1,0:T(8,128)(2,1)S(1)} %bitcast.27, bf16[4,96,768]{2,1,0:T(8,128)(2,1)S(1)} %copy-done.9, bf16[16,768]{1,0:T(8,128)(2,1)S(1)} %copy-done.12, ...), custom_call_target="tpu_custom_call" | custom-call | bytes 12582912 | tf_op jit(solution)/shard_map/owner/pallas_call | solution.py:1374
  422.0 0.0 copy-start.6
  422.0 0.9 copy-done.6
  422.9 0.9 copy-done.8
  423.8 0.6 copy-done.10
  424.4 0.9 reshape.63
  425.3 0.7 multiply_subtract_fusion
  426.0 2.1 copy.31
  428.1 0.9 copy.32
  429.0 0.9 copy.33
  (41 shorter events, 0.2 us)
Async XLA Ops:
  7.2 361.7 %reduce-scatter.2.cloned.1.call-start = ((), (), s32[]{:S(2)}) async-start(), calls=%async_computation.1 | async-start | bytes 10616832 | tf_op jit(solution)/shard_map/reduce_scatter | solution.py:1481
  9.5 2.8 copy-start.14
  14.7 1.2 copy-start
  14.9 1.5 copy-start.13
  119.9 1.7 copy-start.2
  121.5 1.9 copy-start.11
  123.4 4.9 %copy-start.16 = (s32[12,30,3]{1,2,0:T(4,128)S(1)}, s32[12,30,3]{1,2,0:T(4,128)}, u32[]{:S(2)}) copy-start(s32[12,30,3]{1,2,0:T(4,128)} %param.13) | copy-start | bytes 12964
  123.4 46.6 %collective-permute-start = (bf16[512,768]{1,0:T(8,128)(2,1)S(1)}, bf16[512,768]{1,0:T(8,128)(2,1)S(1)}, u32[]{:S(2)}, u32[]{:S(2)}) collective-permute-start(bf16[512,768]{1,0:T(8,128)(2,1)S(1)} %get-tuple-element.50), channel_id=1, source_target_pairs={{0,0},{1,4},{2,2},{3,6},{4,1},{5,5},{6,3},{7,7},{8,8},{9,12},{10,1... | collective-permute-start | bytes 2359304 | tf_op jit(solution)/shard_map/ppermute | solution.py:1470
  124.4 45.5 %collective-permute-start.1 = (bf16[512,768]{1,0:T(8,128)(2,1)S(1)}, bf16[512,768]{1,0:T(8,128)(2,1)S(1)}, u32[]{:S(2)}, u32[]{:S(2)}) collective-permute-start(bf16[512,768]{1,0:T(8,128)(2,1)S(1)} %get-tuple-element.51), channel_id=1, source_target_pairs={{0,2},{1,6},{2,0},{3,4},{4,3},{5,7},{6,1},{7,5},{8,10},{9,14},{10,... | collective-permute-start | bytes 2359304 | tf_op jit(solution)/shard_map/ppermute | solution.py:1470
  241.3 0.7 copy-start.22
  241.3 0.8 copy-start.17
  241.3 0.8 copy-start.19
  241.4 1.4 copy-start.15
  242.9 123.9 %collective-permute-start.2 = (bf16[512,768]{1,0:T(8,128)(2,1)S(1)}, bf16[512,768]{1,0:T(8,128)(2,1)S(1)}, u32[]{:S(2)}, u32[]{:S(2)}) collective-permute-start(bf16[512,768]{1,0:T(8,128)(2,1)S(1)} %get-tuple-element.89), channel_id=1, source_target_pairs={{2,0},{6,1},{0,2},{4,3},{3,4},{7,5},{1,6},{5,7},{10,8},{14,9},{8,1... | collective-permute-start | bytes 2359304 | tf_op jit(solution)/shard_map/ppermute | solution.py:1477
  243.3 123.5 %collective-permute-start.3 = (bf16[512,768]{1,0:T(8,128)(2,1)S(1)}, bf16[512,768]{1,0:T(8,128)(2,1)S(1)}, u32[]{:S(2)}, u32[]{:S(2)}) collective-permute-start(bf16[512,768]{1,0:T(8,128)(2,1)S(1)} %get-tuple-element.90), channel_id=1, source_target_pairs={{0,0},{4,1},{2,2},{6,3},{1,4},{5,5},{3,6},{7,7},{8,8},{12,9},{10,1... | collective-permute-start | bytes 2359304 | tf_op jit(solution)/shard_map/ppermute | solution.py:1477
  366.9 1.9 copy-start.1
  367.0 2.1 copy-start.4
  367.0 2.8 copy-start.5
  369.8 1.3 copy-start.3
  371.1 1.1 copy-start.9
  372.1 0.7 copy-start.12
  372.9 52.4 %copy-start.18 = (f32[288]{0:T(512)S(1)}, f32[288]{0:T(512)}, u32[]{:S(2)}) copy-start(f32[288]{0:T(512)} %param.18) | copy-start | bytes 3460
  372.9 52.4 %copy-start.20 = (f32[288]{0:T(512)S(1)}, f32[288]{0:T(512)}, u32[]{:S(2)}) copy-start(f32[288]{0:T(512)} %param.19) | copy-start | bytes 3460
  372.9 52.4 %copy-start.21 = (f32[288]{0:T(512)S(1)}, f32[288]{0:T(512)}, u32[]{:S(2)}) copy-start(f32[288]{0:T(512)} %param.20) | copy-start | bytes 3460
  422.0 0.9 copy-start.6
  422.9 0.9 copy-start.8
  423.8 0.6 copy-start.10
  424.4 3.7 copy-start.7
Sparse Core Ops, SparseCore 0:
  241.5 112.7 reduce-scatter.1

commit v5 on v4

--- a/solution.py
+++ b/solution.py
@@ -566,131 +566,6 @@
     )
 
 
-def back_kernel(
-    info,
-    gh2_ref,
-    hid_ref,
-    gel_ref,
-    fit_ref,
-    gmt_ref,
-    n1_ref,
-    r1_ref,
-    ctx_ref,
-    small,
-    up_w,
-    down_w,
-    wo,
-    pair_ref,
-    dwo_ref,
-    gh1_ref,
-    dctx_ref,
-    sums_ref,
-    gy,
-    gu,
-):
-    step = pl.program_id(0)
-    tokens, width = gh2_ref.shape
-    tiles = tokens // TILE
-    groups, _, rows, _ = pair_ref.shape
-
-    @pl.when(step == 0)
-    def clear():
-        sums_ref[...] = jnp.zeros_like(sums_ref)
-        gy[...] = gh2_ref[...]
-
-    @pl.when(step < 4)
-    def ffn():
-        up_block = matrix(up_w)
-        down_block = matrix(down_w)
-
-        def one(t, carry):
-            at = pl.ds(pl.multiple_of(t * TILE, TILE), TILE)
-            mixed = gh2_ref[at, :].astype(jnp.bfloat16)
-            grad = wide_dot(mixed, down_block, NN) * gel_ref[0, at, :].astype(jnp.float32)
-            low = grad.astype(jnp.bfloat16)
-            gu[at, :] = low
-            gy[at, :] += wide_dot(low, up_block, NT)
-            sums_ref[pl.ds(step, 1), :] += jnp.sum(
-                low.astype(jnp.float32), axis=0, keepdims=True
-            )
-            return carry
-
-        lax.fori_loop(0, tiles, one, 0)
-        grad_up = wide_dot(fit_ref[...], gu[...], NN).astype(jnp.bfloat16)
-        pair_ref[:, 0:1] = grad_up.reshape(groups, 1, rows, width)
-        grad_down = wide_dot(gmt_ref[...], hid_ref[0], NN).astype(jnp.bfloat16)
-        pair_ref[:, 1:2] = grad_down.reshape(groups, 1, rows, width)
-
-    @pl.when(step == 4)
-    def first_norm():
-        out_w = matrix(wo)
-
-        def one(t, carry):
-            at = pl.ds(pl.multiple_of(t * TILE, TILE), TILE)
-            grad = gy[at, :]
-            n1 = n1_ref[at, :]
-            gh1 = norm_back(grad, n1, r1_ref[at, 0:1], small[3:4, :])
-            gh1_ref[at, :] = gh1
-            low = gh1.astype(jnp.bfloat16)
-            gu[at, :] = low
-            dctx_ref[at, :] = wide_dot(low, out_w, NT).astype(jnp.bfloat16)
-            add_row(sums_ref, 4, low.astype(jnp.float32))
-            add_row(sums_ref, 5, grad * n1)
-            add_row(sums_ref, 6, grad)
-            return carry
-
-        lax.fori_loop(0, tiles, one, 0)
-        grad_out = wide_dot(ctx_ref[...].T, gu[...], NN).astype(jnp.bfloat16)
-        dwo_ref[...] = grad_out.reshape(dwo_ref.shape)
-
-
-def back(info, gh2, hid, gel, fit, gmt, n1, r1, ctx, small, rest):
-    tokens, width = gh2.shape
-    groups, _, rows, _ = rest.shape
-
-    def block(b, info):
-        return (jnp.minimum(b, 3), 0, 0)
-
-    return call(
-        back_kernel,
-        "back",
-        info,
-        5,
-        [
-            fixed((tokens, width)),
-            pl.BlockSpec((1, tokens, width), block),
-            pl.BlockSpec((1, tokens, width), block),
-            fixed((width, tokens)),
-            fixed((width, tokens)),
-            fixed((tokens, width)),
-            fixed((tokens, 128)),
-            fixed((tokens, width)),
-            fixed(small.shape),
-            rest_spec(rest, lambda b: 4 + jnp.minimum(b, 3), False),
-            rest_spec(rest, lambda b: 8 + jnp.minimum(b, 3), False),
-            rest_spec(rest, lambda b: 3),
-        ],
-        [
-            pl.BlockSpec((groups, 2, rows, width), lambda b, info: (0, jnp.minimum(b, 3), 0, 0)),
-            resident((groups, rows, width)),
-            resident((tokens, width)),
-            resident((tokens, width)),
-            resident((8, width)),
-        ],
-        [
-            bf16_of(groups, 8, rows, width),
-            bf16_of(groups, rows, width),
-            f32_of(tokens, width),
-            bf16_of(tokens, width),
-            f32_of(8, width),
-        ],
-        [pltpu.VMEM((tokens, width), jnp.float32), pltpu.VMEM((tokens, width), jnp.bfloat16)],
-        (gh2, hid, gel, fit, gmt, n1, r1, ctx, small, rest, rest, rest),
-        22_000_000_000,
-        40 << 20,
-    )
-
-
 MESH = pl.DeviceIdType.MESH
 KINDS = 3
 
@@ -995,6 +870,212 @@
     )(slots, part, low, xs)
 
 
+def back_kernel(
+    n_ctx,
+    n_tp,
+    gh2_ref,
+    hid_ref,
+    gel_ref,
+    fit_ref,
+    gmt_ref,
+    n1_ref,
+    r1_ref,
+    ctx_ref,
+    small,
+    up_w,
+    down_w,
+    wo,
+    own_ref,
+    x_ref,
+    y_ref,
+    xy_ref,
+    gh1_ref,
+    dctx_ref,
+    sums_ref,
+    gy,
+    gu,
+    grads,
+    arrived,
+    send_sem,
+    recv_sem,
+):
+    z, c, t = place_of()
+    step = pl.program_id(0)
+    tokens, width = gh2_ref.shape
+    tiles = tokens // TILE
+    rows = own_ref.shape[1]
+    others = n_tp - 1
+
+    def beside(dt):
+        return (z, c, lax.rem(t + dt, n_tp))
+
+    @pl.when(step == 0)
+    def start():
+        barrier = pltpu.get_barrier_semaphore()
+        for dt in range(1, n_tp):
+            pl.semaphore_signal(barrier, inc=1, device_id=beside(dt), device_id_type=MESH)
+        pl.semaphore_wait(barrier, others)
+        sums_ref[...] = jnp.zeros_like(sums_ref)
+        gy[...] = gh2_ref[...]
+
+    def moves(b, count):
+        slot = lax.rem(b, 2)
+        return [
+            send(
+                grads.at[slot, :, lax.rem(t + dt, n_tp), 0:count],
+                arrived.at[b, dt - 1, :, 0:count],
+                (send_sem, recv_sem),
+                b * others + dt - 1,
+                beside(dt),
+            )
+            for dt in range(1, n_tp)
+        ]
+
+    def exchange(b, count):
+        for copy in moves(b, count):
+            copy.start()
+
+    def keep(b, count):
+        for copy in moves(b, count):
+            copy.wait()
+        slot = lax.rem(b, 2)
+        for j, out in enumerate((own_ref, x_ref, y_ref, xy_ref)):
+            for i in range(count):
+                value = grads[slot, c ^ j, t, i]
+                for dt in range(others):
+                    value = value + arrived[b, dt, c ^ j, i]
+                out[2 * b + i] = value
+
+    def put(slot, i, value):
+        low = value.astype(jnp.bfloat16)
+        grads[slot, :, :, i] = low.reshape(n_ctx, n_tp, rows, width)
+
+    @pl.when(step < 4)
+    def ffn():
+        up_block = matrix(up_w)
+        down_block = matrix(down_w)
+        slot = lax.rem(step, 2)
+
+        def one(i, carry):
+            at = pl.ds(pl.multiple_of(i * TILE, TILE), TILE)
+            mixed = gh2_ref[at, :].astype(jnp.bfloat16)
+            grad = wide_dot(mixed, down_block, NN) * gel_ref[0, at, :].astype(jnp.float32)
+            low = grad.astype(jnp.bfloat16)
+            gu[at, :] = low
+            gy[at, :] += wide_dot(low, up_block, NT)
+            sums_ref[pl.ds(step, 1), :] += jnp.sum(
+                low.astype(jnp.float32), axis=0, keepdims=True
+            )
+            return carry
+
+        lax.fori_loop(0, tiles, one, 0)
+        put(slot, 0, wide_dot(fit_ref[...], gu[...], NN))
+        put(slot, 1, wide_dot(gmt_ref[...], hid_ref[0], NN))
+        exchange(step, 2)
+
+    @pl.when(step > 0)
+    def settle():
+        keep(step - 1, 2)
+
+    @pl.when(step == 4)
+    def first_norm():
+        def one(i, carry):
+            at = pl.ds(pl.multiple_of(i * TILE, TILE), TILE)
+            grad = gy[at, :]
+            n1 = n1_ref[at, :]
+            gh1 = norm_back(grad, n1, r1_ref[at, 0:1], small[3:4, :])
+            gh1_ref[at, :] = gh1
+            low = gh1.astype(jnp.bfloat16)
+            gu[at, :] = low
+            add_row(sums_ref, 4, low.astype(jnp.float32))
+            add_row(sums_ref, 5, grad * n1)
+            add_row(sums_ref, 6, grad)
+            return carry
+
+        lax.fori_loop(0, tiles, one, 0)
+        put(0, 0, wide_dot(ctx_ref[...].T, gu[...], NN))
+        exchange(4, 1)
+        out_w = matrix(wo)
+
+        def two(i, carry):
+            at = pl.ds(pl.multiple_of(i * TILE, TILE), TILE)
+            dctx_ref[at, :] = wide_dot(gu[at, :], out_w, NT).astype(jnp.bfloat16)
+            return carry
+
+        lax.fori_loop(0, tiles, two, 0)
+        keep(4, 1)
+
+
+def back(gh2, hid, gel, fit, gmt, n1, r1, ctx, small, rest, n_ctx, n_tp):
+    tokens, width = gh2.shape
+    rows = rest.shape[2]
+    dma = pltpu.SemaphoreType.DMA
+
+    def whole(shape):
+        return pl.BlockSpec(shape, lambda b: (0,) * len(shape), pipeline_mode=pl.Buffered(1))
+
+    def block(b):
+        return (jnp.minimum(b, 3), 0, 0)
+
+    def held(first, single=False):
+        return pl.BlockSpec(
+            (n_ctx * n_tp, 1, rows, width),
+            (lambda b: (0, first, 0, 0))
+            if single
+            else (lambda b: (0, first + jnp.minimum(b, 3), 0, 0)),
+            pipeline_mode=pl.Buffered(1) if single else None,
+        )
+
+    def out(shape):
+        return pl.BlockSpec(shape, lambda b: (0,) * len(shape))
+
+    return pl.pallas_call(
+        functools.partial(back_kernel, n_ctx, n_tp),
+        name="back",
+        grid=(5,),
+        in_specs=[
+            whole((tokens, width)),
+            pl.BlockSpec((1, tokens, width), block),
+            pl.BlockSpec((1, tokens, width), block),
+            whole((width, tokens)),
+            whole((width, tokens)),
+            whole((tokens, width)),
+            whole((tokens, 128)),
+            whole((tokens, width)),
+            whole(small.shape),
+            held(1),
+            held(5),
+            held(0, True),
+        ],
+        out_specs=[
+            *[out((9, rows, width))] * 4,
+            out((tokens, width)),
+            out((tokens, width)),
+            out((8, width)),
+        ],
+        out_shape=[
+            *[bf16_of(9, rows, width)] * 4,
+            f32_of(tokens, width),
+            bf16_of(tokens, width),
+            f32_of(8, width),
+        ],
+        scratch_shapes=[
+            pltpu.VMEM((tokens, width), jnp.float32),
+            pltpu.VMEM((tokens, width), jnp.bfloat16),
+            pltpu.VMEM((2, n_ctx, n_tp, 2, rows, width), jnp.bfloat16),
+            pltpu.VMEM((5, n_tp - 1, n_ctx, 2, rows, width), jnp.bfloat16),
+            dma((5 * (n_tp - 1),)),
+            dma((5 * (n_tp - 1),)),
+        ],
+        compiler_params=pltpu.CompilerParams(
+            collective_id=3, has_side_effects=True, vmem_limit_bytes=62 << 20
+        ),
+        cost_estimate=pl.CostEstimate(
+            flops=22_000_000_000, bytes_accessed=40 << 20, transcendentals=0
+        ),
+    )(gh2, hid, gel, fit, gmt, n1, r1, ctx, small, rest, rest, rest)
+
+
 def late_kernel(
     n_ctx,
     n_tp,
@@ -1004,7 +1085,6 @@
     dv_hbm,
     gh1_hbm,
     first_hbm,
-    wo_hbm,
     small_ref,
     home_ref,
     rows_ref,
@@ -1061,7 +1141,6 @@
                 (dq_hbm, dq_s),
                 (first_hbm, first_s),
                 (gh1_hbm, gh1_s),
-                (wo_hbm, grads.at[:, 3]),
             )
         )
     ]
@@ -1092,7 +1171,7 @@
                     grads.at[k * n_tp + other, m],
                     arrived.at[dt - 1, k, m],
                     (c_s, c_r),
-                    ((dt - 1) * n_ctx + k) * 4 + m,
+                    ((dt - 1) * n_ctx + k) * 3 + m,
                     beside(dt),
                 )
                 copy.start()
@@ -1111,13 +1190,11 @@
             partial[k, m] = value
         for j in range(1, n_ctx):
             copy = send(
-                partial.at[c ^ j, m], met.at[j - 1, m], (p_s, p_r), (j - 1) * 4 + m, across(j)
+                partial.at[c ^ j, m], met.at[j - 1, m], (p_s, p_r), (j - 1) * 3 + m, across(j)
             )
             copy.start()
             plane_moves.append(copy)
 
-    loads[6].wait()
-    exchange(3)
     loads[0].wait()
     for a in range(4):
         own = 1 if a < 2 else 0
@@ -1137,7 +1214,6 @@
     loads[1].wait()
     weight_grad(1, slice(None), dk_s)
     exchange(1)
-    meet(3)
     loads[2].wait()
     weight_grad(2, slice(None), dv_s)
     exchange(2)
@@ -1219,7 +1295,7 @@
 
     for copy in plane_moves:
         copy.wait_recv()
-    for m in range(4):
+    for m in range(3):
         value = partial[c, m]
         for j in range(n_ctx - 1):
             value = value + met[j, m]
@@ -1245,22 +1321,22 @@
         copy.wait_send()
 
 
-def late(x_all, dq, dk, dv, gh1, first, out_grad, small, rows, n_ctx, n_tp):
+def late(x_all, dq, dk, dv, gh1, first, small, rows, n_ctx, n_tp):
     _, mid, width = x_all.shape
     groups = n_ctx * n_tp
     anywhere = pl.BlockSpec(memory_space=pl.ANY)
     vmem = pl.BlockSpec(memory_space=pltpu.VMEM)
     dma = pltpu.SemaphoreType.DMA
     low = jnp.bfloat16
-    pairs = [4 * n_ctx * (n_tp - 1), 4 * (n_ctx - 1), 2, 2, n_tp - 1, n_ctx - 1]
+    pairs = [3 * n_ctx * (n_tp - 1), 3 * (n_ctx - 1), 2, 2, n_tp - 1, n_ctx - 1]
     return pl.pallas_call(
         functools.partial(late_kernel, n_ctx, n_tp),
         name="late",
-        in_specs=[anywhere] * 7 + [vmem],
+        in_specs=[anywhere] * 6 + [vmem],
         out_specs=[anywhere, vmem, vmem],
         out_shape=[
             bf16_of(2, mid, width),
-            bf16_of(4, rows, width),
+            bf16_of(3, rows, width),
             bf16_of(*small.shape),
         ],
         scratch_shapes=[
@@ -1271,17 +1347,17 @@
             pltpu.VMEM(gh1.shape, jnp.float32),
             pltpu.VMEM(first.shape, low),
             pltpu.VMEM((width, 4 * mid), low),
-            pltpu.VMEM((groups, 4, rows, width), low),
-            pltpu.VMEM((n_tp - 1, n_ctx, 4, rows, width), low),
-            pltpu.VMEM((n_ctx, 4, rows, width), low),
-            pltpu.VMEM((n_ctx - 1, 4, rows, width), low),
+            pltpu.VMEM((groups, 3, rows, width), low),
+            pltpu.VMEM((n_tp - 1, n_ctx, 3, rows, width), low),
+            pltpu.VMEM((n_ctx, 3, rows, width), low),
+            pltpu.VMEM((n_ctx - 1, 3, rows, width), low),
             pltpu.VMEM((2, mid, width), low),
             pltpu.VMEM((2, mid, width), low),
             pltpu.VMEM((2, mid, width), low),
             pltpu.VMEM(small.shape, low),
             pltpu.VMEM((n_tp - 1, *small.shape), low),
             pltpu.VMEM((n_ctx - 1, *small.shape), low),
-            dma((7,)),
+            dma((6,)),
             *[dma((n,)) for n in pairs for _ in range(2)],
             dma((1,)),
         ],
@@ -1291,7 +1367,7 @@
         cost_estimate=pl.CostEstimate(
             flops=12_000_000_000, bytes_accessed=30 << 20, transcendentals=0
         ),
-    )(x_all, dq, dk, dv, gh1, first, out_grad, small)
+    )(x_all, dq, dk, dv, gh1, first, small)
 
 
 def adam_update(weight, first, second, grad, decay, rate):
@@ -1307,7 +1383,10 @@
 def owner_kernel(
     n_shard,
     holder,
-    early_ref,
+    own_ref,
+    x_ref,
+    y_ref,
+    xy_ref,
     late_ref,
     small_ref,
     w_ref,
@@ -1335,8 +1414,8 @@
     barrier = pltpu.get_barrier_semaphore()
     for dz in range(1, n_shard):
         pl.semaphore_signal(barrier, inc=1, device_id=far(dz), device_id_type=MESH)
-    every[0:4] = late_ref[...]
-    every[4:12] = early_ref[...]
+    every[0:3] = late_ref[...]
+    every[3:12] = own_ref[...] + x_ref[...] + y_ref[...] + xy_ref[...]
     every[12] = jnp.zeros_like(every[12])
     for s in range(n_shard * held):
         packed[s // held, s % held] = every[holder[s]]
@@ -1374,7 +1453,7 @@
     return pl.pallas_call(
         functools.partial(owner_kernel, n_shard),
         name="owner",
-        in_specs=[pl.BlockSpec(memory_space=pltpu.SMEM)] + [vmem] * 6,
+        in_specs=[pl.BlockSpec(memory_space=pltpu.SMEM)] + [vmem] * 9,
         out_specs=[vmem] * 4,
         out_shape=[f32_of(held, rows, width)] * 3 + [f32_of(*small.shape)],
         scratch_shapes=[
@@ -1388,7 +1467,7 @@
             collective_id=2, has_side_effects=True, vmem_limit_bytes=40 << 20
         ),
         cost_estimate=pl.CostEstimate(flops=0, bytes_accessed=12 << 20, transcendentals=0),
-    )(holder, early, late_rows, small, master, one, two)
+    )(holder, *early, late_rows, small, master, one, two)
 
 
 def moves(n_ctx, n_tp, pick):
@@ -1475,26 +1554,31 @@
         info, context, x_all, cot, small, rest
     )
     layer_out = returned(*[lax.ppermute(out_low[p], plane, home[p]) for p in range(2)])
-    ffn_grads, out_grad, gh1, dctx, sums_one = back(
-        info, gh2, hid, gel, fit, gmt, n1, r1, context, small, rest
-    )
-    ffn_rows = lax.psum_scatter(ffn_grads, plane, scatter_dimension=0, tiled=False)
+    *early, gh1, dctx, sums_one = back(
+        gh2, hid, gel, fit, gmt, n1, r1, context, small, rest, n_ctx, n_tp
+    )
+    for j in range(1, n_ctx):
+        crossing = [
+            (a * n_tp + b, (a ^ j) * n_tp + b) for a in range(n_ctx) for b in range(n_tp)
+        ]
+        early[j] = lax.ppermute(early[j], plane, crossing)
+    layer_out, dctx = lax.optimization_barrier((layer_out, dctx))
     dq, dk, dv = attend_back(half_one, rand_blocks, q, k, v, lse, dctx, 5)
     small_rows = jnp.pad(
         jnp.concatenate([sums_one[4:7], sums_one[0:4], sums_two[0:3]]), ((2, 4), (0, 0))
     )
     came, late_rows, small_late = late(
-        x_all, dq, dk, dv, gh1, first, out_grad, small_rows, rows, n_ctx, n_tp
+        x_all, dq, dk, dv, gh1, first, small_rows, rows, n_ctx, n_tp
     )
     input_grad = returned(came[0], came[1])
 
-    stands = jnp.array([0, 1, 2, 3, 4, 6, 8, 10, 5, 7, 9, 11], jnp.int32)
+    stands = jnp.array([0, 1, 2, 11, 3, 5, 7, 9, 4, 6, 8, 10], jnp.int32)
     slots_all = jnp.arange(n_shard * held, dtype=jnp.int32)
     holder = 12 + jnp.sum(
         jnp.where(slot_of[None, :] == slots_all[:, None], stands[None, :] - 12, 0), axis=1
     )
     master_new, first_new, second_new, small_sum = owner(
-        holder.astype(jnp.int32), ffn_rows, late_rows, small_late, master, moment_one, moment_two, n_shard
+        holder.astype(jnp.int32), early, late_rows, small_late, master, moment_one, moment_two, n_shard
     )
     start = ((my_shard * n_ctx + my_ctx) * n_tp + my_tp) * span
     small_owned = lax.dynamic_slice_in_dim(small_sum.reshape(-1), start, span)

time: 438 us -> 421 us (0.961)
  Pallas kernels: 382 us -> 364 us
  between operations: 14.4 us -> 1.23 us
  starting transfers between devices: 3.89 us -> 14.4 us
    pallas_call x0 -> x1, Pallas kernels: none -> 45.3 us  [back(): pl.pallas_call(functools.partial(back_kernel, n_ctx, n_tp), name='back',...]
    pallas_call x3 -> x2, Pallas kernels: 81.6 us -> 40 us  [call(): pl.pallas_call(kernel, name=name, grid_spec=pltpu.PrefetchScalarGridSpec(...]
    pallas_call x1, Pallas kernels: 79.5 us -> 51.5 us  [late(): pl.pallas_call(functools.partial(late_kernel, n_ctx, n_tp), name='late',...]
    ppermute x2, starting transfers between devices: 1.1 us -> 7.94 us  [shards(): lax.ppermute(out_low[p], plane, home[p])]
    pallas_call x1, Pallas kernels: 49.1 us -> 55.8 us  [owner(): pl.pallas_call(functools.partial(owner_kernel, n_shard), name='owner', in...]
    unnamed x52 -> x50, local copies, waits for them, and re-layouts: 18.9 us -> 15.6 us
  transfers between devices with their start and end apart: 5 -> 7, of which waited for: 0 -> 0; matrix products, arithmetic and copies ran while one was open for 2% -> 3% of each run, Pallas kernels for 36% -> 42%
where the time goes in v5:
time: 421 us; the launch traced here: 418 us
  Pallas kernels  364 us (86%)
  local copies, waits for them, and re-layouts  22.6 us (5%)
  other arithmetic  15.3 us (4%)
  starting transfers between devices  14.4 us (3%)
    pallas_call x1, Pallas kernels, bring(): pl.pallas_call(functools.partial(bring_kernel, n_shard, n_ctx, n_tp), nam...  103 us
    pallas_call x1, Pallas kernels, owner(): pl.pallas_call(functools.partial(owner_kernel, n_shard), name='owner', in...  55.8 us
    pallas_call x1, Pallas kernels, late(): pl.pallas_call(functools.partial(late_kernel, n_ctx, n_tp), name='late',...  51.5 us
    pallas_call x1, Pallas kernels, back(): pl.pallas_call(functools.partial(back_kernel, n_ctx, n_tp), name='back',...  45.3 us
    pallas_call x2, Pallas kernels, call(): pl.pallas_call(kernel, name=name, grid_spec=pltpu.PrefetchScalarGridSpec(...  40 us
    pallas_call x1, Pallas kernels, attend_back(): pl.pallas_call(functools.partial(attend_back_kernel, unroll), grid_spec=s...  39.4 us
    pallas_call x1, Pallas kernels, attend(): pl.pallas_call(functools.partial(attend_kernel, unroll), grid_spec=spec,...  28.8 us
    unnamed x50, local copies, waits for them, and re-layouts  15.6 us
  transfers between devices with their start and end apart: 7, of which 0 were waited for; matrix products, arithmetic and copies ran while one was open for 3% of the time, Pallas kernels for 42%

profile of v5, /device:TPU:0, one launch (start us, length us, event | category | flops | bytes accessed | tf_op | source)
XLA Modules:
  0.0 417.9 jit_solution(13134338696024379699)
XLA Ops:
  0.7 1.4 fusion.6
  2.0 0.8 select_convert_fusion
  2.8 0.1 select_n.85
  2.9 0.1 reshape.61
  2.9 0.0 copy-start.15
  3.0 2.2 convert_element_type.45
  5.2 0.6 copy-done.15
  5.8 0.2 convert_element_type.40
  5.9 0.1 broadcast_select_fusion.3
  6.1 0.1 select_bitcast_fusion.2
  6.2 0.7 fusion.4
  6.8 1.3 fusion.2
  8.1 0.0 copy-start
  8.2 0.1 pad_maximum_fusion.xs_ref
  8.3 0.0 copy-start.14
  8.3 1.0 copy-done
  9.3 0.4 select_reduce_fusion.2
  9.7 0.0 copy-start.16
  9.8 103.5 %bring.1 = (bf16[4,512,768]{2,1,0:T(8,128)(2,1)S(1)}, bf16[8,320,768]{2,1,0:T(8,128)(2,1)S(1)}, bf16[8,9,96,768]{3,2,1,0:T(8,128)(2,1)}) custom-call(s32[12]{0:T(128)S(1)} %copy-done.14, bf16[320,768]{1,0:T(8,128)(2,1)S(1)} %pad_maximum_fusion.2.part_ref, bf16[3,96,768]{2,1,0:T(8,128)(2,1)S(1)} %get-tuple-element.92.low_ref, ...), custom_call_target="tpu_custom_call" | custom-call | bytes 41943040 | tf_op jit(solution)/shard_map/bring/pallas_call | solution.py:842
  113.3 0.0 copy-start.2
  113.3 1.7 copy-done.2
  115.0 2.0 copy-done.12
  116.9 1.2 collective-permute-start
  118.1 1.7 collective-permute-start.1
  119.9 0.8 copy.25.table_ref
  120.7 1.0 slice_bitcast_fusion.2
  121.7 0.2 copy.27
  122.0 0.1 reshape.65
  122.1 0.7 reshape.64.small
  122.8 0.6 stack.51.info
  123.4 11.6 %project.1 = (bf16[1024,768]{1,0:T(8,128)(2,1)}, bf16[2048,768]{1,0:T(8,128)(2,1)}, bf16[2048,768]{1,0:T(8,128)(2,1)}) custom-call(s32[5]{0:T(128)} %stack.51.info, bf16[4,512,768]{2,1,0:T(8,128)(2,1)} %copy-done.2, f32[12,768]{1,0:T(8,128)} %reshape.64.small, bf16[8,320,768]{2,1,0:T(8,128)(2,1)} %copy-done.12, bf16[8,320,768]{2,1,0:T(8,128)(2,1)} %copy-done.12, ...), custom_call_target="tpu_custom_call" | custom-call | flops 6000000000 | bytes 16777216 | tf_op jit(solution)/shard_map/project/pallas_call | solution.py:375
  135.0 28.8 %attend.1 = (bf16[1024,768]{1,0:T(8,128)(2,1)}, f32[3,16,256]{2,1,0:T(8,128)}) custom-call(s32[1]{0:T(128)} %bitcast.half_ref, s32[12,30,3]{2,1,0:T(8,128)} %copy.25.table_ref, bf16[1024,768]{1,0:T(8,128)(2,1)} %get-tuple-element.50.q_ref, bf16[2048,768]{1,0:T(8,128)(2,1)} %get-tuple-element.51.k_ref, bf16[2048,768]{1,0:T(8,128)(2,1)} %get-tuple-element.52.v_ref), custom_call_target="tpu_custom_call" | custom-call | flops 60000002048 | bytes 12582912 | tf_op jit(solution)/shard_map/attend/pallas_call | solution.py:168
  163.8 0.1 select_reduce_fusion.3
  164.0 1.3 pad_maximum_fusion.1.cot_ref
  165.2 28.4 %front.1 = (bf16[2,512,768]{2,1,0:T(8,128)(2,1)}, f32[1024,768]{1,0:T(8,128)}, f32[1024,128]{1,0:T(8,128)}, bf16[1024,768]{1,0:T(8,128)(2,1)}, bf16[768,1024]{1,...) custom-call(s32[5]{0:T(128)} %stack.51.info, ...), custom_call_target="tpu_custom_call" | custom-call | flops 11000000512 | bytes 41943040 | tf_op jit(solution)/shard_map/front/pallas_call | solution.py:375
  193.7 2.6 slice_bitcast_fusion.1
  196.3 0.3 collective-permute-start.2
  196.6 7.6 %collective-permute-start.3 = (bf16[512,768]{1,0:T(8,128)(2,1)}, bf16[512,768]{1,0:T(8,128)(2,1)}, u32[]{:S(2)}, u32[]{:S(2)}) collective-permute-start(bf16[512,768]{1,0:T(8,128)(2,1)} %get-tuple-element.98), channel_id=1, source_target_pairs={{0,0},{4,1},{2,2},{6,3},{1,4},{5,5},{3,6},{7,7},{8,8},{12,9},{10,1... | collective-permute-start | bytes 2359304 | tf_op jit(solution)/shard_map/ppermute | solution.py:1556
  204.3 45.3 %back.1 = (bf16[9,96,768]{2,1,0:T(8,128)(2,1)}, bf16[9,96,768]{2,1,0:T(8,128)(2,1)}, bf16[9,96,768]{2,1,0:T(8,128)(2,1)}, bf16[9,96,768]{2,1,0:T(8,128)(2,1)}, f...) custom-call(f32[1024,768]{1,0:T(8,128)} %get-tuple-element.58.gh2_ref, ...), custom_call_target="tpu_custom_call" | custom-call | flops 22000001024 | bytes 41943040 | tf_op jit(solution)/shard_map/back/pallas_call | solution.py:1032
  249.6 0.7 slice.64
  250.3 0.7 slice.63
  251.0 1.8 collective-permute-start.4
  252.8 0.1 collective-permute-start.5
  252.9 1.7 collective-permute-start.6
  254.6 0.6 select_maximum_fusion.small_ref
  255.3 1.5 select_bitcast_fusion.1
  256.7 1.9 maximum_convert_fusion
  258.6 39.4 %attend_back.1 = (bf16[1024,768]{1,0:T(8,128)(2,1)}, bf16[2048,768]{1,0:T(8,128)(2,1)}, bf16[2048,768]{1,0:T(8,128)(2,1)}) custom-call(s32[1]{0:T(128)} %bitcast.half_ref, s32[12,30,3]{2,1,0:T(8,128)} %copy.25.table_ref, bf16[1024,768]{1,0:T(8,128)(2,1)} %get-tuple-element.50.q_ref, bf16[2048,768]{1,0:T(8,128)(2,1)} %get-tuple-element.51.k_ref, ...), custom_call_target="tpu_custom_call" | custom-call | flops 120000004096 | bytes 25165824 | tf_op jit(solution)/shard_map/attend_back/pallas_call | solution.py:307
  298.0 51.5 %late.1 = (bf16[2,512,768]{2,1,0:T(8,128)(2,1)}, bf16[3,96,768]{2,1,0:T(8,128)(2,1)}, bf16[16,768]{1,0:T(8,128)(2,1)}) custom-call(bf16[4,512,768]{2,1,0:T(8,128)(2,1)} %copy-done.2, bf16[1024,768]{1,0:T(8,128)(2,1)} %get-tuple-element.69.dq_hbm, bf16[2048,768]{1,0:T(8,128)(2,1)} %get-tuple-element.70.dk_hbm, bf16[2048,768]{1,0:T(8,128)(2,1)} %get-tuple-element.71.dv_hbm, ...), custom_call_target="tpu_custom_call" | custom-call | flops 12000000000 | bytes 31457280 | tf_op jit(solution)/shard_map/late/pallas_call | solution.py:1332
  349.5 1.5 broadcast_select_fusion.1
  351.0 0.0 copy-start.1
  351.0 1.9 maximum_convert_fusion.1
  352.9 0.6 copy-done.3
  353.5 0.4 copy-done.4
  354.0 0.3 copy-done.5
  354.2 0.1 copy-done.11
  354.3 55.8 %owner.1 = (f32[3,96,768]{2,1,0:T(8,128)S(1)}, f32[3,96,768]{2,1,0:T(8,128)S(1)}, f32[3,96,768]{2,1,0:T(8,128)S(1)}, f32[16,768]{1,0:T(8,128)S(1)}) custom-call(s32[12]{0:T(128)S(1)} %broadcast_add_fusion.holder, bf16[9,96,768]{2,1,0:T(8,128)(2,1)S(1)} %copy-done.3, bf16[9,96,768]{2,1,0:T(8,128)(2,1)S(1)} %collective-permute-done.4.x_ref, ...), custom_call_target="tpu_custom_call" | custom-call | bytes 12582912 | tf_op jit(solution)/shard_map/owner/pallas_call | solution.py:1453
  410.2 0.9 copy-done.6
  411.1 0.9 copy-done.8
  412.0 0.9 copy-done.10
  412.9 0.7 multiply_subtract_fusion
  413.6 2.2 copy.31
  415.8 0.9 copy.32
  416.7 0.9 copy.33
  (42 shorter events, 0.1 us)
Async XLA Ops:
  2.9 2.8 copy-start.15
  8.1 1.2 copy-start
  8.3 1.5 copy-start.14
  9.7 110.1 %copy-start.16 = (s32[12,30,3]{1,2,0:T(4,128)S(1)}, s32[12,30,3]{1,2,0:T(4,128)}, u32[]{:S(2)}) copy-start(s32[12,30,3]{1,2,0:T(4,128)} %param.13) | copy-start | bytes 12964
  113.3 1.7 copy-start.2
  115.0 2.0 copy-start.12
  116.9 47.0 %collective-permute-start = (bf16[512,768]{1,0:T(8,128)(2,1)S(1)}, bf16[512,768]{1,0:T(8,128)(2,1)S(1)}, u32[]{:S(2)}, u32[]{:S(2)}) collective-permute-start(bf16[512,768]{1,0:T(8,128)(2,1)S(1)} %get-tuple-element.54), channel_id=1, source_target_pairs={{0,0},{1,4},{2,2},{3,6},{4,1},{5,5},{6,3},{7,7},{8,8},{9,12},{10,1... | collective-permute-start | bytes 2359304 | tf_op jit(solution)/shard_map/ppermute | solution.py:1549
  118.1 45.8 %collective-permute-start.1 = (bf16[512,768]{1,0:T(8,128)(2,1)S(1)}, bf16[512,768]{1,0:T(8,128)(2,1)S(1)}, u32[]{:S(2)}, u32[]{:S(2)}) collective-permute-start(bf16[512,768]{1,0:T(8,128)(2,1)S(1)} %get-tuple-element.55), channel_id=1, source_target_pairs={{0,2},{1,6},{2,0},{3,4},{4,3},{5,7},{6,1},{7,5},{8,10},{9,14},{10,... | collective-permute-start | bytes 2359304 | tf_op jit(solution)/shard_map/ppermute | solution.py:1549
  135.0 28.8 %copy-start.21 = (s32[12]{0:T(128)S(1)}, s32[12]{0:T(128)}, u32[]{:S(2)}) copy-start(s32[12]{0:T(128)} %constant.71) | copy-start | bytes 148
  196.3 59.0 %collective-permute-start.2 = (bf16[512,768]{1,0:T(8,128)(2,1)}, bf16[512,768]{1,0:T(8,128)(2,1)}, u32[]{:S(2)}, u32[]{:S(2)}) collective-permute-start(bf16[512,768]{1,0:T(8,128)(2,1)} %get-tuple-element.97), channel_id=1, source_target_pairs={{2,0},{6,1},{0,2},{4,3},{3,4},{7,5},{1,6},{5,7},{10,8},{14,9},{8,1... | collective-permute-start | bytes 2359304 | tf_op jit(solution)/shard_map/ppermute | solution.py:1556
  196.6 58.6 %collective-permute-start.3 = (bf16[512,768]{1,0:T(8,128)(2,1)}, bf16[512,768]{1,0:T(8,128)(2,1)}, u32[]{:S(2)}, u32[]{:S(2)}) collective-permute-start(bf16[512,768]{1,0:T(8,128)(2,1)} %get-tuple-element.98), channel_id=1, source_target_pairs={{0,0},{4,1},{2,2},{6,3},{1,4},{5,5},{3,6},{7,7},{8,8},{12,9},{10,1... | collective-permute-start | bytes 2359304 | tf_op jit(solution)/shard_map/ppermute | solution.py:1556
  204.2 46.8 %copy-start.18 = (f32[8,768]{1,0:T(8,128)S(1)}, f32[8,768]{1,0:T(8,128)}, u32[]{:S(2)}) copy-start(f32[8,768]{1,0:T(8,128)} %get-tuple-element.74) | copy-start | bytes 73732
  251.0 101.9 %collective-permute-start.4 = (bf16[9,96,768]{2,1,0:T(8,128)(2,1)}, bf16[9,96,768]{2,1,0:T(8,128)(2,1)S(1)}, u32[]{:S(2)}, u32[]{:S(2)}) collective-permute-start(bf16[9,96,768]{2,1,0:T(8,128)(2,1)} %get-tuple-element.77), channel_id=1, source_target_pairs={{0,2},{1,3},{2,0},{3,1},{4,6},{5,7},{6,4},{7,5},{8,10},{9,11},{10,... | collective-permute-start | bytes 3981320 | tf_op jit(solution)/shard_map/ppermute | solution.py:1564
  252.8 100.1 %collective-permute-start.5 = (bf16[9,96,768]{2,1,0:T(8,128)(2,1)}, bf16[9,96,768]{2,1,0:T(8,128)(2,1)S(1)}, u32[]{:S(2)}, u32[]{:S(2)}) collective-permute-start(bf16[9,96,768]{2,1,0:T(8,128)(2,1)} %get-tuple-element.78), channel_id=1, source_target_pairs={{0,4},{1,5},{2,6},{3,7},{4,0},{5,1},{6,2},{7,3},{8,12},{9,13},{10,... | collective-permute-start | bytes 3981320 | tf_op jit(solution)/shard_map/ppermute | solution.py:1564
  252.9 100.0 %collective-permute-start.6 = (bf16[9,96,768]{2,1,0:T(8,128)(2,1)}, bf16[9,96,768]{2,1,0:T(8,128)(2,1)S(1)}, u32[]{:S(2)}, u32[]{:S(2)}) collective-permute-start(bf16[9,96,768]{2,1,0:T(8,128)(2,1)} %get-tuple-element.79), channel_id=1, source_target_pairs={{0,6},{1,7},{2,4},{3,5},{4,2},{5,3},{6,0},{7,1},{8,14},{9,15},{10,... | collective-permute-start | bytes 3981320 | tf_op jit(solution)/shard_map/ppermute | solution.py:1564
  351.0 2.0 copy-start.1
  351.0 2.5 copy-start.3
  351.0 3.0 copy-start.4
  351.0 3.2 copy-start.5
  351.0 3.3 copy-start.11
  351.0 3.3 copy-start.13
  354.3 58.6 %copy-start.17 = (f32[288]{0:T(512)S(1)}, f32[288]{0:T(512)}, u32[]{:S(2)}) copy-start(f32[288]{0:T(512)} %param.18) | copy-start | bytes 3460
  354.3 58.6 %copy-start.19 = (f32[288]{0:T(512)S(1)}, f32[288]{0:T(512)}, u32[]{:S(2)}) copy-start(f32[288]{0:T(512)} %param.19) | copy-start | bytes 3460
  354.3 58.6 %copy-start.20 = (f32[288]{0:T(512)S(1)}, f32[288]{0:T(512)}, u32[]{:S(2)}) copy-start(f32[288]{0:T(512)} %param.20) | copy-start | bytes 3460
  410.1 0.9 copy-start.6
  411.1 0.9 copy-start.8
  412.0 0.9 copy-start.10
  412.9 2.9 copy-start.9
  413.6 3.1 copy-start.7

commit v6 on v5

--- a/solution.py
+++ b/solution.py
@@ -885,6 +885,7 @@
     up_w,
     down_w,
     wo,
+    layer_ref,
     own_ref,
     x_ref,
     y_ref,
@@ -892,12 +893,16 @@
     gh1_ref,
     dctx_ref,
     sums_ref,
+    home_ref,
     gy,
     gu,
     grads,
     arrived,
     send_sem,
     recv_sem,
+    h_s,
+    h_r,
+    keep_sem,
 ):
     z, c, t = place_of()
     step = pl.program_id(0)
@@ -905,16 +910,43 @@
     tiles = tokens // TILE
     rows = own_ref.shape[1]
     others = n_tp - 1
+    side, core, bit = t // 2, lax.rem(t, 2), lax.rem(c, 2)
 
     def beside(dt):
         return (z, c, lax.rem(t + dt, n_tp))
+
+    stays = c // 2 == core
+    keep_layer = pltpu.make_async_copy(layer_ref.at[0], home_ref.at[bit], keep_sem.at[0])
+    layer_moves = [
+        send(
+            layer_ref.at[p],
+            home_ref.at[bit],
+            (h_s, h_r),
+            p,
+            (z, 2 * core + (p ^ bit), 2 * side + c // 2),
+        )
+        for p in range(2)
+    ]
 
     @pl.when(step == 0)
     def start():
         barrier = pltpu.get_barrier_semaphore()
-        for dt in range(1, n_tp):
-            pl.semaphore_signal(barrier, inc=1, device_id=beside(dt), device_id_type=MESH)
-        pl.semaphore_wait(barrier, others)
+        friends = [beside(dt) for dt in range(1, n_tp)]
+        friends += [(z, c ^ m, t) for m in range(1, n_ctx)]
+        friends += [(z, c ^ m, t ^ 1) for m in range(1, n_ctx)]
+        for friend in friends:
+            pl.semaphore_signal(barrier, inc=1, device_id=friend, device_id_type=MESH)
+        pl.semaphore_wait(barrier, len(friends))
+
+        @pl.when(stays)
+        def kept():
+            keep_layer.start()
+
+        @pl.when(jnp.logical_not(stays))
+        def left():
+            layer_moves[0].start()
+
+        layer_moves[1].start()
         sums_ref[...] = jnp.zeros_like(sums_ref)
         gy[...] = gh2_ref[...]
 
@@ -1005,8 +1037,18 @@
         lax.fori_loop(0, tiles, two, 0)
         keep(4, 1)
 
-
-def back(gh2, hid, gel, fit, gmt, n1, r1, ctx, small, rest, n_ctx, n_tp):
+        @pl.when(stays)
+        def done():
+            keep_layer.wait()
+
+        @pl.when(jnp.logical_not(stays))
+        def gone():
+            layer_moves[0].wait()
+
+        layer_moves[1].wait()
+
+
+def back(gh2, hid, gel, fit, gmt, n1, r1, ctx, small, rest, layer, n_ctx, n_tp):
     tokens, width = gh2.shape
     rows = rest.shape[2]
     dma = pltpu.SemaphoreType.DMA
@@ -1046,18 +1088,21 @@
             held(1),
             held(5),
             held(0, True),
+            pl.BlockSpec(memory_space=pl.ANY),
         ],
         out_specs=[
             *[out((9, rows, width))] * 4,
             out((tokens, width)),
             out((tokens, width)),
             out((8, width)),
+            pl.BlockSpec(memory_space=pl.ANY),
         ],
         out_shape=[
             *[bf16_of(9, rows, width)] * 4,
             f32_of(tokens, width),
             bf16_of(tokens, width),
             f32_of(8, width),
+            bf16_of(*layer.shape),
         ],
         scratch_shapes=[
             pltpu.VMEM((tokens, width), jnp.float32),
@@ -1066,6 +1111,9 @@
             pltpu.VMEM((5, n_tp - 1, n_ctx, 2, rows, width), jnp.bfloat16),
             dma((5 * (n_tp - 1),)),
             dma((5 * (n_tp - 1),)),
+            dma((2,)),
+            dma((2,)),
+            dma((1,)),
         ],
         compiler_params=pltpu.CompilerParams(
             collective_id=3, has_side_effects=True, vmem_limit_bytes=62 << 20
@@ -1073,28 +1121,58 @@
         cost_estimate=pl.CostEstimate(
             flops=22_000_000_000, bytes_accessed=40 << 20, transcendentals=0
         ),
-    )(gh2, hid, gel, fit, gmt, n1, r1, ctx, small, rest, rest, rest)
-
-
-def late_kernel(
+    )(gh2, hid, gel, fit, gmt, n1, r1, ctx, small, rest, rest, rest, layer)
+
+
+LATE = 3
+EARLY = 9
+
+
+def adam_update(weight, first, second, grad, decay, rate):
+    count = float(STEP)
+    first_new = beta_one * first + (1.0 - beta_one) * grad
+    second_new = beta_two * second + (1.0 - beta_two) * grad * grad
+    first_hat = first_new / (1.0 - beta_one**count)
+    second_hat = second_new / (1.0 - beta_two**count)
+    weight_new = weight - rate * (first_hat / (jnp.sqrt(second_hat) + adam_eps) + decay * weight)
+    return (weight_new, first_new, second_new)
+
+
+def finish_kernel(
+    n_shard,
     n_ctx,
     n_tp,
+    holder,
+    late_at,
     x_hbm,
     dq_hbm,
     dk_hbm,
     dv_hbm,
     gh1_hbm,
     first_hbm,
+    e0_hbm,
+    e1_hbm,
+    e2_hbm,
+    e3_hbm,
     small_ref,
+    w_ref,
+    one_ref,
+    two_ref,
     home_ref,
-    rows_ref,
-    total_ref,
+    w_out,
+    one_out,
+    two_out,
+    small_out,
     x_s,
     dq_s,
     dk_s,
     dv_s,
     gh1_s,
     first_s,
+    early,
+    every,
+    packed,
+    slot_met,
     flipped,
     grads,
     arrived,
@@ -1105,7 +1183,13 @@
     back_s,
     small_s,
     small_t,
+    small_m,
     small_p,
+    flat,
+    flat_met,
+    flat_sum,
+    mine_s,
+    pool,
     in_sem,
     c_s,
     c_r,
@@ -1119,17 +1203,23 @@
     sc_r,
     sp_s,
     sp_r,
+    e_s,
+    e_r,
+    a_s,
+    a_r,
+    b_s,
+    b_r,
     keep_sem,
 ):
     z, c, t = place_of()
     side, core, bit = t // 2, lax.rem(t, 2), lax.rem(c, 2)
     _, mid, width = x_s.shape
     tokens = 2 * mid
-    rows = rows_ref.shape[1]
-    groups = n_ctx * n_tp
-    per = groups // 2
+    held, rows, _ = w_ref.shape
+    per = n_ctx * n_tp // 2
     band = width // 2
     tile = mid // 2
+    piece = mine_s.shape[0]
 
     loads = [
         pltpu.make_async_copy(src, dst, in_sem.at[i])
@@ -1141,11 +1231,18 @@
                 (dq_hbm, dq_s),
                 (first_hbm, first_s),
                 (gh1_hbm, gh1_s),
+                (e0_hbm, early.at[0]),
+                (e1_hbm, early.at[1]),
+                (e2_hbm, early.at[2]),
+                (e3_hbm, early.at[3]),
             )
         )
     ]
-    for load in loads:
-        load.start()
+    for i in (6, 7, 8, 9, 0, 1, 2, 3, 4, 5):
+        loads[i].start()
+
+    def far(dz):
+        return (lax.rem(z + dz, n_shard), c, t)
 
     def across(mask):
         return (z, c ^ mask, t)
@@ -1154,12 +1251,26 @@
         return (z, c, lax.rem(t + dt, n_tp))
 
     barrier = pltpu.get_barrier_semaphore()
-    friends = [(z, c ^ m, t) for m in range(1, n_ctx)]
+    friends = [far(dz) for dz in range(1, n_shard)]
+    friends += [(z, c ^ m, t) for m in range(1, n_ctx)]
     friends += [beside(dt) for dt in range(1, n_tp)]
     friends += [(z, c ^ m, t ^ 1) for m in range(1, n_ctx)]
     for friend in friends:
         pl.semaphore_signal(barrier, inc=1, device_id=friend, device_id_type=MESH)
+
+    for i in range(6, 10):
+        loads[i].wait()
+    every[0:EARLY] = early[0] + early[1] + early[2] + early[3]
+    every[EARLY] = jnp.zeros_like(every[EARLY])
+    for s in range(n_shard * held):
+        packed[s // held, s % held] = every[holder[s]]
     pl.semaphore_wait(barrier, len(friends))
+    slot_moves = [
+        send(packed.at[far(dz)[0]], slot_met.at[dz - 1], (e_s, e_r), dz - 1, far(dz))
+        for dz in range(1, n_shard)
+    ]
+    for copy in slot_moves:
+        copy.start()
 
     core_moves = []
 
@@ -1171,7 +1282,7 @@
                     grads.at[k * n_tp + other, m],
                     arrived.at[dt - 1, k, m],
                     (c_s, c_r),
-                    ((dt - 1) * n_ctx + k) * 3 + m,
+                    ((dt - 1) * n_ctx + k) * LATE + m,
                     beside(dt),
                 )
                 copy.start()
@@ -1190,18 +1301,16 @@
             partial[k, m] = value
         for j in range(1, n_ctx):
             copy = send(
-                partial.at[c ^ j, m], met.at[j - 1, m], (p_s, p_r), (j - 1) * 3 + m, across(j)
+                partial.at[c ^ j, m], met.at[j - 1, m], (p_s, p_r), (j - 1) * LATE + m, across(j)
             )
             copy.start()
             plane_moves.append(copy)
 
     loads[0].wait()
     for a in range(4):
-        own = 1 if a < 2 else 0
-        chunk = 2 * (core if own else 1 - core) + ((a % 2) ^ bit)
+        chunk = 2 * (core if a < 2 else 1 - core) + ((a % 2) ^ bit)
         flipped[:, pl.ds(pl.multiple_of(chunk * mid, mid), mid)] = x_s[a].T
 
-    mine = pl.ds(pl.multiple_of(core * tokens, tokens), tokens)
     def weight_grad(m, left_at, right):
         def one(i, carry):
             left = flipped[pl.ds(pl.multiple_of(i * band, band), band), left_at]
@@ -1219,7 +1328,7 @@
     exchange(2)
     meet(1)
     loads[3].wait()
-    weight_grad(0, mine, dq_s)
+    weight_grad(0, pl.ds(pl.multiple_of(core * tokens, tokens), tokens), dq_s)
     exchange(0)
     meet(2)
 
@@ -1248,15 +1357,16 @@
         copy = send(over.at[b], more.at[b], (o_s, o_r), b, (z, c, t ^ 1))
         copy.start()
         over_moves.append(copy)
-
-    meet(0)
+        if b == 0:
+            meet(0)
+
     value = small_s[...]
     for dt, copy in enumerate(small_core):
         copy.wait_recv()
         value = value + small_t[dt]
-    total_ref[...] = value
+    small_m[...] = value
     small_plane = [
-        send(total_ref, small_p.at[j - 1], (sp_s, sp_r), j - 1, across(j)) for j in range(1, n_ctx)
+        send(small_m, small_p.at[j - 1], (sp_s, sp_r), j - 1, across(j)) for j in range(1, n_ctx)
     ]
     for copy in small_plane:
         copy.start()
@@ -1266,6 +1376,7 @@
     home_moves = []
     for copy in over_moves:
         copy.wait_recv()
+    keep = pltpu.make_async_copy(back_s.at[0], home_ref.at[bit], keep_sem.at[0])
     for move in range(2):
         chunk = move ^ bit
         for i in range(2):
@@ -1278,9 +1389,8 @@
             value = value + wide_dot(dv_s[at, :], wv, NT)
             back_s[move, i * tile : (i + 1) * tile, :] = value.astype(jnp.bfloat16)
         target = (z, 2 * core + chunk, 2 * side + c // 2)
-        home_moves.append(send(back_s.at[move], home_ref.at[move], (h_s, h_r), move, target))
+        home_moves.append(send(back_s.at[move], home_ref.at[bit], (h_s, h_r), move, target))
         if move == 0:
-            keep = pltpu.make_async_copy(back_s.at[0], home_ref.at[0], keep_sem.at[0])
 
             @pl.when(stays)
             def kept():
@@ -1293,18 +1403,59 @@
         else:
             home_moves[1].start()
 
+    flat[...] = jnp.zeros_like(flat)
     for copy in plane_moves:
         copy.wait_recv()
-    for m in range(3):
+    for m in range(LATE):
         value = partial[c, m]
         for j in range(n_ctx - 1):
             value = value + met[j, m]
-        rows_ref[m] = value
-    value = total_ref[...]
+        flat[m * rows : (m + 1) * rows, :] = value
+    value = small_m[...]
     for j, copy in enumerate(small_plane):
-        copy.wait()
+        copy.wait_recv()
         value = value + small_p[j]
-    total_ref[...] = value
+    small_rows = small_s.shape[0]
+    flat[LATE * rows : LATE * rows + small_rows, :] = value
+
+    def piece_at(k):
+        return pl.ds(pl.multiple_of(k * piece, piece), piece)
+
+    flat_out = [
+        send(flat.at[piece_at(far(dz)[0])], flat_met.at[dz - 1], (a_s, a_r), dz - 1, far(dz))
+        for dz in range(1, n_shard)
+    ]
+    for copy in flat_out:
+        copy.start()
+    total = flat[piece_at(z), :].astype(jnp.float32)
+    for dz, copy in enumerate(flat_out):
+        copy.wait_recv()
+        total = total + flat_met[dz].astype(jnp.float32)
+    mine_s[...] = total.astype(jnp.bfloat16)
+    flat_back = [
+        send(mine_s, flat_sum.at[piece_at(z)], (b_s, b_r), dz - 1, far(dz))
+        for dz in range(1, n_shard)
+    ]
+    for copy in flat_back:
+        copy.start()
+    flat_sum[piece_at(z), :] = mine_s[...]
+    for copy in slot_moves:
+        copy.wait_recv()
+    for copy in flat_back:
+        copy.wait_recv()
+    for m in range(LATE):
+        pool[m] = flat_sum[m * rows : (m + 1) * rows, :]
+    pool[LATE] = jnp.zeros_like(pool[LATE])
+    for j in range(held):
+        grad = packed[z, j].astype(jnp.float32)
+        for dz in range(n_shard - 1):
+            grad = grad + slot_met[dz, j].astype(jnp.float32)
+        grad = grad + pool[late_at[z * held + j]].astype(jnp.float32)
+        w, one, two = adam_update(w_ref[j], one_ref[j], two_ref[j], grad, 0.01, rate_value)
+        w_out[j] = w
+        one_out[j] = one
+        two_out[j] = two
+    small_out[...] = flat_sum[LATE * rows : LATE * rows + small_rows, :].astype(jnp.float32)
 
     @pl.when(stays)
     def done():
@@ -1317,157 +1468,97 @@
     home_moves[1].wait()
     for _, copy in core_moves:
         copy.wait_send()
-    for copy in (*plane_moves, *over_moves, *small_core):
+    for copy in (
+        *plane_moves,
+        *over_moves,
+        *small_core,
+        *small_plane,
+        *slot_moves,
+        *flat_out,
+        *flat_back,
+    ):
         copy.wait_send()
 
 
-def late(x_all, dq, dk, dv, gh1, first, small, rows, n_ctx, n_tp):
+def finish(
+    holder,
+    late_at,
+    x_all,
+    dq,
+    dk,
+    dv,
+    gh1,
+    first,
+    early,
+    small,
+    master,
+    one,
+    two,
+    n_shard,
+    n_ctx,
+    n_tp,
+):
     _, mid, width = x_all.shape
+    held, rows, _ = master.shape
     groups = n_ctx * n_tp
+    span = 16 * n_shard
+    long = -(-(LATE * rows + small.shape[0]) // span) * span
+    smem = pl.BlockSpec(memory_space=pltpu.SMEM)
     anywhere = pl.BlockSpec(memory_space=pl.ANY)
     vmem = pl.BlockSpec(memory_space=pltpu.VMEM)
     dma = pltpu.SemaphoreType.DMA
     low = jnp.bfloat16
-    pairs = [3 * n_ctx * (n_tp - 1), 3 * (n_ctx - 1), 2, 2, n_tp - 1, n_ctx - 1]
+    pairs = [LATE * n_ctx * (n_tp - 1), LATE * (n_ctx - 1), 2, 2, n_tp - 1, n_ctx - 1]
+    pairs += [n_shard - 1] * 3
+    stored = f32_of(held, rows, width)
+    shapes = [
+        x_all.shape,
+        dq.shape,
+        dk.shape,
+        dv.shape,
+        None,
+        first.shape,
+        (4, EARLY, rows, width),
+        (EARLY + 1, rows, width),
+        (n_shard, held, rows, width),
+        (n_shard - 1, held, rows, width),
+        (width, 4 * mid),
+        (groups, LATE, rows, width),
+        (n_tp - 1, n_ctx, LATE, rows, width),
+        (n_ctx, LATE, rows, width),
+        (n_ctx - 1, LATE, rows, width),
+        (2, mid, width),
+        (2, mid, width),
+        (2, mid, width),
+        small.shape,
+        (n_tp - 1, *small.shape),
+        small.shape,
+        (n_ctx - 1, *small.shape),
+        (long, width),
+        (n_shard - 1, long // n_shard, width),
+        (long, width),
+        (long // n_shard, width),
+        (LATE + 1, rows, width),
+    ]
     return pl.pallas_call(
-        functools.partial(late_kernel, n_ctx, n_tp),
-        name="late",
-        in_specs=[anywhere] * 6 + [vmem],
-        out_specs=[anywhere, vmem, vmem],
-        out_shape=[
-            bf16_of(2, mid, width),
-            bf16_of(3, rows, width),
-            bf16_of(*small.shape),
-        ],
+        functools.partial(finish_kernel, n_shard, n_ctx, n_tp),
+        name="finish",
+        in_specs=[smem] * 2 + [anywhere] * 10 + [vmem] * 4,
+        out_specs=[anywhere] + [vmem] * 4,
+        out_shape=[bf16_of(2, mid, width), stored, stored, stored, f32_of(*small.shape)],
         scratch_shapes=[
-            pltpu.VMEM(x_all.shape, low),
-            pltpu.VMEM(dq.shape, low),
-            pltpu.VMEM(dk.shape, low),
-            pltpu.VMEM(dv.shape, low),
-            pltpu.VMEM(gh1.shape, jnp.float32),
-            pltpu.VMEM(first.shape, low),
-            pltpu.VMEM((width, 4 * mid), low),
-            pltpu.VMEM((groups, 3, rows, width), low),
-            pltpu.VMEM((n_tp - 1, n_ctx, 3, rows, width), low),
-            pltpu.VMEM((n_ctx, 3, rows, width), low),
-            pltpu.VMEM((n_ctx - 1, 3, rows, width), low),
-            pltpu.VMEM((2, mid, width), low),
-            pltpu.VMEM((2, mid, width), low),
-            pltpu.VMEM((2, mid, width), low),
-            pltpu.VMEM(small.shape, low),
-            pltpu.VMEM((n_tp - 1, *small.shape), low),
-            pltpu.VMEM((n_ctx - 1, *small.shape), low),
-            dma((6,)),
-            *[dma((n,)) for n in pairs for _ in range(2)],
-            dma((1,)),
-        ],
+            pltpu.VMEM(s, low) if s else pltpu.VMEM(gh1.shape, jnp.float32) for s in shapes
+        ]
+        + [dma((10,))]
+        + [dma((n,)) for n in pairs for _ in range(2)]
+        + [dma((1,))],
         compiler_params=pltpu.CompilerParams(
-            collective_id=1, has_side_effects=True, vmem_limit_bytes=60 << 20
+            collective_id=1, has_side_effects=True, vmem_limit_bytes=63 << 20
         ),
         cost_estimate=pl.CostEstimate(
-            flops=12_000_000_000, bytes_accessed=30 << 20, transcendentals=0
+            flops=12_000_000_000, bytes_accessed=40 << 20, transcendentals=0
         ),
-    )(x_all, dq, dk, dv, gh1, first, small)
-
-
-def adam_update(weight, first, second, grad, decay, rate):
-    count = float(STEP)
-    first_new = beta_one * first + (1.0 - beta_one) * grad
-    second_new = beta_two * second + (1.0 - beta_two) * grad * grad
-    first_hat = first_new / (1.0 - beta_one**count)
-    second_hat = second_new / (1.0 - beta_two**count)
-    weight_new = weight - rate * (first_hat / (jnp.sqrt(second_hat) + adam_eps) + decay * weight)
-    return (weight_new, first_new, second_new)
-
-
-def owner_kernel(
-    n_shard,
-    holder,
-    own_ref,
-    x_ref,
-    y_ref,
-    xy_ref,
-    late_ref,
-    small_ref,
-    w_ref,
-    one_ref,
-    two_ref,
-    w_out,
-    one_out,
-    two_out,
-    small_out,
-    every,
-    packed,
-    met,
-    small_met,
-    z_s,
-    z_r,
-    s_s,
-    s_r,
-):
-    z, c, t = place_of()
-    held = w_ref.shape[0]
-
-    def far(dz):
-        return (lax.rem(z + dz, n_shard), c, t)
-
-    barrier = pltpu.get_barrier_semaphore()
-    for dz in range(1, n_shard):
-        pl.semaphore_signal(barrier, inc=1, device_id=far(dz), device_id_type=MESH)
-    every[0:3] = late_ref[...]
-    every[3:12] = own_ref[...] + x_ref[...] + y_ref[...] + xy_ref[...]
-    every[12] = jnp.zeros_like(every[12])
-    for s in range(n_shard * held):
-        packed[s // held, s % held] = every[holder[s]]
-    pl.semaphore_wait(barrier, n_shard - 1)
-    moves = [
-        send(packed.at[far(dz)[0]], met.at[dz - 1], (z_s, z_r), dz - 1, far(dz))
-        for dz in range(1, n_shard)
-    ]
-    moves += [
-        send(small_ref, small_met.at[dz - 1], (s_s, s_r), dz - 1, far(dz))
-        for dz in range(1, n_shard)
-    ]
-    for copy in moves:
-        copy.start()
-    for copy in moves:
-        copy.wait()
-    for j in range(held):
-        grad = packed[z, j].astype(jnp.float32)
-        for dz in range(n_shard - 1):
-            grad = grad + met[dz, j].astype(jnp.float32)
-        w, one, two = adam_update(w_ref[j], one_ref[j], two_ref[j], grad, 0.01, rate_value)
-        w_out[j] = w
-        one_out[j] = one
-        two_out[j] = two
-    total = small_ref[...].astype(jnp.float32)
-    for dz in range(n_shard - 1):
-        total = total + small_met[dz].astype(jnp.float32)
-    small_out[...] = total
-
-
-def owner(holder, early, late_rows, small, master, one, two, n_shard):
-    held, rows, width = master.shape
-    vmem = pl.BlockSpec(memory_space=pltpu.VMEM)
-    dma = pltpu.SemaphoreType.DMA
-    return pl.pallas_call(
-        functools.partial(owner_kernel, n_shard),
-        name="owner",
-        in_specs=[pl.BlockSpec(memory_space=pltpu.SMEM)] + [vmem] * 9,
-        out_specs=[vmem] * 4,
-        out_shape=[f32_of(held, rows, width)] * 3 + [f32_of(*small.shape)],
-        scratch_shapes=[
-            pltpu.VMEM((13, rows, width), jnp.bfloat16),
-            pltpu.VMEM((n_shard, held, rows, width), jnp.bfloat16),
-            pltpu.VMEM((n_shard - 1, held, rows, width), jnp.bfloat16),
-            pltpu.VMEM((n_shard - 1, *small.shape), jnp.bfloat16),
-            *[dma((n_shard - 1,)) for _ in range(4)],
-        ],
-        compiler_params=pltpu.CompilerParams(
-            collective_id=2, has_side_effects=True, vmem_limit_bytes=40 << 20
-        ),
-        cost_estimate=pl.CostEstimate(flops=0, bytes_accessed=12 << 20, transcendentals=0),
-    )(holder, *early, late_rows, small, master, one, two)
+    )(holder, late_at, x_all, dq, dk, dv, gh1, first, *early, small, master, one, two)
 
 
 def moves(n_ctx, n_tp, pick):
@@ -1505,8 +1596,6 @@
     half = lax.rem(my_tp, 2)
     plane = ("ctx", "tp")
     forth = [moves(n_ctx, n_tp, pick) for pick in range(2)]
-    home = [[(b, a) for a, b in pairs] for pairs in forth]
-    swap = [(t, t ^ 1) for t in range(n_tp)]
 
     arrival = [(b ^ parity) + 2 * (half ^ (j // 2)) for j, b in enumerate((0, 1, 0, 1))]
     info = jnp.stack([half, *arrival]).astype(jnp.int32)
@@ -1515,13 +1604,6 @@
     def sent(field, pick):
         low = field.astype(jnp.bfloat16)
         return jnp.where(parity == 0, low[pick], low[1 - pick])
-
-    def returned(first, second):
-        swapped = parity == 1
-        out = jnp.stack(
-            [jnp.where(swapped, second, first), jnp.where(swapped, first, second)]
-        )
-        return out.astype(jnp.float32)
 
     low = master.astype(jnp.bfloat16)
     my_shard = lax.axis_index("shard")
@@ -1553,33 +1635,44 @@
     out_low, n1, r1, fi, fit, hid, gel, gh2, gmt, sums_two = front(
         info, context, x_all, cot, small, rest
     )
-    layer_out = returned(*[lax.ppermute(out_low[p], plane, home[p]) for p in range(2)])
-    *early, gh1, dctx, sums_one = back(
-        gh2, hid, gel, fit, gmt, n1, r1, context, small, rest, n_ctx, n_tp
+    *early, gh1, dctx, sums_one, layer_home = back(
+        gh2, hid, gel, fit, gmt, n1, r1, context, small, rest, out_low, n_ctx, n_tp
     )
     for j in range(1, n_ctx):
         crossing = [
             (a * n_tp + b, (a ^ j) * n_tp + b) for a in range(n_ctx) for b in range(n_tp)
         ]
         early[j] = lax.ppermute(early[j], plane, crossing)
-    layer_out, dctx = lax.optimization_barrier((layer_out, dctx))
     dq, dk, dv = attend_back(half_one, rand_blocks, q, k, v, lse, dctx, 5)
     small_rows = jnp.pad(
         jnp.concatenate([sums_one[4:7], sums_one[0:4], sums_two[0:3]]), ((2, 4), (0, 0))
     )
-    came, late_rows, small_late = late(
-        x_all, dq, dk, dv, gh1, first, small_rows, rows, n_ctx, n_tp
+    stands = jnp.array([8, 0, 2, 4, 6, 1, 3, 5, 7], jnp.int32)
+    slots_all = jnp.arange(n_shard * held, dtype=jnp.int32)
+    hits = slot_of[None, :] == slots_all[:, None]
+    holder = EARLY + jnp.sum(jnp.where(hits[:, LATE:], stands[None, :] - EARLY, 0), axis=1)
+    ranks = jnp.arange(LATE, dtype=jnp.int32)[None, :]
+    late_at = LATE + jnp.sum(jnp.where(hits[:, :LATE], ranks - LATE, 0), axis=1)
+    came, master_new, first_new, second_new, small_sum = finish(
+        holder.astype(jnp.int32),
+        late_at.astype(jnp.int32),
+        x_all,
+        dq,
+        dk,
+        dv,
+        gh1,
+        first,
+        early,
+        small_rows,
+        master,
+        moment_one,
+        moment_two,
+        n_shard,
+        n_ctx,
+        n_tp,
     )
-    input_grad = returned(came[0], came[1])
-
-    stands = jnp.array([0, 1, 2, 11, 3, 5, 7, 9, 4, 6, 8, 10], jnp.int32)
-    slots_all = jnp.arange(n_shard * held, dtype=jnp.int32)
-    holder = 12 + jnp.sum(
-        jnp.where(slot_of[None, :] == slots_all[:, None], stands[None, :] - 12, 0), axis=1
-    )
-    master_new, first_new, second_new, small_sum = owner(
-        holder.astype(jnp.int32), early, late_rows, small_late, master, moment_one, moment_two, n_shard
-    )
+    layer_out = layer_home.astype(jnp.float32)
+    input_grad = came.astype(jnp.float32)
     start = ((my_shard * n_ctx + my_ctx) * n_tp + my_tp) * span
     small_owned = lax.dynamic_slice_in_dim(small_sum.reshape(-1), start, span)
     small_new, small_first, small_second = adam_update(

time: 421 us -> 396 us (0.941)
  Pallas kernels: 364 us -> 343 us
  waiting for transfers between devices: 0.02 us -> 14.8 us
  local copies, waits for them, and re-layouts: 22.6 us -> 13.9 us
  starting transfers between devices: 14.4 us -> 6.18 us
    pallas_call x2 -> x1, Pallas kernels: 107 us -> 81.6 us  [finish(): pl.pallas_call(functools.partial(finish_kernel, n_shard, n_ctx, n_tp), na...]
    ppermute x3, waiting for transfers between devices: 0.01 us -> 14.8 us  [shards(): early[j] = lax.ppermute(early[j], plane, crossing)]
    ppermute x2 -> x0, starting transfers between devices: 7.94 us -> none  [shards(): lax.ppermute(out_low[p], plane, home[p])]
    unnamed x50 -> x38, local copies, waits for them, and re-layouts: 15.6 us -> 10.1 us
  transfers between devices with their start and end apart: 7 -> 5, of which waited for: 0 -> 1; matrix products, arithmetic and copies ran while one was open for 3% -> 2% of each run, Pallas kernels for 42% -> 20%
where the time goes in v6:
time: 396 us; the launch traced here: 394 us
  Pallas kernels  343 us (87%)
  waiting for transfers between devices  14.8 us (4%)
  other arithmetic  14.5 us (4%)
  local copies, waits for them, and re-layouts  13.9 us (4%)
  starting transfers between devices  6.18 us (2%)
    pallas_call x1, Pallas kernels, bring(): pl.pallas_call(functools.partial(bring_kernel, n_shard, n_ctx, n_tp), nam...  103 us
    pallas_call x1, Pallas kernels, finish(): pl.pallas_call(functools.partial(finish_kernel, n_shard, n_ctx, n_tp), na...  81.6 us
    pallas_call x1, Pallas kernels, back(): pl.pallas_call(functools.partial(back_kernel, n_ctx, n_tp), name='back',...  49.4 us
    pallas_call x2, Pallas kernels, call(): pl.pallas_call(kernel, name=name, grid_spec=pltpu.PrefetchScalarGridSpec(...  40.1 us
    pallas_call x1, Pallas kernels, attend_back(): pl.pallas_call(functools.partial(attend_back_kernel, unroll), grid_spec=s...  39.5 us
    pallas_call x1, Pallas kernels, attend(): pl.pallas_call(functools.partial(attend_kernel, unroll), grid_spec=spec,...  28.8 us
    ppermute x3, waiting for transfers between devices, shards(): early[j] = lax.ppermute(early[j], plane, crossing)  14.8 us
    unnamed x38, local copies, waits for them, and re-layouts  10.1 us
  transfers between devices with their start and end apart: 5, of which 1 were waited for; matrix products, arithmetic and copies ran while one was open for 2% of the time, Pallas kernels for 20%

profile of v6, /device:TPU:0, one launch (start us, length us, event | category | flops | bytes accessed | tf_op | source)
XLA Modules:
  0.0 393.7 jit_solution(1214041988042073369)
XLA Ops:
  0.7 1.4 fusion.6
  2.0 0.8 select_convert_fusion
  2.8 0.1 select_n.66
  2.9 0.1 reshape.66
  2.9 0.0 copy-start.3
  3.0 2.2 convert_element_type.45
  5.2 0.6 copy-done.3
  5.8 0.2 convert_element_type.40
  5.9 0.1 broadcast_select_fusion.1
  6.1 0.1 select_bitcast_fusion
  6.2 0.7 fusion.4
  6.8 1.3 fusion.2
  8.1 0.0 copy-start.5
  8.2 0.1 pad_maximum_fusion.xs_ref
  8.3 0.0 copy-start.2
  8.3 1.0 copy-done.5
  9.3 0.4 select_reduce_fusion.2
  9.7 0.0 copy-start.9
  9.8 0.0 copy-done.2
  9.8 103.5 %bring.1 = (bf16[4,512,768]{2,1,0:T(8,128)(2,1)S(1)}, bf16[8,320,768]{2,1,0:T(8,128)(2,1)S(1)}, bf16[8,9,96,768]{3,2,1,0:T(8,128)(2,1)}) custom-call(s32[12]{0:T(128)S(1)} %copy-done.2, bf16[320,768]{1,0:T(8,128)(2,1)S(1)} %pad_maximum_fusion.2.part_ref, bf16[3,96,768]{2,1,0:T(8,128)(2,1)S(1)} %get-tuple-element.86.low_ref, ...), custom_call_target="tpu_custom_call" | custom-call | bytes 41943040 | tf_op jit(solution)/shard_map/bring/pallas_call | solution.py:842
  113.3 0.0 copy-start
  113.3 1.7 copy-done
  115.0 1.9 copy-done.1
  116.9 0.9 collective-permute-start
  117.8 1.7 collective-permute-start.1
  119.5 0.0 copy-done.9
  119.5 0.8 copy.25.table_ref
  120.4 1.0 slice_bitcast_fusion
  121.4 0.2 copy.29
  121.6 0.1 reshape.70
  121.7 0.7 reshape.69.small
  122.5 0.6 stack.37.info
  123.1 11.7 %project.1 = (bf16[1024,768]{1,0:T(8,128)(2,1)}, bf16[2048,768]{1,0:T(8,128)(2,1)}, bf16[2048,768]{1,0:T(8,128)(2,1)}) custom-call(s32[5]{0:T(128)} %stack.37.info, bf16[4,512,768]{2,1,0:T(8,128)(2,1)} %copy-done, f32[12,768]{1,0:T(8,128)} %reshape.69.small, bf16[8,320,768]{2,1,0:T(8,128)(2,1)} %copy-done.1, bf16[8,320,768]{2,1,0:T(8,128)(2,1)} %copy-done.1, ...), custom_call_target="tpu_custom_call" | custom-call | flops 6000000000 | bytes 16777216 | tf_op jit(solution)/shard_map/project/pallas_call | solution.py:375
  134.8 28.8 %attend.1 = (bf16[1024,768]{1,0:T(8,128)(2,1)}, f32[3,16,256]{2,1,0:T(8,128)}) custom-call(s32[1]{0:T(128)} %bitcast.half_ref, s32[12,30,3]{2,1,0:T(8,128)} %copy.25.table_ref, bf16[1024,768]{1,0:T(8,128)(2,1)} %get-tuple-element.47.q_ref, bf16[2048,768]{1,0:T(8,128)(2,1)} %get-tuple-element.48.k_ref, bf16[2048,768]{1,0:T(8,128)(2,1)} %get-tuple-element.49.v_ref), custom_call_target="tpu_custom_call" | custom-call | flops 60000002048 | bytes 12582912 | tf_op jit(solution)/shard_map/attend/pallas_call | solution.py:168
  163.5 0.1 iota_compare_fusion.2
  163.6 0.1 select_reduce_fusion.4
  163.7 0.0 copy-done.15
  163.7 0.1 select_reduce_fusion.3
  163.8 0.5 broadcast_add_fusion
  164.3 0.0 collective-permute-done
  164.3 0.0 collective-permute-done.1
  164.3 1.3 pad_maximum_fusion.1.cot_ref
  165.6 28.4 %front.1 = (bf16[2,512,768]{2,1,0:T(8,128)(2,1)}, f32[1024,768]{1,0:T(8,128)}, f32[1024,128]{1,0:T(8,128)}, bf16[1024,768]{1,0:T(8,128)(2,1)}, bf16[768,1024]{1,...) custom-call(s32[5]{0:T(128)} %stack.37.info, ...), custom_call_target="tpu_custom_call" | custom-call | flops 11000000512 | bytes 41943040 | tf_op jit(solution)/shard_map/front/pallas_call | solution.py:375
  194.0 49.4 %back.1 = (bf16[9,96,768]{2,1,0:T(8,128)(2,1)}, bf16[9,96,768]{2,1,0:T(8,128)(2,1)}, bf16[9,96,768]{2,1,0:T(8,128)(2,1)}, bf16[9,96,768]{2,1,0:T(8,128)(2,1)}, f...) custom-call(f32[1024,768]{1,0:T(8,128)} %get-tuple-element.54.gh2_ref, ...), custom_call_target="tpu_custom_call" | custom-call | flops 22000001024 | bytes 41943040 | tf_op jit(solution)/shard_map/back/pallas_call | solution.py:1074
  243.4 0.6 collective-permute-start.2
  244.1 0.8 collective-permute-start.3
  244.9 2.1 collective-permute-start.4
  247.0 39.5 %attend_back.1 = (bf16[1024,768]{1,0:T(8,128)(2,1)}, bf16[2048,768]{1,0:T(8,128)(2,1)}, bf16[2048,768]{1,0:T(8,128)(2,1)}) custom-call(s32[1]{0:T(128)} %bitcast.half_ref, s32[12,30,3]{2,1,0:T(8,128)} %copy.25.table_ref, bf16[1024,768]{1,0:T(8,128)(2,1)} %get-tuple-element.47.q_ref, bf16[2048,768]{1,0:T(8,128)(2,1)} %get-tuple-element.48.k_ref, ...), custom_call_target="tpu_custom_call" | custom-call | flops 120000004096 | bytes 25165824 | tf_op jit(solution)/shard_map/attend_back/pallas_call | solution.py:307
  286.5 0.0 copy-done.10
  286.5 0.0 copy-done.12
  286.6 0.0 copy-done.4
  286.6 1.9 convert_element_type.50
  288.5 0.6 select_maximum_fusion.small_ref
  289.1 0.0 collective-permute-done.2.e1_hbm
  289.1 14.8 %collective-permute-done.3.e2_hbm = bf16[9,96,768]{2,1,0:T(8,128)(2,1)} collective-permute-done((bf16[9,96,768]{2,1,0:T(8,128)(2,1)}, bf16[9,96,768]{2,1,0:T(8,128)(2,1)}, u32[]{:S(2)}, u32[]{:S(2)}) %collective-permute-start.3) | collective-permute-done | bytes 1327136 | tf_op jit(solution)/shard_map/ppermute | solution.py:1645
  303.9 0.0 collective-permute-done.4.e3_hbm
  303.9 81.6 %finish.1 = (bf16[2,512,768]{2,1,0:T(8,128)(2,1)}, f32[3,96,768]{2,1,0:T(8,128)}, f32[3,96,768]{2,1,0:T(8,128)}, f32[3,96,768]{2,1,0:T(8,128)}, f32[16,768]{1,0:T(8,128)}) custom-call(s32[12]{0:T(128)} %get-tuple-element.97.holder, s32[12]{0:T(128)} %get-tuple-element.96.late_at, bf16[4,512,768]{2,1,0:T(8,128)(2,1)} %copy-done, ...), custom_call_target="tpu_custom_call" | custom-call | flops 12000000000 | bytes 41943040 | tf_op jit(solution)/shard_map/finish/pallas_call | solution.py:1543
  385.6 0.8 reshape.68
  386.4 3.4 convert_element_type.51
  389.8 0.0 copy-done.14
  389.8 0.7 multiply_subtract_fusion
  390.5 0.9 copy.33
  391.4 0.9 copy.34
  392.3 0.9 copy.35
  (25 shorter events, 0.1 us)
Async XLA Ops:
  2.9 2.8 copy-start.3
  8.1 1.2 copy-start.5
  8.3 1.5 copy-start.2
  9.7 109.8 %copy-start.9 = (s32[12,30,3]{1,2,0:T(4,128)S(1)}, s32[12,30,3]{1,2,0:T(4,128)}, u32[]{:S(2)}) copy-start(s32[12,30,3]{1,2,0:T(4,128)} %param.13) | copy-start | bytes 12964
  113.3 1.7 copy-start
  115.0 1.9 copy-start.1
  116.9 47.4 %collective-permute-start = (bf16[512,768]{1,0:T(8,128)(2,1)S(1)}, bf16[512,768]{1,0:T(8,128)(2,1)S(1)}, u32[]{:S(2)}, u32[]{:S(2)}) collective-permute-start(bf16[512,768]{1,0:T(8,128)(2,1)S(1)} %get-tuple-element.51), channel_id=1, source_target_pairs={{0,0},{1,4},{2,2},{3,6},{4,1},{5,5},{6,3},{7,7},{8,8},{9,12},{10,1... | collective-permute-start | bytes 2359304 | tf_op jit(solution)/shard_map/ppermute | solution.py:1631
  117.8 46.5 %collective-permute-start.1 = (bf16[512,768]{1,0:T(8,128)(2,1)S(1)}, bf16[512,768]{1,0:T(8,128)(2,1)S(1)}, u32[]{:S(2)}, u32[]{:S(2)}) collective-permute-start(bf16[512,768]{1,0:T(8,128)(2,1)S(1)} %get-tuple-element.52), channel_id=1, source_target_pairs={{0,2},{1,6},{2,0},{3,4},{4,3},{5,7},{6,1},{7,5},{8,10},{9,14},{10,... | collective-permute-start | bytes 2359304 | tf_op jit(solution)/shard_map/ppermute | solution.py:1631
  134.8 28.9 %copy-start.15 = (s32[9]{0:T(128)S(1)}, s32[9]{0:T(128)}, u32[]{:S(2)}) copy-start(s32[9]{0:T(128)} %constant.75) | copy-start | bytes 112
  243.4 45.7 %collective-permute-start.2 = (bf16[9,96,768]{2,1,0:T(8,128)(2,1)}, bf16[9,96,768]{2,1,0:T(8,128)(2,1)}, u32[]{:S(2)}, u32[]{:S(2)}) collective-permute-start(bf16[9,96,768]{2,1,0:T(8,128)(2,1)} %get-tuple-element.70), channel_id=1, source_target_pairs={{0,2},{1,3},{2,0},{3,1},{4,6},{5,7},{6,4},{7,5},{8,10},{9,11},{10,... | collective-permute-start | bytes 3981320 | tf_op jit(solution)/shard_map/ppermute | solution.py:1645
  244.1 59.9 %collective-permute-start.3 = (bf16[9,96,768]{2,1,0:T(8,128)(2,1)}, bf16[9,96,768]{2,1,0:T(8,128)(2,1)}, u32[]{:S(2)}, u32[]{:S(2)}) collective-permute-start(bf16[9,96,768]{2,1,0:T(8,128)(2,1)} %get-tuple-element.71), channel_id=1, source_target_pairs={{0,4},{1,5},{2,6},{3,7},{4,0},{5,1},{6,2},{7,3},{8,12},{9,13},{10,... | collective-permute-start | bytes 3981320 | tf_op jit(solution)/shard_map/ppermute | solution.py:1645
  244.9 59.0 %collective-permute-start.4 = (bf16[9,96,768]{2,1,0:T(8,128)(2,1)}, bf16[9,96,768]{2,1,0:T(8,128)(2,1)}, u32[]{:S(2)}, u32[]{:S(2)}) collective-permute-start(bf16[9,96,768]{2,1,0:T(8,128)(2,1)} %get-tuple-element.72), channel_id=1, source_target_pairs={{0,6},{1,7},{2,4},{3,5},{4,2},{5,3},{6,0},{7,1},{8,14},{9,15},{10,... | collective-permute-start | bytes 3981320 | tf_op jit(solution)/shard_map/ppermute | solution.py:1645
  247.0 39.5 %copy-start.10 = (f32[8,768]{1,0:T(8,128)S(1)}, f32[8,768]{1,0:T(8,128)}, u32[]{:S(2)}) copy-start(f32[8,768]{1,0:T(8,128)} %get-tuple-element.73) | copy-start | bytes 73732
  247.0 39.6 %copy-start.12 = (f32[8,768]{1,0:T(8,128)S(1)}, f32[8,768]{1,0:T(8,128)}, u32[]{:S(2)}) copy-start(f32[8,768]{1,0:T(8,128)} %get-tuple-element.74) | copy-start | bytes 73732
  247.0 39.6 %copy-start.4 = (bf16[2,512,768]{2,1,0:T(8,128)(2,1)S(1)}, bf16[2,512,768]{2,1,0:T(8,128)(2,1)}, u32[]{:S(2)}) copy-start(bf16[2,512,768]{2,1,0:T(8,128)(2,1)} %get-tuple-element.62) | copy-start | bytes 4718596
  386.4 3.4 copy-start.11
  386.4 3.4 copy-start.13
  386.4 3.4 copy-start.14
  386.4 4.1 %copy-start.8 = (f32[3,96,768]{2,1,0:T(8,128)S(1)}, f32[3,96,768]{2,1,0:T(8,128)}, u32[]{:S(2)}) copy-start(f32[3,96,768]{2,1,0:T(8,128)} %get-tuple-element.108) | copy-start | bytes 2654212
  389.8 1.6 copy-start.7
  390.5 1.8 copy-start.6

commit v7 on v6

--- a/solution.py
+++ b/solution.py
@@ -47,15 +47,19 @@
 
 
 def rows_of(ref, index, count=1):
-    return ref[pl.ds(pl.multiple_of(index * BLOCK, BLOCK), count * BLOCK), :]
+    return ref[pl.ds(index, count)].reshape(count * BLOCK, ref.shape[2])
+
+
+def flat_rows(ref, index):
+    return ref[pl.ds(pl.multiple_of(index * BLOCK, BLOCK), BLOCK), :]
 
 
 def picked_rows(ref, picks, low_half):
     halves = []
     for pair in range(PACK // 2):
-        cols = pl.ds(pair * 2 * HEAD, 2 * HEAD)
-        first = ref[pl.ds(pl.multiple_of(picks[2 * pair] * BLOCK, BLOCK), BLOCK), cols]
-        second = ref[pl.ds(pl.multiple_of(picks[2 * pair + 1] * BLOCK, BLOCK), BLOCK), cols]
+        cols = slice(pair * 2 * HEAD, (pair + 1) * 2 * HEAD)
+        first = ref[picks[2 * pair], :, cols]
+        second = ref[picks[2 * pair + 1], :, cols]
         halves.append(jnp.where(low_half, first, second))
     return jnp.concatenate(halves, axis=1)
 
@@ -81,103 +85,6 @@
         ],
         axis=0,
     )
-
-
-def attend_kernel(unroll, half_ref, table_ref, q_ref, k_ref, v_ref, out_ref, lse_ref, kept):
-    half = half_ref[0]
-    group = pl.program_id(0)
-    nblocks = k_ref.shape[0] // BLOCK
-    local = q_ref.shape[0] // BLOCK
-    last = nblocks - 1
-    picks_each = table_ref.shape[2]
-    masks = head_masks(BLOCK)
-    low_half = lax.broadcasted_iota(jnp.int32, (BLOCK, 2 * HEAD), 1) < HEAD
-
-    def middle(step, carry):
-        mine = step + 1 - half
-        block = mine + local * half
-        picks = [
-            [table_ref[group * PACK + h, block - 1, r] for h in range(PACK)]
-            for r in range(picks_each)
-        ]
-        spread = spread_heads(rows_of(q_ref, mine), masks)
-        keys = gathered(k_ref, block, last, picks, low_half)
-        values = gathered(v_ref, block, last, picks, low_half)
-        scores = middle_scores(keys, spread, block, last)
-        top = jnp.max(scores, axis=0, keepdims=True)
-        probs = jnp.exp(scores - top)
-        total = jnp.sum(probs, axis=0, keepdims=True)
-        low = (probs * (1.0 / total)).astype(jnp.bfloat16)
-        full = wide_dot(low, values, ((0,), (0,)))
-        out_ref[pl.ds(pl.multiple_of(mine * BLOCK, BLOCK), BLOCK), :] = own_heads(
-            full, masks
-        ).astype(jnp.bfloat16)
-        lse_ref[0, pl.ds(mine, 1), :] = top + jnp.log(total)
-        return carry
-
-    lax.fori_loop(0, local - 1, middle, 0, unroll=unroll)
-
-    edge = (local - 1) * half
-    spread = spread_heads(rows_of(q_ref, edge), masks)
-    span = 8 * BLOCK
-    chunks = nblocks // 8
-    top = None
-    for c in range(chunks):
-        scores = wide_dot(k_ref[c * span : (c + 1) * span, :], spread, ((1,), (1,)))
-        kept[c * span : (c + 1) * span, :] = scores
-        high = jnp.max(scores, axis=0, keepdims=True)
-        top = high if top is None else jnp.maximum(top, high)
-    total = None
-    for c in range(chunks):
-        probs = jnp.exp(kept[c * span : (c + 1) * span, :] - top)
-        kept[c * span : (c + 1) * span, :] = probs
-        part = jnp.sum(probs, axis=0, keepdims=True)
-        total = part if total is None else total + part
-    scale = 1.0 / total
-    full = None
-    for c in range(chunks):
-        low = (kept[c * span : (c + 1) * span, :] * scale).astype(jnp.bfloat16)
-        part = wide_dot(low, v_ref[c * span : (c + 1) * span, :], ((0,), (0,)))
-        full = part if full is None else full + part
-    out_ref[pl.ds(pl.multiple_of(edge * BLOCK, BLOCK), BLOCK), :] = own_heads(
-        full, masks
-    ).astype(jnp.bfloat16)
-    lse_ref[0, pl.ds(edge, 1), :] = top + jnp.log(total)
-
-
-def attend(half, table, q, k, v, unroll=3):
-    tokens, width = q.shape
-    seq = k.shape[0]
-    lanes = PACK * HEAD
-    groups = width // lanes
-    blocks = tokens // BLOCK
-    spec = pltpu.PrefetchScalarGridSpec(
-        num_scalar_prefetch=2,
-        grid=(groups,),
-        in_specs=[
-            pl.BlockSpec((tokens, lanes), lambda g, *_: (0, g)),
-            pl.BlockSpec((seq, lanes), lambda g, *_: (0, g)),
-            pl.BlockSpec((seq, lanes), lambda g, *_: (0, g)),
-        ],
-        out_specs=[
-            pl.BlockSpec((tokens, lanes), lambda g, *_: (0, g)),
-            pl.BlockSpec((1, blocks, lanes), lambda g, *_: (g, 0, 0)),
-        ],
-        scratch_shapes=[pltpu.VMEM((seq, lanes), jnp.float32)],
-    )
-    return pl.pallas_call(
-        functools.partial(attend_kernel, unroll),
-        grid_spec=spec,
-        out_shape=[
-            jax.ShapeDtypeStruct((tokens, width), jnp.bfloat16),
-            jax.ShapeDtypeStruct((groups, blocks, lanes), jnp.float32),
-        ],
-        name="attend",
-        compiler_params=pltpu.CompilerParams(vmem_limit_bytes=56 << 20),
-        cost_estimate=pl.CostEstimate(
-            flops=60_000_000_000, bytes_accessed=12 << 20, transcendentals=16_000_000
-        ),
-    )(half, table, q, k, v)
 
 
 def attend_back_kernel(
@@ -199,8 +106,8 @@
 ):
     half = half_ref[0]
     group = pl.program_id(0)
-    nblocks = k_ref.shape[0] // BLOCK
-    local = q_ref.shape[0] // BLOCK
+    q_ref, k_ref, v_ref = q_ref.at[0], k_ref.at[0], v_ref.at[0]
+    nblocks, local = k_ref.shape[0], q_ref.shape[0]
     last = nblocks - 1
     picks_each = table_ref.shape[2]
     masks = head_masks(BLOCK)
@@ -210,13 +117,13 @@
 
     edge = (local - 1) * half
     spread = spread_heads(rows_of(q_ref, edge), masks)
-    spread_do = spread_heads(rows_of(do_ref, edge), masks)
+    spread_do = spread_heads(flat_rows(do_ref, edge), masks)
     lse = lse_ref[0, pl.ds(edge, 1), :]
     delta = None
     for c in range(chunks):
         rows = slice(c * span, (c + 1) * span)
-        probs = jnp.exp(wide_dot(k_ref[rows, :], spread, ((1,), (1,))) - lse)
-        gp = wide_dot(v_ref[rows, :], spread_do, ((1,), (1,)))
+        probs = jnp.exp(wide_dot(rows_of(k_ref, c * 8, 8), spread, ((1,), (1,))) - lse)
+        gp = wide_dot(rows_of(v_ref, c * 8, 8), spread_do, ((1,), (1,)))
         kept_p[rows, :] = probs
         kept_g[rows, :] = gp
         part = jnp.sum(probs * gp, axis=0, keepdims=True)
@@ -228,7 +135,7 @@
         ds = (probs * (kept_g[rows, :] - delta)).astype(jnp.bfloat16)
         dv_acc[rows, :] = wide_dot(probs.astype(jnp.bfloat16), spread_do, ((1,), (0,)))
         dk_acc[rows, :] = wide_dot(ds, spread, ((1,), (0,)))
-        part = wide_dot(ds, k_ref[rows, :], ((0,), (0,)))
+        part = wide_dot(ds, rows_of(k_ref, c * 8, 8), ((0,), (0,)))
         full = part if full is None else full + part
     dq_ref[pl.ds(pl.multiple_of(edge * BLOCK, BLOCK), BLOCK), :] = (
         own_heads(full, masks) * 0.125
@@ -261,7 +168,7 @@
             for r in range(picks_each)
         ]
         spread = spread_heads(rows_of(q_ref, mine), masks)
-        spread_do = spread_heads(rows_of(do_ref, mine), masks)
+        spread_do = spread_heads(flat_rows(do_ref, mine), masks)
         keys = gathered(k_ref, block, last, picks, low_half)
         values = gathered(v_ref, block, last, picks, low_half)
         scores = middle_scores(keys, spread, block, last)
@@ -284,10 +191,9 @@
 
 
 def attend_back(half, table, q, k, v, lse, do, unroll=3):
-    tokens, width = q.shape
-    seq = k.shape[0]
-    lanes = PACK * HEAD
-    groups = width // lanes
+    tokens, width = do.shape
+    groups, nblocks, _, lanes = k.shape
+    seq = nblocks * BLOCK
     blocks = tokens // BLOCK
     mine = pl.BlockSpec((tokens, lanes), lambda g, *_: (0, g))
     whole = pl.BlockSpec((seq, lanes), lambda g, *_: (0, g))
@@ -295,9 +201,9 @@
         num_scalar_prefetch=2,
         grid=(groups,),
         in_specs=[
-            mine,
-            whole,
-            whole,
+            pl.BlockSpec((1, blocks, BLOCK, lanes), lambda g, *_: (g, 0, 0, 0)),
+            pl.BlockSpec((1, nblocks, BLOCK, lanes), lambda g, *_: (g, 0, 0, 0)),
+            pl.BlockSpec((1, nblocks, BLOCK, lanes), lambda g, *_: (g, 0, 0, 0)),
             pl.BlockSpec((1, blocks, lanes), lambda g, *_: (g, 0, 0)),
             mine,
         ],
@@ -348,13 +254,6 @@
     ref[row : row + 1, :] += jnp.sum(value, axis=0, keepdims=True)
 
 
-def first_spec(first, rows, which):
-    groups, _, width = first.shape
-    return pl.BlockSpec(
-        (groups, rows, width), lambda step, info: (0, which, 0), pipeline_mode=pl.Buffered(1)
-    )
-
-
 def rest_spec(rest, which, single=True):
     groups, _, rows, width = rest.shape
     mode = pl.Buffered(1) if single else None
@@ -365,10 +264,6 @@
 
 def fixed(shape):
     return pl.BlockSpec(shape, lambda step, info: (0,) * len(shape), pipeline_mode=pl.Buffered(1))
-
-
-def resident(shape):
-    return pl.BlockSpec(shape, lambda step, info: (0,) * len(shape))
 
 
 def call(kernel, name, info, grid, in_specs, out_specs, out_shape, scratch, args, flops, moved):
@@ -403,52 +298,10 @@
 TN = ((0,), (0,))
 
 
-def project_kernel(info, x_ref, small, wq, wk, wv, q_ref, k_ref, v_ref):
-    x = x_ref[0]
-
-    @pl.when(pl.program_id(0) < 2)
-    def own():
-        q = wide_dot(x, matrix(wq), NN) + small[0:1, :]
-        q_ref[...] = q.astype(jnp.bfloat16) * jnp.bfloat16(score_scale)
-
-    k_ref[...] = wide_dot(x, matrix(wk), NN).astype(jnp.bfloat16)
-    v_ref[...] = (wide_dot(x, matrix(wv), NN) + small[1:2, :]).astype(jnp.bfloat16)
-
-
-def project(info, x_all, small, first, rows):
-    _, mid, width = x_all.shape
-
-    def chunk(step, info):
-        return lax.rem(step + 2 * info[0], 4)
-
-    return call(
-        project_kernel,
-        "project",
-        info,
-        4,
-        [
-            pl.BlockSpec((1, mid, width), lambda g, info: (info[1 + chunk(g, info)], 0, 0)),
-            fixed(small.shape),
-            *[first_spec(first, rows, m) for m in range(3)],
-        ],
-        [
-            pl.BlockSpec((mid, width), lambda g, info: (jnp.minimum(g, 1), 0)),
-            pl.BlockSpec((mid, width), lambda g, info: (chunk(g, info), 0)),
-            pl.BlockSpec((mid, width), lambda g, info: (chunk(g, info), 0)),
-        ],
-        [bf16_of(2 * mid, width), bf16_of(4 * mid, width), bf16_of(4 * mid, width)],
-        [],
-        (x_all, small, first, first, first),
-        6_000_000_000,
-        16 << 20,
-    )
-
-
 def front_kernel(
     info,
     ctx_ref,
     x_ref,
-    cot_ref,
     small,
     wo,
     u0,
@@ -462,13 +315,11 @@
     out_ref,
     n1_ref,
     r1_ref,
-    fi_ref,
     fit_ref,
     hid_ref,
     gel_ref,
-    gh2_ref,
-    gmt_ref,
-    sums_ref,
+    n2_ref,
+    r2_ref,
 ):
     attn_out = wide_dot(ctx_ref[...], matrix(wo), NN) + small[2:3, :]
     n1, r1 = normed(x_ref[0].astype(jnp.float32) + attn_out)
@@ -476,7 +327,6 @@
     r1_ref[...] = jnp.broadcast_to(r1, r1_ref.shape)
     after = n1 * small[3:4, :] + small[4:5, :]
     ffn_in = after.astype(jnp.bfloat16)
-    fi_ref[...] = ffn_in
     fit_ref[...] = ffn_in.T
     total = after + small[9:10, :]
     for b, (up_w, down_w) in enumerate(((u0, v0), (u1, v1), (u2, v2), (u3, v3))):
@@ -493,22 +343,11 @@
         total = total + wide_dot(hidden, matrix(down_w), NT)
     n2, r2 = normed(total)
     out_ref[0] = (n2 * small[10:11, :] + small[11:12, :]).astype(jnp.bfloat16)
-    cot = cot_ref[0].astype(jnp.float32)
-    gh2 = norm_back(cot, n2, r2, small[10:11, :])
-    gh2_ref[...] = gh2
-    mixed = gh2.astype(jnp.bfloat16)
-    gmt_ref[...] = mixed.T
-
-    @pl.when(pl.program_id(0) == 0)
-    def clear():
-        sums_ref[...] = jnp.zeros_like(sums_ref)
-
-    add_row(sums_ref, 0, mixed.astype(jnp.float32))
-    add_row(sums_ref, 1, cot * n2)
-    add_row(sums_ref, 2, cot)
-
-
-def front(info, ctx, x_all, cot, small, rest):
+    n2_ref[...] = n2
+    r2_ref[...] = jnp.broadcast_to(r2, r2_ref.shape)
+
+
+def front(info, ctx, x_all, small, rest):
     tokens, width = ctx.shape
     mid = x_all.shape[1]
     per = mid // TILE
@@ -531,7 +370,6 @@
         [
             rows((TILE, width)),
             pl.BlockSpec((1, TILE, width), arrived),
-            pl.BlockSpec((1, TILE, width), arrived),
             fixed(small.shape),
             *specs,
         ],
@@ -539,28 +377,24 @@
             pl.BlockSpec((1, TILE, width), arrived),
             rows((TILE, width)),
             rows((TILE, 128)),
-            rows((TILE, width)),
             flipped,
             wide4,
             wide4,
             rows((TILE, width)),
-            flipped,
-            resident((8, width)),
+            rows((TILE, 128)),
         ],
         [
             bf16_of(2, mid, width),
             f32_of(tokens, width),
             f32_of(tokens, 128),
-            bf16_of(tokens, width),
             bf16_of(width, tokens),
             bf16_of(4, tokens, width),
             bf16_of(4, tokens, width),
             f32_of(tokens, width),
-            bf16_of(width, tokens),
-            f32_of(8, width),
+            f32_of(tokens, 128),
         ],
         [],
-        (ctx, x_all, cot, small, *([rest] * 9)),
+        (ctx, x_all, small, *([rest] * 9)),
         11_000_000_000,
         40 << 20,
     )
@@ -568,6 +402,8 @@
 
 MESH = pl.DeviceIdType.MESH
 KINDS = 3
+CHUNKS = 3
+PER = 3
 
 
 def place_of():
@@ -587,22 +423,44 @@
     )
 
 
-def bring_kernel(
+def begin_kernel(
     n_shard,
     n_ctx,
     n_tp,
     slots,
-    part_ref,
-    low_ref,
-    xs_ref,
+    local_at,
+    table,
+    master_hbm,
+    small_in,
+    input_hbm,
     x_ref,
     first_ref,
     rest_ref,
+    small_ref,
+    q_ref,
+    k_ref,
+    v_ref,
+    ctx_ref,
+    lse_ref,
+    raw,
+    low,
+    given,
+    xs,
+    x_all,
+    part,
     got,
     mine,
     total,
     pool,
     sel,
+    first,
+    weights,
+    small,
+    q_s,
+    k_s,
+    v_s,
+    ctx_s,
+    kept,
     x_s,
     x_r,
     xt_s,
@@ -613,8 +471,8 @@
     zb_r,
     zc_s,
     zc_r,
-    q_s,
-    q_r,
+    qm_s,
+    qm_r,
     qt_s,
     qt_r,
     r_s,
@@ -622,13 +480,24 @@
     rt_s,
     rt_r,
     own_sem,
+    out_sem,
 ):
     z, c, t = place_of()
     side, core, bit = t // 2, lax.rem(t, 2), lax.rem(c, 2)
-    held = low_ref.shape[0]
+    held, rows, width = low.shape[0] - 1, low.shape[1], low.shape[2]
     piece = mine.shape[0]
-    chunks, per = 3, 3
     me = c * n_tp + t
+    _, mid, _ = xs.shape
+    nblocks = 4 * mid // BLOCK
+    local = nblocks // 2
+    lanes = PACK * HEAD
+    groups = width // lanes
+    others = n_tp - 1
+
+    take_raw = pltpu.make_async_copy(master_hbm, raw, own_sem.at[0])
+    take_given = pltpu.make_async_copy(input_hbm, given, own_sem.at[1])
+    take_raw.start()
+    take_given.start()
 
     def far(dz):
         return (lax.rem(z + dz, n_shard), c, t)
@@ -646,26 +515,34 @@
     friends += [(z, c ^ m, t ^ 1) for m in range(1, n_ctx)]
     for friend in friends:
         pl.semaphore_signal(barrier, inc=1, device_id=friend, device_id_type=MESH)
+
+    take_raw.wait()
+    for j in range(held):
+        low[j] = raw[j].astype(jnp.bfloat16)
+    low[held] = jnp.zeros_like(low[held])
+    part[...] = jnp.zeros_like(part)
+    for m in range(KINDS):
+        part[m * rows : (m + 1) * rows, :] = low[local_at[m]]
+    part[KINDS * rows : KINDS * rows + 16, :] = small_in[...].astype(jnp.bfloat16)
     pl.semaphore_wait(barrier, len(friends))
 
-    stays = c // 2 == core
-    goes = [(z, 2 * core + (p ^ bit), 2 * side + c // 2) for p in range(2)]
-    x_moves = [send(xs_ref.at[p], x_ref.at[p], (x_s, x_r), p, goes[p]) for p in range(2)]
-    x_keep = pltpu.make_async_copy(xs_ref.at[0], x_ref.at[0], x_r.at[0])
+    def piece_at(k):
+        return pl.ds(pl.multiple_of(k * piece, piece), piece)
 
     za = [
-        send(
-            part_ref.at[pl.ds(pl.multiple_of(far(dz)[0] * piece, piece), piece)],
-            got.at[dz - 1],
-            (za_s, za_r),
-            dz - 1,
-            far(dz),
-        )
+        send(part.at[piece_at(far(dz)[0])], got.at[dz - 1], (za_s, za_r), dz - 1, far(dz))
         for dz in range(1, n_shard)
     ]
     for copy in za:
         copy.start()
 
+    stays = c // 2 == core
+    goes = [(z, 2 * core + (p ^ bit), 2 * side + c // 2) for p in range(2)]
+    x_moves = [send(xs.at[p], x_all.at[p], (x_s, x_r), p, goes[p]) for p in range(2)]
+    x_keep = pltpu.make_async_copy(xs.at[0], x_all.at[0], own_sem.at[2])
+    take_given.wait()
+    xs[0] = given[bit].astype(jnp.bfloat16)
+
     @pl.when(stays)
     def keep():
         x_keep.start()
@@ -674,50 +551,50 @@
     def leave():
         x_moves[0].start()
 
+    xs[1] = given[1 - bit].astype(jnp.bfloat16)
     x_moves[1].start()
-    summed = part_ref[pl.ds(pl.multiple_of(z * piece, piece), piece), :]
+
+    summed = part[piece_at(z), :]
     for dz, copy in enumerate(za):
         copy.wait_recv()
         summed = summed + got[dz]
     mine[...] = summed
-    here = pl.ds(pl.multiple_of(z * piece, piece), piece)
     zb = [
-        send(mine, total.at[here], (zb_s, zb_r), dz - 1, far(dz)) for dz in range(1, n_shard)
+        send(mine, total.at[piece_at(z)], (zb_s, zb_r), dz - 1, far(dz))
+        for dz in range(1, n_shard)
     ]
     for copy in zb:
         copy.start()
-    total[here, :] = summed
+    total[piece_at(z), :] = summed
     pool_here = pl.ds(z * held, held)
     zc = [
-        send(low_ref, pool.at[pool_here], (zc_s, zc_r), dz - 1, far(dz))
+        send(low.at[0:held], pool.at[pool_here], (zc_s, zc_r), dz - 1, far(dz))
         for dz in range(1, n_shard)
     ]
     for copy in zc:
         copy.start()
-    pool_own = pltpu.make_async_copy(low_ref, pool.at[pool_here], own_sem.at[0])
-    pool_own.start()
+    pool[pool_here] = low[0:held]
     for copy in zb:
         copy.wait_recv()
 
     q_moves = [
-        send(total, first_ref.at[me], (q_s, q_r), k, across(m)) for k, m in enumerate((1, 2, 3))
+        send(total, first.at[me], (qm_s, qm_r), k, across(m)) for k, m in enumerate((1, 2, 3))
     ]
     for copy in q_moves:
         copy.start()
-    first_own = pltpu.make_async_copy(total, first_ref.at[me], own_sem.at[1])
-    first_own.start()
-    qt_own = [
-        send(total, first_ref.at[me], (qt_s, qt_r), dt - 1, beside(dt)) for dt in range(1, n_tp)
+    qt_moves = [
+        send(total, first.at[me], (qt_s, qt_r), dt - 1, beside(dt)) for dt in range(1, n_tp)
     ]
-    for copy in qt_own:
+    for copy in qt_moves:
         copy.start()
+    first[me] = total[...]
 
     x_over = [
-        send(x_ref.at[p], x_ref.at[2 + p], (xt_s, xt_r), p, (z, c, t ^ 1)) for p in range(2)
+        send(x_all.at[p], x_all.at[2 + p], (xt_s, xt_r), p, (z, c, t ^ 1)) for p in range(2)
     ]
 
     @pl.when(stays)
-    def kept():
+    def stayed():
         x_keep.wait()
 
     @pl.when(jnp.logical_not(stays))
@@ -728,156 +605,303 @@
     x_moves[1].wait_recv()
     x_over[1].start()
 
-    qt_on = []
     for k, m in enumerate((1, 2, 3)):
         q_moves[k].wait_recv()
         place = (c ^ m) * n_tp + t
         for dt in range(1, n_tp):
             copy = send(
-                first_ref.at[place],
-                first_ref.at[place],
+                first.at[place],
+                first.at[place],
                 (qt_s, qt_r),
-                (k + 1) * (n_tp - 1) + dt - 1,
+                (k + 1) * others + dt - 1,
                 beside(dt),
             )
             copy.start()
-            qt_on.append(copy)
-
-    for copy in zc:
+            qt_moves.append(copy)
+    for copy in qt_moves:
         copy.wait_recv()
-    pool_own.wait()
-    for m in range(chunks * per):
-        sel[m] = pool[slots[KINDS + m]]
-    rest_own = pltpu.make_async_copy(sel, rest_ref.at[me], own_sem.at[2])
-    rest_own.start()
-    r_moves = []
-    rt_moves = []
-    for k in range(chunks):
-        span = pl.ds(k * per, per)
-        pair = [
+    outs = [pltpu.make_async_copy(first, first_ref, out_sem.at[0])]
+    outs[0].start()
+
+    sums = None
+    for g in range(n_ctx * n_tp):
+        here = first[g, KINDS * rows : KINDS * rows + 16, :].astype(jnp.float32)
+        sums = here if sums is None else sums + here
+    small[...] = sums
+    small_ref[...] = sums
+    for m in range(KINDS):
+        weights[m] = first[:, m * rows : (m + 1) * rows, :].reshape(width, width)
+
+    def split(dst, start, value):
+        low_value = value.astype(jnp.bfloat16)
+        per = TILE // BLOCK
+        for g in range(groups):
+            piece_value = low_value[:, g * lanes : (g + 1) * lanes]
+            dst[g, pl.ds(start, per)] = piece_value.reshape(per, BLOCK, lanes)
+
+    def project(a, chunk, own):
+        def one(i, carry):
+            x = x_all[a, pl.ds(pl.multiple_of(i * TILE, TILE), TILE), :]
+            start = chunk * (mid // BLOCK) + i * (TILE // BLOCK)
+            if own:
+                q_start = (chunk - 2 * core) * (mid // BLOCK) + i * (TILE // BLOCK)
+                q = wide_dot(x, weights[0], NN) + small[0:1, :]
+                split(q_s, q_start, q.astype(jnp.bfloat16) * jnp.bfloat16(score_scale))
+            split(k_s, start, wide_dot(x, weights[1], NN))
+            split(v_s, start, wide_dot(x, weights[2], NN) + small[1:2, :])
+            return carry
+
+        lax.fori_loop(0, mid // TILE, one, 0)
+
+    def own_project(a, carry):
+        project(a, 2 * core + (a ^ bit), True)
+        return carry
+
+    def other_project(a, carry):
+        project(2 + a, 2 * (1 - core) + (a ^ bit), False)
+        return carry
+
+    lax.fori_loop(0, 2, own_project, 0)
+    for copy in x_over:
+        copy.wait_recv()
+    outs.append(pltpu.make_async_copy(x_all, x_ref, out_sem.at[1]))
+    outs[1].start()
+    lax.fori_loop(0, 2, other_project, 0)
+    for i, (src, dst) in enumerate(((q_s, q_ref), (k_s, k_ref), (v_s, v_ref))):
+        outs.append(pltpu.make_async_copy(src, dst, out_sem.at[2 + i]))
+        outs[-1].start()
+
+    def span_of(k):
+        return pl.ds(k * PER, PER)
+
+    rest_own = pltpu.make_async_copy(sel, rest_ref.at[me], own_sem.at[3])
+    direct = [
+        [
             send(
-                sel.at[span],
-                rest_ref.at[me, span],
-                (r_s, r_r),
-                k * 3 + j,
-                across(m),
+                sel.at[span_of(k)], rest_ref.at[me, span_of(k)], (r_s, r_r), k * 3 + j, across(m)
             )
             for j, m in enumerate((1, 2))
         ]
-        for copy in pair:
-            copy.start()
-        r_moves.append(pair)
-        for dt in range(1, n_tp):
-            copy = send(
-                sel.at[span],
-                rest_ref.at[me, span],
-                (rt_s, rt_r),
-                (k * 4) * (n_tp - 1) + dt - 1,
-                beside(dt),
-            )
-            copy.start()
-            rt_moves.append(copy)
-
-    def pass_on(k, which, place):
-        span = pl.ds(k * per, per)
-        for dt in range(1, n_tp):
-            copy = send(
-                rest_ref.at[place, span],
-                rest_ref.at[place, span],
-                (rt_s, rt_r),
-                (k * 4 + which) * (n_tp - 1) + dt - 1,
-                beside(dt),
-            )
-            copy.start()
-            rt_moves.append(copy)
-
+        for k in range(CHUNKS)
+    ]
     onward = []
-    for k in range(chunks):
-        span = pl.ds(k * per, per)
-        for j in range(2):
-            r_moves[k][j].wait_recv()
+    for k in range(CHUNKS):
         odd = lax.rem(core + k, 2)
         source = jnp.where(odd == 0, c ^ 1, c ^ 2) * n_tp + t
         target = (z, jnp.where(odd == 0, c ^ 2, c ^ 1), t)
-        copy = send(
-            rest_ref.at[source, span], rest_ref.at[source, span], (r_s, r_r), k * 3 + 2, target
+        view = rest_ref.at[source, span_of(k)]
+        onward.append(send(view, view, (r_s, r_r), k * 3 + 2, target))
+
+    def passing(k, which):
+        if which == 0:
+            src = sel.at[span_of(k)]
+        else:
+            src = rest_ref.at[(c ^ which) * n_tp + t, span_of(k)]
+        dst = rest_ref.at[(c ^ which) * n_tp + t, span_of(k)]
+        return [
+            send(src, dst, (rt_s, rt_r), (k * 4 + which) * others + dt - 1, beside(dt))
+            for dt in range(1, n_tp)
+        ]
+
+    passed = [[passing(k, which) for which in range(4)] for k in range(CHUNKS)]
+
+    def begin_rest():
+        for copy in zc:
+            copy.wait_recv()
+        for m in range(CHUNKS * PER):
+            sel[m] = pool[slots[KINDS + m]]
+        rest_own.start()
+        for k in range(CHUNKS):
+            for copy in direct[k]:
+                copy.start()
+            for copy in passed[k][0]:
+                copy.start()
+
+    def relay(k):
+        for copy in direct[k]:
+            copy.wait_recv()
+        onward[k].start()
+        for copy in passed[k][1] + passed[k][2]:
+            copy.start()
+
+    def last_relay(k):
+        onward[k].wait_recv()
+        for copy in passed[k][3]:
+            copy.start()
+
+    begin_rest()
+
+    last = nblocks - 1
+    picks_each = table.shape[2]
+    masks = head_masks(BLOCK)
+    low_half = lax.broadcasted_iota(jnp.int32, (BLOCK, 2 * HEAD), 1) < HEAD
+    each = 5
+    subs = (local - 1) // each
+
+    def attend_round(i, carry):
+        g = i // subs
+        sub = lax.rem(i, subs)
+        qg, kg, vg = q_s.at[g], k_s.at[g], v_s.at[g]
+        for k in range(CHUNKS):
+
+            @pl.when(i == 3 + 2 * k)
+            def hook(k=k):
+                relay(k)
+
+        @pl.when(sub == 0)
+        def edge_block():
+            edge = (local - 1) * core
+            spread = spread_heads(rows_of(qg, edge), masks)
+            span = 8 * BLOCK
+            pieces = nblocks // 8
+            top = None
+            for n in range(pieces):
+                scores = wide_dot(rows_of(kg, n * 8, 8), spread, NT)
+                kept[n * span : (n + 1) * span, :] = scores
+                high = jnp.max(scores, axis=0, keepdims=True)
+                top = high if top is None else jnp.maximum(top, high)
+            total_p = None
+            for n in range(pieces):
+                probs = jnp.exp(kept[n * span : (n + 1) * span, :] - top)
+                kept[n * span : (n + 1) * span, :] = probs
+                some = jnp.sum(probs, axis=0, keepdims=True)
+                total_p = some if total_p is None else total_p + some
+            scale = 1.0 / total_p
+            full = None
+            for n in range(pieces):
+                probs = (kept[n * span : (n + 1) * span, :] * scale).astype(jnp.bfloat16)
+                some = wide_dot(probs, rows_of(vg, n * 8, 8), TN)
+                full = some if full is None else full + some
+            at = pl.ds(pl.multiple_of(edge * BLOCK, BLOCK), BLOCK)
+            ctx_s[g, at, :] = own_heads(full, masks).astype(jnp.bfloat16)
+            lse_ref[g, pl.ds(edge, 1), :] = top + jnp.log(total_p)
+
+        for u in range(each):
+            spot = sub * each + u + 1 - core
+            block = spot + local * core
+            picks = [
+                [table[g * PACK + h, block - 1, r] for h in range(PACK)]
+                for r in range(picks_each)
+            ]
+            spread = spread_heads(rows_of(qg, spot), masks)
+            keys = gathered(kg, block, last, picks, low_half)
+            values = gathered(vg, block, last, picks, low_half)
+            scores = middle_scores(keys, spread, block, last)
+            top = jnp.max(scores, axis=0, keepdims=True)
+            probs = jnp.exp(scores - top)
+            total_p = jnp.sum(probs, axis=0, keepdims=True)
+            probs = (probs * (1.0 / total_p)).astype(jnp.bfloat16)
+            full = wide_dot(probs, values, TN)
+            at = pl.ds(pl.multiple_of(spot * BLOCK, BLOCK), BLOCK)
+            ctx_s[g, at, :] = own_heads(full, masks).astype(jnp.bfloat16)
+            lse_ref[g, pl.ds(spot, 1), :] = top + jnp.log(total_p)
+        return carry
+
+    lax.fori_loop(0, groups * subs, attend_round, 0)
+    for g in range(groups):
+        outs.append(
+            pltpu.make_async_copy(
+                ctx_s.at[g], ctx_ref.at[:, g * lanes : (g + 1) * lanes], out_sem.at[5 + g]
+            )
         )
-        copy.start()
-        onward.append(copy)
-        pass_on(k, 1, (c ^ 1) * n_tp + t)
-        pass_on(k, 2, (c ^ 2) * n_tp + t)
-    for k in range(chunks):
-        onward[k].wait_recv()
-        pass_on(k, 3, (c ^ 3) * n_tp + t)
-
-    for copy in x_over:
-        copy.wait()
+        outs[-1].start()
+    for k in range(CHUNKS):
+        last_relay(k)
 
     @pl.when(jnp.logical_not(stays))
     def left():
         x_moves[0].wait_send()
 
     x_moves[1].wait_send()
-    for copy in (*za, *zb, *zc, *q_moves, *onward):
+    for copy in (*x_over, *za, *zb, *zc, *q_moves, *qt_moves, *onward):
         copy.wait_send()
-    for pair in r_moves:
+    for pair in direct:
         for copy in pair:
             copy.wait_send()
-    for copy in (*qt_own, *qt_on, *rt_moves):
+    for chunk in passed:
+        for group in chunk:
+            for copy in group:
+                copy.wait()
+    rest_own.wait()
+    for copy in outs:
         copy.wait()
-    first_own.wait()
-    rest_own.wait()
-
-
-def bring(slots, part, low, xs, n_shard, n_ctx, n_tp):
-    held, rows, width = low.shape
-    total_rows = part.shape[0]
+
+
+def begin(slots, local_at, table, master, small_in, inputs, n_shard, n_ctx, n_tp):
+    held, rows, width = master.shape
+    _, mid, _ = inputs.shape
     groups = n_ctx * n_tp
-    mid = xs.shape[1]
+    long = -(-(KINDS * rows + 16) // (16 * n_shard)) * 16 * n_shard
+    lanes = PACK * HEAD
+    packs = width // lanes
+    tokens, seq = 2 * mid, 4 * mid
     anywhere = pl.BlockSpec(memory_space=pl.ANY)
+    vmem = pl.BlockSpec(memory_space=pltpu.VMEM)
+    smem = pl.BlockSpec(memory_space=pltpu.SMEM)
     dma = pltpu.SemaphoreType.DMA
+    low = jnp.bfloat16
+    f32 = jnp.float32
     pairs = [2, 2, n_shard - 1, n_shard - 1, n_shard - 1, 3]
-    pairs += [4 * (n_tp - 1), 9, 12 * (n_tp - 1)]
-    sems = [dma((n,)) for n in pairs for _ in range(2)]
+    pairs += [4 * (n_tp - 1), 3 * CHUNKS, 4 * CHUNKS * (n_tp - 1)]
     return pl.pallas_call(
-        functools.partial(bring_kernel, n_shard, n_ctx, n_tp),
-        name="bring",
-        in_specs=[
-            pl.BlockSpec(memory_space=pltpu.SMEM),
-            pl.BlockSpec(memory_space=pltpu.VMEM),
-            anywhere,
-            anywhere,
-        ],
-        out_specs=[anywhere, anywhere, anywhere],
+        functools.partial(begin_kernel, n_shard, n_ctx, n_tp),
+        name="begin",
+        in_specs=[smem, smem, smem, anywhere, vmem, anywhere],
+        out_specs=[anywhere, anywhere, anywhere, vmem, anywhere, anywhere, anywhere, anywhere, vmem],
         out_shape=[
-            jax.ShapeDtypeStruct((4, mid, width), jnp.bfloat16),
-            jax.ShapeDtypeStruct((groups, total_rows, width), jnp.bfloat16),
-            jax.ShapeDtypeStruct((groups, 9, rows, width), jnp.bfloat16),
+            bf16_of(4, mid, width),
+            bf16_of(groups, long, width),
+            bf16_of(groups, 9, rows, width),
+            f32_of(16, width),
+            bf16_of(packs, tokens // BLOCK, BLOCK, lanes),
+            bf16_of(packs, seq // BLOCK, BLOCK, lanes),
+            bf16_of(packs, seq // BLOCK, BLOCK, lanes),
+            bf16_of(tokens, width),
+            f32_of(packs, tokens // BLOCK, lanes),
         ],
         scratch_shapes=[
-            pltpu.VMEM((n_shard - 1, total_rows // n_shard, width), jnp.bfloat16),
-            pltpu.VMEM((total_rows // n_shard, width), jnp.bfloat16),
-            pltpu.VMEM((total_rows, width), jnp.bfloat16),
-            pltpu.VMEM((n_shard * held, rows, width), jnp.bfloat16),
-            pltpu.VMEM((9, rows, width), jnp.bfloat16),
-            *sems,
-            dma((3,)),
+            pltpu.VMEM((held, rows, width), f32),
+            pltpu.VMEM((held + 1, rows, width), low),
+            pltpu.VMEM((2, mid, width), f32),
+            pltpu.VMEM((2, mid, width), low),
+            pltpu.VMEM((4, mid, width), low),
+            pltpu.VMEM((long, width), low),
+            pltpu.VMEM((n_shard - 1, long // n_shard, width), low),
+            pltpu.VMEM((long // n_shard, width), low),
+            pltpu.VMEM((long, width), low),
+            pltpu.VMEM((n_shard * held, rows, width), low),
+            pltpu.VMEM((9, rows, width), low),
+            pltpu.VMEM((groups, long, width), low),
+            pltpu.VMEM((3, width, width), low),
+            pltpu.VMEM((16, width), f32),
+            pltpu.VMEM((packs, tokens // BLOCK, BLOCK, lanes), low),
+            pltpu.VMEM((packs, seq // BLOCK, BLOCK, lanes), low),
+            pltpu.VMEM((packs, seq // BLOCK, BLOCK, lanes), low),
+            pltpu.VMEM((packs, tokens, lanes), low),
+            pltpu.VMEM((seq, lanes), f32),
+            *[dma((n,)) for n in pairs for _ in range(2)],
+            dma((4,)),
+            dma((8,)),
         ],
         compiler_params=pltpu.CompilerParams(
-            collective_id=0, has_side_effects=True, vmem_limit_bytes=40 << 20
+            collective_id=0, has_side_effects=True, vmem_limit_bytes=62 << 20
         ),
-        cost_estimate=pl.CostEstimate(flops=0, bytes_accessed=40 << 20, transcendentals=0),
-    )(slots, part, low, xs)
+        cost_estimate=pl.CostEstimate(
+            flops=60_000_000_000, bytes_accessed=60 << 20, transcendentals=16_000_000
+        ),
+    )(slots, local_at, table, master, small_in, inputs)
 
 
 def back_kernel(
     n_ctx,
     n_tp,
-    gh2_ref,
+    n2_hbm,
+    r2_ref,
+    cot0_ref,
+    cot1_ref,
     hid_ref,
     gel_ref,
     fit_ref,
-    gmt_ref,
     n1_ref,
     r1_ref,
     ctx_ref,
@@ -896,6 +920,8 @@
     home_ref,
     gy,
     gu,
+    mixed,
+    mixed_t,
     grads,
     arrived,
     send_sem,
@@ -906,7 +932,7 @@
 ):
     z, c, t = place_of()
     step = pl.program_id(0)
-    tokens, width = gh2_ref.shape
+    tokens, width = gy.shape
     tiles = tokens // TILE
     rows = own_ref.shape[1]
     others = n_tp - 1
@@ -930,6 +956,8 @@
 
     @pl.when(step == 0)
     def start():
+        take = pltpu.make_async_copy(n2_hbm, gy, keep_sem.at[1])
+        take.start()
         barrier = pltpu.get_barrier_semaphore()
         friends = [beside(dt) for dt in range(1, n_tp)]
         friends += [(z, c ^ m, t) for m in range(1, n_ctx)]
@@ -948,7 +976,26 @@
 
         layer_moves[1].start()
         sums_ref[...] = jnp.zeros_like(sums_ref)
-        gy[...] = gh2_ref[...]
+        take.wait()
+        mid = tokens // 2
+        for p, cot_ref in enumerate((cot0_ref, cot1_ref)):
+
+            def one(i, carry, p=p, cot_ref=cot_ref):
+                inside = pl.ds(pl.multiple_of(i * TILE, TILE), TILE)
+                at = pl.ds(pl.multiple_of((p ^ bit) * mid + i * TILE, TILE), TILE)
+                cot = cot_ref[inside, :].astype(jnp.float32)
+                n2 = gy[at, :]
+                add_row(sums_ref, 10, cot * n2)
+                add_row(sums_ref, 11, cot)
+                gh2 = norm_back(cot, n2, r2_ref[at, 0:1], small[10:11, :])
+                gy[at, :] = gh2
+                low = gh2.astype(jnp.bfloat16)
+                mixed[at, :] = low
+                mixed_t[:, at] = low.T
+                add_row(sums_ref, 9, low.astype(jnp.float32))
+                return carry
+
+            lax.fori_loop(0, mid // TILE, one, 0)
 
     def moves(b, count):
         slot = lax.rem(b, 2)
@@ -990,19 +1037,18 @@
 
         def one(i, carry):
             at = pl.ds(pl.multiple_of(i * TILE, TILE), TILE)
-            mixed = gh2_ref[at, :].astype(jnp.bfloat16)
-            grad = wide_dot(mixed, down_block, NN) * gel_ref[0, at, :].astype(jnp.float32)
+            grad = wide_dot(mixed[at, :], down_block, NN) * gel_ref[0, at, :].astype(jnp.float32)
             low = grad.astype(jnp.bfloat16)
             gu[at, :] = low
             gy[at, :] += wide_dot(low, up_block, NT)
-            sums_ref[pl.ds(step, 1), :] += jnp.sum(
+            sums_ref[pl.ds(5 + step, 1), :] += jnp.sum(
                 low.astype(jnp.float32), axis=0, keepdims=True
             )
             return carry
 
         lax.fori_loop(0, tiles, one, 0)
         put(slot, 0, wide_dot(fit_ref[...], gu[...], NN))
-        put(slot, 1, wide_dot(gmt_ref[...], hid_ref[0], NN))
+        put(slot, 1, wide_dot(mixed_t[...], hid_ref[0], NN))
         exchange(step, 2)
 
     @pl.when(step > 0)
@@ -1019,9 +1065,9 @@
             gh1_ref[at, :] = gh1
             low = gh1.astype(jnp.bfloat16)
             gu[at, :] = low
-            add_row(sums_ref, 4, low.astype(jnp.float32))
-            add_row(sums_ref, 5, grad * n1)
-            add_row(sums_ref, 6, grad)
+            add_row(sums_ref, 2, low.astype(jnp.float32))
+            add_row(sums_ref, 3, grad * n1)
+            add_row(sums_ref, 4, grad)
             return carry
 
         lax.fori_loop(0, tiles, one, 0)
@@ -1048,8 +1094,8 @@
         layer_moves[1].wait()
 
 
-def back(gh2, hid, gel, fit, gmt, n1, r1, ctx, small, rest, layer, n_ctx, n_tp):
-    tokens, width = gh2.shape
+def back(n2, r2, cots, hid, gel, fit, n1, r1, ctx, small, rest, layer, n_ctx, n_tp):
+    tokens, width = n2.shape
     rows = rest.shape[2]
     dma = pltpu.SemaphoreType.DMA
 
@@ -1076,10 +1122,12 @@
         name="back",
         grid=(5,),
         in_specs=[
-            whole((tokens, width)),
+            pl.BlockSpec(memory_space=pl.ANY),
+            whole((tokens, 128)),
+            whole((tokens // 2, width)),
+            whole((tokens // 2, width)),
             pl.BlockSpec((1, tokens, width), block),
             pl.BlockSpec((1, tokens, width), block),
-            whole((width, tokens)),
             whole((width, tokens)),
             whole((tokens, width)),
             whole((tokens, 128)),
@@ -1094,26 +1142,28 @@
             *[out((9, rows, width))] * 4,
             out((tokens, width)),
             out((tokens, width)),
-            out((8, width)),
+            out((16, width)),
             pl.BlockSpec(memory_space=pl.ANY),
         ],
         out_shape=[
             *[bf16_of(9, rows, width)] * 4,
             f32_of(tokens, width),
             bf16_of(tokens, width),
-            f32_of(8, width),
+            f32_of(16, width),
             bf16_of(*layer.shape),
         ],
         scratch_shapes=[
             pltpu.VMEM((tokens, width), jnp.float32),
             pltpu.VMEM((tokens, width), jnp.bfloat16),
+            pltpu.VMEM((tokens, width), jnp.bfloat16),
+            pltpu.VMEM((width, tokens), jnp.bfloat16),
             pltpu.VMEM((2, n_ctx, n_tp, 2, rows, width), jnp.bfloat16),
             pltpu.VMEM((5, n_tp - 1, n_ctx, 2, rows, width), jnp.bfloat16),
             dma((5 * (n_tp - 1),)),
             dma((5 * (n_tp - 1),)),
             dma((2,)),
             dma((2,)),
-            dma((1,)),
+            dma((2,)),
         ],
         compiler_params=pltpu.CompilerParams(
             collective_id=3, has_side_effects=True, vmem_limit_bytes=62 << 20
@@ -1121,7 +1171,7 @@
         cost_estimate=pl.CostEstimate(
             flops=22_000_000_000, bytes_accessed=40 << 20, transcendentals=0
         ),
-    )(gh2, hid, gel, fit, gmt, n1, r1, ctx, small, rest, rest, rest, layer)
+    )(n2, r2, *cots, hid, gel, fit, n1, r1, ctx, small, rest, rest, rest, layer)
 
 
 LATE = 3
@@ -1605,38 +1655,23 @@
         low = field.astype(jnp.bfloat16)
         return jnp.where(parity == 0, low[pick], low[1 - pick])
 
-    low = master.astype(jnp.bfloat16)
     my_shard = lax.axis_index("shard")
-    mine = my_shard * held + jnp.arange(held, dtype=jnp.int32)
-    zero = jnp.zeros_like(low)
-    parts = [
-        jnp.sum(jnp.where((slot_of[m] == mine)[:, None, None], low, zero), axis=0, dtype=jnp.float32)
-        for m in range(3)
-    ]
-    spread = (jnp.arange(n_shard) == my_shard)[:, None]
-    small_part = jnp.where(spread, small_params[None, :], 0.0).reshape(-1)
-    used = 3 * rows * width + n_shard * span
-    total_rows = -(-used // (width * 16 * n_shard)) * 16 * n_shard
-    small_part = jnp.pad(small_part, (0, total_rows * width - used)).reshape(-1, width)
-    part = jnp.concatenate([*parts, small_part]).astype(jnp.bfloat16)
-    xs = jnp.stack([sent(inputs, pick) for pick in range(2)])
-    x_all, first, rest = bring(slot_of, part, low, xs, n_shard, n_ctx, n_tp)
-    small = first[:, 3 * rows :, :].reshape(groups, -1)[:, : n_shard * span]
-    small = small.reshape(groups, n_shard, span).transpose(1, 0, 2)
-    small = small.reshape(-1, width).astype(jnp.float32)
-
-    cots, x_all = lax.optimization_barrier(
-        ([sent(cotangent, pick) for pick in range(2)], x_all)
+    start = ((my_shard * n_ctx + my_ctx) * n_tp + my_tp) * span
+    lone = lax.dynamic_update_slice(
+        jnp.zeros((16 * width,), jnp.float32), small_params, (start,)
+    ).reshape(16, width)
+    local_at = slot_of[:LATE] - my_shard * held
+    local_at = jnp.where((local_at >= 0) & (local_at < held), local_at, held)
+    x_all, first, rest, small, q, k, v, context, lse = begin(
+        slot_of, local_at, rand_blocks, master, lone, inputs, n_shard, n_ctx, n_tp
     )
-    cot = jnp.stack([lax.ppermute(cots[pick], plane, forth[pick]) for pick in range(2)])
-
-    q, k, v = project(info, x_all, small, first, rows)
-    context, lse = attend(half_one, rand_blocks, q, k, v, 5)
-    out_low, n1, r1, fi, fit, hid, gel, gh2, gmt, sums_two = front(
-        info, context, x_all, cot, small, rest
+    cots, context = lax.optimization_barrier(
+        ([sent(cotangent, pick) for pick in range(2)], context)
     )
-    *early, gh1, dctx, sums_one, layer_home = back(
-        gh2, hid, gel, fit, gmt, n1, r1, context, small, rest, out_low, n_ctx, n_tp
+    cots = [lax.ppermute(cots[pick], plane, forth[pick]) for pick in range(2)]
+    out_low, n1, r1, fit, hid, gel, n2, r2 = front(info, context, x_all, small, rest)
+    *early, gh1, dctx, sums, layer_home = back(
+        n2, r2, cots, hid, gel, fit, n1, r1, context, small, rest, out_low, n_ctx, n_tp
     )
     for j in range(1, n_ctx):
         crossing = [
@@ -1644,9 +1679,6 @@
         ]
         early[j] = lax.ppermute(early[j], plane, crossing)
     dq, dk, dv = attend_back(half_one, rand_blocks, q, k, v, lse, dctx, 5)
-    small_rows = jnp.pad(
-        jnp.concatenate([sums_one[4:7], sums_one[0:4], sums_two[0:3]]), ((2, 4), (0, 0))
-    )
     stands = jnp.array([8, 0, 2, 4, 6, 1, 3, 5, 7], jnp.int32)
     slots_all = jnp.arange(n_shard * held, dtype=jnp.int32)
     hits = slot_of[None, :] == slots_all[:, None]
@@ -1663,7 +1695,7 @@
         gh1,
         first,
         early,
-        small_rows,
+        sums,
         master,
         moment_one,
         moment_two,
@@ -1673,7 +1705,6 @@
     )
     layer_out = layer_home.astype(jnp.float32)
     input_grad = came.astype(jnp.float32)
-    start = ((my_shard * n_ctx + my_ctx) * n_tp + my_tp) * span
     small_owned = lax.dynamic_slice_in_dim(small_sum.reshape(-1), start, span)
     small_new, small_first, small_second = adam_update(
         small_params, small_one, small_two, small_owned, 0.0, small_rate

time: 396 us -> 356 us (0.90)
  Pallas kernels: 343 us -> 317 us
  local copies, waits for them, and re-layouts: 13.9 us -> 7.37 us
  other arithmetic: 14.5 us -> 9.5 us
    pallas_call x2 -> x1, Pallas kernels: 132 us -> 110 us  [begin(): pl.pallas_call(functools.partial(begin_kernel, n_shard, n_ctx, n_tp), nam...]
    pallas_call x2 -> x1, Pallas kernels: 40.1 us -> 25.8 us  [call(): pl.pallas_call(kernel, name=name, grid_spec=pltpu.PrefetchScalarGridSpec(...]
    pallas_call x1, Pallas kernels: 81.6 us -> 89.2 us  [finish(): pl.pallas_call(functools.partial(finish_kernel, n_shard, n_ctx, n_tp), na...]
    unnamed x38 -> x28, local copies, waits for them, and re-layouts: 10.1 us -> 5.23 us
  transfers between devices with their start and end apart: 5 -> 5, of which waited for: 1 -> 1; matrix products, arithmetic and copies ran while one was open for 2% -> 1% of each run, Pallas kernels for 20% -> 18%
where the time goes in v7:
time: 356 us
  Pallas kernels  317 us (89%)
  waiting for transfers between devices  15.3 us (4%)
  other arithmetic  9.5 us (3%)
  local copies, waits for them, and re-layouts  7.37 us (2%)
  starting transfers between devices  5.88 us (2%)
    pallas_call x1, Pallas kernels, begin(): pl.pallas_call(functools.partial(begin_kernel, n_shard, n_ctx, n_tp), nam...  110 us
    pallas_call x1, Pallas kernels, finish(): pl.pallas_call(functools.partial(finish_kernel, n_shard, n_ctx, n_tp), na...  89.2 us
    pallas_call x1, Pallas kernels, back(): pl.pallas_call(functools.partial(back_kernel, n_ctx, n_tp), name='back',...  51.8 us
    pallas_call x1, Pallas kernels, attend_back(): pl.pallas_call(functools.partial(attend_back_kernel, unroll), grid_spec=s...  39.6 us
    pallas_call x1, Pallas kernels, call(): pl.pallas_call(kernel, name=name, grid_spec=pltpu.PrefetchScalarGridSpec(...  25.8 us
    ppermute x3, waiting for transfers between devices, shards(): early[j] = lax.ppermute(early[j], plane, crossing)  15.3 us
  transfers between devices with their start and end apart: 5, of which 1 were waited for; matrix products, arithmetic and copies ran while one was open for 1% of the time, Pallas kernels for 18%

profile of v7, /device:TPU:0, one launch (start us, length us, event | category | flops | bytes accessed | tf_op | source)
XLA Modules:
  0.0 355.6 jit_solution(8547643668723969442)
XLA Ops:
  0.7 0.9 dynamic_update_slice.3
  1.6 0.6 reshape.34.small_in
  2.2 1.6 copy.21.table.table_ref
  3.8 0.0 copy-start.8
  3.8 2.1 convert_element_type.10
  5.8 0.0 copy-done.8
  5.8 0.5 and_select_fusion.local_at
  6.4 0.1 select_bitcast_fusion
  6.5 0.0 copy-start.9
  6.5 0.0 copy-start.10
  6.5 110.2 %begin.1 = (bf16[4,512,768]{2,1,0:T(8,128)(2,1)}, bf16[8,320,768]{2,1,0:T(8,128)(2,1)}, bf16[8,9,96,768]{3,2,1,0:T(8,128)(2,1)}, f32[16,768]{1,0:T(8,128)}, bf16...) custom-call(s32[12]{0:T(128)} %slots.1, ...), custom_call_target="tpu_custom_call" | custom-call | flops 60000002048 | bytes 62914560 | tf_op jit(solution)/shard_map/begin/pallas_call | solution.py:846
  116.7 0.9 collective-permute-start
  117.6 1.4 collective-permute-start.1
  119.1 0.0 copy-done.9
  119.1 0.1 iota_compare_fusion
  119.2 0.1 select_reduce_fusion.1
  119.2 0.0 copy-done.10
  119.2 0.1 select_reduce_fusion
  119.3 0.6 broadcast_add_fusion
  119.9 0.6 stack.23.info
  120.5 25.8 %front.1 = (bf16[2,512,768]{2,1,0:T(8,128)(2,1)}, f32[1024,768]{1,0:T(8,128)}, f32[1024,128]{1,0:T(8,128)}, bf16[768,1024]{1,0:T(8,128)(2,1)}, bf16[4,1024,768]{...) custom-call(s32[5]{0:T(128)} %stack.23.info, ...), custom_call_target="tpu_custom_call" | custom-call | flops 11000000512 | bytes 41943040 | tf_op jit(solution)/shard_map/front/pallas_call | solution.py:270
  146.4 0.0 collective-permute-done.cot0_ref
  146.4 0.0 copy-start.11
  146.4 0.0 collective-permute-done.1.cot1_ref
  146.4 0.9 copy-done.11
  147.3 51.8 %back.1 = (bf16[9,96,768]{2,1,0:T(8,128)(2,1)}, bf16[9,96,768]{2,1,0:T(8,128)(2,1)}, bf16[9,96,768]{2,1,0:T(8,128)(2,1)}, bf16[9,96,768]{2,1,0:T(8,128)(2,1)}, f...) custom-call(f32[1024,768]{1,0:T(8,128)} %get-tuple-element.49.n2_hbm, ...), custom_call_target="tpu_custom_call" | custom-call | flops 22000001024 | bytes 41943040 | tf_op jit(solution)/shard_map/back/pallas_call | solution.py:1120
  199.1 0.7 collective-permute-start.2
  199.8 0.9 collective-permute-start.3
  200.6 2.0 collective-permute-start.4
  202.6 0.0 copy-start
  202.6 39.6 %attend_back.1 = (bf16[1024,768]{1,0:T(8,128)(2,1)}, bf16[2048,768]{1,0:T(8,128)(2,1)}, bf16[2048,768]{1,0:T(8,128)(2,1)}) custom-call(s32[1]{0:T(128)} %bitcast.half_ref, s32[12,30,3]{2,1,0:T(8,128)} %copy.21.table.table_ref, bf16[3,16,64,256]{3,2,1,0:T(8,128)(2,1)} %get-tuple-element.60.q_ref, bf16[3,32,64,256]{3,2,1,0:T(8,128)(2,1)} %get-tuple-element.61.k_ref, ...), custom_call_target="tpu_custom_call" | custom-call | flops 120000004096 | bytes 25165824 | tf_op jit(solution)/shard_map/attend_back/pallas_call | solution.py:213
  242.2 0.0 copy-done
  242.2 1.9 convert_element_type.11
  244.1 0.0 collective-permute-done.2.e1_hbm
  244.1 15.3 %collective-permute-done.3.e2_hbm = bf16[9,96,768]{2,1,0:T(8,128)(2,1)} collective-permute-done((bf16[9,96,768]{2,1,0:T(8,128)(2,1)}, bf16[9,96,768]{2,1,0:T(8,128)(2,1)}, u32[]{:S(2)}, u32[]{:S(2)}) %collective-permute-start.3) | collective-permute-done | bytes 1327136 | tf_op jit(solution)/shard_map/ppermute | solution.py:1680
  259.4 0.0 collective-permute-done.4.e3_hbm
  259.4 89.2 %finish.1 = (bf16[2,512,768]{2,1,0:T(8,128)(2,1)}, f32[3,96,768]{2,1,0:T(8,128)}, f32[3,96,768]{2,1,0:T(8,128)}, f32[3,96,768]{2,1,0:T(8,128)}, f32[16,768]{1,0:T(8,128)}) custom-call(s32[12]{0:T(128)} %get-tuple-element.86.holder, s32[12]{0:T(128)} %get-tuple-element.85.late_at, bf16[4,512,768]{2,1,0:T(8,128)(2,1)} %get-tuple-element.46.x_ref.x_hbm, ...), custom_call_target="tpu_custom_call" | custom-call | flops 12000000000 | bytes 41943040 | tf_op jit(solution)/shard_map/finish/pallas_call | solution.py:1593
  348.7 0.0 copy-start.4
  348.7 0.0 copy-start.5
  348.7 0.0 copy-start.6
  348.7 0.0 copy-start.7
  348.7 0.0 copy-start.3
  348.7 3.4 convert_element_type.12
  352.1 0.0 copy-start.2
  352.1 0.0 copy-done.4
  352.1 0.0 copy-done.5
  352.1 0.0 copy-done.6
  352.1 0.0 copy-done.7
  352.2 0.7 multiply_subtract_fusion
  352.8 0.0 copy-done.3
  352.8 0.0 copy-start.1
  352.8 0.9 copy.29
  353.8 0.0 copy-done.2
  353.8 0.9 copy.30
  354.7 0.0 copy-done.1
  354.7 0.9 copy.31
  (3 shorter events, 0.0 us)
Async XLA Ops:
  3.8 2.1 copy-start.8
  6.5 112.6 %copy-start.9 = (s32[12]{0:T(128)S(1)}, s32[12]{0:T(128)}, u32[]{:S(2)}) copy-start(s32[12]{0:T(128)} %slots.1) | copy-start | bytes 148
  6.5 112.8 %copy-start.10 = (s32[9]{0:T(128)S(1)}, s32[9]{0:T(128)}, u32[]{:S(2)}) copy-start(s32[9]{0:T(128)} %constant.69) | copy-start | bytes 112
  116.7 29.6 %collective-permute-start = (bf16[512,768]{1,0:T(8,128)(2,1)S(1)}, bf16[512,768]{1,0:T(8,128)(2,1)S(1)}, u32[]{:S(2)}, u32[]{:S(2)}) collective-permute-start(bf16[512,768]{1,0:T(8,128)(2,1)S(1)} %get-tuple-element.51), channel_id=1, source_target_pairs={{0,0},{1,4},{2,2},{3,6},{4,1},{5,5},{6,3},{7,7},{8,8},{9,12},{10,1... | collective-permute-start | bytes 2359304 | tf_op jit(solution)/shard_map/ppermute | solution.py:1671
  117.6 28.8 %collective-permute-start.1 = (bf16[512,768]{1,0:T(8,128)(2,1)S(1)}, bf16[512,768]{1,0:T(8,128)(2,1)}, u32[]{:S(2)}, u32[]{:S(2)}) collective-permute-start(bf16[512,768]{1,0:T(8,128)(2,1)S(1)} %get-tuple-element.52), channel_id=1, source_target_pairs={{0,2},{1,6},{2,0},{3,4},{4,3},{5,7},{6,1},{7,5},{8,10},{9,14},{10,... | collective-permute-start | bytes 2359304 | tf_op jit(solution)/shard_map/ppermute | solution.py:1671
  146.4 0.9 copy-start.11
  199.1 45.1 %collective-permute-start.2 = (bf16[9,96,768]{2,1,0:T(8,128)(2,1)}, bf16[9,96,768]{2,1,0:T(8,128)(2,1)}, u32[]{:S(2)}, u32[]{:S(2)}) collective-permute-start(bf16[9,96,768]{2,1,0:T(8,128)(2,1)} %get-tuple-element.71), channel_id=1, source_target_pairs={{0,2},{1,3},{2,0},{3,1},{4,6},{5,7},{6,4},{7,5},{8,10},{9,11},{10,... | collective-permute-start | bytes 3981320 | tf_op jit(solution)/shard_map/ppermute | solution.py:1680
  199.8 59.6 %collective-permute-start.3 = (bf16[9,96,768]{2,1,0:T(8,128)(2,1)}, bf16[9,96,768]{2,1,0:T(8,128)(2,1)}, u32[]{:S(2)}, u32[]{:S(2)}) collective-permute-start(bf16[9,96,768]{2,1,0:T(8,128)(2,1)} %get-tuple-element.72), channel_id=1, source_target_pairs={{0,4},{1,5},{2,6},{3,7},{4,0},{5,1},{6,2},{7,3},{8,12},{9,13},{10,... | collective-permute-start | bytes 3981320 | tf_op jit(solution)/shard_map/ppermute | solution.py:1680
  200.6 58.8 %collective-permute-start.4 = (bf16[9,96,768]{2,1,0:T(8,128)(2,1)}, bf16[9,96,768]{2,1,0:T(8,128)(2,1)}, u32[]{:S(2)}, u32[]{:S(2)}) collective-permute-start(bf16[9,96,768]{2,1,0:T(8,128)(2,1)} %get-tuple-element.73), channel_id=1, source_target_pairs={{0,6},{1,7},{2,4},{3,5},{4,2},{5,3},{6,0},{7,1},{8,14},{9,15},{10,... | collective-permute-start | bytes 3981320 | tf_op jit(solution)/shard_map/ppermute | solution.py:1680
  202.6 39.6 %copy-start = (bf16[2,512,768]{2,1,0:T(8,128)(2,1)S(1)}, bf16[2,512,768]{2,1,0:T(8,128)(2,1)}, u32[]{:S(2)}) copy-start(bf16[2,512,768]{2,1,0:T(8,128)(2,1)} %get-tuple-element.59) | copy-start | bytes 4718596
  348.7 3.4 copy-start.4
  348.7 3.4 copy-start.5
  348.7 3.4 copy-start.6
  348.7 3.4 copy-start.7
  348.7 4.1 %copy-start.3 = (f32[3,96,768]{2,1,0:T(8,128)S(1)}, f32[3,96,768]{2,1,0:T(8,128)}, u32[]{:S(2)}) copy-start(f32[3,96,768]{2,1,0:T(8,128)} %get-tuple-element.97) | copy-start | bytes 2654212
  352.1 1.6 copy-start.2
  352.8 1.8 copy-start.1

commit v8 on v7

--- a/solution.py
+++ b/solution.py
@@ -471,6 +471,8 @@
     zb_r,
     zc_s,
     zc_r,
+    zd_s,
+    zd_r,
     qm_s,
     qm_r,
     qt_s,
@@ -567,12 +569,44 @@
         copy.start()
     total[piece_at(z), :] = summed
     pool_here = pl.ds(z * held, held)
-    zc = [
-        send(low.at[0:held], pool.at[pool_here], (zc_s, zc_r), dz - 1, far(dz))
-        for dz in range(1, n_shard)
-    ]
-    for copy in zc:
-        copy.start()
+
+    def hop_copy(s, way):
+        sems = (zc_s, zc_r) if way > 0 else (zd_s, zd_r)
+        slot = pl.ds((z - way * (s - 1)) * held, held)
+        return send(
+            pool.at[slot], pool.at[slot], sems, s - 1, (lax.rem(z + way + n_shard, n_shard), c, t)
+        )
+
+    def hop_on(s, way):
+        start = z - way * (s - 1)
+        end = z + way
+        return (start >= 0) & (start < n_shard) & (end >= 0) & (end < n_shard)
+
+    def hop(s):
+        for way in (1, -1):
+
+            @pl.when(hop_on(s, way))
+            def move(way=way):
+                if s > 1:
+                    hop_copy(s - 1, way).wait_recv()
+                hop_copy(s, way).start()
+
+    def hops_end():
+        for way, end in ((1, n_shard - 1), (-1, 0)):
+
+            @pl.when(z == end)
+            def gather(way=way):
+                for s in range(1, n_shard):
+                    hop_copy(s, way).wait_recv()
+
+    def hops_sent():
+        for s in range(1, n_shard):
+            for way in (1, -1):
+
+                @pl.when(hop_on(s, way))
+                def sent(s=s, way=way):
+                    hop_copy(s, way).wait_send()
+
     pool[pool_here] = low[0:held]
     for copy in zb:
         copy.wait_recv()
@@ -582,6 +616,7 @@
     ]
     for copy in q_moves:
         copy.start()
+    hop(1)
     qt_moves = [
         send(total, first.at[me], (qt_s, qt_r), dt - 1, beside(dt)) for dt in range(1, n_tp)
     ]
@@ -618,8 +653,12 @@
             )
             copy.start()
             qt_moves.append(copy)
+        if k == 1:
+            hop(2)
     for copy in qt_moves:
         copy.wait_recv()
+    for s in range(3, n_shard):
+        hop(s)
     outs = [pltpu.make_async_copy(first, first_ref, out_sem.at[0])]
     outs[0].start()
 
@@ -706,8 +745,7 @@
     passed = [[passing(k, which) for which in range(4)] for k in range(CHUNKS)]
 
     def begin_rest():
-        for copy in zc:
-            copy.wait_recv()
+        hops_end()
         for m in range(CHUNKS * PER):
             sel[m] = pool[slots[KINDS + m]]
         rest_own.start()
@@ -813,7 +851,7 @@
         x_moves[0].wait_send()
 
     x_moves[1].wait_send()
-    for copy in (*x_over, *za, *zb, *zc, *q_moves, *qt_moves, *onward):
+    for copy in (*x_over, *za, *zb, *q_moves, *qt_moves, *onward):
         copy.wait_send()
     for pair in direct:
         for copy in pair:
@@ -822,6 +860,7 @@
         for group in chunk:
             for copy in group:
                 copy.wait()
+    hops_sent()
     rest_own.wait()
     for copy in outs:
         copy.wait()
@@ -841,7 +880,7 @@
     dma = pltpu.SemaphoreType.DMA
     low = jnp.bfloat16
     f32 = jnp.float32
-    pairs = [2, 2, n_shard - 1, n_shard - 1, n_shard - 1, 3]
+    pairs = [2, 2, n_shard - 1, n_shard - 1, n_shard - 1, n_shard - 1, 3]
     pairs += [4 * (n_tp - 1), 3 * CHUNKS, 4 * CHUNKS * (n_tp - 1)]
     return pl.pallas_call(
         functools.partial(begin_kernel, n_shard, n_ctx, n_tp),
@@ -892,6 +931,9 @@
     )(slots, local_at, table, master, small_in, inputs)
 
 
+NEAR = 4
+
+
 def back_kernel(
     n_ctx,
     n_tp,
@@ -911,6 +953,7 @@
     wo,
     layer_ref,
     own_ref,
+    near_ref,
     x_ref,
     y_ref,
     xy_ref,
@@ -924,17 +967,21 @@
     mixed_t,
     grads,
     arrived,
+    sums,
     send_sem,
     recv_sem,
     h_s,
     h_r,
+    n_s,
+    n_r,
     keep_sem,
+    out_sem,
 ):
     z, c, t = place_of()
     step = pl.program_id(0)
     tokens, width = gy.shape
     tiles = tokens // TILE
-    rows = own_ref.shape[1]
+    rows = grads.shape[4]
     others = n_tp - 1
     side, core, bit = t // 2, lax.rem(t, 2), lax.rem(c, 2)
 
@@ -1018,12 +1065,37 @@
         for copy in moves(b, count):
             copy.wait()
         slot = lax.rem(b, 2)
-        for j, out in enumerate((own_ref, x_ref, y_ref, xy_ref)):
+        for j in range(n_ctx):
             for i in range(count):
                 value = grads[slot, c ^ j, t, i]
                 for dt in range(others):
                     value = value + arrived[b, dt, c ^ j, i]
-                out[2 * b + i] = value
+                sums[j, 2 * b + i] = value
+
+    near = [
+        send(sums.at[j, 0:NEAR], near_ref.at[j - 1], (n_s, n_r), j - 1, (z, c ^ j, t))
+        for j in range(1, n_ctx)
+    ]
+
+    def outward(part, first, count):
+        moved = [
+            pltpu.make_async_copy(
+                sums.at[0, first : first + count],
+                own_ref.at[first : first + count],
+                out_sem.at[part * n_ctx],
+            )
+        ]
+        begin_at = max(first, NEAR)
+        count -= begin_at - first
+        for j, out in enumerate((x_ref, y_ref, xy_ref)):
+            moved.append(
+                pltpu.make_async_copy(
+                    sums.at[j + 1, begin_at : begin_at + count],
+                    out.at[begin_at - NEAR : begin_at - NEAR + count],
+                    out_sem.at[part * n_ctx + j + 1],
+                )
+            )
+        return moved
 
     def put(slot, i, value):
         low = value.astype(jnp.bfloat16)
@@ -1036,7 +1108,7 @@
         slot = lax.rem(step, 2)
 
         def one(i, carry):
-            at = pl.ds(pl.multiple_of(i * TILE, TILE), TILE)
+            at = pl.ds(pl.multiple_of(i * MID, MID), MID)
             grad = wide_dot(mixed[at, :], down_block, NN) * gel_ref[0, at, :].astype(jnp.float32)
             low = grad.astype(jnp.bfloat16)
             gu[at, :] = low
@@ -1046,7 +1118,7 @@
             )
             return carry
 
-        lax.fori_loop(0, tiles, one, 0)
+        lax.fori_loop(0, tokens // MID, one, 0)
         put(slot, 0, wide_dot(fit_ref[...], gu[...], NN))
         put(slot, 1, wide_dot(mixed_t[...], hid_ref[0], NN))
         exchange(step, 2)
@@ -1055,8 +1127,16 @@
     def settle():
         keep(step - 1, 2)
 
+    @pl.when(step == NEAR // 2)
+    def cross():
+        for copy in near:
+            copy.start()
+
     @pl.when(step == 4)
     def first_norm():
+        for copy in outward(0, 0, 8):
+            copy.start()
+
         def one(i, carry):
             at = pl.ds(pl.multiple_of(i * TILE, TILE), TILE)
             grad = gy[at, :]
@@ -1082,6 +1162,10 @@
 
         lax.fori_loop(0, tiles, two, 0)
         keep(4, 1)
+        for copy in outward(1, 8, 1):
+            copy.start()
+        for copy in (*near, *outward(0, 0, 8), *outward(1, 8, 1)):
+            copy.wait()
 
         @pl.when(stays)
         def done():
@@ -1139,14 +1223,16 @@
             pl.BlockSpec(memory_space=pl.ANY),
         ],
         out_specs=[
-            *[out((9, rows, width))] * 4,
+            *[pl.BlockSpec(memory_space=pl.ANY)] * 5,
             out((tokens, width)),
             out((tokens, width)),
             out((16, width)),
             pl.BlockSpec(memory_space=pl.ANY),
         ],
         out_shape=[
-            *[bf16_of(9, rows, width)] * 4,
+            bf16_of(9, rows, width),
+            bf16_of(n_ctx - 1, NEAR, rows, width),
+            *[bf16_of(9 - NEAR, rows, width)] * 3,
             f32_of(tokens, width),
             bf16_of(tokens, width),
             f32_of(16, width),
@@ -1159,11 +1245,15 @@
             pltpu.VMEM((width, tokens), jnp.bfloat16),
             pltpu.VMEM((2, n_ctx, n_tp, 2, rows, width), jnp.bfloat16),
             pltpu.VMEM((5, n_tp - 1, n_ctx, 2, rows, width), jnp.bfloat16),
+            pltpu.VMEM((n_ctx, 9 + 1, rows, width), jnp.bfloat16),
             dma((5 * (n_tp - 1),)),
             dma((5 * (n_tp - 1),)),
             dma((2,)),
             dma((2,)),
+            dma((n_ctx - 1,)),
+            dma((n_ctx - 1,)),
             dma((2,)),
+            dma((2 * n_ctx,)),
         ],
         compiler_params=pltpu.CompilerParams(
             collective_id=3, has_side_effects=True, vmem_limit_bytes=62 << 20
@@ -1201,6 +1291,7 @@
     gh1_hbm,
     first_hbm,
     e0_hbm,
+    near_hbm,
     e1_hbm,
     e2_hbm,
     e3_hbm,
@@ -1282,13 +1373,14 @@
                 (first_hbm, first_s),
                 (gh1_hbm, gh1_s),
                 (e0_hbm, early.at[0]),
-                (e1_hbm, early.at[1]),
-                (e2_hbm, early.at[2]),
-                (e3_hbm, early.at[3]),
+                (near_hbm, early.at[1:4, 0:NEAR]),
+                (e1_hbm, early.at[1, NEAR:EARLY]),
+                (e2_hbm, early.at[2, NEAR:EARLY]),
+                (e3_hbm, early.at[3, NEAR:EARLY]),
             )
         )
     ]
-    for i in (6, 7, 8, 9, 0, 1, 2, 3, 4, 5):
+    for i in (6, 7, 8, 9, 10, 0, 1, 2, 3, 4, 5):
         loads[i].start()
 
     def far(dz):
@@ -1308,7 +1400,7 @@
     for friend in friends:
         pl.semaphore_signal(barrier, inc=1, device_id=friend, device_id_type=MESH)
 
-    for i in range(6, 10):
+    for i in range(6, 11):
         loads[i].wait()
     every[0:EARLY] = early[0] + early[1] + early[2] + early[3]
     every[EARLY] = jnp.zeros_like(every[EARLY])
@@ -1593,13 +1685,13 @@
     return pl.pallas_call(
         functools.partial(finish_kernel, n_shard, n_ctx, n_tp),
         name="finish",
-        in_specs=[smem] * 2 + [anywhere] * 10 + [vmem] * 4,
+        in_specs=[smem] * 2 + [anywhere] * 11 + [vmem] * 4,
         out_specs=[anywhere] + [vmem] * 4,
         out_shape=[bf16_of(2, mid, width), stored, stored, stored, f32_of(*small.shape)],
         scratch_shapes=[
             pltpu.VMEM(s, low) if s else pltpu.VMEM(gh1.shape, jnp.float32) for s in shapes
         ]
-        + [dma((10,))]
+        + [dma((11,))]
         + [dma((n,)) for n in pairs for _ in range(2)]
         + [dma((1,))],
         compiler_params=pltpu.CompilerParams(
@@ -1677,7 +1769,7 @@
         crossing = [
             (a * n_tp + b, (a ^ j) * n_tp + b) for a in range(n_ctx) for b in range(n_tp)
         ]
-        early[j] = lax.ppermute(early[j], plane, crossing)
+        early[j + 1] = lax.ppermute(early[j + 1], plane, crossing)
     dq, dk, dv = attend_back(half_one, rand_blocks, q, k, v, lse, dctx, 5)
     stands = jnp.array([8, 0, 2, 4, 6, 1, 3, 5, 7], jnp.int32)
     slots_all = jnp.arange(n_shard * held, dtype=jnp.int32)

time: 356 us -> 338 us (0.949); the launches traced: 356 us -> 332 us
  waiting for transfers between devices: 15.3 us -> 0.01 us
  Pallas kernels: 317 us -> 309 us
    pallas_call x1, Pallas kernels: 89.2 us -> 65.8 us  [finish(): pl.pallas_call(functools.partial(finish_kernel, n_shard, n_ctx, n_tp), na...]
    ppermute x3, waiting for transfers between devices: 15.3 us -> 0.01 us  [shards(): early[j + 1] = lax.ppermute(early[j + 1], plane, crossing)]
    pallas_call x1, Pallas kernels: 51.8 us -> 60.5 us  [back(): pl.pallas_call(functools.partial(back_kernel, n_ctx, n_tp), name='back',...]
    pallas_call x1, Pallas kernels: 110 us -> 117 us  [begin(): pl.pallas_call(functools.partial(begin_kernel, n_shard, n_ctx, n_tp), nam...]
  transfers between devices with their start and end apart: 5 -> 5, of which waited for: 1 -> 0; matrix products, arithmetic and copies ran while one was open for 1% -> 1% of each run, Pallas kernels for 18% -> 20%
where the time goes in v8:
time: 338 us; the launch traced here: 332 us
  Pallas kernels  309 us (91%)
  other arithmetic  9.49 us (3%)
  local copies, waits for them, and re-layouts  8.31 us (2%)
  starting transfers between devices  4.51 us (1%)
    pallas_call x1, Pallas kernels, begin(): pl.pallas_call(functools.partial(begin_kernel, n_shard, n_ctx, n_tp), nam...  117 us
    pallas_call x1, Pallas kernels, finish(): pl.pallas_call(functools.partial(finish_kernel, n_shard, n_ctx, n_tp), na...  65.8 us
    pallas_call x1, Pallas kernels, back(): pl.pallas_call(functools.partial(back_kernel, n_ctx, n_tp), name='back',...  60.5 us
    pallas_call x1, Pallas kernels, attend_back(): pl.pallas_call(functools.partial(attend_back_kernel, unroll), grid_spec=s...  39.6 us
    pallas_call x1, Pallas kernels, call(): pl.pallas_call(kernel, name=name, grid_spec=pltpu.PrefetchScalarGridSpec(...  25.8 us
  transfers between devices with their start and end apart: 5, of which 0 were waited for; matrix products, arithmetic and copies ran while one was open for 1% of the time, Pallas kernels for 20%

profile of v8, /device:TPU:0, one launch (start us, length us, event | category | flops | bytes accessed | tf_op | source)
XLA Modules:
  0.0 332.2 jit_solution(14629688859054356373)
XLA Ops:
  0.6 0.0 copy-start.8
  0.7 0.9 dynamic_update_slice.3
  1.6 0.6 reshape.34.small_in
  2.2 1.6 copy.21.table.table_ref
  3.8 2.0 convert_element_type.10
  5.8 0.0 copy-done.8
  5.8 0.5 and_select_fusion.local_at
  6.4 0.1 select_bitcast_fusion
  6.5 0.0 copy-start.9
  6.5 0.0 copy-start.10
  6.5 116.9 %begin.1 = (bf16[4,512,768]{2,1,0:T(8,128)(2,1)}, bf16[8,320,768]{2,1,0:T(8,128)(2,1)}, bf16[8,9,96,768]{3,2,1,0:T(8,128)(2,1)}, f32[16,768]{1,0:T(8,128)}, bf16...) custom-call(s32[12]{0:T(128)} %slots.1, ...), custom_call_target="tpu_custom_call" | custom-call | flops 60000002048 | bytes 62914560 | tf_op jit(solution)/shard_map/begin/pallas_call | solution.py:885
  123.4 0.9 collective-permute-start
  124.3 0.1 collective-permute-start.1
  124.4 0.0 copy-done.9
  124.4 0.1 iota_compare_fusion
  124.5 0.1 select_reduce_fusion.1
  124.5 0.0 copy-done.10
  124.5 0.1 select_reduce_fusion
  124.6 0.5 broadcast_add_fusion
  125.2 0.7 stack.23.info
  125.8 25.8 %front.1 = (bf16[2,512,768]{2,1,0:T(8,128)(2,1)}, f32[1024,768]{1,0:T(8,128)}, f32[1024,128]{1,0:T(8,128)}, bf16[768,1024]{1,0:T(8,128)(2,1)}, bf16[4,1024,768]{...) custom-call(s32[5]{0:T(128)} %stack.23.info, ...), custom_call_target="tpu_custom_call" | custom-call | flops 11000000512 | bytes 41943040 | tf_op jit(solution)/shard_map/front/pallas_call | solution.py:270
  151.7 0.0 collective-permute-done.cot0_ref
  151.7 0.0 copy-start.11
  151.7 0.0 collective-permute-done.1.cot1_ref
  151.7 0.9 copy-done.11
  152.6 60.5 %back.1 = (bf16[9,96,768]{2,1,0:T(8,128)(2,1)}, bf16[3,4,96,768]{3,2,1,0:T(8,128)(2,1)}, bf16[5,96,768]{2,1,0:T(8,128)(2,1)}, bf16[5,96,768]{2,1,0:T(8,128)(2,1)...) custom-call(f32[1024,768]{1,0:T(8,128)} %get-tuple-element.50.n2_hbm, ...), custom_call_target="tpu_custom_call" | custom-call | flops 22000001024 | bytes 41943040 | tf_op jit(solution)/shard_map/back/pallas_call | solution.py:1204
  213.0 1.5 collective-permute-start.2
  214.6 1.2 collective-permute-start.3
  215.7 0.9 collective-permute-start.4
  216.6 0.0 copy-start
  216.6 39.6 %attend_back.1 = (bf16[1024,768]{1,0:T(8,128)(2,1)}, bf16[2048,768]{1,0:T(8,128)(2,1)}, bf16[2048,768]{1,0:T(8,128)(2,1)}) custom-call(s32[1]{0:T(128)} %bitcast.half_ref, s32[12,30,3]{2,1,0:T(8,128)} %copy.21.table.table_ref, bf16[3,16,64,256]{3,2,1,0:T(8,128)(2,1)} %get-tuple-element.61.q_ref, bf16[3,32,64,256]{3,2,1,0:T(8,128)(2,1)} %get-tuple-element.62.k_ref, ...), custom_call_target="tpu_custom_call" | custom-call | flops 120000004096 | bytes 25165824 | tf_op jit(solution)/shard_map/attend_back/pallas_call | solution.py:213
  256.2 0.0 copy-done
  256.2 1.9 convert_element_type.11
  258.1 0.0 collective-permute-done.2.e1_hbm
  258.1 0.0 copy-start.12
  258.1 0.0 collective-permute-done.3.e2_hbm
  258.1 0.0 collective-permute-done.4.e3_hbm
  258.1 0.8 copy-done.12
  259.0 65.8 %finish.1 = (bf16[2,512,768]{2,1,0:T(8,128)(2,1)}, f32[3,96,768]{2,1,0:T(8,128)}, f32[3,96,768]{2,1,0:T(8,128)}, f32[3,96,768]{2,1,0:T(8,128)}, f32[16,768]{1,0:T(8,128)}) custom-call(s32[12]{0:T(128)} %get-tuple-element.88.holder, s32[12]{0:T(128)} %get-tuple-element.87.late_at, bf16[4,512,768]{2,1,0:T(8,128)(2,1)} %get-tuple-element.47.x_ref.x_hbm, ...), custom_call_target="tpu_custom_call" | custom-call | flops 12000000000 | bytes 41943040 | tf_op jit(solution)/shard_map/finish/pallas_call | solution.py:1685
  324.8 0.0 copy-start.4
  324.8 0.0 copy-start.5
  324.8 0.0 copy-start.6
  324.8 0.0 copy-start.7
  324.8 0.0 copy-start.3
  324.9 0.0 copy-start.2
  324.9 0.0 copy-start.1
  324.9 3.5 %convert_element_type.12 = f32[2,512,768]{2,1,0:T(8,128)} convert(bf16[2,512,768]{2,1,0:T(8,128)(2,1)} %get-tuple-element.77) | non-fusion elementwise | flops 786432 | bytes 4718592 | tf_op jit(solution)/shard_map/convert_element_type | solution.py:1799
  328.3 0.0 copy-done.4
  328.3 0.0 copy-done.5
  328.3 0.0 copy-done.6
  328.4 0.0 copy-done.7
  328.4 0.7 multiply_subtract_fusion
  329.1 0.0 copy-done.3
  329.1 0.9 copy.29
  330.0 0.0 copy-done.2
  330.0 0.9 copy.30
  330.9 0.0 copy-done.1
  330.9 0.9 copy.31
  (3 shorter events, 0.0 us)
Async XLA Ops:
  0.6 5.2 %copy-start.8 = (s32[12]{0:T(128)S(1)}, s32[12]{0:T(128)}, u32[]{:S(2)}) copy-start(s32[12]{0:T(128)} %slots.1) | copy-start | bytes 148
  6.5 117.9 %copy-start.9 = (s32[12]{0:T(128)S(1)}, s32[12]{0:T(128)}, u32[]{:S(2)}) copy-start(s32[12]{0:T(128)} %slots.1) | copy-start | bytes 148
  6.5 118.1 %copy-start.10 = (s32[9]{0:T(128)S(1)}, s32[9]{0:T(128)}, u32[]{:S(2)}) copy-start(s32[9]{0:T(128)} %constant.69) | copy-start | bytes 112
  123.4 28.3 %collective-permute-start = (bf16[512,768]{1,0:T(8,128)(2,1)S(1)}, bf16[512,768]{1,0:T(8,128)(2,1)S(1)}, u32[]{:S(2)}, u32[]{:S(2)}) collective-permute-start(bf16[512,768]{1,0:T(8,128)(2,1)S(1)} %get-tuple-element.52), channel_id=1, source_target_pairs={{0,0},{1,4},{2,2},{3,6},{4,1},{5,5},{6,3},{7,7},{8,8},{9,12},{10,1... | collective-permute-start | bytes 2359304 | tf_op jit(solution)/shard_map/ppermute | solution.py:1763
  124.3 27.4 %collective-permute-start.1 = (bf16[512,768]{1,0:T(8,128)(2,1)S(1)}, bf16[512,768]{1,0:T(8,128)(2,1)}, u32[]{:S(2)}, u32[]{:S(2)}) collective-permute-start(bf16[512,768]{1,0:T(8,128)(2,1)S(1)} %get-tuple-element.53), channel_id=1, source_target_pairs={{0,2},{1,6},{2,0},{3,4},{4,3},{5,7},{6,1},{7,5},{8,10},{9,14},{10,... | collective-permute-start | bytes 2359304 | tf_op jit(solution)/shard_map/ppermute | solution.py:1763
  151.7 0.9 copy-start.11
  213.0 45.1 %collective-permute-start.2 = (bf16[5,96,768]{2,1,0:T(8,128)(2,1)}, bf16[5,96,768]{2,1,0:T(8,128)(2,1)S(1)}, u32[]{:S(2)}, u32[]{:S(2)}) collective-permute-start(bf16[5,96,768]{2,1,0:T(8,128)(2,1)} %get-tuple-element.73), channel_id=1, source_target_pairs={{0,2},{1,3},{2,0},{3,1},{4,6},{5,7},{6,4},{7,5},{8,10},{9,11},{10,... | collective-permute-start | bytes 2211848 | tf_op jit(solution)/shard_map/ppermute | solution.py:1772
  214.6 43.6 %collective-permute-start.3 = (bf16[5,96,768]{2,1,0:T(8,128)(2,1)}, bf16[5,96,768]{2,1,0:T(8,128)(2,1)}, u32[]{:S(2)}, u32[]{:S(2)}) collective-permute-start(bf16[5,96,768]{2,1,0:T(8,128)(2,1)} %get-tuple-element.74), channel_id=1, source_target_pairs={{0,4},{1,5},{2,6},{3,7},{4,0},{5,1},{6,2},{7,3},{8,12},{9,13},{10,... | collective-permute-start | bytes 2211848 | tf_op jit(solution)/shard_map/ppermute | solution.py:1772
  215.7 42.4 %collective-permute-start.4 = (bf16[5,96,768]{2,1,0:T(8,128)(2,1)}, bf16[5,96,768]{2,1,0:T(8,128)(2,1)}, u32[]{:S(2)}, u32[]{:S(2)}) collective-permute-start(bf16[5,96,768]{2,1,0:T(8,128)(2,1)} %get-tuple-element.75), channel_id=1, source_target_pairs={{0,6},{1,7},{2,4},{3,5},{4,2},{5,3},{6,0},{7,1},{8,14},{9,15},{10,... | collective-permute-start | bytes 2211848 | tf_op jit(solution)/shard_map/ppermute | solution.py:1772
  216.6 39.6 %copy-start = (bf16[2,512,768]{2,1,0:T(8,128)(2,1)S(1)}, bf16[2,512,768]{2,1,0:T(8,128)(2,1)}, u32[]{:S(2)}) copy-start(bf16[2,512,768]{2,1,0:T(8,128)(2,1)} %get-tuple-element.60) | copy-start | bytes 4718596
  258.1 0.9 copy-start.12
  324.8 3.5 %copy-start.4 = (f32[16,768]{1,0:T(8,128)S(1)}, f32[16,768]{1,0:T(8,128)}, u32[]{:S(2)}) copy-start(f32[16,768]{1,0:T(8,128)} %get-tuple-element.81) | copy-start | bytes 147460
  324.8 3.5 %copy-start.5 = (f32[288]{0:T(512)S(1)}, f32[288]{0:T(512)}, u32[]{:S(2)}) copy-start(f32[288]{0:T(512)} %param.18) | copy-start | bytes 3460
  324.8 3.5 %copy-start.6 = (f32[288]{0:T(512)S(1)}, f32[288]{0:T(512)}, u32[]{:S(2)}) copy-start(f32[288]{0:T(512)} %param.19) | copy-start | bytes 3460
  324.8 3.5 %copy-start.7 = (f32[288]{0:T(512)S(1)}, f32[288]{0:T(512)}, u32[]{:S(2)}) copy-start(f32[288]{0:T(512)} %param.20) | copy-start | bytes 3460
  324.8 4.2 %copy-start.3 = (f32[3,96,768]{2,1,0:T(8,128)S(1)}, f32[3,96,768]{2,1,0:T(8,128)}, u32[]{:S(2)}) copy-start(f32[3,96,768]{2,1,0:T(8,128)} %get-tuple-element.99) | copy-start | bytes 2654212
  324.9 5.1 %copy-start.2 = (f32[3,96,768]{2,1,0:T(8,128)S(1)}, f32[3,96,768]{2,1,0:T(8,128)}, u32[]{:S(2)}) copy-start(f32[3,96,768]{2,1,0:T(8,128)} %get-tuple-element.100) | copy-start | bytes 2654212
  324.9 6.0 %copy-start.1 = (f32[3,96,768]{2,1,0:T(8,128)S(1)}, f32[3,96,768]{2,1,0:T(8,128)}, u32[]{:S(2)}) copy-start(f32[3,96,768]{2,1,0:T(8,128)} %get-tuple-element.101) | copy-start | bytes 2654212

commit v9 on v8

--- a/solution.py
+++ b/solution.py
@@ -403,6 +403,7 @@
 MESH = pl.DeviceIdType.MESH
 KINDS = 3
 CHUNKS = 3
+HOOKS = (4, 5, 6)
 PER = 3
 
 
@@ -522,6 +523,7 @@
     for j in range(held):
         low[j] = raw[j].astype(jnp.bfloat16)
     low[held] = jnp.zeros_like(low[held])
+    pool[pl.ds(z * held, held)] = low[0:held]
     part[...] = jnp.zeros_like(part)
     for m in range(KINDS):
         part[m * rows : (m + 1) * rows, :] = low[local_at[m]]
@@ -530,6 +532,27 @@
 
     def piece_at(k):
         return pl.ds(pl.multiple_of(k * piece, piece), piece)
+
+    def hop_copy(s, way):
+        sems = (zc_s, zc_r) if way > 0 else (zd_s, zd_r)
+        slot = pl.ds((z - way * (s - 1)) * held, held)
+        return send(
+            pool.at[slot], pool.at[slot], sems, s - 1, (lax.rem(z + way + n_shard, n_shard), c, t)
+        )
+
+    def hop_on(s, way):
+        start = z - way * (s - 1)
+        end = z + way
+        return (start >= 0) & (start < n_shard) & (end >= 0) & (end < n_shard)
+
+    def hop(s):
+        for way in (1, -1):
+
+            @pl.when(hop_on(s, way))
+            def move(way=way):
+                if s > 1:
+                    hop_copy(s - 1, way).wait_recv()
+                hop_copy(s, way).start()
 
     za = [
         send(part.at[piece_at(far(dz)[0])], got.at[dz - 1], (za_s, za_r), dz - 1, far(dz))
@@ -567,30 +590,8 @@
     ]
     for copy in zb:
         copy.start()
+    hop(1)
     total[piece_at(z), :] = summed
-    pool_here = pl.ds(z * held, held)
-
-    def hop_copy(s, way):
-        sems = (zc_s, zc_r) if way > 0 else (zd_s, zd_r)
-        slot = pl.ds((z - way * (s - 1)) * held, held)
-        return send(
-            pool.at[slot], pool.at[slot], sems, s - 1, (lax.rem(z + way + n_shard, n_shard), c, t)
-        )
-
-    def hop_on(s, way):
-        start = z - way * (s - 1)
-        end = z + way
-        return (start >= 0) & (start < n_shard) & (end >= 0) & (end < n_shard)
-
-    def hop(s):
-        for way in (1, -1):
-
-            @pl.when(hop_on(s, way))
-            def move(way=way):
-                if s > 1:
-                    hop_copy(s - 1, way).wait_recv()
-                hop_copy(s, way).start()
-
     def hops_end():
         for way, end in ((1, n_shard - 1), (-1, 0)):
 
@@ -607,16 +608,15 @@
                 def sent(s=s, way=way):
                     hop_copy(s, way).wait_send()
 
-    pool[pool_here] = low[0:held]
     for copy in zb:
         copy.wait_recv()
+    hop(2)
 
     q_moves = [
         send(total, first.at[me], (qm_s, qm_r), k, across(m)) for k, m in enumerate((1, 2, 3))
     ]
     for copy in q_moves:
         copy.start()
-    hop(1)
     qt_moves = [
         send(total, first.at[me], (qt_s, qt_r), dt - 1, beside(dt)) for dt in range(1, n_tp)
     ]
@@ -639,6 +639,8 @@
     x_over[0].start()
     x_moves[1].wait_recv()
     x_over[1].start()
+    for s in range(3, n_shard):
+        hop(s)
 
     for k, m in enumerate((1, 2, 3)):
         q_moves[k].wait_recv()
@@ -653,63 +655,8 @@
             )
             copy.start()
             qt_moves.append(copy)
-        if k == 1:
-            hop(2)
     for copy in qt_moves:
         copy.wait_recv()
-    for s in range(3, n_shard):
-        hop(s)
-    outs = [pltpu.make_async_copy(first, first_ref, out_sem.at[0])]
-    outs[0].start()
-
-    sums = None
-    for g in range(n_ctx * n_tp):
-        here = first[g, KINDS * rows : KINDS * rows + 16, :].astype(jnp.float32)
-        sums = here if sums is None else sums + here
-    small[...] = sums
-    small_ref[...] = sums
-    for m in range(KINDS):
-        weights[m] = first[:, m * rows : (m + 1) * rows, :].reshape(width, width)
-
-    def split(dst, start, value):
-        low_value = value.astype(jnp.bfloat16)
-        per = TILE // BLOCK
-        for g in range(groups):
-            piece_value = low_value[:, g * lanes : (g + 1) * lanes]
-            dst[g, pl.ds(start, per)] = piece_value.reshape(per, BLOCK, lanes)
-
-    def project(a, chunk, own):
-        def one(i, carry):
-            x = x_all[a, pl.ds(pl.multiple_of(i * TILE, TILE), TILE), :]
-            start = chunk * (mid // BLOCK) + i * (TILE // BLOCK)
-            if own:
-                q_start = (chunk - 2 * core) * (mid // BLOCK) + i * (TILE // BLOCK)
-                q = wide_dot(x, weights[0], NN) + small[0:1, :]
-                split(q_s, q_start, q.astype(jnp.bfloat16) * jnp.bfloat16(score_scale))
-            split(k_s, start, wide_dot(x, weights[1], NN))
-            split(v_s, start, wide_dot(x, weights[2], NN) + small[1:2, :])
-            return carry
-
-        lax.fori_loop(0, mid // TILE, one, 0)
-
-    def own_project(a, carry):
-        project(a, 2 * core + (a ^ bit), True)
-        return carry
-
-    def other_project(a, carry):
-        project(2 + a, 2 * (1 - core) + (a ^ bit), False)
-        return carry
-
-    lax.fori_loop(0, 2, own_project, 0)
-    for copy in x_over:
-        copy.wait_recv()
-    outs.append(pltpu.make_async_copy(x_all, x_ref, out_sem.at[1]))
-    outs[1].start()
-    lax.fori_loop(0, 2, other_project, 0)
-    for i, (src, dst) in enumerate(((q_s, q_ref), (k_s, k_ref), (v_s, v_ref))):
-        outs.append(pltpu.make_async_copy(src, dst, out_sem.at[2 + i]))
-        outs[-1].start()
-
     def span_of(k):
         return pl.ds(k * PER, PER)
 
@@ -768,6 +715,56 @@
             copy.start()
 
     begin_rest()
+    outs = [pltpu.make_async_copy(first, first_ref, out_sem.at[0])]
+    outs[0].start()
+
+    sums = None
+    for g in range(n_ctx * n_tp):
+        here = first[g, KINDS * rows : KINDS * rows + 16, :].astype(jnp.float32)
+        sums = here if sums is None else sums + here
+    small[...] = sums
+    small_ref[...] = sums
+    for m in range(KINDS):
+        weights[m] = first[:, m * rows : (m + 1) * rows, :].reshape(width, width)
+
+    def split(dst, start, value):
+        low_value = value.astype(jnp.bfloat16)
+        per = TILE // BLOCK
+        for g in range(groups):
+            piece_value = low_value[:, g * lanes : (g + 1) * lanes]
+            dst[g, pl.ds(start, per)] = piece_value.reshape(per, BLOCK, lanes)
+
+    def project(a, chunk, own):
+        def one(i, carry):
+            x = x_all[a, pl.ds(pl.multiple_of(i * TILE, TILE), TILE), :]
+            start = chunk * (mid // BLOCK) + i * (TILE // BLOCK)
+            if own:
+                q_start = (chunk - 2 * core) * (mid // BLOCK) + i * (TILE // BLOCK)
+                q = wide_dot(x, weights[0], NN) + small[0:1, :]
+                split(q_s, q_start, q.astype(jnp.bfloat16) * jnp.bfloat16(score_scale))
+            split(k_s, start, wide_dot(x, weights[1], NN))
+            split(v_s, start, wide_dot(x, weights[2], NN) + small[1:2, :])
+            return carry
+
+        lax.fori_loop(0, mid // TILE, one, 0)
+
+    def own_project(a, carry):
+        project(a, 2 * core + (a ^ bit), True)
+        return carry
+
+    def other_project(a, carry):
+        project(2 + a, 2 * (1 - core) + (a ^ bit), False)
+        return carry
+
+    lax.fori_loop(0, 2, own_project, 0)
+    for copy in x_over:
+        copy.wait_recv()
+    outs.append(pltpu.make_async_copy(x_all, x_ref, out_sem.at[1]))
+    outs[1].start()
+    lax.fori_loop(0, 2, other_project, 0)
+    for i, (src, dst) in enumerate(((q_s, q_ref), (k_s, k_ref), (v_s, v_ref))):
+        outs.append(pltpu.make_async_copy(src, dst, out_sem.at[2 + i]))
+        outs[-1].start()
 
     last = nblocks - 1
     picks_each = table.shape[2]
@@ -782,7 +779,7 @@
         qg, kg, vg = q_s.at[g], k_s.at[g], v_s.at[g]
         for k in range(CHUNKS):
 
-            @pl.when(i == 3 + 2 * k)
+            @pl.when(i == HOOKS[k])
             def hook(k=k):
                 relay(k)
 
@@ -931,7 +928,7 @@
     )(slots, local_at, table, master, small_in, inputs)
 
 
-NEAR = 4
+NEAR = 2
 
 
 def back_kernel(
@@ -1072,10 +1069,18 @@
                     value = value + arrived[b, dt, c ^ j, i]
                 sums[j, 2 * b + i] = value
 
-    near = [
-        send(sums.at[j, 0:NEAR], near_ref.at[j - 1], (n_s, n_r), j - 1, (z, c ^ j, t))
-        for j in range(1, n_ctx)
-    ]
+    def near(b):
+        pair = slice(2 * b, 2 * b + 2)
+        return [
+            send(
+                sums.at[j, pair],
+                near_ref.at[j - 1, pair],
+                (n_s, n_r),
+                b * (n_ctx - 1) + j - 1,
+                (z, c ^ j, t),
+            )
+            for j in range(1, n_ctx)
+        ]
 
     def outward(part, first, count):
         moved = [
@@ -1127,10 +1132,12 @@
     def settle():
         keep(step - 1, 2)
 
-    @pl.when(step == NEAR // 2)
-    def cross():
-        for copy in near:
-            copy.start()
+    for b in range(NEAR // 2):
+
+        @pl.when(step == b + 1)
+        def cross(b=b):
+            for copy in near(b):
+                copy.start()
 
     @pl.when(step == 4)
     def first_norm():
@@ -1164,7 +1171,7 @@
         keep(4, 1)
         for copy in outward(1, 8, 1):
             copy.start()
-        for copy in (*near, *outward(0, 0, 8), *outward(1, 8, 1)):
+        for copy in (*near(0), *outward(0, 0, 8), *outward(1, 8, 1)):
             copy.wait()
 
         @pl.when(stays)
@@ -1313,7 +1320,8 @@
     early,
     every,
     packed,
-    slot_met,
+    right_met,
+    left_met,
     flipped,
     grads,
     arrived,
@@ -1326,10 +1334,14 @@
     small_t,
     small_m,
     small_p,
-    flat,
-    flat_met,
-    flat_sum,
-    mine_s,
+    flat_a,
+    met_a,
+    sum_a,
+    mine_a,
+    flat_b,
+    met_b,
+    sum_b,
+    mine_b,
     pool,
     in_sem,
     c_s,
@@ -1346,10 +1358,16 @@
     sp_r,
     e_s,
     e_r,
+    l_s,
+    l_r,
     a_s,
     a_r,
     b_s,
     b_r,
+    d_s,
+    d_r,
+    f_s,
+    f_r,
     keep_sem,
 ):
     z, c, t = place_of()
@@ -1359,8 +1377,7 @@
     held, rows, _ = w_ref.shape
     per = n_ctx * n_tp // 2
     band = width // 2
-    tile = mid // 2
-    piece = mine_s.shape[0]
+    tile = mid
 
     loads = [
         pltpu.make_async_copy(src, dst, in_sem.at[i])
@@ -1407,12 +1424,52 @@
     for s in range(n_shard * held):
         packed[s // held, s % held] = every[holder[s]]
     pl.semaphore_wait(barrier, len(friends))
-    slot_moves = [
-        send(packed.at[far(dz)[0]], slot_met.at[dz - 1], (e_s, e_r), dz - 1, far(dz))
-        for dz in range(1, n_shard)
-    ]
-    for copy in slot_moves:
-        copy.start()
+
+    def run(owner_at, s, way):
+        met, sems = (right_met, (e_s, e_r)) if way > 0 else (left_met, (l_s, l_r))
+        target = (lax.rem(z + way + n_shard, n_shard), c, t)
+        return send(packed.at[owner_at], met.at[s], sems, s, target)
+
+    def each_run(hop):
+        for s in range(hop + 1):
+            for way in (1, -1):
+                place = hop - s if way > 0 else n_shard - 1 - (hop - s)
+                owner_at = n_shard - 1 - s if way > 0 else s
+                yield s, way, place, owner_at
+
+    def hop(h):
+        for s, way, place, owner_at in each_run(h):
+
+            @pl.when(z == place)
+            def move(s=s, way=way, place=place, owner_at=owner_at):
+                copy = run(owner_at, s, way)
+                if h > s:
+                    copy.wait_recv()
+                    met = right_met if way > 0 else left_met
+                    for j in range(held):
+                        packed[owner_at, j] = packed[owner_at, j] + met[s, j]
+                copy.start()
+
+    def hops_end():
+        for h in range(n_shard - 1):
+            for s, way, place, owner_at in each_run(h):
+
+                @pl.when(z == place)
+                def sent(s=s, way=way, owner_at=owner_at):
+                    run(owner_at, s, way).wait_send()
+
+        for s in range(n_shard - 1):
+            for way in (1, -1):
+                owner_at = n_shard - 1 - s if way > 0 else s
+
+                @pl.when(z == owner_at)
+                def last(s=s, way=way, owner_at=owner_at):
+                    run(owner_at, s, way).wait_recv()
+                    met = right_met if way > 0 else left_met
+                    for j in range(held):
+                        packed[owner_at, j] = packed[owner_at, j] + met[s, j]
+
+    hop(0)
 
     core_moves = []
 
@@ -1446,7 +1503,7 @@
                 partial.at[c ^ j, m], met.at[j - 1, m], (p_s, p_r), (j - 1) * LATE + m, across(j)
             )
             copy.start()
-            plane_moves.append(copy)
+            plane_moves.append((m, copy))
 
     loads[0].wait()
     for a in range(4):
@@ -1473,6 +1530,8 @@
     weight_grad(0, pl.ds(pl.multiple_of(core * tokens, tokens), tokens), dq_s)
     exchange(0)
     meet(2)
+    for h in range(1, n_shard - 2):
+        hop(h)
 
     row = lax.broadcasted_iota(jnp.int32, small_ref.shape, 0)
     q_sum = jnp.sum(dq_s[...].astype(jnp.float32), axis=0, keepdims=True)
@@ -1513,6 +1572,8 @@
     for copy in small_plane:
         copy.start()
 
+    if n_shard > 2:
+        hop(n_shard - 2)
     loads[5].wait()
     stays = c // 2 == core
     home_moves = []
@@ -1521,7 +1582,7 @@
     keep = pltpu.make_async_copy(back_s.at[0], home_ref.at[bit], keep_sem.at[0])
     for move in range(2):
         chunk = move ^ bit
-        for i in range(2):
+        for i in range(mid // tile):
             at = pl.ds(pl.multiple_of(core * tokens + chunk * mid + i * tile, tile), tile)
             here = pl.ds(pl.multiple_of(chunk * mid + i * tile, tile), tile)
             value = gh1_s[here, :]
@@ -1545,59 +1606,73 @@
         else:
             home_moves[1].start()
 
-    flat[...] = jnp.zeros_like(flat)
-    for copy in plane_moves:
-        copy.wait_recv()
-    for m in range(LATE):
+    def gathered_rows(m):
+        for which, copy in plane_moves:
+            if which == m:
+                copy.wait_recv()
         value = partial[c, m]
         for j in range(n_ctx - 1):
             value = value + met[j, m]
-        flat[m * rows : (m + 1) * rows, :] = value
+        return value
+
+    def piece_at(ref, k):
+        piece = ref.shape[0] // n_shard
+        return pl.ds(pl.multiple_of(k * piece, piece), piece)
+
+    def scatter_lot(flat, lot_met, sems):
+        moves = [
+            send(flat.at[piece_at(flat, far(dz)[0])], lot_met.at[dz - 1], sems, dz - 1, far(dz))
+            for dz in range(1, n_shard)
+        ]
+        for copy in moves:
+            copy.start()
+        return moves
+
+    def spread_lot(moves, flat, lot_met, lot_sum, lot_mine, sems):
+        total = flat[piece_at(flat, z), :].astype(jnp.float32)
+        for dz, copy in enumerate(moves):
+            copy.wait_recv()
+            total = total + lot_met[dz].astype(jnp.float32)
+        lot_mine[...] = total.astype(jnp.bfloat16)
+        spreads = [
+            send(lot_mine, lot_sum.at[piece_at(flat, z)], sems, dz - 1, far(dz))
+            for dz in range(1, n_shard)
+        ]
+        for copy in spreads:
+            copy.start()
+        lot_sum[piece_at(flat, z), :] = lot_mine[...]
+        return spreads
+
+    small_rows = small_s.shape[0]
+    flat_a[...] = jnp.zeros_like(flat_a)
+    flat_b[...] = jnp.zeros_like(flat_b)
+    flat_a[0:rows, :] = gathered_rows(1)
+    flat_a[rows : 2 * rows, :] = gathered_rows(2)
+    scatter_a = scatter_lot(flat_a, met_a, (a_s, a_r))
+    flat_b[0:rows, :] = gathered_rows(0)
     value = small_m[...]
     for j, copy in enumerate(small_plane):
         copy.wait_recv()
         value = value + small_p[j]
-    small_rows = small_s.shape[0]
-    flat[LATE * rows : LATE * rows + small_rows, :] = value
-
-    def piece_at(k):
-        return pl.ds(pl.multiple_of(k * piece, piece), piece)
-
-    flat_out = [
-        send(flat.at[piece_at(far(dz)[0])], flat_met.at[dz - 1], (a_s, a_r), dz - 1, far(dz))
-        for dz in range(1, n_shard)
-    ]
-    for copy in flat_out:
-        copy.start()
-    total = flat[piece_at(z), :].astype(jnp.float32)
-    for dz, copy in enumerate(flat_out):
+    flat_b[rows : rows + small_rows, :] = value
+    scatter_b = scatter_lot(flat_b, met_b, (b_s, b_r))
+    spread_a = spread_lot(scatter_a, flat_a, met_a, sum_a, mine_a, (d_s, d_r))
+    spread_b = spread_lot(scatter_b, flat_b, met_b, sum_b, mine_b, (f_s, f_r))
+    hops_end()
+    for copy in (*spread_a, *spread_b):
         copy.wait_recv()
-        total = total + flat_met[dz].astype(jnp.float32)
-    mine_s[...] = total.astype(jnp.bfloat16)
-    flat_back = [
-        send(mine_s, flat_sum.at[piece_at(z)], (b_s, b_r), dz - 1, far(dz))
-        for dz in range(1, n_shard)
-    ]
-    for copy in flat_back:
-        copy.start()
-    flat_sum[piece_at(z), :] = mine_s[...]
-    for copy in slot_moves:
-        copy.wait_recv()
-    for copy in flat_back:
-        copy.wait_recv()
-    for m in range(LATE):
-        pool[m] = flat_sum[m * rows : (m + 1) * rows, :]
+    pool[0] = sum_b[0:rows, :]
+    pool[1] = sum_a[0:rows, :]
+    pool[2] = sum_a[rows : 2 * rows, :]
     pool[LATE] = jnp.zeros_like(pool[LATE])
     for j in range(held):
         grad = packed[z, j].astype(jnp.float32)
-        for dz in range(n_shard - 1):
-            grad = grad + slot_met[dz, j].astype(jnp.float32)
         grad = grad + pool[late_at[z * held + j]].astype(jnp.float32)
         w, one, two = adam_update(w_ref[j], one_ref[j], two_ref[j], grad, 0.01, rate_value)
         w_out[j] = w
         one_out[j] = one
         two_out[j] = two
-    small_out[...] = flat_sum[LATE * rows : LATE * rows + small_rows, :].astype(jnp.float32)
+    small_out[...] = sum_b[rows : rows + small_rows, :].astype(jnp.float32)
 
     @pl.when(stays)
     def done():
@@ -1608,16 +1683,16 @@
         home_moves[0].wait()
 
     home_moves[1].wait()
-    for _, copy in core_moves:
+    for _, copy in (*core_moves, *plane_moves):
         copy.wait_send()
     for copy in (
-        *plane_moves,
         *over_moves,
         *small_core,
         *small_plane,
-        *slot_moves,
-        *flat_out,
-        *flat_back,
+        *scatter_a,
+        *scatter_b,
+        *spread_a,
+        *spread_b,
     ):
         copy.wait_send()
 
@@ -1644,14 +1719,15 @@
     held, rows, _ = master.shape
     groups = n_ctx * n_tp
     span = 16 * n_shard
-    long = -(-(LATE * rows + small.shape[0]) // span) * span
+    long_a = -(-2 * rows // span) * span
+    long_b = -(-(rows + small.shape[0]) // span) * span
     smem = pl.BlockSpec(memory_space=pltpu.SMEM)
     anywhere = pl.BlockSpec(memory_space=pl.ANY)
     vmem = pl.BlockSpec(memory_space=pltpu.VMEM)
     dma = pltpu.SemaphoreType.DMA
     low = jnp.bfloat16
     pairs = [LATE * n_ctx * (n_tp - 1), LATE * (n_ctx - 1), 2, 2, n_tp - 1, n_ctx - 1]
-    pairs += [n_shard - 1] * 3
+    pairs += [n_shard - 1] * 6
     stored = f32_of(held, rows, width)
     shapes = [
         x_all.shape,
@@ -1663,6 +1739,7 @@
         (4, EARLY, rows, width),
         (EARLY + 1, rows, width),
         (n_shard, held, rows, width),
+        (n_shard - 1, held, rows, width),
         (n_shard - 1, held, rows, width),
         (width, 4 * mid),
         (groups, LATE, rows, width),
@@ -1676,10 +1753,16 @@
         (n_tp - 1, *small.shape),
         small.shape,
         (n_ctx - 1, *small.shape),
-        (long, width),
-        (n_shard - 1, long // n_shard, width),
-        (long, width),
-        (long // n_shard, width),
+        *[
+            shape
+            for long in (long_a, long_b)
+            for shape in (
+                (long, width),
+                (n_shard - 1, long // n_shard, width),
+                (long, width),
+                (long // n_shard, width),
+            )
+        ],
         (LATE + 1, rows, width),
     ]
     return pl.pallas_call(

time: 338 us -> 322 us (0.953)
  Pallas kernels: 309 us -> 289 us
    pallas_call x1, Pallas kernels: 60.5 us -> 48.4 us  [back(): pl.pallas_call(functools.partial(back_kernel, n_ctx, n_tp), name='back',...]
    pallas_call x1, Pallas kernels: 117 us -> 107 us  [begin(): pl.pallas_call(functools.partial(begin_kernel, n_shard, n_ctx, n_tp), nam...]
  transfers between devices with their start and end apart: 5 -> 5, of which waited for: 0 -> 1; matrix products, arithmetic and copies ran while one was open for 1% -> 1% of each run, Pallas kernels for 20% -> 21%
where the time goes in v9:
time: 322 us; the launch traced here: 316 us
  Pallas kernels  289 us (90%)
  other arithmetic  9.56 us (3%)
  local copies, waits for them, and re-layouts  7.38 us (2%)
  starting transfers between devices  5.99 us (2%)
    pallas_call x1, Pallas kernels, begin(): pl.pallas_call(functools.partial(begin_kernel, n_shard, n_ctx, n_tp), nam...  107 us
    pallas_call x1, Pallas kernels, finish(): pl.pallas_call(functools.partial(finish_kernel, n_shard, n_ctx, n_tp), na...  68.3 us
    pallas_call x1, Pallas kernels, back(): pl.pallas_call(functools.partial(back_kernel, n_ctx, n_tp), name='back',...  48.4 us
    pallas_call x1, Pallas kernels, attend_back(): pl.pallas_call(functools.partial(attend_back_kernel, unroll), grid_spec=s...  39.6 us
    pallas_call x1, Pallas kernels, call(): pl.pallas_call(kernel, name=name, grid_spec=pltpu.PrefetchScalarGridSpec(...  25.8 us
  transfers between devices with their start and end apart: 5, of which 1 were waited for; matrix products, arithmetic and copies ran while one was open for 1% of the time, Pallas kernels for 21%

profile of v9, /device:TPU:0, one launch (start us, length us, event | category | flops | bytes accessed | tf_op | source)
XLA Modules:
  0.0 316.0 jit_solution(9037117817056346932)
XLA Ops:
  0.6 0.0 copy-start.8
  0.7 0.9 dynamic_update_slice.3
  1.6 0.6 reshape.34.small_in
  2.2 1.6 copy.21.table.table_ref
  3.8 2.0 convert_element_type.10
  5.8 0.0 copy-done.8
  5.8 0.5 and_select_fusion.local_at
  6.3 0.1 select_bitcast_fusion
  6.5 0.0 copy-start.9
  6.5 0.0 copy-start.10
  6.5 107.0 %begin.1 = (bf16[4,512,768]{2,1,0:T(8,128)(2,1)}, bf16[8,320,768]{2,1,0:T(8,128)(2,1)}, bf16[8,9,96,768]{3,2,1,0:T(8,128)(2,1)}, f32[16,768]{1,0:T(8,128)}, bf16...) custom-call(s32[12]{0:T(128)} %slots.1, ...), custom_call_target="tpu_custom_call" | custom-call | flops 60000002048 | bytes 62914560 | tf_op jit(solution)/shard_map/begin/pallas_call | solution.py:882
  113.5 0.9 collective-permute-start
  114.4 1.5 collective-permute-start.1
  115.9 0.0 copy-done.9
  115.9 0.1 iota_compare_fusion
  116.0 0.1 select_reduce_fusion.1
  116.1 0.0 copy-done.10
  116.1 0.1 select_reduce_fusion
  116.2 0.6 broadcast_add_fusion
  116.8 0.6 stack.23.info
  117.4 25.8 %front.1 = (bf16[2,512,768]{2,1,0:T(8,128)(2,1)}, f32[1024,768]{1,0:T(8,128)}, f32[1024,128]{1,0:T(8,128)}, bf16[768,1024]{1,0:T(8,128)(2,1)}, bf16[4,1024,768]{...) custom-call(s32[5]{0:T(128)} %stack.23.info, ...), custom_call_target="tpu_custom_call" | custom-call | flops 11000000512 | bytes 41943040 | tf_op jit(solution)/shard_map/front/pallas_call | solution.py:270
  143.2 0.0 collective-permute-done.cot0_ref
  143.2 0.0 copy-start.11
  143.2 0.0 collective-permute-done.1.cot1_ref
  143.2 0.9 copy-done.11
  144.1 48.4 %back.1 = (bf16[9,96,768]{2,1,0:T(8,128)(2,1)}, bf16[3,2,96,768]{3,2,1,0:T(8,128)(2,1)}, bf16[7,96,768]{2,1,0:T(8,128)(2,1)}, bf16[7,96,768]{2,1,0:T(8,128)(2,1)...) custom-call(f32[1024,768]{1,0:T(8,128)} %get-tuple-element.50.n2_hbm, ...), custom_call_target="tpu_custom_call" | custom-call | flops 22000001024 | bytes 41943040 | tf_op jit(solution)/shard_map/back/pallas_call | solution.py:1211
  192.4 0.9 collective-permute-start.2
  193.3 1.6 collective-permute-start.3
  194.9 1.1 collective-permute-start.4
  196.0 0.0 copy-start
  196.0 39.6 %attend_back.1 = (bf16[1024,768]{1,0:T(8,128)(2,1)}, bf16[2048,768]{1,0:T(8,128)(2,1)}, bf16[2048,768]{1,0:T(8,128)(2,1)}) custom-call(s32[1]{0:T(128)} %bitcast.half_ref, s32[12,30,3]{2,1,0:T(8,128)} %copy.21.table.table_ref, bf16[3,16,64,256]{3,2,1,0:T(8,128)(2,1)} %get-tuple-element.61.q_ref, bf16[3,32,64,256]{3,2,1,0:T(8,128)(2,1)} %get-tuple-element.62.k_ref, ...), custom_call_target="tpu_custom_call" | custom-call | flops 120000004096 | bytes 25165824 | tf_op jit(solution)/shard_map/attend_back/pallas_call | solution.py:213
  235.6 0.0 copy-done
  235.6 1.9 convert_element_type.11
  237.5 0.0 collective-permute-done.2.e1_hbm
  237.5 2.9 collective-permute-done.3.e2_hbm
  240.3 0.0 collective-permute-done.4.e3_hbm
  240.3 68.3 %finish.1 = (bf16[2,512,768]{2,1,0:T(8,128)(2,1)}, f32[3,96,768]{2,1,0:T(8,128)}, f32[3,96,768]{2,1,0:T(8,128)}, f32[3,96,768]{2,1,0:T(8,128)}, f32[16,768]{1,0:T(8,128)}) custom-call(s32[12]{0:T(128)} %get-tuple-element.88.holder, s32[12]{0:T(128)} %get-tuple-element.87.late_at, bf16[4,512,768]{2,1,0:T(8,128)(2,1)} %get-tuple-element.47.x_ref.x_hbm, ...), custom_call_target="tpu_custom_call" | custom-call | flops 12000000000 | bytes 41943040 | tf_op jit(solution)/shard_map/finish/pallas_call | solution.py:1768
  308.6 0.0 copy-start.4
  308.6 0.0 copy-start.5
  308.6 0.0 copy-start.6
  308.6 0.0 copy-start.7
  308.7 0.0 copy-start.3
  308.7 0.0 copy-start.2
  308.7 0.0 copy-start.1
  308.7 3.5 %convert_element_type.12 = f32[2,512,768]{2,1,0:T(8,128)} convert(bf16[2,512,768]{2,1,0:T(8,128)(2,1)} %get-tuple-element.77) | non-fusion elementwise | flops 786432 | bytes 4718592 | tf_op jit(solution)/shard_map/convert_element_type | solution.py:1882
  312.1 0.0 copy-done.4
  312.1 0.0 copy-done.5
  312.2 0.0 copy-done.6
  312.2 0.0 copy-done.7
  312.2 0.7 multiply_subtract_fusion
  312.9 0.0 copy-done.3
  312.9 0.9 copy.29
  313.8 0.0 copy-done.2
  313.8 0.9 copy.30
  314.7 0.0 copy-done.1
  314.7 0.9 copy.31
  (3 shorter events, 0.0 us)
Async XLA Ops:
  0.6 5.2 %copy-start.8 = (s32[12]{0:T(128)S(1)}, s32[12]{0:T(128)}, u32[]{:S(2)}) copy-start(s32[12]{0:T(128)} %slots.1) | copy-start | bytes 148
  6.5 109.5 %copy-start.9 = (s32[12]{0:T(128)S(1)}, s32[12]{0:T(128)}, u32[]{:S(2)}) copy-start(s32[12]{0:T(128)} %slots.1) | copy-start | bytes 148
  6.5 109.6 %copy-start.10 = (s32[9]{0:T(128)S(1)}, s32[9]{0:T(128)}, u32[]{:S(2)}) copy-start(s32[9]{0:T(128)} %constant.69) | copy-start | bytes 112
  113.5 29.7 %collective-permute-start = (bf16[512,768]{1,0:T(8,128)(2,1)S(1)}, bf16[512,768]{1,0:T(8,128)(2,1)S(1)}, u32[]{:S(2)}, u32[]{:S(2)}) collective-permute-start(bf16[512,768]{1,0:T(8,128)(2,1)S(1)} %get-tuple-element.52), channel_id=1, source_target_pairs={{0,0},{1,4},{2,2},{3,6},{4,1},{5,5},{6,3},{7,7},{8,8},{9,12},{10,1... | collective-permute-start | bytes 2359304 | tf_op jit(solution)/shard_map/ppermute | solution.py:1846
  114.4 28.8 %collective-permute-start.1 = (bf16[512,768]{1,0:T(8,128)(2,1)S(1)}, bf16[512,768]{1,0:T(8,128)(2,1)}, u32[]{:S(2)}, u32[]{:S(2)}) collective-permute-start(bf16[512,768]{1,0:T(8,128)(2,1)S(1)} %get-tuple-element.53), channel_id=1, source_target_pairs={{0,2},{1,6},{2,0},{3,4},{4,3},{5,7},{6,1},{7,5},{8,10},{9,14},{10,... | collective-permute-start | bytes 2359304 | tf_op jit(solution)/shard_map/ppermute | solution.py:1846
  143.2 0.9 copy-start.11
  192.4 45.0 %collective-permute-start.2 = (bf16[7,96,768]{2,1,0:T(8,128)(2,1)}, bf16[7,96,768]{2,1,0:T(8,128)(2,1)}, u32[]{:S(2)}, u32[]{:S(2)}) collective-permute-start(bf16[7,96,768]{2,1,0:T(8,128)(2,1)} %get-tuple-element.73), channel_id=1, source_target_pairs={{0,2},{1,3},{2,0},{3,1},{4,6},{5,7},{6,4},{7,5},{8,10},{9,11},{10,... | collective-permute-start | bytes 3096584 | tf_op jit(solution)/shard_map/ppermute | solution.py:1855
  193.3 47.0 %collective-permute-start.3 = (bf16[7,96,768]{2,1,0:T(8,128)(2,1)}, bf16[7,96,768]{2,1,0:T(8,128)(2,1)}, u32[]{:S(2)}, u32[]{:S(2)}) collective-permute-start(bf16[7,96,768]{2,1,0:T(8,128)(2,1)} %get-tuple-element.74), channel_id=1, source_target_pairs={{0,4},{1,5},{2,6},{3,7},{4,0},{5,1},{6,2},{7,3},{8,12},{9,13},{10,... | collective-permute-start | bytes 3096584 | tf_op jit(solution)/shard_map/ppermute | solution.py:1855
  194.9 45.5 %collective-permute-start.4 = (bf16[7,96,768]{2,1,0:T(8,128)(2,1)}, bf16[7,96,768]{2,1,0:T(8,128)(2,1)}, u32[]{:S(2)}, u32[]{:S(2)}) collective-permute-start(bf16[7,96,768]{2,1,0:T(8,128)(2,1)} %get-tuple-element.75), channel_id=1, source_target_pairs={{0,6},{1,7},{2,4},{3,5},{4,2},{5,3},{6,0},{7,1},{8,14},{9,15},{10,... | collective-permute-start | bytes 3096584 | tf_op jit(solution)/shard_map/ppermute | solution.py:1855
  196.0 39.6 %copy-start = (bf16[2,512,768]{2,1,0:T(8,128)(2,1)S(1)}, bf16[2,512,768]{2,1,0:T(8,128)(2,1)}, u32[]{:S(2)}) copy-start(bf16[2,512,768]{2,1,0:T(8,128)(2,1)} %get-tuple-element.60) | copy-start | bytes 4718596
  308.6 3.5 %copy-start.4 = (f32[16,768]{1,0:T(8,128)S(1)}, f32[16,768]{1,0:T(8,128)}, u32[]{:S(2)}) copy-start(f32[16,768]{1,0:T(8,128)} %get-tuple-element.81) | copy-start | bytes 147460
  308.6 3.5 %copy-start.5 = (f32[288]{0:T(512)S(1)}, f32[288]{0:T(512)}, u32[]{:S(2)}) copy-start(f32[288]{0:T(512)} %param.18) | copy-start | bytes 3460
  308.6 3.5 %copy-start.6 = (f32[288]{0:T(512)S(1)}, f32[288]{0:T(512)}, u32[]{:S(2)}) copy-start(f32[288]{0:T(512)} %param.19) | copy-start | bytes 3460
  308.6 3.5 %copy-start.7 = (f32[288]{0:T(512)S(1)}, f32[288]{0:T(512)}, u32[]{:S(2)}) copy-start(f32[288]{0:T(512)} %param.20) | copy-start | bytes 3460
  308.7 4.2 %copy-start.3 = (f32[3,96,768]{2,1,0:T(8,128)S(1)}, f32[3,96,768]{2,1,0:T(8,128)}, u32[]{:S(2)}) copy-start(f32[3,96,768]{2,1,0:T(8,128)} %get-tuple-element.99) | copy-start | bytes 2654212
  308.7 5.1 %copy-start.2 = (f32[3,96,768]{2,1,0:T(8,128)S(1)}, f32[3,96,768]{2,1,0:T(8,128)}, u32[]{:S(2)}) copy-start(f32[3,96,768]{2,1,0:T(8,128)} %get-tuple-element.100) | copy-start | bytes 2654212
  308.7 6.0 %copy-start.1 = (f32[3,96,768]{2,1,0:T(8,128)S(1)}, f32[3,96,768]{2,1,0:T(8,128)}, u32[]{:S(2)}) copy-start(f32[3,96,768]{2,1,0:T(8,128)} %get-tuple-element.101) | copy-start | bytes 2654212

commit v10 on v9

--- a/solution.py
+++ b/solution.py
@@ -254,37 +254,6 @@
     ref[row : row + 1, :] += jnp.sum(value, axis=0, keepdims=True)
 
 
-def rest_spec(rest, which, single=True):
-    groups, _, rows, width = rest.shape
-    mode = pl.Buffered(1) if single else None
-    return pl.BlockSpec(
-        (groups, 1, rows, width), lambda step, info: (0, which(step) - 3, 0, 0), pipeline_mode=mode
-    )
-
-
-def fixed(shape):
-    return pl.BlockSpec(shape, lambda step, info: (0,) * len(shape), pipeline_mode=pl.Buffered(1))
-
-
-def call(kernel, name, info, grid, in_specs, out_specs, out_shape, scratch, args, flops, moved):
-    return pl.pallas_call(
-        kernel,
-        name=name,
-        grid_spec=pltpu.PrefetchScalarGridSpec(
-            num_scalar_prefetch=1,
-            grid=(grid,),
-            in_specs=in_specs,
-            out_specs=out_specs,
-            scratch_shapes=scratch,
-        ),
-        out_shape=out_shape,
-        compiler_params=pltpu.CompilerParams(vmem_limit_bytes=60 << 20),
-        cost_estimate=pl.CostEstimate(
-            flops=flops, bytes_accessed=moved, transcendentals=0
-        ),
-    )(info, *args)
-
-
 def bf16_of(*shape):
     return jax.ShapeDtypeStruct(shape, jnp.bfloat16)
 
@@ -298,112 +267,10 @@
 TN = ((0,), (0,))
 
 
-def front_kernel(
-    info,
-    ctx_ref,
-    x_ref,
-    small,
-    wo,
-    u0,
-    u1,
-    u2,
-    u3,
-    v0,
-    v1,
-    v2,
-    v3,
-    out_ref,
-    n1_ref,
-    r1_ref,
-    fit_ref,
-    hid_ref,
-    gel_ref,
-    n2_ref,
-    r2_ref,
-):
-    attn_out = wide_dot(ctx_ref[...], matrix(wo), NN) + small[2:3, :]
-    n1, r1 = normed(x_ref[0].astype(jnp.float32) + attn_out)
-    n1_ref[...] = n1
-    r1_ref[...] = jnp.broadcast_to(r1, r1_ref.shape)
-    after = n1 * small[3:4, :] + small[4:5, :]
-    ffn_in = after.astype(jnp.bfloat16)
-    fit_ref[...] = ffn_in.T
-    total = after + small[9:10, :]
-    for b, (up_w, down_w) in enumerate(((u0, v0), (u1, v1), (u2, v2), (u3, v3))):
-        up = wide_dot(ffn_in, matrix(up_w), NN) + small[5 + b : 6 + b, :]
-        square = up * up
-        bent = jnp.tanh(gelu_root * up * (1.0 + gelu_cube * square))
-        rise = 0.5 * (1.0 + bent)
-        hidden = (up * rise).astype(jnp.bfloat16)
-        hid_ref[b] = hidden
-        slope = rise + (0.5 * gelu_root) * up * (1.0 - bent * bent) * (
-            1.0 + (3.0 * gelu_cube) * square
-        )
-        gel_ref[b] = slope.astype(jnp.bfloat16)
-        total = total + wide_dot(hidden, matrix(down_w), NT)
-    n2, r2 = normed(total)
-    out_ref[0] = (n2 * small[10:11, :] + small[11:12, :]).astype(jnp.bfloat16)
-    n2_ref[...] = n2
-    r2_ref[...] = jnp.broadcast_to(r2, r2_ref.shape)
-
-
-def front(info, ctx, x_all, small, rest):
-    tokens, width = ctx.shape
-    mid = x_all.shape[1]
-    per = mid // TILE
-    steps = tokens // TILE
-
-    def arrived(t, info):
-        return (info[1 + 2 * info[0] + t // per], t % per, 0)
-
-    def rows(dtype_shape):
-        return pl.BlockSpec(dtype_shape, lambda t, info: (t, 0))
-
-    specs = [rest_spec(rest, lambda t, m=m: m) for m in range(3, 12)]
-    wide4 = pl.BlockSpec((4, TILE, width), lambda t, info: (0, t, 0))
-    flipped = pl.BlockSpec((width, TILE), lambda t, info: (0, t))
-    return call(
-        front_kernel,
-        "front",
-        info,
-        steps,
-        [
-            rows((TILE, width)),
-            pl.BlockSpec((1, TILE, width), arrived),
-            fixed(small.shape),
-            *specs,
-        ],
-        [
-            pl.BlockSpec((1, TILE, width), arrived),
-            rows((TILE, width)),
-            rows((TILE, 128)),
-            flipped,
-            wide4,
-            wide4,
-            rows((TILE, width)),
-            rows((TILE, 128)),
-        ],
-        [
-            bf16_of(2, mid, width),
-            f32_of(tokens, width),
-            f32_of(tokens, 128),
-            bf16_of(width, tokens),
-            bf16_of(4, tokens, width),
-            bf16_of(4, tokens, width),
-            f32_of(tokens, width),
-            f32_of(tokens, 128),
-        ],
-        [],
-        (ctx, x_all, small, *([rest] * 9)),
-        11_000_000_000,
-        40 << 20,
-    )
-
-
 MESH = pl.DeviceIdType.MESH
 KINDS = 3
 CHUNKS = 3
-HOOKS = (4, 5, 6)
+HOOKS = (2, 3, 7)
 PER = 3
 
 
@@ -434,15 +301,25 @@
     master_hbm,
     small_in,
     input_hbm,
+    cot_hbm,
     x_ref,
     first_ref,
-    rest_ref,
+    rest_out,
     small_ref,
     q_ref,
     k_ref,
     v_ref,
     ctx_ref,
     lse_ref,
+    cot_ref,
+    layer_ref,
+    n1_ref,
+    r1_ref,
+    n2_ref,
+    r2_ref,
+    fit_ref,
+    hid_ref,
+    gel_ref,
     raw,
     low,
     given,
@@ -455,13 +332,18 @@
     pool,
     sel,
     first,
-    weights,
+    rest_ref,
     small,
     q_s,
     k_s,
     v_s,
     ctx_s,
     kept,
+    n1_s,
+    gel_s,
+    hid_s,
+    fit_s,
+    layer_s,
     x_s,
     x_r,
     xt_s,
@@ -482,8 +364,12 @@
     r_r,
     rt_s,
     rt_r,
+    y_s,
+    y_r,
     own_sem,
     out_sem,
+    tile_sem,
+    end_sem,
 ):
     z, c, t = place_of()
     side, core, bit = t // 2, lax.rem(t, 2), lax.rem(c, 2)
@@ -696,11 +582,12 @@
         for m in range(CHUNKS * PER):
             sel[m] = pool[slots[KINDS + m]]
         rest_own.start()
-        for k in range(CHUNKS):
-            for copy in direct[k]:
-                copy.start()
-            for copy in passed[k][0]:
-                copy.start()
+        launch(0)
+        launch(1)
+
+    def launch(k):
+        for copy in (*direct[k], *passed[k][0]):
+            copy.start()
 
     def relay(k):
         for copy in direct[k]:
@@ -724,8 +611,8 @@
         sums = here if sums is None else sums + here
     small[...] = sums
     small_ref[...] = sums
-    for m in range(KINDS):
-        weights[m] = first[:, m * rows : (m + 1) * rows, :].reshape(width, width)
+    def weight(m):
+        return first[:, m * rows : (m + 1) * rows, :].reshape(width, width)
 
     def split(dst, start, value):
         low_value = value.astype(jnp.bfloat16)
@@ -740,10 +627,10 @@
             start = chunk * (mid // BLOCK) + i * (TILE // BLOCK)
             if own:
                 q_start = (chunk - 2 * core) * (mid // BLOCK) + i * (TILE // BLOCK)
-                q = wide_dot(x, weights[0], NN) + small[0:1, :]
+                q = wide_dot(x, weight(0), NN) + small[0:1, :]
                 split(q_s, q_start, q.astype(jnp.bfloat16) * jnp.bfloat16(score_scale))
-            split(k_s, start, wide_dot(x, weights[1], NN))
-            split(v_s, start, wide_dot(x, weights[2], NN) + small[1:2, :])
+            split(k_s, start, wide_dot(x, weight(1), NN))
+            split(v_s, start, wide_dot(x, weight(2), NN) + small[1:2, :])
             return carry
 
         lax.fori_loop(0, mid // TILE, one, 0)
@@ -756,12 +643,22 @@
         project(2 + a, 2 * (1 - core) + (a ^ bit), False)
         return carry
 
+    @pl.when(jnp.logical_not(stays))
+    def left():
+        x_moves[0].wait_send()
+
+    x_moves[1].wait_send()
+    take_cot = pltpu.make_async_copy(cot_hbm, given, own_sem.at[2])
+    take_cot.start()
     lax.fori_loop(0, 2, own_project, 0)
     for copy in x_over:
         copy.wait_recv()
     outs.append(pltpu.make_async_copy(x_all, x_ref, out_sem.at[1]))
     outs[1].start()
     lax.fori_loop(0, 2, other_project, 0)
+    take_cot.wait()
+    xs[0] = given[bit].astype(jnp.bfloat16)
+    xs[1] = given[1 - bit].astype(jnp.bfloat16)
     for i, (src, dst) in enumerate(((q_s, q_ref), (k_s, k_ref), (v_s, v_ref))):
         outs.append(pltpu.make_async_copy(src, dst, out_sem.at[2 + i]))
         outs[-1].start()
@@ -782,6 +679,13 @@
             @pl.when(i == HOOKS[k])
             def hook(k=k):
                 relay(k)
+                if k == 0:
+                    launch(2)
+
+        @pl.when(i == groups * subs - 1)
+        def late_hook():
+            last_relay(0)
+            last_relay(1)
 
         @pl.when(sub == 0)
         def edge_block():
@@ -840,14 +744,129 @@
             )
         )
         outs[-1].start()
-    for k in range(CHUNKS):
-        last_relay(k)
+    last_relay(2)
+
+    cot_moves = [send(xs.at[p], cot_ref.at[p], (y_s, y_r), p, goes[p]) for p in range(2)]
+    cot_keep = pltpu.make_async_copy(xs.at[0], cot_ref.at[0], own_sem.at[1])
+
+    @pl.when(stays)
+    def keep_cot():
+        cot_keep.start()
 
     @pl.when(jnp.logical_not(stays))
-    def left():
-        x_moves[0].wait_send()
-
-    x_moves[1].wait_send()
+    def leave_cot():
+        cot_moves[0].start()
+
+    cot_moves[1].start()
+
+    for k in range(2):
+        for group in passed[k]:
+            for copy in group:
+                copy.wait_recv()
+    rest_own.wait()
+    tiles = 2 * mid // TILE
+    per = mid // TILE
+
+    def held_out(m):
+        return rest_ref[:, m].reshape(width, width)
+
+    def tile_out(i, slot):
+        at = pl.ds(pl.multiple_of(i * TILE, TILE), TILE)
+        return (
+            pltpu.make_async_copy(n1_s.at[slot], n1_ref.at[at], tile_sem.at[slot]),
+            pltpu.make_async_copy(gel_s.at[slot], gel_ref.at[:, at], tile_sem.at[2 + slot]),
+        )
+
+    def rise_tile(i, carry):
+        slot = lax.rem(i, 2)
+        at = pl.ds(pl.multiple_of(i * TILE, TILE), TILE)
+        inside = pl.ds(pl.multiple_of(lax.rem(i, per) * TILE, TILE), TILE)
+
+        @pl.when(i >= 2)
+        def free():
+            for copy in tile_out(i - 2, slot):
+                copy.wait()
+
+        context = jnp.concatenate([ctx_s[g, at, :] for g in range(groups)], axis=1)
+        attn_out = wide_dot(context, held_out(0), NN) + small[2:3, :]
+        x = x_all[(i // per) ^ bit, inside, :].astype(jnp.float32)
+        n1, r1 = normed(x + attn_out)
+        n1_s[slot] = n1
+        r1_ref[at, :] = jnp.broadcast_to(r1, (TILE, r1_ref.shape[1]))
+        after = n1 * small[3:4, :] + small[4:5, :]
+        ffn_in = after.astype(jnp.bfloat16)
+        fit_s[:, at] = ffn_in.T
+        given[i // per, inside, :] = after + small[9:10, :]
+        for b in range(4):
+            up = wide_dot(ffn_in, held_out(1 + b), NN) + small[5 + b : 6 + b, :]
+            square = up * up
+            bent = jnp.tanh(gelu_root * up * (1.0 + gelu_cube * square))
+            rise = 0.5 * (1.0 + bent)
+            hid_s[b, at, :] = (up * rise).astype(jnp.bfloat16)
+            slope = rise + (0.5 * gelu_root) * up * (1.0 - bent * bent) * (
+                1.0 + (3.0 * gelu_cube) * square
+            )
+            gel_s[slot, b] = slope.astype(jnp.bfloat16)
+        for copy in tile_out(i, slot):
+            copy.start()
+        return carry
+
+    lax.fori_loop(0, tiles, rise_tile, 0)
+    for i in range(tiles - 2, tiles):
+        for copy in tile_out(i, i % 2):
+            copy.wait()
+    for i, (src, dst) in enumerate(((hid_s, hid_ref), (fit_s, fit_ref))):
+        outs.append(pltpu.make_async_copy(src, dst, out_sem.at[5 + groups + i]))
+        outs[-1].start()
+    for group in passed[2]:
+        for copy in group:
+            copy.wait_recv()
+    outs.append(pltpu.make_async_copy(rest_ref, rest_out, out_sem.at[7 + groups]))
+    outs[-1].start()
+
+    def end_out(i):
+        at = pl.ds(pl.multiple_of(i * TILE, TILE), TILE)
+        inside = pl.ds(pl.multiple_of(lax.rem(i, per) * TILE, TILE), TILE)
+        chunk = i // per
+        return (
+            pltpu.make_async_copy(given.at[chunk, inside], n2_ref.at[at], end_sem.at[i]),
+            pltpu.make_async_copy(
+                layer_s.at[chunk ^ bit, inside],
+                layer_ref.at[chunk ^ bit, inside],
+                end_sem.at[tiles + i],
+            ),
+        )
+
+    def fall_tile(i, carry):
+        at = pl.ds(pl.multiple_of(i * TILE, TILE), TILE)
+        inside = pl.ds(pl.multiple_of(lax.rem(i, per) * TILE, TILE), TILE)
+        summed = given[i // per, inside, :]
+        for b in range(4):
+            summed = summed + wide_dot(hid_s[b, at, :], held_out(5 + b), NT)
+        n2, r2 = normed(summed)
+        layer_s[(i // per) ^ bit, inside, :] = (n2 * small[10:11, :] + small[11:12, :]).astype(
+            jnp.bfloat16
+        )
+        given[i // per, inside, :] = n2
+        r2_ref[at, :] = jnp.broadcast_to(r2, (TILE, r2_ref.shape[1]))
+        for copy in end_out(i):
+            copy.start()
+        return carry
+
+    lax.fori_loop(0, tiles, fall_tile, 0)
+    for i in range(tiles):
+        for copy in end_out(i):
+            copy.wait()
+
+    @pl.when(stays)
+    def kept_cot():
+        cot_keep.wait()
+
+    @pl.when(jnp.logical_not(stays))
+    def left_cot():
+        cot_moves[0].wait()
+
+    cot_moves[1].wait()
     for copy in (*x_over, *za, *zb, *q_moves, *qt_moves, *onward):
         copy.wait_send()
     for pair in direct:
@@ -856,14 +875,13 @@
     for chunk in passed:
         for group in chunk:
             for copy in group:
-                copy.wait()
+                copy.wait_send()
     hops_sent()
-    rest_own.wait()
     for copy in outs:
         copy.wait()
 
 
-def begin(slots, local_at, table, master, small_in, inputs, n_shard, n_ctx, n_tp):
+def begin(slots, local_at, table, master, small_in, inputs, cot, n_shard, n_ctx, n_tp):
     held, rows, width = master.shape
     _, mid, _ = inputs.shape
     groups = n_ctx * n_tp
@@ -878,12 +896,18 @@
     low = jnp.bfloat16
     f32 = jnp.float32
     pairs = [2, 2, n_shard - 1, n_shard - 1, n_shard - 1, n_shard - 1, 3]
-    pairs += [4 * (n_tp - 1), 3 * CHUNKS, 4 * CHUNKS * (n_tp - 1)]
+    pairs += [4 * (n_tp - 1), 3 * CHUNKS, 4 * CHUNKS * (n_tp - 1), 2]
     return pl.pallas_call(
         functools.partial(begin_kernel, n_shard, n_ctx, n_tp),
         name="begin",
-        in_specs=[smem, smem, smem, anywhere, vmem, anywhere],
-        out_specs=[anywhere, anywhere, anywhere, vmem, anywhere, anywhere, anywhere, anywhere, vmem],
+        in_specs=[smem, smem, smem, anywhere, vmem, anywhere, anywhere],
+        out_specs=[anywhere] * 3
+        + [vmem]
+        + [anywhere] * 4
+        + [vmem]
+        + [anywhere] * 3
+        + [vmem, anywhere, vmem]
+        + [anywhere] * 3,
         out_shape=[
             bf16_of(4, mid, width),
             bf16_of(groups, long, width),
@@ -894,6 +918,15 @@
             bf16_of(packs, seq // BLOCK, BLOCK, lanes),
             bf16_of(tokens, width),
             f32_of(packs, tokens // BLOCK, lanes),
+            bf16_of(2, mid, width),
+            bf16_of(2, mid, width),
+            f32_of(tokens, width),
+            f32_of(tokens, 128),
+            f32_of(tokens, width),
+            f32_of(tokens, 128),
+            bf16_of(width, tokens),
+            bf16_of(4, tokens, width),
+            bf16_of(4, tokens, width),
         ],
         scratch_shapes=[
             pltpu.VMEM((held, rows, width), f32),
@@ -908,24 +941,31 @@
             pltpu.VMEM((n_shard * held, rows, width), low),
             pltpu.VMEM((9, rows, width), low),
             pltpu.VMEM((groups, long, width), low),
-            pltpu.VMEM((3, width, width), low),
+            pltpu.VMEM((groups, 9, rows, width), low),
             pltpu.VMEM((16, width), f32),
             pltpu.VMEM((packs, tokens // BLOCK, BLOCK, lanes), low),
             pltpu.VMEM((packs, seq // BLOCK, BLOCK, lanes), low),
             pltpu.VMEM((packs, seq // BLOCK, BLOCK, lanes), low),
             pltpu.VMEM((packs, tokens, lanes), low),
             pltpu.VMEM((seq, lanes), f32),
+            pltpu.VMEM((2, TILE, width), f32),
+            pltpu.VMEM((2, 4, TILE, width), low),
+            pltpu.VMEM((4, tokens, width), low),
+            pltpu.VMEM((width, tokens), low),
+            pltpu.VMEM((2, mid, width), low),
             *[dma((n,)) for n in pairs for _ in range(2)],
             dma((4,)),
-            dma((8,)),
+            dma((8 + packs,)),
+            dma((4,)),
+            dma((2 * (tokens // TILE),)),
         ],
         compiler_params=pltpu.CompilerParams(
-            collective_id=0, has_side_effects=True, vmem_limit_bytes=62 << 20
+            collective_id=0, has_side_effects=True, vmem_limit_bytes=64000 << 10
         ),
         cost_estimate=pl.CostEstimate(
             flops=60_000_000_000, bytes_accessed=60 << 20, transcendentals=16_000_000
         ),
-    )(slots, local_at, table, master, small_in, inputs)
+    )(slots, local_at, table, master, small_in, inputs, cot)
 
 
 NEAR = 2
@@ -936,8 +976,7 @@
     n_tp,
     n2_hbm,
     r2_ref,
-    cot0_ref,
-    cot1_ref,
+    cots_ref,
     hid_ref,
     gel_ref,
     fit_ref,
@@ -1022,12 +1061,12 @@
         sums_ref[...] = jnp.zeros_like(sums_ref)
         take.wait()
         mid = tokens // 2
-        for p, cot_ref in enumerate((cot0_ref, cot1_ref)):
-
-            def one(i, carry, p=p, cot_ref=cot_ref):
+        for p in range(2):
+
+            def one(i, carry, p=p):
                 inside = pl.ds(pl.multiple_of(i * TILE, TILE), TILE)
                 at = pl.ds(pl.multiple_of((p ^ bit) * mid + i * TILE, TILE), TILE)
-                cot = cot_ref[inside, :].astype(jnp.float32)
+                cot = cots_ref[p, inside, :].astype(jnp.float32)
                 n2 = gy[at, :]
                 add_row(sums_ref, 10, cot * n2)
                 add_row(sums_ref, 11, cot)
@@ -1215,8 +1254,7 @@
         in_specs=[
             pl.BlockSpec(memory_space=pl.ANY),
             whole((tokens, 128)),
-            whole((tokens // 2, width)),
-            whole((tokens // 2, width)),
+            whole((2, tokens // 2, width)),
             pl.BlockSpec((1, tokens, width), block),
             pl.BlockSpec((1, tokens, width), block),
             whole((width, tokens)),
@@ -1268,7 +1306,7 @@
         cost_estimate=pl.CostEstimate(
             flops=22_000_000_000, bytes_accessed=40 << 20, transcendentals=0
         ),
-    )(n2, r2, *cots, hid, gel, fit, n1, r1, ctx, small, rest, rest, rest, layer)
+    )(n2, r2, cots, hid, gel, fit, n1, r1, ctx, small, rest, rest, rest, layer)
 
 
 LATE = 3
@@ -1526,12 +1564,12 @@
     weight_grad(2, slice(None), dv_s)
     exchange(2)
     meet(1)
+    for h in range(1, n_shard - 2):
+        hop(h)
     loads[3].wait()
     weight_grad(0, pl.ds(pl.multiple_of(core * tokens, tokens), tokens), dq_s)
     exchange(0)
     meet(2)
-    for h in range(1, n_shard - 2):
-        hop(h)
 
     row = lax.broadcasted_iota(jnp.int32, small_ref.shape, 0)
     q_sum = jnp.sum(dq_s[...].astype(jnp.float32), axis=0, keepdims=True)
@@ -1560,6 +1598,8 @@
         over_moves.append(copy)
         if b == 0:
             meet(0)
+            if n_shard > 2:
+                hop(n_shard - 2)
 
     value = small_s[...]
     for dt, copy in enumerate(small_core):
@@ -1572,8 +1612,6 @@
     for copy in small_plane:
         copy.start()
 
-    if n_shard > 2:
-        hop(n_shard - 2)
     loads[5].wait()
     stays = c // 2 == core
     home_moves = []
@@ -1786,17 +1824,6 @@
     )(holder, late_at, x_all, dq, dk, dv, gh1, first, *early, small, master, one, two)
 
 
-def moves(n_ctx, n_tp, pick):
-    pairs = []
-    for c in range(n_ctx):
-        for t in range(n_tp):
-            side, core = t // 2, t % 2
-            to_ctx = 2 * core + (pick ^ (c & 1))
-            to_tp = 2 * side + c // 2
-            pairs.append((c * n_tp + t, to_ctx * n_tp + to_tp))
-    return pairs
-
-
 def shards(
     inputs,
     cotangent,
@@ -1817,19 +1844,10 @@
     span = small_params.shape[0]
     my_ctx = lax.axis_index("ctx")
     my_tp = lax.axis_index("tp")
-    parity = lax.rem(my_ctx, 2)
     half = lax.rem(my_tp, 2)
     plane = ("ctx", "tp")
-    forth = [moves(n_ctx, n_tp, pick) for pick in range(2)]
-
-    arrival = [(b ^ parity) + 2 * (half ^ (j // 2)) for j, b in enumerate((0, 1, 0, 1))]
-    info = jnp.stack([half, *arrival]).astype(jnp.int32)
-    half_one = info[:1]
-
-    def sent(field, pick):
-        low = field.astype(jnp.bfloat16)
-        return jnp.where(parity == 0, low[pick], low[1 - pick])
-
+
+    half_one = half.astype(jnp.int32).reshape(1)
     my_shard = lax.axis_index("shard")
     start = ((my_shard * n_ctx + my_ctx) * n_tp + my_tp) * span
     lone = lax.dynamic_update_slice(
@@ -1837,14 +1855,20 @@
     ).reshape(16, width)
     local_at = slot_of[:LATE] - my_shard * held
     local_at = jnp.where((local_at >= 0) & (local_at < held), local_at, held)
-    x_all, first, rest, small, q, k, v, context, lse = begin(
-        slot_of, local_at, rand_blocks, master, lone, inputs, n_shard, n_ctx, n_tp
+    begun = begin(
+        slot_of,
+        local_at,
+        rand_blocks,
+        master,
+        lone,
+        inputs,
+        cotangent,
+        n_shard,
+        n_ctx,
+        n_tp,
     )
-    cots, context = lax.optimization_barrier(
-        ([sent(cotangent, pick) for pick in range(2)], context)
-    )
-    cots = [lax.ppermute(cots[pick], plane, forth[pick]) for pick in range(2)]
-    out_low, n1, r1, fit, hid, gel, n2, r2 = front(info, context, x_all, small, rest)
+    x_all, first, rest, small, q, k, v, context, lse = begun[:9]
+    cots, out_low, n1, r1, n2, r2, fit, hid, gel = begun[9:]
     *early, gh1, dctx, sums, layer_home = back(
         n2, r2, cots, hid, gel, fit, n1, r1, context, small, rest, out_low, n_ctx, n_tp
     )

time: 322 us -> 312 us (0.969)
  the two profiles are of different devices: /device:TPU:0 before, /device:TPU:1 now
where the time goes in v10:
time: 312 us; the launch traced here: 308 us
  Pallas kernels  290 us (93%)
  other arithmetic  7.98 us (3%)
  local copies, waits for them, and re-layouts  5.9 us (2%)
    pallas_call x1, Pallas kernels, begin(): pl.pallas_call(functools.partial(begin_kernel, n_shard, n_ctx, n_tp), nam...  128 us
    pallas_call x1, Pallas kernels, finish(): pl.pallas_call(functools.partial(finish_kernel, n_shard, n_ctx, n_tp), na...  63.4 us
    pallas_call x1, Pallas kernels, back(): pl.pallas_call(functools.partial(back_kernel, n_ctx, n_tp), name='back',...  49.9 us
    pallas_call x1, Pallas kernels, attend_back(): pl.pallas_call(functools.partial(attend_back_kernel, unroll), grid_spec=s...  48.9 us
  transfers between devices with their start and end apart: 3, of which 0 were waited for; matrix products, arithmetic and copies ran while one was open for 1% of the time, Pallas kernels for 16%

profile of v10, /device:TPU:1, one launch (start us, length us, event | category | flops | bytes accessed | tf_op | source)
XLA Modules:
  0.0 307.7 jit_solution(5192835770546059240)
XLA Ops:
  0.7 0.9 dynamic_update_slice.3
  1.6 0.6 reshape.33.small_in
  2.2 1.6 copy.21.table.table_ref
  3.8 1.2 and_select_fusion.local_at
  4.9 127.9 %begin.1 = (bf16[4,512,768]{2,1,0:T(8,128)(2,1)}, bf16[8,320,768]{2,1,0:T(8,128)(2,1)}, bf16[8,9,96,768]{3,2,1,0:T(8,128)(2,1)}, f32[16,768]{1,0:T(8,128)}, bf16...) custom-call(s32[12]{0:T(128)} %slots.1, ...), custom_call_target="tpu_custom_call" | custom-call | flops 60000002048 | bytes 62914560 | tf_op jit(solution)/shard_map/begin/pallas_call | solution.py:900
  132.8 49.9 %back.1 = (bf16[9,96,768]{2,1,0:T(8,128)(2,1)}, bf16[3,2,96,768]{3,2,1,0:T(8,128)(2,1)}, bf16[7,96,768]{2,1,0:T(8,128)(2,1)}, bf16[7,96,768]{2,1,0:T(8,128)(2,1)...) custom-call(f32[1024,768]{1,0:T(8,128)} %get-tuple-element.43.n2_hbm, ...), custom_call_target="tpu_custom_call" | custom-call | flops 22000001024 | bytes 41943040 | tf_op jit(solution)/shard_map/back/pallas_call | solution.py:1250
  182.7 0.1 collective-permute-start
  182.8 0.6 collective-permute-start.1
  183.4 2.1 collective-permute-start.2
  185.4 0.0 copy-start
  185.4 48.9 %attend_back.1 = (bf16[1024,768]{1,0:T(8,128)(2,1)}, bf16[2048,768]{1,0:T(8,128)(2,1)}, bf16[2048,768]{1,0:T(8,128)(2,1)}) custom-call(s32[1]{0:T(128)} %bitcast.half_ref, s32[12,30,3]{2,1,0:T(8,128)} %copy.21.table.table_ref, bf16[3,16,64,256]{3,2,1,0:T(8,128)(2,1)} %get-tuple-element.57.q_ref, bf16[3,32,64,256]{3,2,1,0:T(8,128)(2,1)} %get-tuple-element.58.k_ref, ...), custom_call_target="tpu_custom_call" | custom-call | flops 120000004096 | bytes 25165824 | tf_op jit(solution)/shard_map/attend_back/pallas_call | solution.py:213
  234.3 0.0 copy-start.8
  234.4 0.0 copy-start.9
  234.4 0.0 copy-done
  234.4 1.9 convert_element_type.6
  236.3 0.0 copy-done.8
  236.3 0.1 iota_compare_fusion
  236.4 0.1 select_reduce_fusion.1
  236.4 0.0 copy-done.9
  236.5 0.1 select_reduce_fusion
  236.5 0.5 broadcast_add_fusion
  237.1 0.0 collective-permute-done.e1_hbm
  237.1 0.0 collective-permute-done.1.e2_hbm
  237.1 0.0 collective-permute-done.2.e3_hbm
  237.1 63.4 %finish.1 = (bf16[2,512,768]{2,1,0:T(8,128)(2,1)}, f32[3,96,768]{2,1,0:T(8,128)}, f32[3,96,768]{2,1,0:T(8,128)}, f32[3,96,768]{2,1,0:T(8,128)}, f32[16,768]{1,0:T(8,128)}) custom-call(s32[12]{0:T(128)} %get-tuple-element.82.holder, s32[12]{0:T(128)} %get-tuple-element.81.late_at, bf16[4,512,768]{2,1,0:T(8,128)(2,1)} %get-tuple-element.56.x_hbm, ...), custom_call_target="tpu_custom_call" | custom-call | flops 12000000000 | bytes 41943040 | tf_op jit(solution)/shard_map/finish/pallas_call | solution.py:1806
  300.5 0.0 copy-start.4
  300.5 0.0 copy-start.5
  300.5 0.0 copy-start.6
  300.5 0.0 copy-start.7
  300.5 0.0 copy-start.3
  300.6 0.0 copy-start.2
  300.6 0.0 copy-start.1
  300.6 3.5 %convert_element_type.7 = f32[2,512,768]{2,1,0:T(8,128)} convert(bf16[2,512,768]{2,1,0:T(8,128)(2,1)} %get-tuple-element.73) | non-fusion elementwise | flops 786432 | bytes 4718592 | tf_op jit(solution)/shard_map/convert_element_type | solution.py:1906
  304.0 0.0 copy-done.4
  304.0 0.0 copy-done.5
  304.0 0.0 copy-done.6
  304.1 0.0 copy-done.7
  304.1 0.7 multiply_subtract_fusion
  304.7 0.0 copy-done.3
  304.7 0.9 copy.29
  305.7 0.0 copy-done.2
  305.7 0.9 copy.30
  306.6 0.0 copy-done.1
  306.6 0.9 copy.31
  (3 shorter events, 0.0 us)
Async XLA Ops:
  182.7 54.3 %collective-permute-start = (bf16[7,96,768]{2,1,0:T(8,128)(2,1)}, bf16[7,96,768]{2,1,0:T(8,128)(2,1)}, u32[]{:S(2)}, u32[]{:S(2)}) collective-permute-start(bf16[7,96,768]{2,1,0:T(8,128)(2,1)} %get-tuple-element.69), channel_id=1, source_target_pairs={{0,2},{1,3},{2,0},{3,1},{4,6},{5,7},{6,4},{7,5},{8,10},{9,11},{10,... | collective-permute-start | bytes 3096584 | tf_op jit(solution)/shard_map/ppermute | solution.py:1879
  182.8 54.3 %collective-permute-start.1 = (bf16[7,96,768]{2,1,0:T(8,128)(2,1)}, bf16[7,96,768]{2,1,0:T(8,128)(2,1)}, u32[]{:S(2)}, u32[]{:S(2)}) collective-permute-start(bf16[7,96,768]{2,1,0:T(8,128)(2,1)} %get-tuple-element.70), channel_id=1, source_target_pairs={{0,4},{1,5},{2,6},{3,7},{4,0},{5,1},{6,2},{7,3},{8,12},{9,13},{10,... | collective-permute-start | bytes 3096584 | tf_op jit(solution)/shard_map/ppermute | solution.py:1879
  183.4 53.7 %collective-permute-start.2 = (bf16[7,96,768]{2,1,0:T(8,128)(2,1)}, bf16[7,96,768]{2,1,0:T(8,128)(2,1)}, u32[]{:S(2)}, u32[]{:S(2)}) collective-permute-start(bf16[7,96,768]{2,1,0:T(8,128)(2,1)} %get-tuple-element.71), channel_id=1, source_target_pairs={{0,6},{1,7},{2,4},{3,5},{4,2},{5,3},{6,0},{7,1},{8,14},{9,15},{10,... | collective-permute-start | bytes 3096584 | tf_op jit(solution)/shard_map/ppermute | solution.py:1879
  185.4 48.9 %copy-start = (bf16[2,512,768]{2,1,0:T(8,128)(2,1)S(1)}, bf16[2,512,768]{2,1,0:T(8,128)(2,1)}, u32[]{:S(2)}) copy-start(bf16[2,512,768]{2,1,0:T(8,128)(2,1)} %get-tuple-element.55) | copy-start | bytes 4718596
  234.3 1.9 copy-start.8
  234.4 2.1 copy-start.9
  300.5 3.5 %copy-start.4 = (f32[16,768]{1,0:T(8,128)S(1)}, f32[16,768]{1,0:T(8,128)}, u32[]{:S(2)}) copy-start(f32[16,768]{1,0:T(8,128)} %get-tuple-element.77) | copy-start | bytes 147460
  300.5 3.5 %copy-start.5 = (f32[288]{0:T(512)S(1)}, f32[288]{0:T(512)}, u32[]{:S(2)}) copy-start(f32[288]{0:T(512)} %param.18) | copy-start | bytes 3460
  300.5 3.5 %copy-start.6 = (f32[288]{0:T(512)S(1)}, f32[288]{0:T(512)}, u32[]{:S(2)}) copy-start(f32[288]{0:T(512)} %param.19) | copy-start | bytes 3460
  300.5 3.5 %copy-start.7 = (f32[288]{0:T(512)S(1)}, f32[288]{0:T(512)}, u32[]{:S(2)}) copy-start(f32[288]{0:T(512)} %param.20) | copy-start | bytes 3460
  300.5 4.2 %copy-start.3 = (f32[3,96,768]{2,1,0:T(8,128)S(1)}, f32[3,96,768]{2,1,0:T(8,128)}, u32[]{:S(2)}) copy-start(f32[3,96,768]{2,1,0:T(8,128)} %get-tuple-element.93) | copy-start | bytes 2654212
  300.6 5.1 %copy-start.2 = (f32[3,96,768]{2,1,0:T(8,128)S(1)}, f32[3,96,768]{2,1,0:T(8,128)}, u32[]{:S(2)}) copy-start(f32[3,96,768]{2,1,0:T(8,128)} %get-tuple-element.94) | copy-start | bytes 2654212
  300.6 6.0 %copy-start.1 = (f32[3,96,768]{2,1,0:T(8,128)S(1)}, f32[3,96,768]{2,1,0:T(8,128)}, u32[]{:S(2)}) copy-start(f32[3,96,768]{2,1,0:T(8,128)} %get-tuple-element.95) | copy-start | bytes 2654212
